TPU v7x, 32 devices: a whole 2x2x4 slice. The times are simulated.
32 devices in a mesh: wide: 8 (over z, y), narrow: 4 (over x, core).
Axes of the slice: x: 2, y: 2, z: 4, core: 2. Of those that a mesh axis runs over, the one named last changes fastest.
Arguments:
- tokens: bfloat16 [64, 512, 768], P(('wide', 'narrow')), may hold values from -6 to 6
- segment_ids: int32 [64, 512], P(('wide', 'narrow')), may hold values from 0 to 3, never falling along the last dimension, each value on 1 to 256 neighbouring positions
- cotangent: bfloat16 [64, 512, 768], P(('wide', 'narrow')), may hold values from -6 to 6
- blocks: float32 [12, 768, 768], P(None, ('wide', 'narrow'))
- vectors: float32 [13, 768], P(None, ('wide', 'narrow'))
- stat_left: float32 [32, 768, 768], P(('wide', 'narrow'))
- stat_right: float32 [32, 768, 768], P(('wide', 'narrow'))
- root_left: float32 [32, 768, 768], P(('wide', 'narrow'))
- root_right: float32 [32, 768, 768], P(('wide', 'narrow'))
- vec_stat: float32 [13, 768], P(None, ('wide', 'narrow')), may hold values from 0.5 to 4
- owners: int32 [12], replicated, may hold values from 0 to 31, as said below
Outputs:
- output: bfloat16 [64, 512, 768], P(('wide', 'narrow'))
- grad_tokens: bfloat16 [64, 512, 768], P(('wide', 'narrow'))
- clipped_blocks: float32 [12, 768, 768], P(None, ('wide', 'narrow'))
- clipped_vectors: float32 [13, 768], P(None, ('wide', 'narrow'))
- grad_norm: float32 [], replicated
- new_left: float32 [32, 768, 768], P(('wide', 'narrow'))
- new_right: float32 [32, 768, 768], P(('wide', 'narrow'))
- new_vec_stat: float32 [13, 768], P(None, ('wide', 'narrow'))
- new_blocks: float32 [12, 768, 768], P(None, ('wide', 'narrow'))
- new_vectors: float32 [13, 768], P(None, ('wide', 'narrow'))
- blocks_copy: bfloat16 [12, 768, 768], P(None, ('wide', 'narrow'))
- vectors_copy: bfloat16 [13, 768], P(None, ('wide', 'narrow'))
Inputs may be any that keep to these rules, and one draw needn't show every extreme that they name: `owners`: distinct device numbers; device 0 and device 32 - 1 are always among them. `segment_ids`: within each row never falling, each segment at most 256 tokens.
All inputs are finite; a program needn't handle non-finite values.
Results may differ from a plain program's by a relative error of at most 0.007.
The roundings to bfloat16 on the way count: a program that leaves them out, or rounds other values in their place, can miss the bound.
Values may be sent and summed in bfloat16 or wider, within the bound.
No kernel may reach another device: no remote copies, remote signals or barrier semaphores. Data moves between devices by JAX's collectives and lax.ppermute only.
A program may use at most 256 MiB of HBM per device.

v0:
```python
import functools
import math

import jax
import jax.numpy as jnp
from jax import lax
from jax.experimental import pallas as pl
from jax.experimental.pallas import tpu as pltpu
from jax.sharding import PartitionSpec as P

H = 12
FF = 3072
ROT = 16
NPARAM = 7087872
LONGEST = 256

clip_level = 1.0
matrix_rate = 0.03
vector_rate = 0.2
decay_beta = 0.5
norm_epsilon = 1e-05

f32 = jnp.float32
bf16 = jnp.bfloat16
AXES = ("wide", "narrow")
LANES = 128
MIB = 2**20

NN = (((1,), (0,)), ((), ()))
NT = (((1,), (1,)), ((), ()))
TN = (((0,), (0,)), ((), ()))


def mm(left, right, dims):
    return lax.dot_general(left, right, dims, preferred_element_type=f32)


def call(body, flops, moved, vmem=60, after=(), **rest):
    spec = rest.pop("grid_spec", None)
    grid = spec.grid if spec is not None else rest.get("grid", ())
    later = len(after)
    if later:
        held = [pl.BlockSpec(memory_space=pl.ANY)] * later
        if spec is not None:
            first = spec.num_scalar_prefetch + len(spec.in_specs)
            spec = pltpu.PrefetchScalarGridSpec(
                num_scalar_prefetch=spec.num_scalar_prefetch,
                grid=spec.grid,
                in_specs=list(spec.in_specs) + held,
                out_specs=spec.out_specs,
                scratch_shapes=spec.scratch_shapes,
            )
        else:
            first = len(rest["in_specs"])
            rest["in_specs"] = list(rest["in_specs"]) + held
        inner = body

        def body(*refs):
            inner(*refs[:first], *refs[first + later :])

    if spec is not None:
        rest["grid_spec"] = spec
    made = pl.pallas_call(
        body,
        compiler_params=pltpu.CompilerParams(
            vmem_limit_bytes=vmem * MIB,
            dimension_semantics=("arbitrary",) * len(grid),
        ),
        cost_estimate=pl.CostEstimate(
            flops=int(flops), bytes_accessed=int(moved), transcendentals=0
        ),
        **rest,
    )
    return lambda *operands: made(*operands, *after)


def sub_sum(values):
    return jnp.sum(values.reshape(-1, 8, values.shape[-1]), axis=0)


def rotary_tables(segment_ids):
    rows, length = segment_ids.shape
    start = jnp.sum(
        (segment_ids[:, None, :] < segment_ids[:, :, None]).astype(jnp.int32), axis=-1
    )
    offset = (jnp.arange(length, dtype=jnp.int32)[None] - start).astype(f32).reshape(-1, 1)
    half = ROT // 2
    lane = jnp.arange(LANES) % 64
    rates = jnp.power(10000.0, -2.0 * jnp.arange(half, dtype=f32) / ROT)
    angle = offset * jnp.where(lane < ROT, rates[lane % half], 0.0)[None]
    cosine, sine = jnp.cos(angle), jnp.sin(angle)
    first = jnp.where(lane[None] < half, -sine, 0.0)
    second = jnp.where((lane[None] >= half) & (lane[None] < ROT), sine, 0.0)
    return cosine, first, second


def rotate(values, cosine, first, second):
    parts = []
    for at in range(0, values.shape[1], LANES):
        part = values[:, at : at + LANES]
        parts.append(
            part * cosine
            + pltpu.roll(part, LANES - ROT // 2, 1) * first
            + pltpu.roll(part, ROT // 2, 1) * second
        )
    return jnp.concatenate(parts, axis=1)


def rotate_back(values, cosine, first, second):
    return (
        values * cosine
        - pltpu.roll(values, LANES - ROT // 2, 1) * first
        - pltpu.roll(values, ROT // 2, 1) * second
    )


def project_body(a1_ref, dy_ref, w_ref, vec_ref, c_ref, a_ref, b_ref, q_ref, k_ref, v_ref, do_ref):
    a1, tables = a1_ref[...], (c_ref[...], a_ref[...], b_ref[...])
    q_ref[...] = rotate(mm(a1, w_ref[0], NN) + vec_ref[4:5, :], *tables).astype(bf16)
    k_ref[...] = rotate(mm(a1, w_ref[1], NN) + vec_ref[5:6, :], *tables).astype(bf16)
    v_ref[...] = (mm(a1, w_ref[2], NN) + vec_ref[6:7, :]).astype(bf16)
    do_ref[...] = mm(dy_ref[...], w_ref[3], NT).astype(bf16)


def project(a1, dy, weights, vecs, tables, after=(), step=256):
    count, width = a1.shape
    token = pl.BlockSpec((step, width), lambda i: (i, 0))
    table = pl.BlockSpec((step, LANES), lambda i: (i, 0))
    return call(
        project_body,
        8 * count * width * width,
        12 * count * width + 8 * width * width,
        grid=(count // step,),
        in_specs=[
            token,
            token,
            pl.BlockSpec((4, width, width), lambda i: (0, 0, 0)),
            pl.BlockSpec(vecs.shape, lambda i: (0, 0)),
            table,
            table,
            table,
        ],
        out_specs=[token] * 4,
        out_shape=[jax.ShapeDtypeStruct((count, width), bf16)] * 4,
    )(a1, dy, weights, vecs, *tables)


def attend_body(
    col_ref, row_ref, q_ref, k_ref, v_ref, do_ref, c_ref, a_ref, b_ref,
    o_ref, g_ref, sum_ref, mask_ref, dk_acc, dv_acc, *, block,
):
    length = q_ref.shape[0]
    steps = length // block

    def reach(i):
        return max(0, (i * block - (LONGEST - 1)) // block * block), (i + 1) * block

    @pl.when(pl.program_id(1) == 0)
    def _():
        for i in range(steps):
            lo, hi = reach(i)
            key = lax.broadcasted_iota(jnp.int32, (hi - lo, block), 0) + lo
            query = lax.broadcasted_iota(jnp.int32, (hi - lo, block), 1) + i * block
            same = col_ref[lo:hi, :] == row_ref[0, :, i * block : hi]
            mask = jnp.where(same & (key <= query), 0.0, -jnp.inf)
            mask_ref[i, 0 : hi - lo, 0:block] = mask
            mask_ref[i, 0 : hi - lo, block:] = mask

    low = lax.broadcasted_iota(jnp.int32, (1, LANES), 1) < 64
    eighth = jnp.asarray(0.125, bf16)
    zero = jnp.zeros((), bf16)
    keys, values, grads = k_ref[...], v_ref[...], do_ref[...]
    queries = q_ref[...] * eighth
    keys_t, values_t = (keys * eighth).T, values.T

    def both(part):
        return jnp.concatenate([jnp.where(low, part, zero), jnp.where(low, zero, part)], axis=0)

    def unstack(part):
        return jnp.concatenate([part[0:64, 0:block], part[64:, block:]], axis=0).T

    dk_acc[...] = jnp.zeros_like(dk_acc)
    dv_acc[...] = jnp.zeros_like(dv_acc)
    q_sum = jnp.zeros((8, LANES), f32)
    for i in range(steps):
        lo, hi = reach(i)
        here = slice(i * block, hi)
        q2, do2 = both(queries[here]), both(grads[here])
        scores = mm(keys[lo:hi], q2, NT) + mask_ref[i, 0 : hi - lo, :]
        raised = jnp.exp(scores - jnp.max(scores, axis=0, keepdims=True))
        soft = raised * (1.0 / jnp.sum(raised, axis=0, keepdims=True))
        d_soft = mm(values[lo:hi], do2, NT)
        inner = jnp.sum(soft * d_soft, axis=0, keepdims=True)
        soft_low = soft.astype(bf16)
        d_scores = (soft * (d_soft - inner)).astype(bf16)
        o_ref[here, :] = unstack(mm(values_t[:, lo:hi], soft_low, NN)).astype(bf16)
        dq = rotate_back(
            unstack(mm(keys_t[:, lo:hi], d_scores, NN)), c_ref[here, :], a_ref[here, :], b_ref[here, :]
        ).astype(bf16)
        g_ref[0, here, :] = dq
        q_sum = q_sum + sub_sum(dq.astype(f32))
        dk_acc[lo:hi, :] += mm(d_scores, q2, NN)
        dv_acc[lo:hi, :] += mm(soft_low, do2, NN)
    dk = rotate_back(dk_acc[...], c_ref[...], a_ref[...], b_ref[...]).astype(bf16)
    dv = dv_acc[...].astype(bf16)
    g_ref[1] = dk
    g_ref[2] = dv
    sum_ref[0] = q_sum
    sum_ref[1] = sub_sum(dk.astype(f32))
    sum_ref[2] = sub_sum(dv.astype(f32))


def attend(segment_ids, q, k, v, do, tables, block=256):
    rows, length = segment_ids.shape
    count, width = q.shape
    block = min(block, length)
    token = pl.BlockSpec((length, LANES), lambda r, h: (r, h))
    table = pl.BlockSpec((length, LANES), lambda r, h: (r, 0))
    return call(
        functools.partial(attend_body, block=block),
        24 * count * length * width,
        24 * count * width,
        grid=(rows, width // LANES),
        in_specs=[
            pl.BlockSpec((length, 1), lambda r, h: (r, 0)),
            pl.BlockSpec((1, 1, length), lambda r, h: (r, 0, 0)),
            token,
            token,
            token,
            token,
            table,
            table,
            table,
        ],
        out_specs=[
            token,
            pl.BlockSpec((3, length, LANES), lambda r, h: (0, r, h)),
            pl.BlockSpec((3, 8, LANES), lambda r, h: (0, r, h)),
        ],
        out_shape=[
            jax.ShapeDtypeStruct((count, width), bf16),
            jax.ShapeDtypeStruct((3, count, width), bf16),
            jax.ShapeDtypeStruct((3, 8 * rows, width), f32),
        ],
        scratch_shapes=[
            pltpu.VMEM((length // block, length, 2 * block), f32),
            pltpu.VMEM((length, LANES), f32),
            pltpu.VMEM((length, LANES), f32),
        ],
    )(
        segment_ids.reshape(-1, 1),
        segment_ids.reshape(rows, 1, length),
        q,
        k,
        v,
        do,
        *tables,
    )


def half_grads_body(place_ref, *refs, first):
    l1o, l1p, l2o, l2p, r1o, r1p, r2o, r2p, ka_ref, sa_ref, kb_ref, sb_ref, acc = refs
    n = pl.program_id(0)
    y, x = place_ref[1], place_ref[2]
    half = ka_ref.shape[-1]

    @pl.when(n < first)
    def _():
        acc[...] = (mm(l1o[...], r1o[0], TN) + mm(l1p[...], r1p[0], TN)).reshape(acc.shape)

    @pl.when(n >= first)
    def _():
        acc[...] = (mm(l2o[0], r2o[...], TN) + mm(l2p[0], r2p[...], TN)).reshape(acc.shape)

    for ref, at in ((ka_ref, x), (sa_ref, 1 - x)):
        ref[0] = acc[:, :, at, :, :, :half].astype(ref.dtype)
    for ref, at in ((kb_ref, y), (sb_ref, 1 - y)):
        ref[0] = acc[:, at, :, :, :, half:].astype(ref.dtype)


def half_grads(place, left_one, left_two, right_one, right_two, shard, after=()):
    count, width = left_one[0].shape
    first, second = right_one[0].shape[0], left_two[0].shape[0]
    half = width // 2
    blocks = first + second
    one = pl.BlockSpec((count, half), lambda n, s: (0, s[3]))
    two = pl.BlockSpec((1, count, half), lambda n, s: (jnp.maximum(n - first, 0), 0, s[3]))
    part = pl.BlockSpec((1, 2, 2, 2, shard, half), lambda n, s: (n, 0, 0, 0, 0, 0))
    shape = (blocks, 2, 2, 2, shard, half)
    return call(
        functools.partial(half_grads_body, first=first),
        blocks * 2 * count * width * width,
        blocks * 4 * count * width,
        after=after,
        grid_spec=pltpu.PrefetchScalarGridSpec(
            num_scalar_prefetch=1,
            grid=(blocks,),
            in_specs=[one, one, two, two]
            + [pl.BlockSpec((1, count, width), lambda n, s: (jnp.minimum(n, first - 1), 0, 0))] * 2
            + [pl.BlockSpec((count, width), lambda n, s: (0, 0))] * 2,
            out_specs=[part] * 4,
            scratch_shapes=[pltpu.VMEM((2, 2, 2, 2, shard, width), f32)],
        ),
        out_shape=[jax.ShapeDtypeStruct(shape, k) for k in (f32, bf16, f32, bf16)],
    )(place, *left_one, *left_two, *right_one, *right_two)


def full_grads(left_one, left_two, right_one, right_two):
    one = jnp.einsum("td,nte->nde", left_one, right_one, preferred_element_type=f32)
    two = jnp.einsum("ntd,te->nde", left_two, right_two, preferred_element_type=f32)
    return jnp.concatenate([one, two], axis=0)


def gelu_parts(u):
    raised = jnp.exp(-0.5 * (u * u))
    t = 1.0 / (1.0 + (0.3275911 * math.sqrt(0.5)) * jnp.abs(u))
    poly = 1.061405429 * t - 1.453152027
    poly = poly * t + 1.421413741
    poly = poly * t - 0.284496736
    poly = (poly * t + 0.254829592) * t
    tail = 0.5 * poly * raised
    return jnp.where(u < 0, tail, 1.0 - tail), raised * (1.0 / math.sqrt(2.0 * math.pi))


def hidden_body(a2_ref, dy_ref, wu_ref, wd_ref, bu_ref, e_ref, du_ref, sum_ref):
    u = mm(a2_ref[...], wu_ref[0], NN) + bu_ref[0]
    de = mm(dy_ref[...], wd_ref[0], NT)
    dist, density = gelu_parts(u)
    e_ref[0] = (u * dist).astype(bf16)
    du = (de * (dist + u * density)).astype(bf16)
    du_ref[0] = du
    part = sub_sum(du.astype(f32))

    @pl.when(pl.program_id(1) == 0)
    def _():
        sum_ref[0] = part

    @pl.when(pl.program_id(1) > 0)
    def _():
        sum_ref[0] += part


def hidden(first, blocks, a2, dy, weights, vecs, after=(), step=512):
    count, width = a2.shape
    splits = weights.shape[0] // 2
    token = pl.BlockSpec((step, width), lambda j, i: (i, 0))
    out = pl.BlockSpec((1, step, width), lambda j, i: (j, i, 0))
    return call(
        hidden_body,
        blocks * 4 * count * width * width,
        blocks * (8 * count * width + 4 * width * width),
        after=after,
        grid=(blocks, count // step),
        in_specs=[
            token,
            token,
            pl.BlockSpec((1, width, width), lambda j, i: (first + j, 0, 0)),
            pl.BlockSpec((1, width, width), lambda j, i: (splits + first + j, 0, 0)),
            pl.BlockSpec((1, 1, width), lambda j, i: (8 + first + j, 0, 0)),
        ],
        out_specs=[out, out, pl.BlockSpec((1, 8, width), lambda j, i: (j, 0, 0))],
        out_shape=[
            jax.ShapeDtypeStruct((blocks, count, width), bf16),
            jax.ShapeDtypeStruct((blocks, count, width), bf16),
            jax.ShapeDtypeStruct((blocks, 8, width), f32),
        ],
    )(a2, dy, weights, weights, vecs[:, None, :])


def norm_back(grad, unit, scale, gain):
    grad = grad * gain
    first = jnp.mean(grad, axis=1, keepdims=True)
    second = jnp.mean(grad * unit, axis=1, keepdims=True)
    return scale * (grad - first - unit * second)


def hidden_sum(hidden_refs, w_ref, at, dims, acc):
    for ref in hidden_refs:
        for m in range(ref.shape[0]):
            part = mm(ref[m], w_ref[at], dims)
            acc = part if acc is None else acc + part
            at += 1
    return acc


def output_body(x_ref, o_ref, *refs, splits):
    *e_refs, wo_ref, wm_ref, vec_ref, out_ref = refs
    acc = hidden_sum(e_refs, wm_ref, 0, NN, mm(o_ref[...], wo_ref[0], NN))
    bias = vec_ref[7:8, :] + vec_ref[8 + splits : 9 + splits, :]
    out_ref[...] = (x_ref[...].astype(f32) + acc + bias).astype(bf16)


def resident(blocks, width, at):
    return pl.BlockSpec((blocks, width, width), lambda i: (at, 0, 0), pipeline_mode=pl.Buffered(1))


def stacked(value, step):
    return pl.BlockSpec((value.shape[0], step, value.shape[2]), lambda i: (0, i, 0))


def output(x, o, es, wa, wm, vecs, after=(), step=256):
    count, width = x.shape
    splits = wm.shape[0] // 2
    token = pl.BlockSpec((step, width), lambda i: (i, 0))
    return call(
        functools.partial(output_body, splits=splits),
        10 * count * width * width,
        14 * count * width + 10 * width * width,
        after=after,
        grid=(count // step,),
        in_specs=[token, token]
        + [stacked(e, step) for e in es]
        + [resident(1, width, 3), resident(splits, width, 1), pl.BlockSpec(vecs.shape, lambda i: (0, 0))],
        out_specs=token,
        out_shape=jax.ShapeDtypeStruct((count, width), bf16),
    )(x, o, *es, wa, wm, vecs)


def normed(x):
    centred = x - jnp.mean(x, axis=1, keepdims=True)
    scale = lax.rsqrt(jnp.mean(centred * centred, axis=1, keepdims=True) + norm_epsilon)
    return centred * scale, scale


def add_sums(sum_ref, sums):
    sums = [sub_sum(t) for t in sums]

    @pl.when(pl.program_id(0) == 0)
    def _():
        for n, s in enumerate(sums):
            sum_ref[n] = s

    @pl.when(pl.program_id(0) > 0)
    def _():
        for n, s in enumerate(sums):
            sum_ref[n] += s


def grad_two_body(x_ref, dy_ref, *refs):
    *du_refs, wm_ref, vec_ref, part_ref, sum_ref = refs
    dy = dy_ref[...].astype(f32)
    grad = hidden_sum(du_refs, wm_ref, 0, NT, None)
    unit, scale = normed(x_ref[...].astype(f32))
    part_ref[...] = dy + norm_back(grad, unit, scale, vec_ref[2:3, :])
    add_sums(sum_ref, (grad * unit, grad, dy))


def grad_two(x, dy, dus, wm, vecs, after=(), step=256):
    count, width = x.shape
    splits = wm.shape[0] // 2
    token = pl.BlockSpec((step, width), lambda i: (i, 0))
    return call(
        grad_two_body,
        8 * count * width * width,
        16 * count * width + 8 * width * width,
        after=after,
        grid=(count // step,),
        in_specs=[token, token]
        + [stacked(d, step) for d in dus]
        + [resident(splits, width, 0), pl.BlockSpec(vecs.shape, lambda i: (0, 0))],
        out_specs=[token, pl.BlockSpec((3, 8, width), lambda i: (0, 0, 0))],
        out_shape=[jax.ShapeDtypeStruct((count, width), f32), jax.ShapeDtypeStruct((3, 8, width), f32)],
    )(x, dy, *dus, wm, vecs)


def grad_one_body(x_ref, part_ref, g_ref, wa_ref, vec_ref, grad_ref, sum_ref):
    grad = mm(g_ref[0], wa_ref[0], NT) + mm(g_ref[1], wa_ref[1], NT) + mm(g_ref[2], wa_ref[2], NT)
    unit, scale = normed(x_ref[...].astype(f32))
    grad_ref[...] = (part_ref[...] + norm_back(grad, unit, scale, vec_ref[0:1, :])).astype(bf16)
    add_sums(sum_ref, (grad * unit, grad))


def grad_one(x, part, g, wa, vecs, after=(), step=256):
    count, width = x.shape
    token = pl.BlockSpec((step, width), lambda i: (i, 0))
    return call(
        grad_one_body,
        6 * count * width * width,
        14 * count * width + 6 * width * width,
        after=after,
        grid=(count // step,),
        in_specs=[
            token,
            token,
            stacked(g, step),
            resident(3, width, 0),
            pl.BlockSpec(vecs.shape, lambda i: (0, 0)),
        ],
        out_specs=[token, pl.BlockSpec((2, 8, width), lambda i: (0, 0, 0))],
        out_shape=[jax.ShapeDtypeStruct((count, width), bf16), jax.ShapeDtypeStruct((2, 8, width), f32)],
    )(x, part, g, wa, vecs)


def grid_places():
    wide, narrow = lax.axis_index("wide"), lax.axis_index("narrow")
    return wide // 2, wide % 2, narrow // 2, narrow % 2


def to_place(move):
    pairs = []
    for z in range(4):
        for y in range(2):
            for x in range(2):
                for c in range(2):
                    a, b, d, e = move(z, y, x, c)
                    pairs.append((((z * 2 + y) * 2 + x) * 2 + c, ((a * 2 + b) * 2 + d) * 2 + e))
    return pairs


def over_c(value):
    return lax.ppermute(value, AXES, to_place(lambda z, y, x, c: (z, y, x, 1 - c)))


def over_x(value):
    return lax.ppermute(value, AXES, to_place(lambda z, y, x, c: (z, y, 1 - x, c)))


def over_y(value):
    return lax.ppermute(value, AXES, to_place(lambda z, y, x, c: (z, 1 - y, x, c)))


def over_z(value, by):
    return lax.ppermute(value, AXES, to_place(lambda z, y, x, c: ((z + by) % 4, y, x, c)))


def gather_order_body(place_ref, *refs):
    z, y, x, c = place_ref[0], place_ref[1], place_ref[2], place_ref[3]
    out_ref = refs[-1]
    blocks = out_ref.shape[0]
    near = lax.rem(z - pl.program_id(0) + 4, 4) < 2
    for rc in range(2):
        own, by_x, by_y, lower, upper = refs[rc * 5 : rc * 5 + 5]
        at = (y * 2 + x) * 2 + (c ^ rc)
        for n in range(blocks):
            out_ref[n, at] = own[0, n]
            out_ref[n, at ^ 2] = by_x[0, n]
            out_ref[n, at ^ 4] = by_y[0, n]

        @pl.when(near)
        def _(lower=lower, at=at):
            for n in range(blocks):
                out_ref[n, at ^ 6] = lower[0, n]

        @pl.when(jnp.logical_not(near))
        def _(upper=upper, at=at):
            for n in range(blocks):
                out_ref[n, at ^ 6] = upper[0, n]


def gather_staged(place, shards, after=()):
    blocks, shard, width = shards.shape
    own = jnp.stack([shards] + [over_z(shards, s) for s in (1, 2, 3)])
    by_x, by_y = over_x(own), over_y(own)
    lower, upper = over_y(by_x[:2]), over_x(by_y[2:])
    here = [own, by_x, by_y, lower, upper]
    pieces = here + [over_c(v) for v in here]

    def piece(first, count):
        def index(t, s):
            apart = lax.rem(s[0] - t + 4, 4)
            return (jnp.clip(apart - first, 0, count - 1), 0, 0, 0)

        return pl.BlockSpec((1, blocks, shard, width), index)

    weights = call(
        gather_order_body,
        0,
        64 * blocks * shard * width * 2,
        after=after,
        grid_spec=pltpu.PrefetchScalarGridSpec(
            num_scalar_prefetch=1,
            grid=(4,),
            in_specs=([piece(0, 4)] * 3 + [piece(0, 2), piece(2, 2)]) * 2,
            out_specs=pl.BlockSpec((blocks, 8, shard, width), lambda t, s: (0, t, 0, 0)),
        ),
        out_shape=jax.ShapeDtypeStruct((blocks, 32, shard, width), bf16),
    )(place, *pieces)
    return weights.reshape(blocks, width, width)


def chip_pair_body(place_ref, ka_ref, ga_ref, kb_ref, gb_ref, ka2_ref, sa_ref, kb2_ref, sb_ref):
    y, x = place_ref[1], place_ref[2]
    for mine, k_ref, g_ref, k2_ref, s2_ref in (
        (y, ka_ref, ga_ref, ka2_ref, sa_ref),
        (x, kb_ref, gb_ref, kb2_ref, sb_ref),
    ):
        k2_ref[...] = k_ref[:, :, mine] + g_ref[:, :, mine].astype(f32)
        s2_ref[...] = (k_ref[:, :, 1 - mine] + g_ref[:, :, 1 - mine].astype(f32)).astype(bf16)


def plane_body(place_ref, ka_ref, ga_ref, kb_ref, gb_ref, *out_refs):
    half = ka_ref.shape[-1]
    for m, ref in enumerate(out_refs):
        at = place_ref[0] ^ m
        for lo, k_ref, g_ref in ((0, ka_ref, ga_ref), (half, kb_ref, gb_ref)):
            ref[:, :, lo : lo + half] = (k_ref[:, at >> 1, at & 1] + g_ref[:, at >> 1, at & 1].astype(f32)).astype(
                bf16
            )


def summed(body, place, operands, shapes, after, steps=2):
    def spec(s):
        n = len(s.shape)
        return pl.BlockSpec((s.shape[0] // steps, *s.shape[1:]), lambda b, p: (b,) + (0,) * (n - 1))

    return call(
        body,
        0,
        sum(v.size * v.dtype.itemsize for v in operands) * 2,
        after=after,
        grid_spec=pltpu.PrefetchScalarGridSpec(
            num_scalar_prefetch=1,
            grid=(steps,),
            in_specs=[spec(v) for v in operands],
            out_specs=[spec(s) for s in shapes],
        ),
        out_shape=shapes,
    )(place, *operands)


class Reduction:
    def __init__(self, place, ka, sa, kb, sb):
        self.place, self.made = place, ka
        self.held = (ka, over_x(sa), kb, over_y(sb))

    def first(self, after):
        blocks, two, _, c, shard, half = self.held[0].shape
        shapes = [jax.ShapeDtypeStruct((blocks, two, c, shard, half), k) for k in (f32, bf16, f32, bf16)]
        ka, sa, kb, sb = summed(chip_pair_body, self.place, self.held, shapes, after)
        self.held = (ka, over_y(sa), kb, over_x(sb))
        self.made = ka

    def second(self, after):
        blocks, _, _, shard, half = self.held[0].shape
        shapes = [jax.ShapeDtypeStruct((blocks, shard, 2 * half), bf16)] * 4
        parts = summed(plane_body, self.place, self.held, shapes, after)
        self.made = parts[0]
        self.terms = [
            lax.ppermute(
                v, AXES, to_place(lambda z, y, x, c, m=m: (2 * c + ((z ^ m) >> 1), y, x, (z ^ m) & 1))
            )
            for m, v in enumerate(parts)
        ]


def everywhere(value):
    for move in (
        lambda z, y, x, c: (z, y, x, 1 - c),
        lambda z, y, x, c: (z, y, 1 - x, c),
        lambda z, y, x, c: (z, 1 - y, x, c),
        lambda z, y, x, c: (z ^ 1, y, x, c),
        lambda z, y, x, c: (3 - z, y, x, c),
    ):
        value = value + lax.ppermute(value, AXES, to_place(move))
    return value


def pack_body(slot_ref, *refs, orders, per):
    terms, (shard_ref, out_ref, square_ref) = refs[: len(orders) * per], refs[len(orders) * per :]
    total = jnp.zeros(square_ref.shape, f32)
    for n, order in enumerate(orders):
        for m, b in enumerate(order):
            value = terms[n * per][m].astype(f32)
            for t in range(1, per):
                value = value + terms[n * per + t][m].astype(f32)
            shard_ref[b] = value
            total = total + value * value
    square_ref[...] = total

    def one(j, carry):
        b = slot_ref[j]

        @pl.when(b >= 0)
        def _():
            out_ref[j] = shard_ref[jnp.maximum(b, 0)].astype(bf16)

        @pl.when(b < 0)
        def _():
            out_ref[j] = jnp.zeros(out_ref.shape[1:], bf16)

        return carry

    lax.fori_loop(0, out_ref.shape[0], one, 0)


def pack(slots, terms, orders, after=()):
    per = len(terms[0])
    _, shard, width = terms[0][0].shape
    terms = [v for t in terms for v in t]
    vmem = pl.BlockSpec(memory_space=pltpu.VMEM)
    return call(
        functools.partial(pack_body, orders=orders, per=per),
        0,
        sum(v.size * v.dtype.itemsize for v in terms) * 2,
        after=after,
        in_specs=[pl.BlockSpec(memory_space=pltpu.SMEM)] + [vmem] * len(terms),
        out_specs=[vmem] * 3,
        out_shape=[
            jax.ShapeDtypeStruct((sum(map(len, orders)), shard, width), f32),
            jax.ShapeDtypeStruct((slots.shape[0], shard, width), bf16),
            jax.ShapeDtypeStruct((shard, width), f32),
        ],
    )(slots, *terms)


def precondition_body(scale_ref, s_ref, l_ref, r_ref, p_ref, s_low, r_low):
    @pl.when(pl.program_id(0) == 0)
    def _():
        s_low[...] = (s_ref[...].astype(f32) * scale_ref[0]).astype(bf16)
        r_low[...] = r_ref[...].astype(bf16)

    left = mm(l_ref[...].astype(bf16), s_low[...], NN)
    p_ref[...] = (scale_ref[1] * mm(left.astype(bf16), r_low[...], NN)).astype(bf16)


def precondition(scales, block, left, right, step=256):
    width = block.shape[0]
    whole = pl.BlockSpec((width, width), lambda i: (0, 0))
    rows = pl.BlockSpec((step, width), lambda i: (i, 0))
    return call(
        precondition_body,
        4 * width**3,
        12 * width**2,
        grid=(width // step,),
        in_specs=[pl.BlockSpec(memory_space=pltpu.SMEM), whole, rows, whole],
        out_specs=rows,
        out_shape=jax.ShapeDtypeStruct((width, width), bf16),
        scratch_shapes=[pltpu.VMEM((width, width), bf16), pltpu.VMEM((width, width), bf16)],
    )(scales, block, left, right)


def statistics_body(has_ref, scale_ref, s_ref, l_ref, r_ref, nl_ref, nr_ref, s_low, *, step):
    i = pl.program_id(0)
    width = s_ref.shape[0]

    @pl.when(i == 0)
    def _():
        s_low[...] = (s_ref[...].astype(f32) * scale_ref[0]).astype(bf16)

    factor = (1.0 - decay_beta) * (scale_ref[1] * scale_ref[1] / width)
    at = pl.multiple_of(i * step, step)

    @pl.when(has_ref[0] != 0)
    def _():
        nl_ref[...] = decay_beta * l_ref[...] + factor * mm(s_low[pl.ds(at, step), :], s_low[...], NT)
        nr_ref[...] = decay_beta * r_ref[...] + factor * mm(s_low[:, pl.ds(at, step)], s_low[...], TN)

    @pl.when(has_ref[0] == 0)
    def _():
        nl_ref[...] = l_ref[...]
        nr_ref[...] = r_ref[...]


def statistics(has, scales, block, left, right, step=256):
    width = block.shape[0]
    whole = pl.BlockSpec((width, width), lambda i: (0, 0))
    rows = pl.BlockSpec((step, width), lambda i: (i, 0))
    smem = pl.BlockSpec(memory_space=pltpu.SMEM)
    return call(
        functools.partial(statistics_body, step=step),
        4 * width**3,
        18 * width**2,
        grid=(width // step,),
        in_specs=[smem, smem, whole, rows, rows],
        out_specs=[rows, rows],
        out_shape=[jax.ShapeDtypeStruct((width, width), f32)] * 2,
        scratch_shapes=[pltpu.VMEM((width, width), bf16)],
    )(has, scales, block, left, right)


def update_body(owner_ref, factor_ref, p_ref, shard_ref, block_ref, clip_ref, new_ref, copy_ref):
    for b in range(shard_ref.shape[0]):
        clip_ref[b] = shard_ref[b] * factor_ref[0]
        value = block_ref[b] - matrix_rate * p_ref[owner_ref[b]].astype(f32)
        new_ref[b] = value
        copy_ref[b] = value.astype(bf16)


def update(owners, factor, returned, shards, blocks):
    smem, vmem = pl.BlockSpec(memory_space=pltpu.SMEM), pl.BlockSpec(memory_space=pltpu.VMEM)
    return call(
        update_body,
        0,
        returned.size * 2 + shards.size * 18,
        in_specs=[smem, smem, vmem, vmem, vmem],
        out_specs=[vmem] * 3,
        out_shape=[
            jax.ShapeDtypeStruct(shards.shape, f32),
            jax.ShapeDtypeStruct(shards.shape, f32),
            jax.ShapeDtypeStruct(shards.shape, bf16),
        ],
    )(owners, factor, returned, shards, blocks)


def layer_inputs(tokens, vecs):
    values = tokens.astype(f32)
    centred = values - jnp.mean(values, axis=-1, keepdims=True)
    spread = jnp.mean(centred * centred, axis=-1, keepdims=True)
    unit = centred * lax.rsqrt(spread + norm_epsilon)
    one = (unit * vecs[0] + vecs[1]).astype(bf16)
    two = (unit * vecs[2] + vecs[3]).astype(bf16)
    return one, two


def to_all(value):
    return lax.all_to_all(value, AXES, split_axis=0, concat_axis=0, tiled=True)


def per_device(
    tokens,
    segment_ids,
    cotangent,
    blocks,
    vectors,
    stat_left,
    stat_right,
    root_left,
    root_right,
    vec_stat,
    owners,
    *,
    paired,
):
    rows_here, seq_len, width = tokens.shape
    count = rows_here * seq_len
    splits = FF // width
    slot_count = lax.axis_size(AXES)
    my_index = lax.axis_index(AXES)
    shard = width // slot_count
    vec_rows = vectors.shape[0]

    low_blocks, low_vectors = blocks.astype(bf16), vectors.astype(bf16)
    everyone = jnp.broadcast_to(low_vectors.reshape(1, -1), (slot_count, vec_rows * shard))
    vecs = to_all(everyone).reshape(slot_count, vec_rows, shard)
    vecs = vecs.transpose(1, 0, 2).reshape(vec_rows, width).astype(f32)
    mlp_weights = lax.all_gather(low_blocks[4:], AXES, axis=1, tiled=True)

    flat_tokens = tokens.reshape(count, width)
    dy = cotangent.reshape(count, width)
    tables = rotary_tables(segment_ids)
    a1, a2 = layer_inputs(flat_tokens, vecs)
    place = jnp.stack(grid_places()).astype(jnp.int32)
    if paired:
        attn_weights = gather_staged(place, low_blocks[:4], after=(*tables, a1, a2))
    else:
        attn_weights = lax.all_gather(low_blocks[:4], AXES, axis=1, tiled=True)

    q, k, v, do = project(a1, dy, attn_weights, vecs, tables)
    o, g, attn_sums = attend(segment_ids, q, k, v, do, tables)
    half = splits // 2
    orders = [list(range(4))]
    for first in (0, half):
        orders.append([base + first + j for base in (4, 4 + splits) for j in range(half)])
    if paired:

        def pair(v):
            return v, over_c(v)

        a1s, a2s, dys = pair(a1), pair(a2), pair(dy)
        os, gs = pair(o[None]), pair(g)
        e0, du0, up_sum0 = hidden(0, half, a2, dy, mlp_weights, vecs, after=(o,))
        es, dus = [pair(e0)], [pair(du0)]
        attn = Reduction(place, *half_grads(place, a1s, os, gs, dys, shard, after=(e0,)))
        e1, du1, up_sum1 = hidden(half, half, a2, dy, mlp_weights, vecs, after=(attn.made,))
        es.append(pair(e1))
        dus.append(pair(du1))
        low = Reduction(place, *half_grads(place, a2s, es[0], dus[0], dys, shard, after=(e1,)))
        attn.first(after=(low.made,))
        high = Reduction(place, *half_grads(place, a2s, es[1], dus[1], dys, shard, after=(attn.made,)))
        out = output(flat_tokens, o, [e0, e1], attn_weights, mlp_weights, vecs, after=(high.made,))
        low.first(after=(out,))
        attn.second(after=(low.made,))
        part, two_sums = grad_two(flat_tokens, dy, [du0, du1], mlp_weights, vecs, after=(attn.made,))
        high.first(after=(part,))
        low.second(after=(high.made,))
        grad_in, one_sums = grad_one(flat_tokens, part, g, attn_weights, vecs, after=(low.made,))
        high.second(after=(grad_in,))
        terms = [r.terms for r in (attn, low, high)]
    else:
        e0, du0, up_sum0 = hidden(0, half, a2, dy, mlp_weights, vecs)
        e1, du1, up_sum1 = hidden(half, half, a2, dy, mlp_weights, vecs)
        grads = [
            full_grads(a1, o[None], g, dy),
            full_grads(a2, e0, du0, dy),
            full_grads(a2, e1, du1, dy),
        ]
        terms = [[lax.psum_scatter(v, AXES, scatter_dimension=1, tiled=True)] for v in grads]
        out = output(flat_tokens, o, [e0, e1], attn_weights, mlp_weights, vecs)
        part, two_sums = grad_two(flat_tokens, dy, [du0, du1], mlp_weights, vecs)
        grad_in, one_sums = grad_one(flat_tokens, part, g, attn_weights, vecs)
    up_sums = [up_sum0, up_sum1]

    one_sums, two_sums = jnp.sum(one_sums, axis=1), jnp.sum(two_sums, axis=1)
    qkv_sums = jnp.sum(attn_sums, axis=1)
    up_sums = jnp.sum(jnp.concatenate(up_sums, axis=0), axis=1)
    bias_sum = two_sums[2:]
    grad_vectors = jnp.concatenate(
        [one_sums, two_sums[:2], qkv_sums, bias_sum, up_sums, bias_sum], axis=0
    )
    by_slot = grad_vectors.reshape(vec_rows, slot_count, shard).transpose(1, 0, 2)
    shard_vectors = jnp.sum(to_all(by_slot.reshape(slot_count, -1)), axis=0).reshape(vec_rows, shard)

    slot_ids = jnp.arange(slot_count, dtype=jnp.int32)
    match = owners[None, :] == slot_ids[:, None]
    slots = jnp.sum(jnp.where(match, jnp.arange(1, owners.shape[0] + 1, dtype=jnp.int32)[None], 0), axis=1) - 1
    has_block = jnp.any(owners == my_index)
    shards, outgoing, squares = pack(slots, terms, orders, after=(grad_in,))
    local = jnp.sum(squares) + jnp.sum(shard_vectors * shard_vectors)
    if paired:
        square_sum = everywhere(jnp.broadcast_to(local, (8, LANES)))[0, 0]
    else:
        square_sum = jnp.sum(to_all(jnp.broadcast_to(local, (slot_count, LANES)))[:, 0])
    grad_norm = jnp.sqrt(square_sum)
    factor = jnp.minimum(1.0, clip_level / grad_norm)
    root_count = math.sqrt(NPARAM)

    scale = factor * root_count
    power = jnp.exp2(jnp.floor(jnp.log2(jnp.maximum(scale, 1e-30)))).astype(bf16).astype(f32)
    scales = jnp.stack([power, scale / power])
    owned = to_all(outgoing).reshape(width, width)
    precond = precondition(scales, owned, root_left[0], root_right[0])
    returned = to_all(precond.reshape(slot_count, shard, width))
    new_left, new_right = statistics(
        has_block.astype(jnp.int32).reshape(1), scales, owned, stat_left[0], stat_right[0]
    )
    clipped_blocks, new_blocks, blocks_copy = update(owners, factor.reshape(1), returned, shards, blocks)
    clipped_vectors = shard_vectors * factor
    scaled_vectors = clipped_vectors * root_count
    new_vec_stat = decay_beta * vec_stat + (1.0 - decay_beta) * (scaled_vectors * scaled_vectors)
    new_vectors = vectors - vector_rate * scaled_vectors * lax.rsqrt(new_vec_stat)
    return (
        out.reshape(tokens.shape),
        grad_in.reshape(tokens.shape),
        clipped_blocks,
        clipped_vectors,
        grad_norm,
        new_left[None],
        new_right[None],
        new_vec_stat,
        new_blocks,
        new_vectors,
        blocks_copy,
        new_vectors.astype(bf16),
    )


def solution(mesh):
    rows = P(AXES, None, None)
    split_rows = P(None, AXES, None)
    split_columns = P(None, AXES)
    paired = dict(mesh.shape) == {"wide": 8, "narrow": 4}
    return jax.shard_map(
        functools.partial(per_device, paired=paired),
        mesh=mesh,
        in_specs=(
            rows, P(AXES, None), rows, split_rows, split_columns,
            rows, rows, rows, rows, split_columns, P(),
        ),
        out_specs=(
            rows, rows, split_rows, split_columns, P(), rows, rows,
            split_columns, split_rows, split_columns, split_rows, split_columns,
        ),
        check_vma=False,
    )
```

profile of v0, /device:TPU:0, one launch (start us, length us, event | category | flops | bytes accessed | tf_op | source)
XLA Modules:
  0.0 389.8 jit_solution(17890215485864890509)
XLA Ops:
  9.4 4.1 %collective-permute-start.1 = (bf16[4,24,768]{2,1,0:T(8,128)(2,1)S(1)}, bf16[4,24,768]{2,1,0:T(8,128)(2,1)S(1)}, u32[]{:S(2)}, u32[]{:S(2)}) collective-permute-start(bf16[4,24,768]{2,1,0:T(8,128)(2,1)S(1)} %get-tuple-element.140), channel_id=1, source_target_pairs={{0,16},{1,17},{2,18},{3,19},{4,20},{5,21},{6,22},{7,23},{8,24},{9,... | collective-permute-start | bytes 442376 | tf_op jit(solution)/shard_map/ppermute | solution.py:523
  24.2 5.2 %compare_select_fusion.9 = f32[128]{0:T(128)S(1)} fusion(f32[]{:T(128)} %bitcast.15, f32[]{:T(128)} %bitcast.16, f32[]{:T(128)} %bitcast.17, f32[]{:T(128)} %bitcast.18, f32[]{:T(128)} %bitcast.19, f32[]{:T(128)} %bitcast.21, f32[]{:T(128)} %bitcast.20, f32[]{:T(128)} %bitcast.14), kind=kLoop, calls=%fused_computation.40 | loop fusion | flops 5376 | bytes 544 | tf_op jit(solution)/shard_map/jit(_where)/select_n | solution.py:90
  33.0 3.3 fusion.2
  38.8 9.2 %collective-permute-done.4.refs_3_ = bf16[4,4,24,768]{3,2,1,0:T(8,128)(2,1)S(1)} collective-permute-done((bf16[4,4,24,768]{3,2,1,0:T(8,128)(2,1)S(1)}, bf16[4,4,24,768]{3,2,1,0:T(8,128)(2,1)S(1)}, u32[]{:S(2)}, u32[]{:S(2)}) %collective-permute-start.4) | collective-permute-done | bytes 589856 | tf_op jit(solution)/shard_map/ppermute | solution.py:519
  56.3 5.2 %collective-permute-done.6.refs_5_ = bf16[2,4,24,768]{3,2,1,0:T(8,128)(2,1)} collective-permute-done((bf16[2,4,24,768]{3,2,1,0:T(8,128)(2,1)}, bf16[2,4,24,768]{3,2,1,0:T(8,128)(2,1)}, u32[]{:S(2)}, u32[]{:S(2)}) %collective-permute-start.6) | collective-permute-done | bytes 294944 | tf_op jit(solution)/shard_map/ppermute | solution.py:515
  65.4 6.0 %shard_map.202 = bf16[4,32,24,768]{3,2,1,0:T(8,128)(2,1)} custom-call(s32[4]{0:T(128)} %pad_add_fusion.refs_0_, bf16[4,4,24,768]{3,2,1,0:T(8,128)(2,1)} %copy-done.7, bf16[4,4,24,768]{3,2,1,0:T(8,128)(2,1)} %collective-permute-done.3.refs_2_, bf16[4,4,24,768]{3,2,1,0:T(8,128)(2,1)} %copy-done.8, bf16[2,4,24,768]{3,2,1,0:T(8,128)(2,1)} %collective-permute-done.5.refs_4_, ...), custom_call_target="tpu_custom_call" | custom-call | bytes 9437184 | tf_op jit(solution)/shard_map/pallas_call | solution.py:74
  71.3 10.4 %shard_map.203 = (bf16[1024,768]{1,0:T(8,128)(2,1)}, bf16[1024,768]{1,0:T(8,128)(2,1)}, bf16[1024,768]{1,0:T(8,128)(2,1)}, bf16[1024,768]{1,0:T(8,128)(2,1)}) custom-call(bf16[1024,768]{1,0:T(8,128)(2,1)} %get-tuple-element.138.refs_14_.a1_ref.refs_1_, bf16[1024,768]{1,0:T(8,128)(2,1)} %bitcast.70, bf16[4,768,768]{2,1,0:T(8,128)(2,1)} %bitcast.78, ...), custom_call_target="tpu_custom_call" | custom-call | flops 4831838208 | bytes 14155776 | tf_op jit(solution)/shard_map/pallas_call | solution.py:74
  81.7 27.3 %shard_map.204 = (bf16[1024,768]{1,0:T(8,128)(2,1)}, bf16[3,1024,768]{2,1,0:T(8,128)(2,1)}, f32[3,16,768]{2,1,0:T(8,128)}) custom-call(s32[1024,1]{1,0:T(8,128)} %bitcast.92, s32[2,1,512]{2,1,0:T(1,128)} %reshape.251.row_ref, bf16[1024,768]{1,0:T(8,128)(2,1)} %get-tuple-element.73.q_ref, bf16[1024,768]{1,0:T(8,128)(2,1)} %get-tuple-element.74.k_ref, ...), custom_call_target="tpu_custom_call" | custom-call | flops 9663676416 | bytes 18874368 | tf_op jit(solution)/shard_map/pallas_call | solution.py:74
  110.9 12.6 %shard_map.205 = (bf16[2,1024,768]{2,1,0:T(8,128)(2,1)}, bf16[2,1024,768]{2,1,0:T(8,128)(2,1)}, f32[2,8,768]{2,1,0:T(8,128)}) custom-call(bf16[1024,768]{1,0:T(8,128)(2,1)} %get-tuple-element.137.refs_15_.refs_0_.refs_1_, bf16[1024,768]{1,0:T(8,128)(2,1)} %bitcast.71, bf16[8,768,768]{2,1,0:T(8,128)(2,1)} %all-gather.2.cloned.1.call-done.refs_2_.refs_3_.refs_5_.refs_4_, ...), custom_call_target="tpu_custom_call" | custom-call | flops 4831838208 | bytes 17301504 | tf_op jit(solution)/shard_map/pallas_call | solution.py:74
  125.0 12.3 %shard_map.206 = (f32[4,2,2,2,24,384]{5,4,3,2,1,0:T(8,128)}, bf16[4,2,2,2,24,384]{5,4,3,2,1,0:T(8,128)(2,1)}, f32[4,2,2,2,24,384]{5,4,3,2,1,0:T(8,128)}, bf16[4,2,2,2,24,384]{5,4,3,2,1,0:T(8,128)(2,1)}) custom-call(s32[4]{0:T(128)} %pad_add_fusion.refs_0_, bf16[1024,768]{1,0:T(8,128)(2,1)} %get-tuple-element.138.refs_14_.a1_ref.refs_1_, ...), custom_call_target="tpu_custom_call" | custom-call | flops 4831838208 | bytes 12582912 | tf_op jit(solution)/shard_map/pallas_call | solution.py:74
  137.3 13.0 %shard_map.207 = (bf16[2,1024,768]{2,1,0:T(8,128)(2,1)}, bf16[2,1024,768]{2,1,0:T(8,128)(2,1)}, f32[2,8,768]{2,1,0:T(8,128)}) custom-call(bf16[1024,768]{1,0:T(8,128)(2,1)} %get-tuple-element.137.refs_15_.refs_0_.refs_1_, bf16[1024,768]{1,0:T(8,128)(2,1)} %bitcast.73, bf16[8,768,768]{2,1,0:T(8,128)(2,1)} %all-gather.2.cloned.1.call-done.refs_2_.refs_3_.refs_5_.refs_4_, ...), custom_call_target="tpu_custom_call" | custom-call | flops 4831838208 | bytes 17301504 | tf_op jit(solution)/shard_map/pallas_call | solution.py:74
  151.0 9.5 %collective-permute-done.16.refs_2_ = bf16[1024,768]{1,0:T(8,128)(2,1)S(1)} collective-permute-done((bf16[1024,768]{1,0:T(8,128)(2,1)S(1)}, bf16[1024,768]{1,0:T(8,128)(2,1)S(1)}, u32[]{:S(2)}, u32[]{:S(2)}) %collective-permute-start.16) | collective-permute-done | bytes 1572896 | tf_op jit(solution)/shard_map/ppermute | solution.py:511
  163.1 11.7 %shard_map.208 = (f32[4,2,2,2,24,384]{5,4,3,2,1,0:T(8,128)}, bf16[4,2,2,2,24,384]{5,4,3,2,1,0:T(8,128)(2,1)}, f32[4,2,2,2,24,384]{5,4,3,2,1,0:T(8,128)}, bf16[4,2,2,2,24,384]{5,4,3,2,1,0:T(8,128)(2,1)}) custom-call(s32[4]{0:T(128)} %pad_add_fusion.refs_0_, bf16[1024,768]{1,0:T(8,128)(2,1)} %get-tuple-element.137.refs_15_.refs_0_.refs_1_, ...), custom_call_target="tpu_custom_call" | custom-call | flops 4831838208 | bytes 12582912 | tf_op jit(solution)/shard_map/pallas_call | solution.py:74
  178.3 3.8 shard_map.209
  184.7 11.6 %shard_map.210 = (f32[4,2,2,2,24,384]{5,4,3,2,1,0:T(8,128)}, bf16[4,2,2,2,24,384]{5,4,3,2,1,0:T(8,128)(2,1)}, f32[4,2,2,2,24,384]{5,4,3,2,1,0:T(8,128)}, bf16[4,2,2,2,24,384]{5,4,3,2,1,0:T(8,128)(2,1)}) custom-call(s32[4]{0:T(128)} %pad_add_fusion.refs_0_, bf16[1024,768]{1,0:T(8,128)(2,1)} %get-tuple-element.137.refs_15_.refs_0_.refs_1_, ...), custom_call_target="tpu_custom_call" | custom-call | flops 4831838208 | bytes 12582912 | tf_op jit(solution)/shard_map/pallas_call | solution.py:74
  198.7 11.0 %shard_map.211.refs_5_ = bf16[1024,768]{1,0:T(8,128)(2,1)} custom-call(bf16[1024,768]{1,0:T(8,128)(2,1)} %bitcast.67, bf16[1024,768]{1,0:T(8,128)(2,1)} %get-tuple-element.77.refs_5_.refs_1_, bf16[2,1024,768]{2,1,0:T(8,128)(2,1)} %get-tuple-element.78.refs_9_.refs_3_.refs_2_, bf16[2,1024,768]{2,1,0:T(8,128)(2,1)} %get-tuple-element.81.refs_9_.refs_3_, ...), custom_call_target="tpu_custom_call" | custom-call | flops 6039797760 | bytes 16908288 | tf_op jit(solution)/shard_map/pallas_call | solution.py:74
  210.5 3.7 shard_map.212
  219.6 11.4 %shard_map.214 = (f32[1024,768]{1,0:T(8,128)}, f32[3,8,768]{2,1,0:T(8,128)}) custom-call(bf16[1024,768]{1,0:T(8,128)(2,1)} %bitcast.68, bf16[1024,768]{1,0:T(8,128)(2,1)} %bitcast.76, bf16[2,1024,768]{2,1,0:T(8,128)(2,1)} %get-tuple-element.86.refs_5_.refs_2_, bf16[2,1024,768]{2,1,0:T(8,128)(2,1)} %get-tuple-element.82.refs_5_.refs_3_, ...), custom_call_target="tpu_custom_call" | custom-call | flops 4831838208 | bytes 17301504 | tf_op jit(solution)/shard_map/pallas_call | solution.py:74
  232.1 3.8 shard_map.215
  244.2 6.7 %collective-permute-start.34 = (bf16[4,24,768]{2,1,0:T(8,128)(2,1)S(1)}, bf16[4,24,768]{2,1,0:T(8,128)(2,1)S(1)}, u32[]{:S(2)}, u32[]{:S(2)}) collective-permute-start(bf16[4,24,768]{2,1,0:T(8,128)(2,1)S(1)} %copy-done.49), channel_id=1, source_target_pairs={{0,9},{1,25},{2,11},{3,27},{4,13},{5,29},{6,15},{7,31},{8,8},{9,24... | collective-permute-start | bytes 442376 | tf_op jit(solution)/shard_map/ppermute | solution.py:639
  256.2 9.6 %shard_map.217 = (bf16[1024,768]{1,0:T(8,128)(2,1)}, f32[2,8,768]{2,1,0:T(8,128)}) custom-call(bf16[1024,768]{1,0:T(8,128)(2,1)} %bitcast.69, f32[1024,768]{1,0:T(8,128)} %get-tuple-element.98.refs_5_.refs_1_, bf16[3,1024,768]{2,1,0:T(8,128)(2,1)} %get-tuple-element.79.refs_5_.refs_2_, bf16[4,768,768]{2,1,0:T(8,128)(2,1)} %bitcast.80, ...), custom_call_target="tpu_custom_call" | custom-call | flops 3623878656 | bytes 14548992 | tf_op jit(solution)/shard_map/pallas_call | solution.py:74
  267.7 5.1 %all-to-all-start.1 = ((f32[32,1,312]{2,1,0:T(1,128)}), f32[32,1,312]{2,1,0:T(1,128)S(1)}, u32[]{:S(2)}, u32[]{:S(2)}) async-start(f32[32,1,312]{2,1,0:T(1,128)} %copy.56), calls=%async_computation.1 | async-start | bytes 98304 | tf_op jit(solution)/shard_map/all_to_all | solution.py:806
  278.0 5.0 %collective-permute-start.42 = (bf16[4,24,768]{2,1,0:T(8,128)(2,1)}, bf16[4,24,768]{2,1,0:T(8,128)(2,1)S(1)}, u32[]{:S(2)}, u32[]{:S(2)}) collective-permute-start(bf16[4,24,768]{2,1,0:T(8,128)(2,1)} %get-tuple-element.118), channel_id=1, source_target_pairs={{0,1},{1,17},{2,3},{3,19},{4,5},{5,21},{6,7},{7,23},{8,0},{9,16},{... | collective-permute-start | bytes 442376 | tf_op jit(solution)/shard_map/ppermute | solution.py:639
  288.9 7.7 %collective-permute-done.43.refs_11_ = bf16[4,24,768]{2,1,0:T(8,128)(2,1)S(1)} collective-permute-done((bf16[4,24,768]{2,1,0:T(8,128)(2,1)}, bf16[4,24,768]{2,1,0:T(8,128)(2,1)S(1)}, u32[]{:S(2)}, u32[]{:S(2)}) %collective-permute-start.43) | collective-permute-done | bytes 147488 | tf_op jit(solution)/shard_map/ppermute | solution.py:639
  297.9 3.8 shard_map.219
  301.7 5.2 %all-to-all-start.2 = ((bf16[32,24,768]{2,1,0:T(8,128)(2,1)}), bf16[32,24,768]{2,1,0:T(8,128)(2,1)S(1)}, u32[]{:S(2)}, u32[]{:S(2)}) async-start(bf16[32,24,768]{2,1,0:T(8,128)(2,1)} %get-tuple-element.127), calls=%async_computation.2 | async-start | bytes 2359296 | tf_op jit(solution)/shard_map/all_to_all | solution.py:806
  320.1 6.8 %collective-permute-done.48 = f32[8,128]{1,0:T(8,128)S(1)} collective-permute-done((f32[8,128]{1,0:T(8,128)S(1)}, f32[8,128]{1,0:T(8,128)S(1)}, u32[]{:S(2)}, u32[]{:S(2)}) %collective-permute-start.48) | collective-permute-done | bytes 4128 | tf_op jit(solution)/shard_map/ppermute | solution.py:654
  326.9 3.5 collective-permute-start.49
  337.2 6.4 %shard_map.220 = bf16[768,768]{1,0:T(8,128)(2,1)} custom-call(f32[2]{0:T(128)} %pad_maximum_fusion.1.scale_ref, bf16[768,768]{1,0:T(8,128)(2,1)} %bitcast.85, f32[768,768]{1,0:T(8,128)} %bitcast.88, f32[768,768]{1,0:T(8,128)} %bitcast.89), custom_call_target="tpu_custom_call" | custom-call | flops 1811939328 | bytes 7077888 | tf_op jit(solution)/shard_map/pallas_call | solution.py:74
  343.6 4.8 %all-to-all-start.3 = ((bf16[32,24,768]{2,1,0:T(8,128)(2,1)}), bf16[32,24,768]{2,1,0:T(8,128)(2,1)S(1)}, u32[]{:S(2)}, u32[]{:S(2)}) async-start(bf16[32,24,768]{2,1,0:T(8,128)(2,1)} %bitcast.87), calls=%async_computation.3 | async-start | bytes 2359296 | tf_op jit(solution)/shard_map/all_to_all | solution.py:806
  350.4 7.1 %shard_map.222 = (f32[768,768]{1,0:T(8,128)}, f32[768,768]{1,0:T(8,128)}) custom-call(s32[1]{0:T(128)} %bitcast.37.has_ref, f32[2]{0:T(128)} %pad_maximum_fusion.1.scale_ref, bf16[768,768]{1,0:T(8,128)(2,1)} %bitcast.86, f32[768,768]{1,0:T(8,128)} %bitcast.102, f32[768,768]{1,0:T(8,128)} %bitcast.103), custom_call_target="tpu_custom_call" | custom-call | flops 1811939328 | bytes 10616832 | tf_op jit(solution)/shard_map/pallas_call | solution.py:74
  357.6 19.9 %all-to-all-done.3.p_ref = bf16[32,24,768]{2,1,0:T(8,128)(2,1)S(1)} async-done(((bf16[32,24,768]{2,1,0:T(8,128)(2,1)}), bf16[32,24,768]{2,1,0:T(8,128)(2,1)S(1)}, u32[]{:S(2)}, u32[]{:S(2)}) %all-to-all-start.3) | async-done | bytes 1179680 | tf_op jit(solution)/shard_map/all_to_all | solution.py:806
  (278 shorter events, 104.2 us)
Async XLA Ops:
  7.2 103.7 %all-gather.2.cloned.1.call-start = ((), (), s32[]{:S(2)}) async-start(), calls=%async_computation.4 | async-start | bytes 9732096 | tf_op jit(solution)/shard_map/all_gather | solution.py:836
  9.4 20.1 %collective-permute-start.1 = (bf16[4,24,768]{2,1,0:T(8,128)(2,1)S(1)}, bf16[4,24,768]{2,1,0:T(8,128)(2,1)S(1)}, u32[]{:S(2)}, u32[]{:S(2)}) collective-permute-start(bf16[4,24,768]{2,1,0:T(8,128)(2,1)S(1)} %get-tuple-element.140), channel_id=1, source_target_pairs={{0,16},{1,17},{2,18},{3,19},{4,20},{5,21},{6,22},{7,23},{8,24},{9,... | collective-permute-start | bytes 442376 | tf_op jit(solution)/shard_map/ppermute | solution.py:523
  13.5 16.0 %collective-permute-start = (bf16[4,24,768]{2,1,0:T(8,128)(2,1)S(1)}, bf16[4,24,768]{2,1,0:T(8,128)(2,1)S(1)}, u32[]{:S(2)}, u32[]{:S(2)}) collective-permute-start(bf16[4,24,768]{2,1,0:T(8,128)(2,1)S(1)} %get-tuple-element.140), channel_id=1, source_target_pairs={{0,8},{1,9},{2,10},{3,11},{4,12},{5,13},{6,14},{7,15},{8,16},{9,17... | collective-permute-start | bytes 442376 | tf_op jit(solution)/shard_map/ppermute | solution.py:523
  19.5 19.0 %all-to-all-start = ((bf16[32,2,156]{2,1,0:T(2,128)(2,1)}), bf16[32,2,156]{2,1,0:T(2,128)(2,1)S(1)}, u32[]{:S(2)}, u32[]{:S(2)}) async-start(bf16[32,2,156]{2,1,0:T(2,128)(2,1)} %reshape.313), calls=%async_computation | async-start | bytes 65536 | tf_op jit(solution)/shard_map/all_to_all | solution.py:806
  29.6 18.4 %collective-permute-start.4 = (bf16[4,4,24,768]{3,2,1,0:T(8,128)(2,1)S(1)}, bf16[4,4,24,768]{3,2,1,0:T(8,128)(2,1)S(1)}, u32[]{:S(2)}, u32[]{:S(2)}) collective-permute-start(bf16[4,4,24,768]{3,2,1,0:T(8,128)(2,1)S(1)} %pad_maximum_fusion.refs_1_), channel_id=1, source_target_pairs={{0,4},{1,5},{2,6},{3,7},{4,0},{5,1},{6,2},{7,3},{8,12},{9,13},{10,... | collective-permute-start | bytes 1769480 | tf_op jit(solution)/shard_map/ppermute | solution.py:519
  31.5 20.0 %collective-permute-start.3 = (bf16[4,4,24,768]{3,2,1,0:T(8,128)(2,1)S(1)}, bf16[4,4,24,768]{3,2,1,0:T(8,128)(2,1)}, u32[]{:S(2)}, u32[]{:S(2)}) collective-permute-start(bf16[4,4,24,768]{3,2,1,0:T(8,128)(2,1)S(1)} %pad_maximum_fusion.refs_1_), channel_id=1, source_target_pairs={{0,2},{1,3},{2,0},{3,1},{4,6},{5,7},{6,4},{7,5},{8,10},{9,11},{10,... | collective-permute-start | bytes 1769480 | tf_op jit(solution)/shard_map/ppermute | solution.py:515
  38.7 25.8 %collective-permute-start.7 = (bf16[4,4,24,768]{3,2,1,0:T(8,128)(2,1)S(1)}, bf16[4,4,24,768]{3,2,1,0:T(8,128)(2,1)}, u32[]{:S(2)}, u32[]{:S(2)}) collective-permute-start(bf16[4,4,24,768]{3,2,1,0:T(8,128)(2,1)S(1)} %pad_maximum_fusion.refs_1_), channel_id=1, source_target_pairs={{0,1},{1,0},{2,3},{3,2},{4,5},{5,4},{6,7},{7,6},{8,9},{9,8},{10,11... | collective-permute-start | bytes 1769480 | tf_op jit(solution)/shard_map/ppermute | solution.py:511
  109.1 15.1 %collective-permute-start.14 = (bf16[3,1024,768]{2,1,0:T(8,128)(2,1)}, bf16[3,1024,768]{2,1,0:T(8,128)(2,1)}, u32[]{:S(2)}, u32[]{:S(2)}) collective-permute-start(bf16[3,1024,768]{2,1,0:T(8,128)(2,1)} %get-tuple-element.79.refs_5_.refs_2_), channel_id=1, source_target_pairs={{0,1},{1,0},{2,3},{3,2},{4,5},{5,4},{6,7},{7,6},{8,9},{9,8},{10,11... | collective-permute-start | bytes 14155784 | tf_op jit(solution)/shard_map/ppermute | solution.py:511
  123.5 38.7 %collective-permute-start.22 = (bf16[2,1024,768]{2,1,0:T(8,128)(2,1)}, bf16[2,1024,768]{2,1,0:T(8,128)(2,1)}, u32[]{:S(2)}, u32[]{:S(2)}) collective-permute-start(bf16[2,1024,768]{2,1,0:T(8,128)(2,1)} %get-tuple-element.86.refs_5_.refs_2_), channel_id=1, source_target_pairs={{0,1},{1,0},{2,3},{3,2},{4,5},{5,4},{6,7},{7,6},{8,9},{9,8},{10,11... | collective-permute-start | bytes 9437192 | tf_op jit(solution)/shard_map/ppermute | solution.py:511
  123.9 39.2 %collective-permute-start.21 = (bf16[2,1024,768]{2,1,0:T(8,128)(2,1)}, bf16[2,1024,768]{2,1,0:T(8,128)(2,1)}, u32[]{:S(2)}, u32[]{:S(2)}) collective-permute-start(bf16[2,1024,768]{2,1,0:T(8,128)(2,1)} %get-tuple-element.78.refs_9_.refs_3_.refs_2_), channel_id=1, source_target_pairs={{0,1},{1,0},{2,3},{3,2},{4,5},{5,4},{6,7},{7,6},{8,9},{9,8},{10,11... | collective-permute-start | bytes 9437192 | tf_op jit(solution)/shard_map/ppermute | solution.py:511
  150.3 33.3 %collective-permute-start.18 = (bf16[2,1024,768]{2,1,0:T(8,128)(2,1)}, bf16[2,1024,768]{2,1,0:T(8,128)(2,1)}, u32[]{:S(2)}, u32[]{:S(2)}) collective-permute-start(bf16[2,1024,768]{2,1,0:T(8,128)(2,1)} %get-tuple-element.82.refs_5_.refs_3_), channel_id=1, source_target_pairs={{0,1},{1,0},{2,3},{3,2},{4,5},{5,4},{6,7},{7,6},{8,9},{9,8},{10,11... | collective-permute-start | bytes 9437192 | tf_op jit(solution)/shard_map/ppermute | solution.py:511
  150.5 34.2 %collective-permute-start.17 = (bf16[2,1024,768]{2,1,0:T(8,128)(2,1)}, bf16[2,1024,768]{2,1,0:T(8,128)(2,1)}, u32[]{:S(2)}, u32[]{:S(2)}) collective-permute-start(bf16[2,1024,768]{2,1,0:T(8,128)(2,1)} %get-tuple-element.81.refs_9_.refs_3_), channel_id=1, source_target_pairs={{0,1},{1,0},{2,3},{3,2},{4,5},{5,4},{6,7},{7,6},{8,9},{9,8},{10,11... | collective-permute-start | bytes 9437192 | tf_op jit(solution)/shard_map/ppermute | solution.py:511
  160.5 15.7 %collective-permute-start.19 = (bf16[4,2,2,2,24,384]{5,4,3,2,1,0:T(8,128)(2,1)}, bf16[4,2,2,2,24,384]{5,4,3,2,1,0:T(8,128)(2,1)S(1)}, u32[]{:S(2)}, u32[]{:S(2)}) collective-permute-start(bf16[4,2,2,2,24,384]{5,4,3,2,1,0:T(8,128)(2,1)} %get-tuple-element.83), channel_id=1, source_target_pairs={{0,2},{1,3},{2,0},{3,1},{4,6},{5,7},{6,4},{7,5},{8,10},{9,11},{10,... | collective-permute-start | bytes 1769480 | tf_op jit(solution)/shard_map/ppermute | solution.py:515
  162.2 15.2 %collective-permute-start.20 = (bf16[4,2,2,2,24,384]{5,4,3,2,1,0:T(8,128)(2,1)S(1)}, bf16[4,2,2,2,24,384]{5,4,3,2,1,0:T(8,128)(2,1)S(1)}, u32[]{:S(2)}, u32[]{:S(2)}) collective-permute-start(bf16[4,2,2,2,24,384]{5,4,3,2,1,0:T(8,128)(2,1)S(1)} %copy-done.48), channel_id=1, source_target_pairs={{0,4},{1,5},{2,6},{3,7},{4,0},{5,1},{6,2},{7,3},{8,12},{9,13},{10,... | collective-permute-start | bytes 1769480 | tf_op jit(solution)/shard_map/ppermute | solution.py:519
  174.8 23.0 %collective-permute-start.25 = (bf16[4,2,2,2,24,384]{5,4,3,2,1,0:T(8,128)(2,1)}, bf16[4,2,2,2,24,384]{5,4,3,2,1,0:T(8,128)(2,1)S(1)}, u32[]{:S(2)}, u32[]{:S(2)}) collective-permute-start(bf16[4,2,2,2,24,384]{5,4,3,2,1,0:T(8,128)(2,1)} %get-tuple-element.93), channel_id=1, source_target_pairs={{0,2},{1,3},{2,0},{3,1},{4,6},{5,7},{6,4},{7,5},{8,10},{9,11},{10,... | collective-permute-start | bytes 1769480 | tf_op jit(solution)/shard_map/ppermute | solution.py:515
  182.0 33.3 %collective-permute-start.23 = (bf16[4,2,2,24,384]{4,3,2,1,0:T(8,128)(2,1)}, bf16[4,2,2,24,384]{4,3,2,1,0:T(8,128)(2,1)S(1)}, u32[]{:S(2)}, u32[]{:S(2)}) collective-permute-start(bf16[4,2,2,24,384]{4,3,2,1,0:T(8,128)(2,1)} %get-tuple-element.90), channel_id=1, source_target_pairs={{0,4},{1,5},{2,6},{3,7},{4,0},{5,1},{6,2},{7,3},{8,12},{9,13},{10,... | collective-permute-start | bytes 884744 | tf_op jit(solution)/shard_map/ppermute | solution.py:519
  182.9 33.1 %collective-permute-start.24 = (bf16[4,2,2,24,384]{4,3,2,1,0:T(8,128)(2,1)}, bf16[4,2,2,24,384]{4,3,2,1,0:T(8,128)(2,1)S(1)}, u32[]{:S(2)}, u32[]{:S(2)}) collective-permute-start(bf16[4,2,2,24,384]{4,3,2,1,0:T(8,128)(2,1)} %get-tuple-element.92), channel_id=1, source_target_pairs={{0,2},{1,3},{2,0},{3,1},{4,6},{5,7},{6,4},{7,5},{8,10},{9,11},{10,... | collective-permute-start | bytes 884744 | tf_op jit(solution)/shard_map/ppermute | solution.py:515
  183.6 26.1 %collective-permute-start.26 = (bf16[4,2,2,2,24,384]{5,4,3,2,1,0:T(8,128)(2,1)S(1)}, bf16[4,2,2,2,24,384]{5,4,3,2,1,0:T(8,128)(2,1)S(1)}, u32[]{:S(2)}, u32[]{:S(2)}) collective-permute-start(bf16[4,2,2,2,24,384]{5,4,3,2,1,0:T(8,128)(2,1)S(1)} %copy-done.47), channel_id=1, source_target_pairs={{0,4},{1,5},{2,6},{3,7},{4,0},{5,1},{6,2},{7,3},{8,12},{9,13},{10,... | collective-permute-start | bytes 1769480 | tf_op jit(solution)/shard_map/ppermute | solution.py:519
  196.3 34.7 %collective-permute-start.29 = (bf16[4,2,2,2,24,384]{5,4,3,2,1,0:T(8,128)(2,1)}, bf16[4,2,2,2,24,384]{5,4,3,2,1,0:T(8,128)(2,1)S(1)}, u32[]{:S(2)}, u32[]{:S(2)}) collective-permute-start(bf16[4,2,2,2,24,384]{5,4,3,2,1,0:T(8,128)(2,1)} %get-tuple-element.102), channel_id=1, source_target_pairs={{0,2},{1,3},{2,0},{3,1},{4,6},{5,7},{6,4},{7,5},{8,10},{9,11},{10,... | collective-permute-start | bytes 1769480 | tf_op jit(solution)/shard_map/ppermute | solution.py:515
  197.7 33.3 %collective-permute-start.30 = (bf16[4,2,2,2,24,384]{5,4,3,2,1,0:T(8,128)(2,1)}, bf16[4,2,2,2,24,384]{5,4,3,2,1,0:T(8,128)(2,1)S(1)}, u32[]{:S(2)}, u32[]{:S(2)}) collective-permute-start(bf16[4,2,2,2,24,384]{5,4,3,2,1,0:T(8,128)(2,1)} %get-tuple-element.104), channel_id=1, source_target_pairs={{0,4},{1,5},{2,6},{3,7},{4,0},{5,1},{6,2},{7,3},{8,12},{9,13},{10,... | collective-permute-start | bytes 1769480 | tf_op jit(solution)/shard_map/ppermute | solution.py:519
  214.2 24.0 %collective-permute-start.27 = (bf16[4,2,2,24,384]{4,3,2,1,0:T(8,128)(2,1)}, bf16[4,2,2,24,384]{4,3,2,1,0:T(8,128)(2,1)S(1)}, u32[]{:S(2)}, u32[]{:S(2)}) collective-permute-start(bf16[4,2,2,24,384]{4,3,2,1,0:T(8,128)(2,1)} %get-tuple-element.99), channel_id=1, source_target_pairs={{0,4},{1,5},{2,6},{3,7},{4,0},{5,1},{6,2},{7,3},{8,12},{9,13},{10,... | collective-permute-start | bytes 884744 | tf_op jit(solution)/shard_map/ppermute | solution.py:519
  215.3 25.3 %collective-permute-start.28 = (bf16[4,2,2,24,384]{4,3,2,1,0:T(8,128)(2,1)}, bf16[4,2,2,24,384]{4,3,2,1,0:T(8,128)(2,1)S(1)}, u32[]{:S(2)}, u32[]{:S(2)}) collective-permute-start(bf16[4,2,2,24,384]{4,3,2,1,0:T(8,128)(2,1)} %get-tuple-element.101), channel_id=1, source_target_pairs={{0,2},{1,3},{2,0},{3,1},{4,6},{5,7},{6,4},{7,5},{8,10},{9,11},{10,... | collective-permute-start | bytes 884744 | tf_op jit(solution)/shard_map/ppermute | solution.py:515
  235.9 16.4 %collective-permute-start.39 = (bf16[4,2,2,24,384]{4,3,2,1,0:T(8,128)(2,1)}, bf16[4,2,2,24,384]{4,3,2,1,0:T(8,128)(2,1)S(1)}, u32[]{:S(2)}, u32[]{:S(2)}) collective-permute-start(bf16[4,2,2,24,384]{4,3,2,1,0:T(8,128)(2,1)} %get-tuple-element.114), channel_id=1, source_target_pairs={{0,4},{1,5},{2,6},{3,7},{4,0},{5,1},{6,2},{7,3},{8,12},{9,13},{10,... | collective-permute-start | bytes 884744 | tf_op jit(solution)/shard_map/ppermute | solution.py:519
  236.8 17.4 %collective-permute-start.40 = (bf16[4,2,2,24,384]{4,3,2,1,0:T(8,128)(2,1)}, bf16[4,2,2,24,384]{4,3,2,1,0:T(8,128)(2,1)S(1)}, u32[]{:S(2)}, u32[]{:S(2)}) collective-permute-start(bf16[4,2,2,24,384]{4,3,2,1,0:T(8,128)(2,1)} %get-tuple-element.116), channel_id=1, source_target_pairs={{0,2},{1,3},{2,0},{3,1},{4,6},{5,7},{6,4},{7,5},{8,10},{9,11},{10,... | collective-permute-start | bytes 884744 | tf_op jit(solution)/shard_map/ppermute | solution.py:515
  240.6 35.8 %collective-permute-start.31 = (bf16[4,24,768]{2,1,0:T(8,128)(2,1)S(1)}, bf16[4,24,768]{2,1,0:T(8,128)(2,1)S(1)}, u32[]{:S(2)}, u32[]{:S(2)}) collective-permute-start(bf16[4,24,768]{2,1,0:T(8,128)(2,1)S(1)} %copy-done.23), channel_id=1, source_target_pairs={{0,0},{1,16},{2,2},{3,18},{4,4},{5,20},{6,6},{7,22},{8,1},{9,17},{... | collective-permute-start | bytes 442376 | tf_op jit(solution)/shard_map/ppermute | solution.py:639
  244.2 31.5 %collective-permute-start.34 = (bf16[4,24,768]{2,1,0:T(8,128)(2,1)S(1)}, bf16[4,24,768]{2,1,0:T(8,128)(2,1)S(1)}, u32[]{:S(2)}, u32[]{:S(2)}) collective-permute-start(bf16[4,24,768]{2,1,0:T(8,128)(2,1)S(1)} %copy-done.49), channel_id=1, source_target_pairs={{0,9},{1,25},{2,11},{3,27},{4,13},{5,29},{6,15},{7,31},{8,8},{9,24... | collective-permute-start | bytes 442376 | tf_op jit(solution)/shard_map/ppermute | solution.py:639
  252.2 25.8 %collective-permute-start.36 = (bf16[4,24,768]{2,1,0:T(8,128)(2,1)}, bf16[4,24,768]{2,1,0:T(8,128)(2,1)S(1)}, u32[]{:S(2)}, u32[]{:S(2)}) collective-permute-start(bf16[4,24,768]{2,1,0:T(8,128)(2,1)} %get-tuple-element.111), channel_id=1, source_target_pairs={{0,1},{1,17},{2,3},{3,19},{4,5},{5,21},{6,7},{7,23},{8,0},{9,16},{... | collective-permute-start | bytes 442376 | tf_op jit(solution)/shard_map/ppermute | solution.py:639
  252.2 30.8 %collective-permute-start.37 = (bf16[4,24,768]{2,1,0:T(8,128)(2,1)}, bf16[4,24,768]{2,1,0:T(8,128)(2,1)S(1)}, u32[]{:S(2)}, u32[]{:S(2)}) collective-permute-start(bf16[4,24,768]{2,1,0:T(8,128)(2,1)} %get-tuple-element.112), channel_id=1, source_target_pairs={{0,8},{1,24},{2,10},{3,26},{4,12},{5,28},{6,14},{7,30},{8,9},{9,25... | collective-permute-start | bytes 442376 | tf_op jit(solution)/shard_map/ppermute | solution.py:639
  254.2 29.9 %collective-permute-start.38 = (bf16[4,24,768]{2,1,0:T(8,128)(2,1)}, bf16[4,24,768]{2,1,0:T(8,128)(2,1)S(1)}, u32[]{:S(2)}, u32[]{:S(2)}) collective-permute-start(bf16[4,24,768]{2,1,0:T(8,128)(2,1)} %get-tuple-element.113), channel_id=1, source_target_pairs={{0,9},{1,25},{2,11},{3,27},{4,13},{5,29},{6,15},{7,31},{8,8},{9,24... | collective-permute-start | bytes 442376 | tf_op jit(solution)/shard_map/ppermute | solution.py:639
  267.7 34.0 %all-to-all-start.1 = ((f32[32,1,312]{2,1,0:T(1,128)}), f32[32,1,312]{2,1,0:T(1,128)S(1)}, u32[]{:S(2)}, u32[]{:S(2)}) async-start(f32[32,1,312]{2,1,0:T(1,128)} %copy.56), calls=%async_computation.1 | async-start | bytes 98304 | tf_op jit(solution)/shard_map/all_to_all | solution.py:806
  301.7 34.5 %all-to-all-start.2 = ((bf16[32,24,768]{2,1,0:T(8,128)(2,1)}), bf16[32,24,768]{2,1,0:T(8,128)(2,1)S(1)}, u32[]{:S(2)}, u32[]{:S(2)}) async-start(bf16[32,24,768]{2,1,0:T(8,128)(2,1)} %get-tuple-element.127), calls=%async_computation.2 | async-start | bytes 2359296 | tf_op jit(solution)/shard_map/all_to_all | solution.py:806
  343.6 33.9 %all-to-all-start.3 = ((bf16[32,24,768]{2,1,0:T(8,128)(2,1)}), bf16[32,24,768]{2,1,0:T(8,128)(2,1)S(1)}, u32[]{:S(2)}, u32[]{:S(2)}) async-start(bf16[32,24,768]{2,1,0:T(8,128)(2,1)} %bitcast.87), calls=%async_computation.3 | async-start | bytes 2359296 | tf_op jit(solution)/shard_map/all_to_all | solution.py:806
  (75 other events, 677.4 us)
Sparse Core Ops, SparseCore 0:
  11.0 93.1 all-gather.1
where the time goes:
time: 391 us; the launch traced here: 390 us
  Pallas kernels  177 us (45%)
  starting transfers between devices  80.7 us (21%)
  waiting for transfers between devices  73.4 us (19%)
  other arithmetic  19.9 us (5%)
  local copies, waits for them, and re-layouts  19.5 us (5%)
  between operations  18.9 us (5%)
    pallas_call x21, Pallas kernels, call(): return lambda *operands: made(*operands, *after)  177 us
    ppermute x12, starting transfers between devices, second(): lax.ppermute(v, AXES, to_place(lambda z, y, x, c, m=m: (2 * c + ((z ^ m)...  24.7 us
    all_to_all x4, waiting for transfers between devices, to_all(): return lax.all_to_all(value, AXES, split_axis=0, concat_axis=0, tiled=True)  21.7 us
    all_to_all x4, starting transfers between devices, to_all(): return lax.all_to_all(value, AXES, split_axis=0, concat_axis=0, tiled=True)  17.9 us
    ppermute x5, waiting for transfers between devices, everywhere(): value = value + lax.ppermute(value, AXES, to_place(move))  13.7 us
    ppermute x8, waiting for transfers between devices, over_y(): lax.ppermute(value, AXES, to_place(lambda z, y, x, c: (z, 1 - y, x, c)))  10.5 us
    unnamed x111, local copies, waits for them, and re-layouts  10.3 us
    ppermute x12, waiting for transfers between devices, second(): lax.ppermute(v, AXES, to_place(lambda z, y, x, c, m=m: (2 * c + ((z ^ m)...  10.3 us
  transfers between devices with their start and end apart: 55, of which 17 were waited for; matrix products, arithmetic and copies ran while one was open for 7% of the time, Pallas kernels for 43%

commit v1 on v0

--- a/solution.py
+++ b/solution.py
@@ -115,15 +115,15 @@
 
 
 def project_body(a1_ref, dy_ref, w_ref, vec_ref, c_ref, a_ref, b_ref, q_ref, k_ref, v_ref, do_ref):
-    a1, tables = a1_ref[...], (c_ref[...], a_ref[...], b_ref[...])
+    a1, tables = a1_ref[0], (c_ref[...], a_ref[...], b_ref[...])
     q_ref[...] = rotate(mm(a1, w_ref[0], NN) + vec_ref[4:5, :], *tables).astype(bf16)
     k_ref[...] = rotate(mm(a1, w_ref[1], NN) + vec_ref[5:6, :], *tables).astype(bf16)
     v_ref[...] = (mm(a1, w_ref[2], NN) + vec_ref[6:7, :]).astype(bf16)
     do_ref[...] = mm(dy_ref[...], w_ref[3], NT).astype(bf16)
 
 
-def project(a1, dy, weights, vecs, tables, after=(), step=256):
-    count, width = a1.shape
+def project(acts, dy, weights, vecs, tables, step=256):
+    _, count, width = acts.shape
     token = pl.BlockSpec((step, width), lambda i: (i, 0))
     table = pl.BlockSpec((step, LANES), lambda i: (i, 0))
     return call(
@@ -132,7 +132,7 @@
         12 * count * width + 8 * width * width,
         grid=(count // step,),
         in_specs=[
-            token,
+            pl.BlockSpec((1, step, width), lambda i: (0, i, 0)),
             token,
             pl.BlockSpec((4, width, width), lambda i: (0, 0, 0)),
             pl.BlockSpec(vecs.shape, lambda i: (0, 0)),
@@ -142,12 +142,12 @@
         ],
         out_specs=[token] * 4,
         out_shape=[jax.ShapeDtypeStruct((count, width), bf16)] * 4,
-    )(a1, dy, weights, vecs, *tables)
+    )(acts, dy, weights, vecs, *tables)
 
 
 def attend_body(
     col_ref, row_ref, q_ref, k_ref, v_ref, do_ref, c_ref, a_ref, b_ref,
-    o_ref, g_ref, sum_ref, mask_ref, dk_acc, dv_acc, *, block,
+    g_ref, sum_ref, mask_ref, dk_acc, dv_acc, *, block,
 ):
     length = q_ref.shape[0]
     steps = length // block
@@ -193,7 +193,7 @@
         inner = jnp.sum(soft * d_soft, axis=0, keepdims=True)
         soft_low = soft.astype(bf16)
         d_scores = (soft * (d_soft - inner)).astype(bf16)
-        o_ref[here, :] = unstack(mm(values_t[:, lo:hi], soft_low, NN)).astype(bf16)
+        g_ref[3, here, :] = unstack(mm(values_t[:, lo:hi], soft_low, NN)).astype(bf16)
         dq = rotate_back(
             unstack(mm(keys_t[:, lo:hi], d_scores, NN)), c_ref[here, :], a_ref[here, :], b_ref[here, :]
         ).astype(bf16)
@@ -210,7 +210,7 @@
     sum_ref[2] = sub_sum(dv.astype(f32))
 
 
-def attend(segment_ids, q, k, v, do, tables, block=256):
+def attend(segment_ids, q, k, v, do, tables, after=(), block=256):
     rows, length = segment_ids.shape
     count, width = q.shape
     block = min(block, length)
@@ -220,6 +220,7 @@
         functools.partial(attend_body, block=block),
         24 * count * length * width,
         24 * count * width,
+        after=after,
         grid=(rows, width // LANES),
         in_specs=[
             pl.BlockSpec((length, 1), lambda r, h: (r, 0)),
@@ -233,13 +234,11 @@
             table,
         ],
         out_specs=[
-            token,
-            pl.BlockSpec((3, length, LANES), lambda r, h: (0, r, h)),
+            pl.BlockSpec((4, length, LANES), lambda r, h: (0, r, h)),
             pl.BlockSpec((3, 8, LANES), lambda r, h: (0, r, h)),
         ],
         out_shape=[
-            jax.ShapeDtypeStruct((count, width), bf16),
-            jax.ShapeDtypeStruct((3, count, width), bf16),
+            jax.ShapeDtypeStruct((4, count, width), bf16),
             jax.ShapeDtypeStruct((3, 8 * rows, width), f32),
         ],
         scratch_shapes=[
@@ -258,51 +257,62 @@
     )
 
 
-def half_grads_body(place_ref, *refs, first):
+def half_grads_body(place_ref, *refs, first, second, steps):
     l1o, l1p, l2o, l2p, r1o, r1p, r2o, r2p, ka_ref, sa_ref, kb_ref, sb_ref, acc = refs
-    n = pl.program_id(0)
+    i = pl.program_id(0)
     y, x = place_ref[1], place_ref[2]
     half = ka_ref.shape[-1]
 
-    @pl.when(n < first)
-    def _():
-        acc[...] = (mm(l1o[...], r1o[0], TN) + mm(l1p[...], r1p[0], TN)).reshape(acc.shape)
-
-    @pl.when(n >= first)
-    def _():
-        acc[...] = (mm(l2o[0], r2o[...], TN) + mm(l2p[0], r2p[...], TN)).reshape(acc.shape)
-
-    for ref, at in ((ka_ref, x), (sa_ref, 1 - x)):
-        ref[0] = acc[:, :, at, :, :, :half].astype(ref.dtype)
-    for ref, at in ((kb_ref, y), (sb_ref, 1 - y)):
-        ref[0] = acc[:, at, :, :, :, half:].astype(ref.dtype)
-
-
-def half_grads(place, left_one, left_two, right_one, right_two, shard, after=()):
-    count, width = left_one[0].shape
-    first, second = right_one[0].shape[0], left_two[0].shape[0]
+    @pl.when(i == 0)
+    def _():
+        acc[...] = jnp.zeros_like(acc)
+
+    for n in range(first + second):
+        if n < first:
+            part = mm(l1o[0], r1o[n], TN) + mm(l1p[0], r1p[n], TN)
+        else:
+            part = mm(l2o[n - first], r2o[...], TN) + mm(l2p[n - first], r2p[...], TN)
+        acc[n] += part.reshape(acc.shape[1:])
+
+    @pl.when(i == steps - 1)
+    def _():
+        for n in range(first + second):
+            for ref, at in ((ka_ref, x), (sa_ref, 1 - x)):
+                ref[n] = acc[n, :, :, at, :, :, :half].astype(ref.dtype)
+            for ref, at in ((kb_ref, y), (sb_ref, 1 - y)):
+                ref[n] = acc[n, :, at, :, :, :, half:].astype(ref.dtype)
+
+
+def layers(part, step, lanes, half=False):
+    _, first, count = part
+    return pl.BlockSpec((count, step, lanes), lambda i, *s: (first // count, i, s[0][3] if half else 0))
+
+
+def half_grads(place, left_one, left_two, right_one, right_two, shard, after=(), step=256):
+    first, second = right_one[2], left_two[2]
+    count, width = right_two[0].shape
     half = width // 2
     blocks = first + second
-    one = pl.BlockSpec((count, half), lambda n, s: (0, s[3]))
-    two = pl.BlockSpec((1, count, half), lambda n, s: (jnp.maximum(n - first, 0), 0, s[3]))
-    part = pl.BlockSpec((1, 2, 2, 2, shard, half), lambda n, s: (n, 0, 0, 0, 0, 0))
+    steps = count // step
     shape = (blocks, 2, 2, 2, shard, half)
+    out = pl.BlockSpec(shape, lambda i, s: (0, 0, 0, 0, 0, 0))
     return call(
-        functools.partial(half_grads_body, first=first),
+        functools.partial(half_grads_body, first=first, second=second, steps=steps),
         blocks * 2 * count * width * width,
         blocks * 4 * count * width,
         after=after,
         grid_spec=pltpu.PrefetchScalarGridSpec(
             num_scalar_prefetch=1,
-            grid=(blocks,),
-            in_specs=[one, one, two, two]
-            + [pl.BlockSpec((1, count, width), lambda n, s: (jnp.minimum(n, first - 1), 0, 0))] * 2
-            + [pl.BlockSpec((count, width), lambda n, s: (0, 0))] * 2,
-            out_specs=[part] * 4,
-            scratch_shapes=[pltpu.VMEM((2, 2, 2, 2, shard, width), f32)],
+            grid=(steps,),
+            in_specs=[layers(left_one, step, half, True)] * 2
+            + [layers(left_two, step, half, True)] * 2
+            + [layers(right_one, step, width)] * 2
+            + [pl.BlockSpec((step, width), lambda i, s: (i, 0))] * 2,
+            out_specs=[out] * 4,
+            scratch_shapes=[pltpu.VMEM((blocks, 2, 2, 2, 2, shard, width), f32)],
         ),
         out_shape=[jax.ShapeDtypeStruct(shape, k) for k in (f32, bf16, f32, bf16)],
-    )(place, *left_one, *left_two, *right_one, *right_two)
+    )(place, *left_one[0], *left_two[0], *right_one[0], *right_two)
 
 
 def full_grads(left_one, left_two, right_one, right_two):
@@ -322,13 +332,13 @@
     return jnp.where(u < 0, tail, 1.0 - tail), raised * (1.0 / math.sqrt(2.0 * math.pi))
 
 
-def hidden_body(a2_ref, dy_ref, wu_ref, wd_ref, bu_ref, e_ref, du_ref, sum_ref):
-    u = mm(a2_ref[...], wu_ref[0], NN) + bu_ref[0]
+def hidden_body(a2_ref, dy_ref, wu_ref, wd_ref, bu_ref, out_ref, sum_ref):
+    u = mm(a2_ref[0], wu_ref[0], NN) + bu_ref[0]
     de = mm(dy_ref[...], wd_ref[0], NT)
     dist, density = gelu_parts(u)
-    e_ref[0] = (u * dist).astype(bf16)
+    out_ref[0, 0] = (u * dist).astype(bf16)
     du = (de * (dist + u * density)).astype(bf16)
-    du_ref[0] = du
+    out_ref[1, 0] = du
     part = sub_sum(du.astype(f32))
 
     @pl.when(pl.program_id(1) == 0)
@@ -340,31 +350,33 @@
         sum_ref[0] += part
 
 
-def hidden(first, blocks, a2, dy, weights, vecs, after=(), step=512):
-    count, width = a2.shape
+def hidden(first, blocks, acts, dy, weights, vecs, after=(), step=512):
+    _, count, width = acts.shape
     splits = weights.shape[0] // 2
     token = pl.BlockSpec((step, width), lambda j, i: (i, 0))
-    out = pl.BlockSpec((1, step, width), lambda j, i: (j, i, 0))
-    return call(
+    both, sums = call(
         hidden_body,
         blocks * 4 * count * width * width,
         blocks * (8 * count * width + 4 * width * width),
         after=after,
         grid=(blocks, count // step),
         in_specs=[
-            token,
+            pl.BlockSpec((1, step, width), lambda j, i: (1, i, 0)),
             token,
             pl.BlockSpec((1, width, width), lambda j, i: (first + j, 0, 0)),
             pl.BlockSpec((1, width, width), lambda j, i: (splits + first + j, 0, 0)),
             pl.BlockSpec((1, 1, width), lambda j, i: (8 + first + j, 0, 0)),
         ],
-        out_specs=[out, out, pl.BlockSpec((1, 8, width), lambda j, i: (j, 0, 0))],
+        out_specs=[
+            pl.BlockSpec((2, 1, step, width), lambda j, i: (0, j, i, 0)),
+            pl.BlockSpec((1, 8, width), lambda j, i: (j, 0, 0)),
+        ],
         out_shape=[
-            jax.ShapeDtypeStruct((blocks, count, width), bf16),
-            jax.ShapeDtypeStruct((blocks, count, width), bf16),
+            jax.ShapeDtypeStruct((2, blocks, count, width), bf16),
             jax.ShapeDtypeStruct((blocks, 8, width), f32),
         ],
-    )(a2, dy, weights, weights, vecs[:, None, :])
+    )(acts, dy, weights, weights, vecs[:, None, :])
+    return both.reshape(2 * blocks, count, width), sums
 
 
 def norm_back(grad, unit, scale, gain):
@@ -385,17 +397,13 @@
 
 def output_body(x_ref, o_ref, *refs, splits):
     *e_refs, wo_ref, wm_ref, vec_ref, out_ref = refs
-    acc = hidden_sum(e_refs, wm_ref, 0, NN, mm(o_ref[...], wo_ref[0], NN))
+    acc = hidden_sum(e_refs, wm_ref, 0, NN, mm(o_ref[0], wo_ref[0], NN))
     bias = vec_ref[7:8, :] + vec_ref[8 + splits : 9 + splits, :]
     out_ref[...] = (x_ref[...].astype(f32) + acc + bias).astype(bf16)
 
 
 def resident(blocks, width, at):
     return pl.BlockSpec((blocks, width, width), lambda i: (at, 0, 0), pipeline_mode=pl.Buffered(1))
-
-
-def stacked(value, step):
-    return pl.BlockSpec((value.shape[0], step, value.shape[2]), lambda i: (0, i, 0))
 
 
 def output(x, o, es, wa, wm, vecs, after=(), step=256):
@@ -408,12 +416,12 @@
         14 * count * width + 10 * width * width,
         after=after,
         grid=(count // step,),
-        in_specs=[token, token]
-        + [stacked(e, step) for e in es]
+        in_specs=[token]
+        + [layers(v, step, width) for v in (o, *es)]
         + [resident(1, width, 3), resident(splits, width, 1), pl.BlockSpec(vecs.shape, lambda i: (0, 0))],
         out_specs=token,
         out_shape=jax.ShapeDtypeStruct((count, width), bf16),
-    )(x, o, *es, wa, wm, vecs)
+    )(x, *[v[0] for v in (o, *es)], wa, wm, vecs)
 
 
 def normed(x):
@@ -436,41 +444,15 @@
             sum_ref[n] += s
 
 
-def grad_two_body(x_ref, dy_ref, *refs):
-    *du_refs, wm_ref, vec_ref, part_ref, sum_ref = refs
+def grad_one_body(x_ref, dy_ref, g_ref, wa_ref, vec_ref, part_ref, sum_ref):
     dy = dy_ref[...].astype(f32)
-    grad = hidden_sum(du_refs, wm_ref, 0, NT, None)
-    unit, scale = normed(x_ref[...].astype(f32))
-    part_ref[...] = dy + norm_back(grad, unit, scale, vec_ref[2:3, :])
-    add_sums(sum_ref, (grad * unit, grad, dy))
-
-
-def grad_two(x, dy, dus, wm, vecs, after=(), step=256):
-    count, width = x.shape
-    splits = wm.shape[0] // 2
-    token = pl.BlockSpec((step, width), lambda i: (i, 0))
-    return call(
-        grad_two_body,
-        8 * count * width * width,
-        16 * count * width + 8 * width * width,
-        after=after,
-        grid=(count // step,),
-        in_specs=[token, token]
-        + [stacked(d, step) for d in dus]
-        + [resident(splits, width, 0), pl.BlockSpec(vecs.shape, lambda i: (0, 0))],
-        out_specs=[token, pl.BlockSpec((3, 8, width), lambda i: (0, 0, 0))],
-        out_shape=[jax.ShapeDtypeStruct((count, width), f32), jax.ShapeDtypeStruct((3, 8, width), f32)],
-    )(x, dy, *dus, wm, vecs)
-
-
-def grad_one_body(x_ref, part_ref, g_ref, wa_ref, vec_ref, grad_ref, sum_ref):
     grad = mm(g_ref[0], wa_ref[0], NT) + mm(g_ref[1], wa_ref[1], NT) + mm(g_ref[2], wa_ref[2], NT)
     unit, scale = normed(x_ref[...].astype(f32))
-    grad_ref[...] = (part_ref[...] + norm_back(grad, unit, scale, vec_ref[0:1, :])).astype(bf16)
-    add_sums(sum_ref, (grad * unit, grad))
-
-
-def grad_one(x, part, g, wa, vecs, after=(), step=256):
+    part_ref[...] = dy + norm_back(grad, unit, scale, vec_ref[0:1, :])
+    add_sums(sum_ref, (grad * unit, grad, dy))
+
+
+def grad_one(x, dy, g, wa, vecs, after=(), step=256):
     count, width = x.shape
     token = pl.BlockSpec((step, width), lambda i: (i, 0))
     return call(
@@ -482,13 +464,39 @@
         in_specs=[
             token,
             token,
-            stacked(g, step),
+            layers(g, step, width),
             resident(3, width, 0),
             pl.BlockSpec(vecs.shape, lambda i: (0, 0)),
         ],
+        out_specs=[token, pl.BlockSpec((3, 8, width), lambda i: (0, 0, 0))],
+        out_shape=[jax.ShapeDtypeStruct((count, width), f32), jax.ShapeDtypeStruct((3, 8, width), f32)],
+    )(x, dy, g[0], wa, vecs)
+
+
+def grad_two_body(x_ref, part_ref, *refs):
+    *du_refs, wm_ref, vec_ref, grad_ref, sum_ref = refs
+    grad = hidden_sum(du_refs, wm_ref, 0, NT, None)
+    unit, scale = normed(x_ref[...].astype(f32))
+    grad_ref[...] = (part_ref[...] + norm_back(grad, unit, scale, vec_ref[2:3, :])).astype(bf16)
+    add_sums(sum_ref, (grad * unit, grad))
+
+
+def grad_two(x, part, dus, wm, vecs, after=(), step=256):
+    count, width = x.shape
+    splits = wm.shape[0] // 2
+    token = pl.BlockSpec((step, width), lambda i: (i, 0))
+    return call(
+        grad_two_body,
+        8 * count * width * width,
+        16 * count * width + 8 * width * width,
+        after=after,
+        grid=(count // step,),
+        in_specs=[token, token]
+        + [layers(v, step, width) for v in dus]
+        + [resident(splits, width, 0), pl.BlockSpec(vecs.shape, lambda i: (0, 0))],
         out_specs=[token, pl.BlockSpec((2, 8, width), lambda i: (0, 0, 0))],
         out_shape=[jax.ShapeDtypeStruct((count, width), bf16), jax.ShapeDtypeStruct((2, 8, width), f32)],
-    )(x, part, g, wa, vecs)
+    )(x, part, *[v[0] for v in dus], wm, vecs)
 
 
 def grid_places():
@@ -598,12 +606,33 @@
             )
 
 
-def summed(body, place, operands, shapes, after, steps=2):
-    def spec(s):
+class Reduction:
+    def __init__(self, ka, sa, kb, sb):
+        self.made = ka
+        self.held = (ka, over_x(sa), kb, over_y(sb))
+
+
+def advance(place, pairs, planes, after=(), steps=2):
+    blocks, *_, shard, half = (pairs + planes)[0].held[0].shape
+    shapes = [jax.ShapeDtypeStruct((blocks, 2, 2, shard, half), k) for k in (f32, bf16, f32, bf16)] * len(pairs)
+    if planes:
+        shapes += [jax.ShapeDtypeStruct((len(planes), blocks, shard, 2 * half), bf16)] * 4
+    operands = [v for r in pairs + planes for v in r.held]
+
+    def spec(s, at=0):
         n = len(s.shape)
-        return pl.BlockSpec((s.shape[0] // steps, *s.shape[1:]), lambda b, p: (b,) + (0,) * (n - 1))
-
-    return call(
+        block = tuple(d // steps if m == at else d for m, d in enumerate(s.shape))
+        return pl.BlockSpec(block, lambda b, p: (0,) * at + (b,) + (0,) * (n - 1 - at))
+
+    def body(place_ref, *refs):
+        ins, outs = refs[: len(operands)], refs[len(operands) :]
+        for n in range(len(pairs)):
+            chip_pair_body(place_ref, *ins[4 * n : 4 * n + 4], *outs[4 * n : 4 * n + 4])
+        for n in range(len(planes)):
+            m = 4 * (len(pairs) + n)
+            plane_body(place_ref, *ins[m : m + 4], *[ref.at[n] for ref in outs[4 * len(pairs) :]])
+
+    outs = call(
         body,
         0,
         sum(v.size * v.dtype.itemsize for v in operands) * 2,
@@ -612,35 +641,24 @@
             num_scalar_prefetch=1,
             grid=(steps,),
             in_specs=[spec(v) for v in operands],
-            out_specs=[spec(s) for s in shapes],
+            out_specs=[spec(s, n >= 4 * len(pairs)) for n, s in enumerate(shapes)],
         ),
         out_shape=shapes,
     )(place, *operands)
-
-
-class Reduction:
-    def __init__(self, place, ka, sa, kb, sb):
-        self.place, self.made = place, ka
-        self.held = (ka, over_x(sa), kb, over_y(sb))
-
-    def first(self, after):
-        blocks, two, _, c, shard, half = self.held[0].shape
-        shapes = [jax.ShapeDtypeStruct((blocks, two, c, shard, half), k) for k in (f32, bf16, f32, bf16)]
-        ka, sa, kb, sb = summed(chip_pair_body, self.place, self.held, shapes, after)
-        self.held = (ka, over_y(sa), kb, over_x(sb))
-        self.made = ka
-
-    def second(self, after):
-        blocks, _, _, shard, half = self.held[0].shape
-        shapes = [jax.ShapeDtypeStruct((blocks, shard, 2 * half), bf16)] * 4
-        parts = summed(plane_body, self.place, self.held, shapes, after)
-        self.made = parts[0]
-        self.terms = [
+    for n, r in enumerate(pairs):
+        ka, sa, kb, sb = outs[4 * n : 4 * n + 4]
+        r.made = ka
+        r.held = (ka, over_y(sa), kb, over_x(sb))
+    terms = []
+    for m, v in enumerate(outs[4 * len(pairs) :]):
+        planes[0].made = v
+        v = v.reshape(-1, shard, 2 * half)
+        terms.append(
             lax.ppermute(
                 v, AXES, to_place(lambda z, y, x, c, m=m: (2 * c + ((z ^ m) >> 1), y, x, (z ^ m) & 1))
             )
-            for m, v in enumerate(parts)
-        ]
+        )
+    return terms
 
 
 def everywhere(value):
@@ -797,9 +815,7 @@
     centred = values - jnp.mean(values, axis=-1, keepdims=True)
     spread = jnp.mean(centred * centred, axis=-1, keepdims=True)
     unit = centred * lax.rsqrt(spread + norm_epsilon)
-    one = (unit * vecs[0] + vecs[1]).astype(bf16)
-    two = (unit * vecs[2] + vecs[3]).astype(bf16)
-    return one, two
+    return jnp.stack([unit * vecs[0] + vecs[1], unit * vecs[2] + vecs[3]]).astype(bf16)
 
 
 def to_all(value):
@@ -838,78 +854,84 @@
     flat_tokens = tokens.reshape(count, width)
     dy = cotangent.reshape(count, width)
     tables = rotary_tables(segment_ids)
-    a1, a2 = layer_inputs(flat_tokens, vecs)
+    acts = layer_inputs(flat_tokens, vecs)
     place = jnp.stack(grid_places()).astype(jnp.int32)
     if paired:
-        attn_weights = gather_staged(place, low_blocks[:4], after=(*tables, a1, a2))
+        attn_weights = gather_staged(place, low_blocks[:4], after=(*tables, acts))
     else:
         attn_weights = lax.all_gather(low_blocks[:4], AXES, axis=1, tiled=True)
 
-    q, k, v, do = project(a1, dy, attn_weights, vecs, tables)
-    o, g, attn_sums = attend(segment_ids, q, k, v, do, tables)
+    def pair(v):
+        return (v, over_c(v)) if paired else (v, v)
+
+    def pair(v):
+        return (v, over_c(v)) if paired else (v, v)
+
+    q, k, v, do = project(acts, dy, attn_weights, vecs, tables)
+    both_acts, dys = pair(acts), pair(dy)
+    og, attn_sums = attend(segment_ids, q, k, v, do, tables, after=(both_acts[1], dys[1]))
     half = splits // 2
     orders = [list(range(4))]
     for first in (0, half):
         orders.append([base + first + j for base in (4, 4 + splits) for j in range(half)])
     if paired:
-
-        def pair(v):
-            return v, over_c(v)
-
-        a1s, a2s, dys = pair(a1), pair(a2), pair(dy)
-        os, gs = pair(o[None]), pair(g)
-        e0, du0, up_sum0 = hidden(0, half, a2, dy, mlp_weights, vecs, after=(o,))
-        es, dus = [pair(e0)], [pair(du0)]
-        attn = Reduction(place, *half_grads(place, a1s, os, gs, dys, shard, after=(e0,)))
-        e1, du1, up_sum1 = hidden(half, half, a2, dy, mlp_weights, vecs, after=(attn.made,))
-        es.append(pair(e1))
-        dus.append(pair(du1))
-        low = Reduction(place, *half_grads(place, a2s, es[0], dus[0], dys, shard, after=(e1,)))
-        attn.first(after=(low.made,))
-        high = Reduction(place, *half_grads(place, a2s, es[1], dus[1], dys, shard, after=(attn.made,)))
-        out = output(flat_tokens, o, [e0, e1], attn_weights, mlp_weights, vecs, after=(high.made,))
-        low.first(after=(out,))
-        attn.second(after=(low.made,))
-        part, two_sums = grad_two(flat_tokens, dy, [du0, du1], mlp_weights, vecs, after=(attn.made,))
-        high.first(after=(part,))
-        low.second(after=(high.made,))
-        grad_in, one_sums = grad_one(flat_tokens, part, g, attn_weights, vecs, after=(low.made,))
-        high.second(after=(grad_in,))
-        terms = [r.terms for r in (attn, low, high)]
+        ogs = pair(og)
+        ed0, up_sum0 = hidden(0, half, acts, dy, mlp_weights, vecs, after=(og,))
+        ed1, up_sum1 = hidden(half, half, acts, dy, mlp_weights, vecs, after=(ed0,))
+        ed0s, ed1s = pair(ed0), pair(ed1)
+        attn = Reduction(
+            *half_grads(place, (both_acts, 0, 1), (ogs, 3, 1), (ogs, 0, 3), dys, shard, after=(ed1,))
+        )
+        low = Reduction(
+            *half_grads(
+                place, (both_acts, 1, 1), (ed0s, 0, half), (ed0s, half, half), dys, shard, after=(attn.made,)
+            )
+        )
+        high = Reduction(
+            *half_grads(
+                place, (both_acts, 1, 1), (ed1s, 0, half), (ed1s, half, half), dys, shard, after=(low.made,)
+            )
+        )
+        es, dus = [(v, 0, half) for v in (ed0, ed1)], [(v, half, half) for v in (ed0, ed1)]
+        advance(place, [attn], [], after=(high.made,))
+        out = output(flat_tokens, (og, 3, 1), es, attn_weights, mlp_weights, vecs, after=(attn.made,))
+        terms = [advance(place, [low], [attn], after=(out,))]
+        part, one_sums = grad_one(flat_tokens, dy, (og, 0, 3), attn_weights, vecs, after=(low.made,))
+        terms.append(advance(place, [high], [low], after=(part, *terms[0])))
+        terms.append(advance(place, [], [high]))
+        grad_in, two_sums = grad_two(flat_tokens, part, dus, mlp_weights, vecs, after=(high.made, *terms[1]))
     else:
-        e0, du0, up_sum0 = hidden(0, half, a2, dy, mlp_weights, vecs)
-        e1, du1, up_sum1 = hidden(half, half, a2, dy, mlp_weights, vecs)
+        ed0, up_sum0 = hidden(0, half, acts, dy, mlp_weights, vecs)
+        ed1, up_sum1 = hidden(half, half, acts, dy, mlp_weights, vecs)
         grads = [
-            full_grads(a1, o[None], g, dy),
-            full_grads(a2, e0, du0, dy),
-            full_grads(a2, e1, du1, dy),
+            full_grads(acts[0], og[3:], og[:3], dy),
+            full_grads(acts[1], ed0[:half], ed0[half:], dy),
+            full_grads(acts[1], ed1[:half], ed1[half:], dy),
         ]
         terms = [[lax.psum_scatter(v, AXES, scatter_dimension=1, tiled=True)] for v in grads]
-        out = output(flat_tokens, o, [e0, e1], attn_weights, mlp_weights, vecs)
-        part, two_sums = grad_two(flat_tokens, dy, [du0, du1], mlp_weights, vecs)
-        grad_in, one_sums = grad_one(flat_tokens, part, g, attn_weights, vecs)
+        es, dus = [(v, 0, half) for v in (ed0, ed1)], [(v, half, half) for v in (ed0, ed1)]
+        out = output(flat_tokens, (og, 3, 1), es, attn_weights, mlp_weights, vecs)
+        part, one_sums = grad_one(flat_tokens, dy, (og, 0, 3), attn_weights, vecs)
+        grad_in, two_sums = grad_two(flat_tokens, part, dus, mlp_weights, vecs)
     up_sums = [up_sum0, up_sum1]
 
     one_sums, two_sums = jnp.sum(one_sums, axis=1), jnp.sum(two_sums, axis=1)
     qkv_sums = jnp.sum(attn_sums, axis=1)
     up_sums = jnp.sum(jnp.concatenate(up_sums, axis=0), axis=1)
-    bias_sum = two_sums[2:]
+    bias_sum = one_sums[2:]
     grad_vectors = jnp.concatenate(
-        [one_sums, two_sums[:2], qkv_sums, bias_sum, up_sums, bias_sum], axis=0
+        [one_sums[:2], two_sums, qkv_sums, bias_sum, up_sums, bias_sum], axis=0
     )
-    by_slot = grad_vectors.reshape(vec_rows, slot_count, shard).transpose(1, 0, 2)
-    shard_vectors = jnp.sum(to_all(by_slot.reshape(slot_count, -1)), axis=0).reshape(vec_rows, shard)
-
     slot_ids = jnp.arange(slot_count, dtype=jnp.int32)
     match = owners[None, :] == slot_ids[:, None]
     slots = jnp.sum(jnp.where(match, jnp.arange(1, owners.shape[0] + 1, dtype=jnp.int32)[None], 0), axis=1) - 1
     has_block = jnp.any(owners == my_index)
     shards, outgoing, squares = pack(slots, terms, orders, after=(grad_in,))
-    local = jnp.sum(squares) + jnp.sum(shard_vectors * shard_vectors)
-    if paired:
-        square_sum = everywhere(jnp.broadcast_to(local, (8, LANES)))[0, 0]
-    else:
-        square_sum = jnp.sum(to_all(jnp.broadcast_to(local, (slot_count, LANES)))[:, 0])
+    local = jnp.concatenate([grad_vectors, jnp.sum(squares, axis=0)[None], jnp.zeros((2, width), f32)])
+    total = everywhere(local) if paired else lax.psum(local, AXES)
+    vector_sums = total[:vec_rows]
+    square_sum = jnp.sum(total[vec_rows]) + jnp.sum(vector_sums * vector_sums)
+    shard_vectors = lax.dynamic_slice_in_dim(vector_sums, my_index * shard, shard, axis=1)
     grad_norm = jnp.sqrt(square_sum)
     factor = jnp.minimum(1.0, clip_level / grad_norm)
     root_count = math.sqrt(NPARAM)

time: 391 us -> 401 us (1.026)
  waiting for transfers between devices: 73.4 us -> 89.7 us
  Pallas kernels: 177 us -> 172 us
    ppermute x8, waiting for transfers between devices: 10.5 us -> 27.1 us  [over_y(): lax.ppermute(value, AXES, to_place(lambda z, y, x, c: (z, 1 - y, x, c)))]
    ppermute x14 -> x10, waiting for transfers between devices: 9.6 us -> 0.03 us  [over_c(): lax.ppermute(value, AXES, to_place(lambda z, y, x, c: (z, y, x, 1 - c)))]
    ppermute x3, waiting for transfers between devices: 0.01 us -> 9.18 us  [over_z(): lax.ppermute(value, AXES, to_place(lambda z, y, x, c: ((z + by) % 4, y, x...]
    ppermute x12, waiting for transfers between devices: 10.3 us -> 2.05 us  [advance(): lax.ppermute(v, AXES, to_place(lambda z, y, x, c, m=m: (2 * c + ((z ^ m)...]
    ppermute x5, waiting for transfers between devices: 13.7 us -> 21.6 us  [everywhere(): value = value + lax.ppermute(value, AXES, to_place(move))]
    ppermute x12, starting transfers between devices: 24.7 us -> 30.6 us  [advance(): lax.ppermute(v, AXES, to_place(lambda z, y, x, c, m=m: (2 * c + ((z ^ m)...]
    pallas_call x21 -> x19, Pallas kernels: 177 us -> 172 us  [call(): return lambda *operands: made(*operands, *after)]
    all_to_all x4 -> x3, waiting for transfers between devices: 21.7 us -> 24.2 us  [to_all(): return lax.all_to_all(value, AXES, split_axis=0, concat_axis=0, tiled=True)]
  transfers between devices with their start and end apart: 55 -> 50, of which waited for: 17 -> 15; matrix products, arithmetic and copies ran while one was open for 7% -> 8% of each run, Pallas kernels for 43% -> 38%
where the time goes in v1:
time: 401 us; the launch traced here: 400 us
  Pallas kernels  172 us (43%)
  waiting for transfers between devices  89.7 us (22%)
  starting transfers between devices  78.7 us (20%)
  other arithmetic  22.8 us (6%)
  local copies, waits for them, and re-layouts  18.7 us (5%)
  between operations  18.1 us (5%)
    pallas_call x19, Pallas kernels, call(): return lambda *operands: made(*operands, *after)  172 us
    ppermute x12, starting transfers between devices, advance(): lax.ppermute(v, AXES, to_place(lambda z, y, x, c, m=m: (2 * c + ((z ^ m)...  30.6 us
    ppermute x8, waiting for transfers between devices, over_y(): lax.ppermute(value, AXES, to_place(lambda z, y, x, c: (z, 1 - y, x, c)))  27.1 us
    all_to_all x3, waiting for transfers between devices, to_all(): return lax.all_to_all(value, AXES, split_axis=0, concat_axis=0, tiled=True)  24.2 us
    ppermute x5, waiting for transfers between devices, everywhere(): value = value + lax.ppermute(value, AXES, to_place(move))  21.6 us
    all_to_all x3, starting transfers between devices, to_all(): return lax.all_to_all(value, AXES, split_axis=0, concat_axis=0, tiled=True)  18.3 us
    unnamed x89, local copies, waits for them, and re-layouts  9.81 us
    ppermute x8, starting transfers between devices, over_y(): lax.ppermute(value, AXES, to_place(lambda z, y, x, c: (z, 1 - y, x, c)))  9.39 us
  transfers between devices with their start and end apart: 50, of which 15 were waited for; matrix products, arithmetic and copies ran while one was open for 8% of the time, Pallas kernels for 38%

profile of v1, /device:TPU:0, one launch (start us, length us, event | category | flops | bytes accessed | tf_op | source)
XLA Modules:
  0.0 399.6 jit_solution(13855702179063394020)
XLA Ops:
  12.9 7.3 %all-to-all-start = ((bf16[32,2,156]{2,1,0:T(2,128)(2,1)}), bf16[32,2,156]{2,1,0:T(2,128)(2,1)S(1)}, u32[]{:S(2)}, u32[]{:S(2)}) async-start(bf16[32,2,156]{2,1,0:T(2,128)(2,1)} %reshape.564), calls=%async_computation | async-start | bytes 65536 | tf_op jit(solution)/shard_map/all_to_all | solution.py:822
  23.2 4.3 %all-to-all-done = bf16[32,2,156]{2,1,0:T(2,128)(2,1)S(1)} async-done(((bf16[32,2,156]{2,1,0:T(2,128)(2,1)}), bf16[32,2,156]{2,1,0:T(2,128)(2,1)S(1)}, u32[]{:S(2)}, u32[]{:S(2)}) %all-to-all-start) | async-done | bytes 20000 | tf_op jit(solution)/shard_map/all_to_all | solution.py:822
  37.2 9.1 %collective-permute-done.1 = bf16[4,24,768]{2,1,0:T(8,128)(2,1)S(1)} collective-permute-done((bf16[4,24,768]{2,1,0:T(8,128)(2,1)S(1)}, bf16[4,24,768]{2,1,0:T(8,128)(2,1)S(1)}, u32[]{:S(2)}, u32[]{:S(2)}) %collective-permute-start.1) | collective-permute-done | bytes 147488 | tf_op jit(solution)/shard_map/ppermute | solution.py:531
  49.9 13.1 %collective-permute-done.4.refs_3_ = bf16[4,4,24,768]{3,2,1,0:T(8,128)(2,1)} collective-permute-done((bf16[4,4,24,768]{3,2,1,0:T(8,128)(2,1)}, bf16[4,4,24,768]{3,2,1,0:T(8,128)(2,1)}, u32[]{:S(2)}, u32[]{:S(2)}) %collective-permute-start.4) | collective-permute-done | bytes 589856 | tf_op jit(solution)/shard_map/ppermute | solution.py:527
  73.9 9.9 %collective-permute-done.5.refs_4_ = bf16[2,4,24,768]{3,2,1,0:T(8,128)(2,1)} collective-permute-done((bf16[2,4,24,768]{3,2,1,0:T(8,128)(2,1)S(1)}, bf16[2,4,24,768]{3,2,1,0:T(8,128)(2,1)}, u32[]{:S(2)}, u32[]{:S(2)}) %collective-permute-start.5) | collective-permute-done | bytes 294944 | tf_op jit(solution)/shard_map/ppermute | solution.py:527
  84.4 5.0 %compare_select_fusion.9 = f32[128]{0:T(128)S(1)} fusion(f32[]{:T(128)} %bitcast.16, f32[]{:T(128)} %bitcast.17, f32[]{:T(128)} %bitcast.18, f32[]{:T(128)} %bitcast.19, f32[]{:T(128)} %bitcast.20, f32[]{:T(128)} %bitcast.22, f32[]{:T(128)} %bitcast.21, f32[]{:T(128)} %bitcast.15), kind=kLoop, calls=%fused_computation.41 | loop fusion | flops 5376 | bytes 544 | tf_op jit(solution)/shard_map/jit(_where)/select_n | solution.py:90
  95.9 6.0 %shard_map.202 = bf16[4,32,24,768]{3,2,1,0:T(8,128)(2,1)} custom-call(s32[4]{0:T(128)} %pad_add_fusion.refs_0_.place_ref, bf16[4,4,24,768]{3,2,1,0:T(8,128)(2,1)} %pad_maximum_fusion.1.refs_1_, bf16[4,4,24,768]{3,2,1,0:T(8,128)(2,1)} %collective-permute-done.3.refs_2_, bf16[4,4,24,768]{3,2,1,0:T(8,128)(2,1)} %collective-permute-done.4.refs_3_, ...), custom_call_target="tpu_custom_call" | custom-call | bytes 9437184 | tf_op jit(solution)/shard_map/pallas_call | solution.py:74
  101.9 9.9 %shard_map.203 = (bf16[1024,768]{1,0:T(8,128)(2,1)}, bf16[1024,768]{1,0:T(8,128)(2,1)}, bf16[1024,768]{1,0:T(8,128)(2,1)}, bf16[1024,768]{1,0:T(8,128)(2,1)}) custom-call(bf16[2,1024,768]{2,1,0:T(8,128)(2,1)} %copy-done, bf16[1024,768]{1,0:T(8,128)(2,1)} %bitcast.5.dy_ref.refs_1_.refs_7_, bf16[4,768,768]{2,1,0:T(8,128)(2,1)} %bitcast.99, ...), custom_call_target="tpu_custom_call" | custom-call | flops 4831838208 | bytes 14155776 | tf_op jit(solution)/shard_map/pallas_call | solution.py:74
  111.9 27.3 %shard_map.204 = (bf16[4,1024,768]{2,1,0:T(8,128)(2,1)}, f32[3,16,768]{2,1,0:T(8,128)}) custom-call(s32[1024,1]{1,0:T(8,128)} %bitcast.110, s32[2,1,512]{2,1,0:T(1,128)} %reshape.488.refs_1_, bf16[1024,768]{1,0:T(8,128)(2,1)} %get-tuple-element.70.refs_2_, bf16[1024,768]{1,0:T(8,128)(2,1)} %get-tuple-element.71.refs_3_, ...), custom_call_target="tpu_custom_call" | custom-call | flops 9663676416 | bytes 18874368 | tf_op jit(solution)/shard_map/pallas_call | solution.py:74
  139.3 12.6 %shard_map.205 = (bf16[2,2,1024,768]{3,2,1,0:T(8,128)(2,1)}, f32[2,8,768]{2,1,0:T(8,128)}) custom-call(bf16[2,1024,768]{2,1,0:T(8,128)(2,1)} %copy-done, bf16[1024,768]{1,0:T(8,128)(2,1)} %bitcast.5.dy_ref.refs_1_.refs_7_, bf16[8,768,768]{2,1,0:T(8,128)(2,1)} %all-gather.2.cloned.1.call-done.refs_2_.refs_3_.refs_5_.refs_4_, ...), custom_call_target="tpu_custom_call" | custom-call | flops 4831838208 | bytes 17301504 | tf_op jit(solution)/shard_map/pallas_call | solution.py:74
  152.3 12.6 %shard_map.206 = (bf16[2,2,1024,768]{3,2,1,0:T(8,128)(2,1)}, f32[2,8,768]{2,1,0:T(8,128)}) custom-call(bf16[2,1024,768]{2,1,0:T(8,128)(2,1)} %copy-done, bf16[1024,768]{1,0:T(8,128)(2,1)} %bitcast.5.dy_ref.refs_1_.refs_7_, bf16[8,768,768]{2,1,0:T(8,128)(2,1)} %all-gather.2.cloned.1.call-done.refs_2_.refs_3_.refs_5_.refs_4_, ...), custom_call_target="tpu_custom_call" | custom-call | flops 4831838208 | bytes 17301504 | tf_op jit(solution)/shard_map/pallas_call | solution.py:74
  165.0 11.9 %shard_map.207 = (f32[4,2,2,2,24,384]{5,4,3,2,1,0:T(8,128)}, bf16[4,2,2,2,24,384]{5,4,3,2,1,0:T(8,128)(2,1)}, f32[4,2,2,2,24,384]{5,4,3,2,1,0:T(8,128)}, bf16[4,2,2,2,24,384]{5,4,3,2,1,0:T(8,128)(2,1)}) custom-call(s32[4]{0:T(128)} %pad_add_fusion.refs_0_.place_ref, bf16[2,1024,768]{2,1,0:T(8,128)(2,1)} %copy-done, ...), custom_call_target="tpu_custom_call" | custom-call | flops 4831838208 | bytes 12582912 | tf_op jit(solution)/shard_map/pallas_call | solution.py:74
  179.6 11.8 %shard_map.208 = (f32[4,2,2,2,24,384]{5,4,3,2,1,0:T(8,128)}, bf16[4,2,2,2,24,384]{5,4,3,2,1,0:T(8,128)(2,1)}, f32[4,2,2,2,24,384]{5,4,3,2,1,0:T(8,128)}, bf16[4,2,2,2,24,384]{5,4,3,2,1,0:T(8,128)(2,1)}) custom-call(s32[4]{0:T(128)} %pad_add_fusion.refs_0_.place_ref, bf16[2,1024,768]{2,1,0:T(8,128)(2,1)} %copy-done, ...), custom_call_target="tpu_custom_call" | custom-call | flops 4831838208 | bytes 12582912 | tf_op jit(solution)/shard_map/pallas_call | solution.py:74
  191.4 11.7 %shard_map.209 = (f32[4,2,2,2,24,384]{5,4,3,2,1,0:T(8,128)}, bf16[4,2,2,2,24,384]{5,4,3,2,1,0:T(8,128)(2,1)}, f32[4,2,2,2,24,384]{5,4,3,2,1,0:T(8,128)}, bf16[4,2,2,2,24,384]{5,4,3,2,1,0:T(8,128)(2,1)}) custom-call(s32[4]{0:T(128)} %pad_add_fusion.refs_0_.place_ref, bf16[2,1024,768]{2,1,0:T(8,128)(2,1)} %copy-done, ...), custom_call_target="tpu_custom_call" | custom-call | flops 4831838208 | bytes 12582912 | tf_op jit(solution)/shard_map/pallas_call | solution.py:74
  204.1 3.7 shard_map.210
  213.8 4.1 %collective-permute-done.21.refs_6_ = bf16[4,2,2,24,384]{4,3,2,1,0:T(8,128)(2,1)S(1)} collective-permute-done((bf16[4,2,2,24,384]{4,3,2,1,0:T(8,128)(2,1)}, bf16[4,2,2,24,384]{4,3,2,1,0:T(8,128)(2,1)S(1)}, u32[]{:S(2)}, u32[]{:S(2)}) %collective-permute-start.21) | collective-permute-done | bytes 294944 | tf_op jit(solution)/shard_map/ppermute | solution.py:527
  217.9 11.1 %shard_map.211.refs_9_ = bf16[1024,768]{1,0:T(8,128)(2,1)} custom-call(bf16[1024,768]{1,0:T(8,128)(2,1)} %bitcast.96, bf16[4,1024,768]{2,1,0:T(8,128)(2,1)} %get-tuple-element.74.refs_5_.refs_3_.refs_1_.refs_2_, bf16[4,1024,768]{2,1,0:T(8,128)(2,1)} %bitcast.88, bf16[4,1024,768]{2,1,0:T(8,128)(2,1)} %bitcast.94, bf16[4,768,768]{2,1,0:T(8,128)(2,1)} %bitcast.100, ...), custom_call_target="tpu_custom_call" | custom-call | flops 6039797760 | bytes 16908288 | tf_op jit(solution)/shard_map/pallas_call | solution.py:74
  231.7 4.3 %shard_map.212 = (f32[4,2,2,24,384]{4,3,2,1,0:T(8,128)}, bf16[4,2,2,24,384]{4,3,2,1,0:T(8,128)(2,1)}, f32[4,2,2,24,384]{4,3,2,1,0:T(8,128)}, bf16[4,2,2,24,384]{...) custom-call(s32[4]{0:T(128)} %pad_add_fusion.refs_0_.place_ref, ...), custom_call_target="tpu_custom_call" | custom-call | bytes 10616832 | tf_op jit(solution)/shard_map/pallas_call | solution.py:74
  237.6 7.2 %collective-permute-start.28 = (bf16[4,24,768]{2,1,0:T(8,128)(2,1)}, bf16[4,24,768]{2,1,0:T(8,128)(2,1)S(1)}, u32[]{:S(2)}, u32[]{:S(2)}) collective-permute-start(bf16[4,24,768]{2,1,0:T(8,128)(2,1)} %bitcast.129), channel_id=1, source_target_pairs={{0,1},{1,17},{2,3},{3,19},{4,5},{5,21},{6,7},{7,23},{8,0},{9,16},{... | collective-permute-start | bytes 442376 | tf_op jit(solution)/shard_map/ppermute | solution.py:657
  246.8 3.9 collective-permute-start.30
  251.9 9.8 %shard_map.213 = (f32[1024,768]{1,0:T(8,128)}, f32[3,8,768]{2,1,0:T(8,128)}) custom-call(bf16[1024,768]{1,0:T(8,128)(2,1)} %bitcast.97, bf16[1024,768]{1,0:T(8,128)(2,1)} %bitcast.5.dy_ref.refs_1_.refs_7_, bf16[4,1024,768]{2,1,0:T(8,128)(2,1)} %get-tuple-element.74.refs_5_.refs_3_.refs_1_.refs_2_, bf16[4,768,768]{2,1,0:T(8,128)(2,1)} %bitcast.101, ...), custom_call_target="tpu_custom_call" | custom-call | flops 3623878656 | bytes 14548992 | tf_op jit(solution)/shard_map/pallas_call | solution.py:74
  262.7 4.4 %shard_map.214 = (f32[4,2,2,24,384]{4,3,2,1,0:T(8,128)}, bf16[4,2,2,24,384]{4,3,2,1,0:T(8,128)(2,1)}, f32[4,2,2,24,384]{4,3,2,1,0:T(8,128)}, bf16[4,2,2,24,384]{...) custom-call(s32[4]{0:T(128)} %pad_add_fusion.refs_0_.place_ref, ...), custom_call_target="tpu_custom_call" | custom-call | bytes 10616832 | tf_op jit(solution)/shard_map/pallas_call | solution.py:74
  293.0 11.0 %shard_map.216 = (bf16[1024,768]{1,0:T(8,128)(2,1)}, f32[2,8,768]{2,1,0:T(8,128)}) custom-call(bf16[1024,768]{1,0:T(8,128)(2,1)} %bitcast.98, f32[1024,768]{1,0:T(8,128)} %get-tuple-element.91.refs_9_.refs_1_, bf16[4,1024,768]{2,1,0:T(8,128)(2,1)} %bitcast.89, bf16[4,1024,768]{2,1,0:T(8,128)(2,1)} %bitcast.95, ...), custom_call_target="tpu_custom_call" | custom-call | flops 4831838208 | bytes 17301504 | tf_op jit(solution)/shard_map/pallas_call | solution.py:74
  304.8 3.8 shard_map.217
  308.6 5.1 %all-to-all-start.1 = ((bf16[32,24,768]{2,1,0:T(8,128)(2,1)}), bf16[32,24,768]{2,1,0:T(8,128)(2,1)S(1)}, u32[]{:S(2)}, u32[]{:S(2)}) async-start(bf16[32,24,768]{2,1,0:T(8,128)(2,1)} %get-tuple-element.121), calls=%async_computation.1 | async-start | bytes 2359296 | tf_op jit(solution)/shard_map/all_to_all | solution.py:822
  317.0 7.5 %collective-permute-done.42 = f32[16,768]{1,0:T(8,128)S(1)} collective-permute-done((f32[16,768]{1,0:T(8,128)S(1)}, f32[16,768]{1,0:T(8,128)S(1)}, u32[]{:S(2)}, u32[]{:S(2)}) %collective-permute-start.42) | collective-permute-done | bytes 49184 | tf_op jit(solution)/shard_map/ppermute | solution.py:672
  325.6 3.8 collective-permute-done.43
  329.7 5.8 %collective-permute-done.44 = f32[16,768]{1,0:T(8,128)S(1)} collective-permute-done((f32[16,768]{1,0:T(8,128)S(1)}, f32[16,768]{1,0:T(8,128)S(1)}, u32[]{:S(2)}, u32[]{:S(2)}) %collective-permute-start.44) | collective-permute-done | bytes 49184 | tf_op jit(solution)/shard_map/ppermute | solution.py:672
  345.9 6.5 %shard_map.218 = bf16[768,768]{1,0:T(8,128)(2,1)} custom-call(f32[2]{0:T(128)} %pad_maximum_fusion.2.scale_ref, bf16[768,768]{1,0:T(8,128)(2,1)} %bitcast.104, f32[768,768]{1,0:T(8,128)} %bitcast.107, f32[768,768]{1,0:T(8,128)} %bitcast.108), custom_call_target="tpu_custom_call" | custom-call | flops 1811939328 | bytes 7077888 | tf_op jit(solution)/shard_map/pallas_call | solution.py:74
  352.4 5.9 %all-to-all-start.2 = ((bf16[32,24,768]{2,1,0:T(8,128)(2,1)}), bf16[32,24,768]{2,1,0:T(8,128)(2,1)S(1)}, u32[]{:S(2)}, u32[]{:S(2)}) async-start(bf16[32,24,768]{2,1,0:T(8,128)(2,1)} %bitcast.106), calls=%async_computation.2 | async-start | bytes 2359296 | tf_op jit(solution)/shard_map/all_to_all | solution.py:822
  360.3 7.2 %shard_map.220 = (f32[768,768]{1,0:T(8,128)}, f32[768,768]{1,0:T(8,128)}) custom-call(s32[1]{0:T(128)} %bitcast.48.has_ref, f32[2]{0:T(128)} %pad_maximum_fusion.2.scale_ref, bf16[768,768]{1,0:T(8,128)(2,1)} %bitcast.105, f32[768,768]{1,0:T(8,128)} %bitcast.121, f32[768,768]{1,0:T(8,128)} %bitcast.122), custom_call_target="tpu_custom_call" | custom-call | flops 1811939328 | bytes 10616832 | tf_op jit(solution)/shard_map/pallas_call | solution.py:74
  367.4 19.9 %all-to-all-done.2.p_ref = bf16[32,24,768]{2,1,0:T(8,128)(2,1)S(1)} async-done(((bf16[32,24,768]{2,1,0:T(8,128)(2,1)}), bf16[32,24,768]{2,1,0:T(8,128)(2,1)S(1)}, u32[]{:S(2)}, u32[]{:S(2)}) %all-to-all-start.2) | async-done | bytes 1179680 | tf_op jit(solution)/shard_map/all_to_all | solution.py:822
  (241 shorter events, 104.1 us)
Async XLA Ops:
  7.2 132.1 %all-gather.2.cloned.1.call-start = ((), (), s32[]{:S(2)}) async-start(), calls=%async_computation.3 | async-start | bytes 9732096 | tf_op jit(solution)/shard_map/all_gather | solution.py:852
  12.9 14.6 %all-to-all-start = ((bf16[32,2,156]{2,1,0:T(2,128)(2,1)}), bf16[32,2,156]{2,1,0:T(2,128)(2,1)S(1)}, u32[]{:S(2)}, u32[]{:S(2)}) async-start(bf16[32,2,156]{2,1,0:T(2,128)(2,1)} %reshape.564), calls=%async_computation | async-start | bytes 65536 | tf_op jit(solution)/shard_map/all_to_all | solution.py:822
  31.5 80.4 %collective-permute-start.12 = (bf16[2,1024,768]{2,1,0:T(8,128)(2,1)S(1)}, bf16[2,1024,768]{2,1,0:T(8,128)(2,1)}, u32[]{:S(2)}, u32[]{:S(2)}) collective-permute-start(bf16[2,1024,768]{2,1,0:T(8,128)(2,1)S(1)} %pad_maximum_fusion.refs_14_.a1_ref.refs_0_.refs_1_), channel_id=1, source_target_pairs={{0,1},{1,0},{2,3},{3,2},{4,5},{5,4},{6,7},{7,6},{8,9},{9,8},{10,11... | collective-permute-start | bytes 9437192 | tf_op jit(solution)/shard_map/ppermute | solution.py:519
  47.3 15.7 %collective-permute-start.4 = (bf16[4,4,24,768]{3,2,1,0:T(8,128)(2,1)}, bf16[4,4,24,768]{3,2,1,0:T(8,128)(2,1)}, u32[]{:S(2)}, u32[]{:S(2)}) collective-permute-start(bf16[4,4,24,768]{3,2,1,0:T(8,128)(2,1)} %pad_maximum_fusion.1.refs_1_), channel_id=1, source_target_pairs={{0,4},{1,5},{2,6},{3,7},{4,0},{5,1},{6,2},{7,3},{8,12},{9,13},{10,... | collective-permute-start | bytes 1769480 | tf_op jit(solution)/shard_map/ppermute | solution.py:527
  47.9 19.4 %collective-permute-start.3 = (bf16[4,4,24,768]{3,2,1,0:T(8,128)(2,1)}, bf16[4,4,24,768]{3,2,1,0:T(8,128)(2,1)}, u32[]{:S(2)}, u32[]{:S(2)}) collective-permute-start(bf16[4,4,24,768]{3,2,1,0:T(8,128)(2,1)} %pad_maximum_fusion.1.refs_1_), channel_id=1, source_target_pairs={{0,2},{1,3},{2,0},{3,1},{4,6},{5,7},{6,4},{7,5},{8,10},{9,11},{10,... | collective-permute-start | bytes 1769480 | tf_op jit(solution)/shard_map/ppermute | solution.py:523
  48.7 20.0 %collective-permute-start.7 = (bf16[4,4,24,768]{3,2,1,0:T(8,128)(2,1)}, bf16[4,4,24,768]{3,2,1,0:T(8,128)(2,1)}, u32[]{:S(2)}, u32[]{:S(2)}) collective-permute-start(bf16[4,4,24,768]{3,2,1,0:T(8,128)(2,1)} %pad_maximum_fusion.1.refs_1_), channel_id=1, source_target_pairs={{0,1},{1,0},{2,3},{3,2},{4,5},{5,4},{6,7},{7,6},{8,9},{9,8},{10,11... | collective-permute-start | bytes 1769480 | tf_op jit(solution)/shard_map/ppermute | solution.py:519
  48.7 63.1 %collective-permute-start.13 = (bf16[1024,768]{1,0:T(8,128)(2,1)}, bf16[1024,768]{1,0:T(8,128)(2,1)}, u32[]{:S(2)}, u32[]{:S(2)}) collective-permute-start(bf16[1024,768]{1,0:T(8,128)(2,1)} %bitcast.5.dy_ref.refs_1_.refs_7_), channel_id=1, source_target_pairs={{0,1},{1,0},{2,3},{3,2},{4,5},{5,4},{6,7},{7,6},{8,9},{9,8},{10,11... | collective-permute-start | bytes 4718600 | tf_op jit(solution)/shard_map/ppermute | solution.py:519
  67.3 16.5 %collective-permute-start.9 = (bf16[4,4,24,768]{3,2,1,0:T(8,128)(2,1)}, bf16[4,4,24,768]{3,2,1,0:T(8,128)(2,1)}, u32[]{:S(2)}, u32[]{:S(2)}) collective-permute-start(bf16[4,4,24,768]{3,2,1,0:T(8,128)(2,1)} %collective-permute-done.4.refs_3_), channel_id=1, source_target_pairs={{0,1},{1,0},{2,3},{3,2},{4,5},{5,4},{6,7},{7,6},{8,9},{9,8},{10,11... | collective-permute-start | bytes 1769480 | tf_op jit(solution)/shard_map/ppermute | solution.py:519
  68.8 15.1 %collective-permute-start.5 = (bf16[2,4,24,768]{3,2,1,0:T(8,128)(2,1)S(1)}, bf16[2,4,24,768]{3,2,1,0:T(8,128)(2,1)}, u32[]{:S(2)}, u32[]{:S(2)}) collective-permute-start(bf16[2,4,24,768]{3,2,1,0:T(8,128)(2,1)S(1)} %slice.66), channel_id=1, source_target_pairs={{0,4},{1,5},{2,6},{3,7},{4,0},{5,1},{6,2},{7,3},{8,12},{9,13},{10,... | collective-permute-start | bytes 884744 | tf_op jit(solution)/shard_map/ppermute | solution.py:527
  73.9 22.0 %collective-permute-start.8 = (bf16[4,4,24,768]{3,2,1,0:T(8,128)(2,1)}, bf16[4,4,24,768]{3,2,1,0:T(8,128)(2,1)}, u32[]{:S(2)}, u32[]{:S(2)}) collective-permute-start(bf16[4,4,24,768]{3,2,1,0:T(8,128)(2,1)} %collective-permute-done.3.refs_2_), channel_id=1, source_target_pairs={{0,1},{1,0},{2,3},{3,2},{4,5},{5,4},{6,7},{7,6},{8,9},{9,8},{10,11... | collective-permute-start | bytes 1769480 | tf_op jit(solution)/shard_map/ppermute | solution.py:519
  139.2 25.8 %collective-permute-start.14 = (bf16[4,1024,768]{2,1,0:T(8,128)(2,1)}, bf16[4,1024,768]{2,1,0:T(8,128)(2,1)}, u32[]{:S(2)}, u32[]{:S(2)}) collective-permute-start(bf16[4,1024,768]{2,1,0:T(8,128)(2,1)} %get-tuple-element.74.refs_5_.refs_3_.refs_1_.refs_2_), channel_id=1, source_target_pairs={{0,1},{1,0},{2,3},{3,2},{4,5},{5,4},{6,7},{7,6},{8,9},{9,8},{10,11... | collective-permute-start | bytes 18874376 | tf_op jit(solution)/shard_map/ppermute | solution.py:519
  151.8 27.7 %collective-permute-start.18 = (bf16[4,1024,768]{2,1,0:T(8,128)(2,1)}, bf16[4,1024,768]{2,1,0:T(8,128)(2,1)}, u32[]{:S(2)}, u32[]{:S(2)}) collective-permute-start(bf16[4,1024,768]{2,1,0:T(8,128)(2,1)} %bitcast.84), channel_id=1, source_target_pairs={{0,1},{1,0},{2,3},{3,2},{4,5},{5,4},{6,7},{7,6},{8,9},{9,8},{10,11... | collective-permute-start | bytes 18874376 | tf_op jit(solution)/shard_map/ppermute | solution.py:519
  164.9 26.5 %collective-permute-start.17 = (bf16[4,1024,768]{2,1,0:T(8,128)(2,1)}, bf16[4,1024,768]{2,1,0:T(8,128)(2,1)}, u32[]{:S(2)}, u32[]{:S(2)}) collective-permute-start(bf16[4,1024,768]{2,1,0:T(8,128)(2,1)} %bitcast.90), channel_id=1, source_target_pairs={{0,1},{1,0},{2,3},{3,2},{4,5},{5,4},{6,7},{7,6},{8,9},{9,8},{10,11... | collective-permute-start | bytes 18874376 | tf_op jit(solution)/shard_map/ppermute | solution.py:519
  176.8 26.3 %collective-permute-start.15 = (bf16[4,2,2,2,24,384]{5,4,3,2,1,0:T(8,128)(2,1)}, bf16[4,2,2,2,24,384]{5,4,3,2,1,0:T(8,128)(2,1)S(1)}, u32[]{:S(2)}, u32[]{:S(2)}) collective-permute-start(bf16[4,2,2,2,24,384]{5,4,3,2,1,0:T(8,128)(2,1)} %get-tuple-element.78), channel_id=1, source_target_pairs={{0,2},{1,3},{2,0},{3,1},{4,6},{5,7},{6,4},{7,5},{8,10},{9,11},{10,... | collective-permute-start | bytes 1769480 | tf_op jit(solution)/shard_map/ppermute | solution.py:523
  176.8 26.3 %collective-permute-start.16 = (bf16[4,2,2,2,24,384]{5,4,3,2,1,0:T(8,128)(2,1)}, bf16[4,2,2,2,24,384]{5,4,3,2,1,0:T(8,128)(2,1)S(1)}, u32[]{:S(2)}, u32[]{:S(2)}) collective-permute-start(bf16[4,2,2,2,24,384]{5,4,3,2,1,0:T(8,128)(2,1)} %get-tuple-element.80), channel_id=1, source_target_pairs={{0,4},{1,5},{2,6},{3,7},{4,0},{5,1},{6,2},{7,3},{8,12},{9,13},{10,... | collective-permute-start | bytes 1769480 | tf_op jit(solution)/shard_map/ppermute | solution.py:527
  207.9 22.8 %collective-permute-start.19 = (bf16[4,2,2,2,24,384]{5,4,3,2,1,0:T(8,128)(2,1)}, bf16[4,2,2,2,24,384]{5,4,3,2,1,0:T(8,128)(2,1)S(1)}, u32[]{:S(2)}, u32[]{:S(2)}) collective-permute-start(bf16[4,2,2,2,24,384]{5,4,3,2,1,0:T(8,128)(2,1)} %get-tuple-element.84), channel_id=1, source_target_pairs={{0,2},{1,3},{2,0},{3,1},{4,6},{5,7},{6,4},{7,5},{8,10},{9,11},{10,... | collective-permute-start | bytes 1769480 | tf_op jit(solution)/shard_map/ppermute | solution.py:523
  209.9 20.8 %collective-permute-start.20 = (bf16[4,2,2,2,24,384]{5,4,3,2,1,0:T(8,128)(2,1)}, bf16[4,2,2,2,24,384]{5,4,3,2,1,0:T(8,128)(2,1)S(1)}, u32[]{:S(2)}, u32[]{:S(2)}) collective-permute-start(bf16[4,2,2,2,24,384]{5,4,3,2,1,0:T(8,128)(2,1)} %get-tuple-element.86), channel_id=1, source_target_pairs={{0,4},{1,5},{2,6},{3,7},{4,0},{5,1},{6,2},{7,3},{8,12},{9,13},{10,... | collective-permute-start | bytes 1769480 | tf_op jit(solution)/shard_map/ppermute | solution.py:527
  211.8 18.8 %collective-permute-start.22 = (bf16[4,2,2,24,384]{4,3,2,1,0:T(8,128)(2,1)}, bf16[4,2,2,24,384]{4,3,2,1,0:T(8,128)(2,1)S(1)}, u32[]{:S(2)}, u32[]{:S(2)}) collective-permute-start(bf16[4,2,2,24,384]{4,3,2,1,0:T(8,128)(2,1)} %get-tuple-element.89), channel_id=1, source_target_pairs={{0,2},{1,3},{2,0},{3,1},{4,6},{5,7},{6,4},{7,5},{8,10},{9,11},{10,... | collective-permute-start | bytes 884744 | tf_op jit(solution)/shard_map/ppermute | solution.py:523
  211.9 34.9 %collective-permute-start.23 = (bf16[4,2,2,2,24,384]{5,4,3,2,1,0:T(8,128)(2,1)S(1)}, bf16[4,2,2,2,24,384]{5,4,3,2,1,0:T(8,128)(2,1)S(1)}, u32[]{:S(2)}, u32[]{:S(2)}) collective-permute-start(bf16[4,2,2,2,24,384]{5,4,3,2,1,0:T(8,128)(2,1)S(1)} %copy-done.40), channel_id=1, source_target_pairs={{0,2},{1,3},{2,0},{3,1},{4,6},{5,7},{6,4},{7,5},{8,10},{9,11},{10,... | collective-permute-start | bytes 1769480 | tf_op jit(solution)/shard_map/ppermute | solution.py:523
  217.9 32.9 %collective-permute-start.24 = (bf16[4,2,2,2,24,384]{5,4,3,2,1,0:T(8,128)(2,1)S(1)}, bf16[4,2,2,2,24,384]{5,4,3,2,1,0:T(8,128)(2,1)S(1)}, u32[]{:S(2)}, u32[]{:S(2)}) collective-permute-start(bf16[4,2,2,2,24,384]{5,4,3,2,1,0:T(8,128)(2,1)S(1)} %copy-done.39), channel_id=1, source_target_pairs={{0,4},{1,5},{2,6},{3,7},{4,0},{5,1},{6,2},{7,3},{8,12},{9,13},{10,... | collective-permute-start | bytes 1769480 | tf_op jit(solution)/shard_map/ppermute | solution.py:527
  236.0 15.2 %collective-permute-start.27 = (bf16[4,24,768]{2,1,0:T(8,128)(2,1)}, bf16[4,24,768]{2,1,0:T(8,128)(2,1)S(1)}, u32[]{:S(2)}, u32[]{:S(2)}) collective-permute-start(bf16[4,24,768]{2,1,0:T(8,128)(2,1)} %bitcast.133), channel_id=1, source_target_pairs={{0,0},{1,16},{2,2},{3,18},{4,4},{5,20},{6,6},{7,22},{8,1},{9,17},{... | collective-permute-start | bytes 442376 | tf_op jit(solution)/shard_map/ppermute | solution.py:657
  237.6 24.1 %collective-permute-start.28 = (bf16[4,24,768]{2,1,0:T(8,128)(2,1)}, bf16[4,24,768]{2,1,0:T(8,128)(2,1)S(1)}, u32[]{:S(2)}, u32[]{:S(2)}) collective-permute-start(bf16[4,24,768]{2,1,0:T(8,128)(2,1)} %bitcast.129), channel_id=1, source_target_pairs={{0,1},{1,17},{2,3},{3,19},{4,5},{5,21},{6,7},{7,23},{8,0},{9,16},{... | collective-permute-start | bytes 442376 | tf_op jit(solution)/shard_map/ppermute | solution.py:657
  244.8 17.0 %collective-permute-start.29 = (bf16[4,24,768]{2,1,0:T(8,128)(2,1)}, bf16[4,24,768]{2,1,0:T(8,128)(2,1)S(1)}, u32[]{:S(2)}, u32[]{:S(2)}) collective-permute-start(bf16[4,24,768]{2,1,0:T(8,128)(2,1)} %bitcast.128), channel_id=1, source_target_pairs={{0,8},{1,24},{2,10},{3,26},{4,12},{5,28},{6,14},{7,30},{8,9},{9,25... | collective-permute-start | bytes 442376 | tf_op jit(solution)/shard_map/ppermute | solution.py:657
  246.8 15.0 %collective-permute-start.30 = (bf16[4,24,768]{2,1,0:T(8,128)(2,1)}, bf16[4,24,768]{2,1,0:T(8,128)(2,1)S(1)}, u32[]{:S(2)}, u32[]{:S(2)}) collective-permute-start(bf16[4,24,768]{2,1,0:T(8,128)(2,1)} %bitcast.127), channel_id=1, source_target_pairs={{0,9},{1,25},{2,11},{3,27},{4,13},{5,29},{6,15},{7,31},{8,8},{9,24... | collective-permute-start | bytes 442376 | tf_op jit(solution)/shard_map/ppermute | solution.py:657
  271.8 14.4 %collective-permute-start.34 = (bf16[4,24,768]{2,1,0:T(8,128)(2,1)}, bf16[4,24,768]{2,1,0:T(8,128)(2,1)S(1)}, u32[]{:S(2)}, u32[]{:S(2)}) collective-permute-start(bf16[4,24,768]{2,1,0:T(8,128)(2,1)} %bitcast.125), channel_id=1, source_target_pairs={{0,1},{1,17},{2,3},{3,19},{4,5},{5,21},{6,7},{7,23},{8,0},{9,16},{... | collective-permute-start | bytes 442376 | tf_op jit(solution)/shard_map/ppermute | solution.py:657
  275.2 15.2 %collective-permute-start.35 = (bf16[4,24,768]{2,1,0:T(8,128)(2,1)}, bf16[4,24,768]{2,1,0:T(8,128)(2,1)S(1)}, u32[]{:S(2)}, u32[]{:S(2)}) collective-permute-start(bf16[4,24,768]{2,1,0:T(8,128)(2,1)} %bitcast.124), channel_id=1, source_target_pairs={{0,8},{1,24},{2,10},{3,26},{4,12},{5,28},{6,14},{7,30},{8,9},{9,25... | collective-permute-start | bytes 442376 | tf_op jit(solution)/shard_map/ppermute | solution.py:657
  276.3 16.1 %collective-permute-start.36 = (bf16[4,24,768]{2,1,0:T(8,128)(2,1)}, bf16[4,24,768]{2,1,0:T(8,128)(2,1)S(1)}, u32[]{:S(2)}, u32[]{:S(2)}) collective-permute-start(bf16[4,24,768]{2,1,0:T(8,128)(2,1)} %bitcast.123), channel_id=1, source_target_pairs={{0,9},{1,25},{2,11},{3,27},{4,13},{5,29},{6,15},{7,31},{8,8},{9,24... | collective-permute-start | bytes 442376 | tf_op jit(solution)/shard_map/ppermute | solution.py:657
  283.9 20.1 %collective-permute-start.38 = (bf16[4,24,768]{2,1,0:T(8,128)(2,1)}, bf16[4,24,768]{2,1,0:T(8,128)(2,1)S(1)}, u32[]{:S(2)}, u32[]{:S(2)}) collective-permute-start(bf16[4,24,768]{2,1,0:T(8,128)(2,1)} %bitcast.132), channel_id=1, source_target_pairs={{0,1},{1,17},{2,3},{3,19},{4,5},{5,21},{6,7},{7,23},{8,0},{9,16},{... | collective-permute-start | bytes 442376 | tf_op jit(solution)/shard_map/ppermute | solution.py:657
  284.7 19.3 %collective-permute-start.37 = (bf16[4,24,768]{2,1,0:T(8,128)(2,1)}, bf16[4,24,768]{2,1,0:T(8,128)(2,1)S(1)}, u32[]{:S(2)}, u32[]{:S(2)}) collective-permute-start(bf16[4,24,768]{2,1,0:T(8,128)(2,1)} %bitcast.131), channel_id=1, source_target_pairs={{0,0},{1,16},{2,2},{3,18},{4,4},{5,20},{6,6},{7,22},{8,1},{9,17},{... | collective-permute-start | bytes 442376 | tf_op jit(solution)/shard_map/ppermute | solution.py:657
  286.3 17.7 %collective-permute-start.39 = (bf16[4,24,768]{2,1,0:T(8,128)(2,1)}, bf16[4,24,768]{2,1,0:T(8,128)(2,1)S(1)}, u32[]{:S(2)}, u32[]{:S(2)}) collective-permute-start(bf16[4,24,768]{2,1,0:T(8,128)(2,1)} %bitcast.130), channel_id=1, source_target_pairs={{0,8},{1,24},{2,10},{3,26},{4,12},{5,28},{6,14},{7,30},{8,9},{9,25... | collective-permute-start | bytes 442376 | tf_op jit(solution)/shard_map/ppermute | solution.py:657
  308.6 36.2 %all-to-all-start.1 = ((bf16[32,24,768]{2,1,0:T(8,128)(2,1)}), bf16[32,24,768]{2,1,0:T(8,128)(2,1)S(1)}, u32[]{:S(2)}, u32[]{:S(2)}) async-start(bf16[32,24,768]{2,1,0:T(8,128)(2,1)} %get-tuple-element.121), calls=%async_computation.1 | async-start | bytes 2359296 | tf_op jit(solution)/shard_map/all_to_all | solution.py:822
  352.4 35.0 %all-to-all-start.2 = ((bf16[32,24,768]{2,1,0:T(8,128)(2,1)}), bf16[32,24,768]{2,1,0:T(8,128)(2,1)S(1)}, u32[]{:S(2)}, u32[]{:S(2)}) async-start(bf16[32,24,768]{2,1,0:T(8,128)(2,1)} %bitcast.106), calls=%async_computation.2 | async-start | bytes 2359296 | tf_op jit(solution)/shard_map/all_to_all | solution.py:822
  (59 other events, 468.5 us)
Sparse Core Ops, SparseCore 0:
  11.0 99.6 all-gather.1

commit v2 on v1

--- a/solution.py
+++ b/solution.py
@@ -119,10 +119,10 @@
     q_ref[...] = rotate(mm(a1, w_ref[0], NN) + vec_ref[4:5, :], *tables).astype(bf16)
     k_ref[...] = rotate(mm(a1, w_ref[1], NN) + vec_ref[5:6, :], *tables).astype(bf16)
     v_ref[...] = (mm(a1, w_ref[2], NN) + vec_ref[6:7, :]).astype(bf16)
-    do_ref[...] = mm(dy_ref[...], w_ref[3], NT).astype(bf16)
-
-
-def project(acts, dy, weights, vecs, tables, step=256):
+    do_ref[...] = mm(dy_ref[0], w_ref[3], NT).astype(bf16)
+
+
+def project(acts, weights, vecs, tables, step=256):
     _, count, width = acts.shape
     token = pl.BlockSpec((step, width), lambda i: (i, 0))
     table = pl.BlockSpec((step, LANES), lambda i: (i, 0))
@@ -133,7 +133,7 @@
         grid=(count // step,),
         in_specs=[
             pl.BlockSpec((1, step, width), lambda i: (0, i, 0)),
-            token,
+            pl.BlockSpec((1, step, width), lambda i: (2, i, 0)),
             pl.BlockSpec((4, width, width), lambda i: (0, 0, 0)),
             pl.BlockSpec(vecs.shape, lambda i: (0, 0)),
             table,
@@ -142,12 +142,12 @@
         ],
         out_specs=[token] * 4,
         out_shape=[jax.ShapeDtypeStruct((count, width), bf16)] * 4,
-    )(acts, dy, weights, vecs, *tables)
+    )(acts, acts, weights, vecs, *tables)
 
 
 def attend_body(
-    col_ref, row_ref, q_ref, k_ref, v_ref, do_ref, c_ref, a_ref, b_ref,
-    g_ref, sum_ref, mask_ref, dk_acc, dv_acc, *, block,
+    acts_ref, col_ref, row_ref, q_ref, k_ref, v_ref, do_ref, c_ref, a_ref, b_ref,
+    g_ref, sum_ref, acts_out_ref, mask_ref, dk_acc, dv_acc, *, block,
 ):
     length = q_ref.shape[0]
     steps = length // block
@@ -210,7 +210,7 @@
     sum_ref[2] = sub_sum(dv.astype(f32))
 
 
-def attend(segment_ids, q, k, v, do, tables, after=(), block=256):
+def attend(segment_ids, q, k, v, do, tables, acts, block=256):
     rows, length = segment_ids.shape
     count, width = q.shape
     block = min(block, length)
@@ -220,9 +220,10 @@
         functools.partial(attend_body, block=block),
         24 * count * length * width,
         24 * count * width,
-        after=after,
         grid=(rows, width // LANES),
+        input_output_aliases={0: 2},
         in_specs=[
+            pl.BlockSpec(memory_space=pl.ANY),
             pl.BlockSpec((length, 1), lambda r, h: (r, 0)),
             pl.BlockSpec((1, 1, length), lambda r, h: (r, 0, 0)),
             token,
@@ -236,10 +237,12 @@
         out_specs=[
             pl.BlockSpec((4, length, LANES), lambda r, h: (0, r, h)),
             pl.BlockSpec((3, 8, LANES), lambda r, h: (0, r, h)),
+            pl.BlockSpec(memory_space=pl.ANY),
         ],
         out_shape=[
             jax.ShapeDtypeStruct((4, count, width), bf16),
             jax.ShapeDtypeStruct((3, 8 * rows, width), f32),
+            jax.ShapeDtypeStruct(acts.shape, acts.dtype),
         ],
         scratch_shapes=[
             pltpu.VMEM((length // block, length, 2 * block), f32),
@@ -247,6 +250,7 @@
             pltpu.VMEM((length, LANES), f32),
         ],
     )(
+        acts,
         segment_ids.reshape(-1, 1),
         segment_ids.reshape(rows, 1, length),
         q,
@@ -271,7 +275,7 @@
         if n < first:
             part = mm(l1o[0], r1o[n], TN) + mm(l1p[0], r1p[n], TN)
         else:
-            part = mm(l2o[n - first], r2o[...], TN) + mm(l2p[n - first], r2p[...], TN)
+            part = mm(l2o[n - first], r2o[0], TN) + mm(l2p[n - first], r2p[0], TN)
         acc[n] += part.reshape(acc.shape[1:])
 
     @pl.when(i == steps - 1)
@@ -290,7 +294,7 @@
 
 def half_grads(place, left_one, left_two, right_one, right_two, shard, after=(), step=256):
     first, second = right_one[2], left_two[2]
-    count, width = right_two[0].shape
+    _, count, width = right_two[0][0].shape
     half = width // 2
     blocks = first + second
     steps = count // step
@@ -307,12 +311,12 @@
             in_specs=[layers(left_one, step, half, True)] * 2
             + [layers(left_two, step, half, True)] * 2
             + [layers(right_one, step, width)] * 2
-            + [pl.BlockSpec((step, width), lambda i, s: (i, 0))] * 2,
+            + [layers(right_two, step, width)] * 2,
             out_specs=[out] * 4,
             scratch_shapes=[pltpu.VMEM((blocks, 2, 2, 2, 2, shard, width), f32)],
         ),
         out_shape=[jax.ShapeDtypeStruct(shape, k) for k in (f32, bf16, f32, bf16)],
-    )(place, *left_one[0], *left_two[0], *right_one[0], *right_two)
+    )(place, *left_one[0], *left_two[0], *right_one[0], *right_two[0])
 
 
 def full_grads(left_one, left_two, right_one, right_two):
@@ -334,7 +338,7 @@
 
 def hidden_body(a2_ref, dy_ref, wu_ref, wd_ref, bu_ref, out_ref, sum_ref):
     u = mm(a2_ref[0], wu_ref[0], NN) + bu_ref[0]
-    de = mm(dy_ref[...], wd_ref[0], NT)
+    de = mm(dy_ref[0], wd_ref[0], NT)
     dist, density = gelu_parts(u)
     out_ref[0, 0] = (u * dist).astype(bf16)
     du = (de * (dist + u * density)).astype(bf16)
@@ -350,10 +354,9 @@
         sum_ref[0] += part
 
 
-def hidden(first, blocks, acts, dy, weights, vecs, after=(), step=512):
+def hidden(first, blocks, acts, weights, vecs, after=(), step=512):
     _, count, width = acts.shape
     splits = weights.shape[0] // 2
-    token = pl.BlockSpec((step, width), lambda j, i: (i, 0))
     both, sums = call(
         hidden_body,
         blocks * 4 * count * width * width,
@@ -362,7 +365,7 @@
         grid=(blocks, count // step),
         in_specs=[
             pl.BlockSpec((1, step, width), lambda j, i: (1, i, 0)),
-            token,
+            pl.BlockSpec((1, step, width), lambda j, i: (2, i, 0)),
             pl.BlockSpec((1, width, width), lambda j, i: (first + j, 0, 0)),
             pl.BlockSpec((1, width, width), lambda j, i: (splits + first + j, 0, 0)),
             pl.BlockSpec((1, 1, width), lambda j, i: (8 + first + j, 0, 0)),
@@ -375,7 +378,7 @@
             jax.ShapeDtypeStruct((2, blocks, count, width), bf16),
             jax.ShapeDtypeStruct((blocks, 8, width), f32),
         ],
-    )(acts, dy, weights, weights, vecs[:, None, :])
+    )(acts, acts, weights, weights, vecs[:, None, :])
     return both.reshape(2 * blocks, count, width), sums
 
 
@@ -810,12 +813,13 @@
     )(owners, factor, returned, shards, blocks)
 
 
-def layer_inputs(tokens, vecs):
+def layer_inputs(tokens, dy, vecs):
     values = tokens.astype(f32)
     centred = values - jnp.mean(values, axis=-1, keepdims=True)
     spread = jnp.mean(centred * centred, axis=-1, keepdims=True)
     unit = centred * lax.rsqrt(spread + norm_epsilon)
-    return jnp.stack([unit * vecs[0] + vecs[1], unit * vecs[2] + vecs[3]]).astype(bf16)
+    norms = [(unit * vecs[n] + vecs[n + 1]).astype(bf16) for n in (0, 2)]
+    return jnp.stack([*norms, dy])
 
 
 def to_all(value):
@@ -854,7 +858,7 @@
     flat_tokens = tokens.reshape(count, width)
     dy = cotangent.reshape(count, width)
     tables = rotary_tables(segment_ids)
-    acts = layer_inputs(flat_tokens, vecs)
+    acts = layer_inputs(flat_tokens, dy, vecs)
     place = jnp.stack(grid_places()).astype(jnp.int32)
     if paired:
         attn_weights = gather_staged(place, low_blocks[:4], after=(*tables, acts))
@@ -867,42 +871,43 @@
     def pair(v):
         return (v, over_c(v)) if paired else (v, v)
 
-    q, k, v, do = project(acts, dy, attn_weights, vecs, tables)
-    both_acts, dys = pair(acts), pair(dy)
-    og, attn_sums = attend(segment_ids, q, k, v, do, tables, after=(both_acts[1], dys[1]))
+    q, k, v, do = project(acts, attn_weights, vecs, tables)
+    og, attn_sums, acts = attend(segment_ids, q, k, v, do, tables, acts)
     half = splits // 2
     orders = [list(range(4))]
     for first in (0, half):
         orders.append([base + first + j for base in (4, 4 + splits) for j in range(half)])
     if paired:
-        ogs = pair(og)
-        ed0, up_sum0 = hidden(0, half, acts, dy, mlp_weights, vecs, after=(og,))
-        ed1, up_sum1 = hidden(half, half, acts, dy, mlp_weights, vecs, after=(ed0,))
-        ed0s, ed1s = pair(ed0), pair(ed1)
+        acts_pair, og_pair = (acts, over_c(acts)), (og, over_c(og))
+        dys = (acts_pair, 2, 1)
+        ed0, up_sum0 = hidden(0, half, acts, mlp_weights, vecs)
+        ed1, up_sum1 = hidden(half, half, acts, mlp_weights, vecs, after=(ed0, acts_pair[1]))
+        pairs = [(v, over_c(v)) for v in (ed0, ed1)]
         attn = Reduction(
-            *half_grads(place, (both_acts, 0, 1), (ogs, 3, 1), (ogs, 0, 3), dys, shard, after=(ed1,))
+            *half_grads(place, (acts_pair, 0, 1), (og_pair, 3, 1), (og_pair, 0, 3), dys, shard, after=(ed1,))
         )
         low = Reduction(
             *half_grads(
-                place, (both_acts, 1, 1), (ed0s, 0, half), (ed0s, half, half), dys, shard, after=(attn.made,)
+                place, (acts_pair, 1, 1), (pairs[0], 0, half), (pairs[0], half, half), dys, shard, after=(attn.made,)
             )
         )
+        advance(place, [attn], [], after=(low.made,))
         high = Reduction(
             *half_grads(
-                place, (both_acts, 1, 1), (ed1s, 0, half), (ed1s, half, half), dys, shard, after=(low.made,)
+                place, (acts_pair, 1, 1), (pairs[1], 0, half), (pairs[1], half, half), dys, shard, after=(attn.made,)
             )
         )
+        advance(place, [low], [], after=(high.made,))
         es, dus = [(v, 0, half) for v in (ed0, ed1)], [(v, half, half) for v in (ed0, ed1)]
-        advance(place, [attn], [], after=(high.made,))
-        out = output(flat_tokens, (og, 3, 1), es, attn_weights, mlp_weights, vecs, after=(attn.made,))
-        terms = [advance(place, [low], [attn], after=(out,))]
-        part, one_sums = grad_one(flat_tokens, dy, (og, 0, 3), attn_weights, vecs, after=(low.made,))
-        terms.append(advance(place, [high], [low], after=(part, *terms[0])))
-        terms.append(advance(place, [], [high]))
-        grad_in, two_sums = grad_two(flat_tokens, part, dus, mlp_weights, vecs, after=(high.made, *terms[1]))
+        out = output(flat_tokens, (og, 3, 1), es, attn_weights, mlp_weights, vecs, after=(low.made,))
+        terms = [advance(place, [high], [attn, low], after=(out,))]
+        part, one_sums = grad_one(flat_tokens, dy, (og, 0, 3), attn_weights, vecs, after=(high.made,))
+        terms.append(advance(place, [], [high], after=(part,)))
+        orders = [orders[0] + orders[1], orders[2]]
+        grad_in, two_sums = grad_two(flat_tokens, part, dus, mlp_weights, vecs, after=(high.made,))
     else:
-        ed0, up_sum0 = hidden(0, half, acts, dy, mlp_weights, vecs)
-        ed1, up_sum1 = hidden(half, half, acts, dy, mlp_weights, vecs)
+        ed0, up_sum0 = hidden(0, half, acts, mlp_weights, vecs)
+        ed1, up_sum1 = hidden(half, half, acts, mlp_weights, vecs)
         grads = [
             full_grads(acts[0], og[3:], og[:3], dy),
             full_grads(acts[1], ed0[:half], ed0[half:], dy),

time: 401 us -> 362 us (0.903)
  waiting for transfers between devices: 89.7 us -> 59.8 us
  starting transfers between devices: 78.7 us -> 61.7 us
    ppermute x8, waiting for transfers between devices: 27.1 us -> 1.9 us  [over_y(): lax.ppermute(value, AXES, to_place(lambda z, y, x, c: (z, 1 - y, x, c)))]
    ppermute x12 -> x8, starting transfers between devices: 30.6 us -> 15.4 us  [advance(): lax.ppermute(v, AXES, to_place(lambda z, y, x, c, m=m: (2 * c + ((z ^ m)...]
    ppermute x3, waiting for transfers between devices: 9.18 us -> 0.01 us  [over_z(): lax.ppermute(value, AXES, to_place(lambda z, y, x, c: ((z + by) % 4, y, x...]
    ppermute x8, waiting for transfers between devices: 5.45 us -> 14.4 us  [over_x(): lax.ppermute(value, AXES, to_place(lambda z, y, x, c: (z, y, 1 - x, c)))]
    all_to_all x3, starting transfers between devices: 18.3 us -> 13 us  [to_all(): return lax.all_to_all(value, AXES, split_axis=0, concat_axis=0, tiled=True)]
    all_to_all x3, waiting for transfers between devices: 24.2 us -> 19.9 us  [to_all(): return lax.all_to_all(value, AXES, split_axis=0, concat_axis=0, tiled=True)]
    unnamed x89 -> x95, local copies, waits for them, and re-layouts: 9.81 us -> 13.4 us
  transfers between devices with their start and end apart: 50 -> 45, of which waited for: 15 -> 14; matrix products, arithmetic and copies ran while one was open for 8% -> 11% of each run, Pallas kernels for 38% -> 43%
where the time goes in v2:
time: 362 us; the launch traced here: 360 us
  Pallas kernels  172 us (48%)
  starting transfers between devices  61.7 us (17%)
  waiting for transfers between devices  59.8 us (17%)
  other arithmetic  26.7 us (7%)
  local copies, waits for them, and re-layouts  21.6 us (6%)
  between operations  18 us (5%)
    pallas_call x19, Pallas kernels, call(): return lambda *operands: made(*operands, *after)  172 us
    ppermute x5, waiting for transfers between devices, everywhere(): value = value + lax.ppermute(value, AXES, to_place(move))  20.4 us
    all_to_all x3, waiting for transfers between devices, to_all(): return lax.all_to_all(value, AXES, split_axis=0, concat_axis=0, tiled=True)  19.9 us
    ppermute x8, starting transfers between devices, advance(): lax.ppermute(v, AXES, to_place(lambda z, y, x, c, m=m: (2 * c + ((z ^ m)...  15.4 us
    ppermute x8, waiting for transfers between devices, over_x(): lax.ppermute(value, AXES, to_place(lambda z, y, x, c: (z, y, 1 - x, c)))  14.4 us
    unnamed x95, local copies, waits for them, and re-layouts  13.4 us
    all_to_all x3, starting transfers between devices, to_all(): return lax.all_to_all(value, AXES, split_axis=0, concat_axis=0, tiled=True)  13 us
    ppermute x8, starting transfers between devices, over_x(): lax.ppermute(value, AXES, to_place(lambda z, y, x, c: (z, y, 1 - x, c)))  9.57 us
  transfers between devices with their start and end apart: 45, of which 14 were waited for; matrix products, arithmetic and copies ran while one was open for 11% of the time, Pallas kernels for 43%

profile of v2, /device:TPU:0, one launch (start us, length us, event | category | flops | bytes accessed | tf_op | source)
XLA Modules:
  0.0 359.9 jit_solution(16830311672172537883)
XLA Ops:
  19.2 3.2 all-to-all-start
  24.2 5.2 %compare_select_fusion.9 = f32[128]{0:T(128)S(1)} fusion(f32[]{:T(128)} %bitcast.16, f32[]{:T(128)} %bitcast.17, f32[]{:T(128)} %bitcast.18, f32[]{:T(128)} %bitcast.19, f32[]{:T(128)} %bitcast.20, f32[]{:T(128)} %bitcast.22, f32[]{:T(128)} %bitcast.21, f32[]{:T(128)} %bitcast.15), kind=kLoop, calls=%fused_computation.41 | loop fusion | flops 5376 | bytes 544 | tf_op jit(solution)/shard_map/jit(_where)/select_n | solution.py:90
  30.3 3.2 fusion.1
  49.9 6.5 %collective-permute-done.3.refs_2_ = bf16[4,4,24,768]{3,2,1,0:T(8,128)(2,1)S(1)} collective-permute-done((bf16[4,4,24,768]{3,2,1,0:T(8,128)(2,1)S(1)}, bf16[4,4,24,768]{3,2,1,0:T(8,128)(2,1)S(1)}, u32[]{:S(2)}, u32[]{:S(2)}) %collective-permute-start.3) | collective-permute-done | bytes 589856 | tf_op jit(solution)/shard_map/ppermute | solution.py:526
  69.9 6.5 %shard_map.202 = bf16[4,32,24,768]{3,2,1,0:T(8,128)(2,1)} custom-call(s32[4]{0:T(128)} %pad_add_fusion.refs_0_, bf16[4,4,24,768]{3,2,1,0:T(8,128)(2,1)} %copy-done.4, bf16[4,4,24,768]{3,2,1,0:T(8,128)(2,1)} %copy-done.5, bf16[4,4,24,768]{3,2,1,0:T(8,128)(2,1)} %copy-done.6, bf16[2,4,24,768]{3,2,1,0:T(8,128)(2,1)} %copy-done.26, ...), custom_call_target="tpu_custom_call" | custom-call | bytes 9437184 | tf_op jit(solution)/shard_map/pallas_call | solution.py:74
  76.4 9.9 %shard_map.203 = (bf16[1024,768]{1,0:T(8,128)(2,1)}, bf16[1024,768]{1,0:T(8,128)(2,1)}, bf16[1024,768]{1,0:T(8,128)(2,1)}, bf16[1024,768]{1,0:T(8,128)(2,1)}) custom-call(bf16[3,1024,768]{2,1,0:T(8,128)(2,1)} %pad_maximum_fusion.refs_14_.a1_ref.dy_ref.acts_ref, bf16[3,1024,768]{2,1,0:T(8,128)(2,1)} %pad_maximum_fusion.refs_14_.a1_ref.dy_ref.acts_ref, ...), custom_call_target="tpu_custom_call" | custom-call | flops 4831838208 | bytes 14155776 | tf_op jit(solution)/shard_map/pallas_call | solution.py:74
  86.3 27.3 %shard_map.204 = (bf16[4,1024,768]{2,1,0:T(8,128)(2,1)}, f32[3,16,768]{2,1,0:T(8,128)}, bf16[3,1024,768]{2,1,0:T(8,128)(2,1)}) custom-call(bf16[3,1024,768]{2,1,0:T(8,128)(2,1)} %pad_maximum_fusion.refs_14_.a1_ref.dy_ref.acts_ref, s32[1024,1]{1,0:T(8,128)} %bitcast.109, s32[2,1,512]{2,1,0:T(1,128)} %reshape.482.row_ref, ...), custom_call_target="tpu_custom_call", output_to_operand_aliasing={{2}: (0, {})} | custom-call | flops 9663676416 | bytes 18874368 | tf_op jit(solution)/shard_map/pallas_call | solution.py:74
  115.0 12.6 %shard_map.205 = (bf16[2,2,1024,768]{3,2,1,0:T(8,128)(2,1)}, f32[2,8,768]{2,1,0:T(8,128)}) custom-call(bf16[3,1024,768]{2,1,0:T(8,128)(2,1)} %get-tuple-element.72.a2_ref.dy_ref.refs_0_.refs_1_.refs_7_, bf16[3,1024,768]{2,1,0:T(8,128)(2,1)} %get-tuple-element.72.a2_ref.dy_ref.refs_0_.refs_1_.refs_7_, ...), custom_call_target="tpu_custom_call" | custom-call | flops 4831838208 | bytes 17301504 | tf_op jit(solution)/shard_map/pallas_call | solution.py:74
  128.0 12.8 %shard_map.206 = (bf16[2,2,1024,768]{3,2,1,0:T(8,128)(2,1)}, f32[2,8,768]{2,1,0:T(8,128)}) custom-call(bf16[3,1024,768]{2,1,0:T(8,128)(2,1)} %get-tuple-element.72.a2_ref.dy_ref.refs_0_.refs_1_.refs_7_, bf16[3,1024,768]{2,1,0:T(8,128)(2,1)} %get-tuple-element.72.a2_ref.dy_ref.refs_0_.refs_1_.refs_7_, ...), custom_call_target="tpu_custom_call" | custom-call | flops 4831838208 | bytes 17301504 | tf_op jit(solution)/shard_map/pallas_call | solution.py:74
  140.9 11.9 %shard_map.207 = (f32[4,2,2,2,24,384]{5,4,3,2,1,0:T(8,128)}, bf16[4,2,2,2,24,384]{5,4,3,2,1,0:T(8,128)(2,1)}, f32[4,2,2,2,24,384]{5,4,3,2,1,0:T(8,128)}, bf16[4,2,2,2,24,384]{5,4,3,2,1,0:T(8,128)(2,1)}) custom-call(s32[4]{0:T(128)} %pad_add_fusion.refs_0_, bf16[3,1024,768]{2,1,0:T(8,128)(2,1)} %get-tuple-element.72.a2_ref.dy_ref.refs_0_.refs_1_.refs_7_, ...), custom_call_target="tpu_custom_call" | custom-call | flops 4831838208 | bytes 12582912 | tf_op jit(solution)/shard_map/pallas_call | solution.py:74
  155.4 11.6 %shard_map.208 = (f32[4,2,2,2,24,384]{5,4,3,2,1,0:T(8,128)}, bf16[4,2,2,2,24,384]{5,4,3,2,1,0:T(8,128)(2,1)}, f32[4,2,2,2,24,384]{5,4,3,2,1,0:T(8,128)}, bf16[4,2,2,2,24,384]{5,4,3,2,1,0:T(8,128)(2,1)}) custom-call(s32[4]{0:T(128)} %pad_add_fusion.refs_0_, bf16[3,1024,768]{2,1,0:T(8,128)(2,1)} %get-tuple-element.72.a2_ref.dy_ref.refs_0_.refs_1_.refs_7_, ...), custom_call_target="tpu_custom_call" | custom-call | flops 4831838208 | bytes 12582912 | tf_op jit(solution)/shard_map/pallas_call | solution.py:74
  171.5 3.7 %shard_map.209 = (f32[4,2,2,24,384]{4,3,2,1,0:T(8,128)}, bf16[4,2,2,24,384]{4,3,2,1,0:T(8,128)(2,1)}, f32[4,2,2,24,384]{4,3,2,1,0:T(8,128)}, bf16[4,2,2,24,384]{4,3,2,1,0:T(8,128)(2,1)}) custom-call(s32[4]{0:T(128)} %pad_add_fusion.refs_0_, f32[4,2,2,2,24,384]{5,4,3,2,1,0:T(8,128)} %get-tuple-element.75.refs_9_.refs_1_, ...), custom_call_target="tpu_custom_call" | custom-call | bytes 7077888 | tf_op jit(solution)/shard_map/pallas_call | solution.py:74
  175.4 11.7 %shard_map.210 = (f32[4,2,2,2,24,384]{5,4,3,2,1,0:T(8,128)}, bf16[4,2,2,2,24,384]{5,4,3,2,1,0:T(8,128)(2,1)}, f32[4,2,2,2,24,384]{5,4,3,2,1,0:T(8,128)}, bf16[4,2,2,2,24,384]{5,4,3,2,1,0:T(8,128)(2,1)}) custom-call(s32[4]{0:T(128)} %pad_add_fusion.refs_0_, bf16[3,1024,768]{2,1,0:T(8,128)(2,1)} %get-tuple-element.72.a2_ref.dy_ref.refs_0_.refs_1_.refs_7_, ...), custom_call_target="tpu_custom_call" | custom-call | flops 4831838208 | bytes 12582912 | tf_op jit(solution)/shard_map/pallas_call | solution.py:74
  192.3 3.7 %shard_map.211 = (f32[4,2,2,24,384]{4,3,2,1,0:T(8,128)}, bf16[4,2,2,24,384]{4,3,2,1,0:T(8,128)(2,1)}, f32[4,2,2,24,384]{4,3,2,1,0:T(8,128)}, bf16[4,2,2,24,384]{4,3,2,1,0:T(8,128)(2,1)}) custom-call(s32[4]{0:T(128)} %pad_add_fusion.refs_0_, f32[4,2,2,2,24,384]{5,4,3,2,1,0:T(8,128)} %get-tuple-element.76.refs_5_.refs_1_, ...), custom_call_target="tpu_custom_call" | custom-call | bytes 7077888 | tf_op jit(solution)/shard_map/pallas_call | solution.py:74
  196.7 11.0 %shard_map.212.refs_13_ = bf16[1024,768]{1,0:T(8,128)(2,1)} custom-call(bf16[1024,768]{1,0:T(8,128)(2,1)} %bitcast.93, bf16[4,1024,768]{2,1,0:T(8,128)(2,1)} %get-tuple-element.71.refs_3_.refs_5_.refs_1_.refs_2_, bf16[4,1024,768]{2,1,0:T(8,128)(2,1)} %bitcast.91, bf16[4,1024,768]{2,1,0:T(8,128)(2,1)} %bitcast.85, bf16[4,768,768]{2,1,0:T(8,128)(2,1)} %bitcast.97, ...), custom_call_target="tpu_custom_call" | custom-call | flops 6039797760 | bytes 16908288 | tf_op jit(solution)/shard_map/pallas_call | solution.py:74
  210.0 4.3 %collective-permute-done.25.refs_12_ = bf16[4,2,2,24,384]{4,3,2,1,0:T(8,128)(2,1)S(1)} collective-permute-done((bf16[4,2,2,24,384]{4,3,2,1,0:T(8,128)(2,1)}, bf16[4,2,2,24,384]{4,3,2,1,0:T(8,128)(2,1)S(1)}, u32[]{:S(2)}, u32[]{:S(2)}) %collective-permute-start.25) | collective-permute-done | bytes 294944 | tf_op jit(solution)/shard_map/ppermute | solution.py:526
  215.0 5.0 %shard_map.213 = (f32[4,2,2,24,384]{4,3,2,1,0:T(8,128)}, bf16[4,2,2,24,384]{4,3,2,1,0:T(8,128)(2,1)}, f32[4,2,2,24,384]{4,3,2,1,0:T(8,128)}, bf16[4,2,2,24,384]{...) custom-call(s32[4]{0:T(128)} %pad_add_fusion.refs_0_, ...), custom_call_target="tpu_custom_call" | custom-call | bytes 14155776 | tf_op jit(solution)/shard_map/pallas_call | solution.py:74
  223.7 3.3 collective-permute-start.29
  227.0 10.0 %shard_map.214 = (f32[1024,768]{1,0:T(8,128)}, f32[3,8,768]{2,1,0:T(8,128)}) custom-call(bf16[1024,768]{1,0:T(8,128)(2,1)} %bitcast.94, bf16[1024,768]{1,0:T(8,128)(2,1)} %bitcast.101, bf16[4,1024,768]{2,1,0:T(8,128)(2,1)} %get-tuple-element.71.refs_3_.refs_5_.refs_1_.refs_2_, bf16[4,768,768]{2,1,0:T(8,128)(2,1)} %bitcast.98, ...), custom_call_target="tpu_custom_call" | custom-call | flops 3623878656 | bytes 14548992 | tf_op jit(solution)/shard_map/pallas_call | solution.py:74
  245.1 3.4 collective-permute-start.33
  253.9 11.0 %shard_map.216 = (bf16[1024,768]{1,0:T(8,128)(2,1)}, f32[2,8,768]{2,1,0:T(8,128)}) custom-call(bf16[1024,768]{1,0:T(8,128)(2,1)} %bitcast.95, f32[1024,768]{1,0:T(8,128)} %get-tuple-element.96.refs_5_.refs_1_, bf16[4,1024,768]{2,1,0:T(8,128)(2,1)} %bitcast.92, bf16[4,1024,768]{2,1,0:T(8,128)(2,1)} %bitcast.86, ...), custom_call_target="tpu_custom_call" | custom-call | flops 4831838208 | bytes 17301504 | tf_op jit(solution)/shard_map/pallas_call | solution.py:74
  266.1 3.7 %shard_map.217 = (f32[12,24,768]{2,1,0:T(8,128)}, bf16[32,24,768]{2,1,0:T(8,128)(2,1)}, f32[24,768]{1,0:T(8,128)}) custom-call(s32[32]{0:T(128)} %broadcast_add_fusion.refs_0_, bf16[8,24,768]{2,1,0:T(8,128)(2,1)} %copy-done.22, bf16[8,24,768]{2,1,0:T(8,128)(2,1)} %copy-done.23, bf16[8,24,768]{2,1,0:T(8,128)(2,1)} %copy-done.24, ...), custom_call_target="tpu_custom_call" | custom-call | bytes 3538944 | tf_op jit(solution)/shard_map/pallas_call | solution.py:74
  269.8 3.9 %all-to-all-start.1 = ((bf16[32,24,768]{2,1,0:T(8,128)(2,1)}), bf16[32,24,768]{2,1,0:T(8,128)(2,1)S(1)}, u32[]{:S(2)}, u32[]{:S(2)}) async-start(bf16[32,24,768]{2,1,0:T(8,128)(2,1)} %get-tuple-element.115), calls=%async_computation.1 | async-start | bytes 2359296 | tf_op jit(solution)/shard_map/all_to_all | solution.py:826
  278.1 6.6 %collective-permute-done.37 = f32[16,768]{1,0:T(8,128)S(1)} collective-permute-done((f32[16,768]{1,0:T(8,128)S(1)}, f32[16,768]{1,0:T(8,128)S(1)}, u32[]{:S(2)}, u32[]{:S(2)}) %collective-permute-start.37) | collective-permute-done | bytes 49184 | tf_op jit(solution)/shard_map/ppermute | solution.py:675
  285.8 3.8 %collective-permute-done.38 = f32[16,768]{1,0:T(8,128)S(1)} collective-permute-done((f32[16,768]{1,0:T(8,128)S(1)}, f32[16,768]{1,0:T(8,128)S(1)}, u32[]{:S(2)}, u32[]{:S(2)}) %collective-permute-start.38) | collective-permute-done | bytes 49184 | tf_op jit(solution)/shard_map/ppermute | solution.py:675
  289.9 5.8 %collective-permute-done.39 = f32[16,768]{1,0:T(8,128)S(1)} collective-permute-done((f32[16,768]{1,0:T(8,128)S(1)}, f32[16,768]{1,0:T(8,128)S(1)}, u32[]{:S(2)}, u32[]{:S(2)}) %collective-permute-start.39) | collective-permute-done | bytes 49184 | tf_op jit(solution)/shard_map/ppermute | solution.py:675
  298.5 3.2 collective-permute-done.40
  306.1 6.5 %shard_map.218 = bf16[768,768]{1,0:T(8,128)(2,1)} custom-call(f32[2]{0:T(128)} %pad_maximum_fusion.2.scale_ref, bf16[768,768]{1,0:T(8,128)(2,1)} %bitcast.103, f32[768,768]{1,0:T(8,128)} %bitcast.106, f32[768,768]{1,0:T(8,128)} %bitcast.107), custom_call_target="tpu_custom_call" | custom-call | flops 1811939328 | bytes 7077888 | tf_op jit(solution)/shard_map/pallas_call | solution.py:74
  312.6 5.9 %all-to-all-start.2 = ((bf16[32,24,768]{2,1,0:T(8,128)(2,1)}), bf16[32,24,768]{2,1,0:T(8,128)(2,1)S(1)}, u32[]{:S(2)}, u32[]{:S(2)}) async-start(bf16[32,24,768]{2,1,0:T(8,128)(2,1)} %bitcast.105), calls=%async_computation.2 | async-start | bytes 2359296 | tf_op jit(solution)/shard_map/all_to_all | solution.py:826
  320.5 7.2 %shard_map.220 = (f32[768,768]{1,0:T(8,128)}, f32[768,768]{1,0:T(8,128)}) custom-call(s32[1]{0:T(128)} %bitcast.45.has_ref, f32[2]{0:T(128)} %pad_maximum_fusion.2.scale_ref, bf16[768,768]{1,0:T(8,128)(2,1)} %bitcast.104, f32[768,768]{1,0:T(8,128)} %bitcast.120, f32[768,768]{1,0:T(8,128)} %bitcast.121), custom_call_target="tpu_custom_call" | custom-call | flops 1811939328 | bytes 10616832 | tf_op jit(solution)/shard_map/pallas_call | solution.py:74
  327.7 19.9 %all-to-all-done.2.p_ref = bf16[32,24,768]{2,1,0:T(8,128)(2,1)S(1)} async-done(((bf16[32,24,768]{2,1,0:T(8,128)(2,1)}), bf16[32,24,768]{2,1,0:T(8,128)(2,1)S(1)}, u32[]{:S(2)}, u32[]{:S(2)}) %all-to-all-start.2) | async-done | bytes 1179680 | tf_op jit(solution)/shard_map/all_to_all | solution.py:826
  348.7 3.3 shard_map.219
  (237 shorter events, 94.5 us)
Async XLA Ops:
  7.2 107.8 %all-gather.2.cloned.1.call-start = ((), (), s32[]{:S(2)}) async-start(), calls=%async_computation.3 | async-start | bytes 9732096 | tf_op jit(solution)/shard_map/all_gather | solution.py:856
  9.4 24.8 %collective-permute-start = (bf16[4,24,768]{2,1,0:T(8,128)(2,1)S(1)}, bf16[4,24,768]{2,1,0:T(8,128)(2,1)S(1)}, u32[]{:S(2)}, u32[]{:S(2)}) collective-permute-start(bf16[4,24,768]{2,1,0:T(8,128)(2,1)S(1)} %get-tuple-element.129), channel_id=1, source_target_pairs={{0,8},{1,9},{2,10},{3,11},{4,12},{5,13},{6,14},{7,15},{8,16},{9,17... | collective-permute-start | bytes 442376 | tf_op jit(solution)/shard_map/ppermute | solution.py:534
  12.4 21.7 %collective-permute-start.1 = (bf16[4,24,768]{2,1,0:T(8,128)(2,1)S(1)}, bf16[4,24,768]{2,1,0:T(8,128)(2,1)S(1)}, u32[]{:S(2)}, u32[]{:S(2)}) collective-permute-start(bf16[4,24,768]{2,1,0:T(8,128)(2,1)S(1)} %get-tuple-element.129), channel_id=1, source_target_pairs={{0,16},{1,17},{2,18},{3,19},{4,20},{5,21},{6,22},{7,23},{8,24},{9,... | collective-permute-start | bytes 442376 | tf_op jit(solution)/shard_map/ppermute | solution.py:534
  15.0 19.1 %collective-permute-start.2 = (bf16[4,24,768]{2,1,0:T(8,128)(2,1)S(1)}, bf16[4,24,768]{2,1,0:T(8,128)(2,1)S(1)}, u32[]{:S(2)}, u32[]{:S(2)}) collective-permute-start(bf16[4,24,768]{2,1,0:T(8,128)(2,1)S(1)} %get-tuple-element.129), channel_id=1, source_target_pairs={{0,24},{1,25},{2,26},{3,27},{4,28},{5,29},{6,30},{7,31},{8,0},{9,1... | collective-permute-start | bytes 442376 | tf_op jit(solution)/shard_map/ppermute | solution.py:534
  19.2 25.7 %all-to-all-start = ((bf16[32,2,156]{2,1,0:T(2,128)(2,1)}), bf16[32,2,156]{2,1,0:T(2,128)(2,1)}, u32[]{:S(2)}, u32[]{:S(2)}) async-start(bf16[32,2,156]{2,1,0:T(2,128)(2,1)} %reshape.554), calls=%async_computation | async-start | bytes 65536 | tf_op jit(solution)/shard_map/all_to_all | solution.py:826
  34.3 22.1 %collective-permute-start.3 = (bf16[4,4,24,768]{3,2,1,0:T(8,128)(2,1)S(1)}, bf16[4,4,24,768]{3,2,1,0:T(8,128)(2,1)S(1)}, u32[]{:S(2)}, u32[]{:S(2)}) collective-permute-start(bf16[4,4,24,768]{3,2,1,0:T(8,128)(2,1)S(1)} %pad_maximum_fusion.1.refs_1_), channel_id=1, source_target_pairs={{0,2},{1,3},{2,0},{3,1},{4,6},{5,7},{6,4},{7,5},{8,10},{9,11},{10,... | collective-permute-start | bytes 1769480 | tf_op jit(solution)/shard_map/ppermute | solution.py:526
  35.9 22.0 %collective-permute-start.4 = (bf16[4,4,24,768]{3,2,1,0:T(8,128)(2,1)S(1)}, bf16[4,4,24,768]{3,2,1,0:T(8,128)(2,1)S(1)}, u32[]{:S(2)}, u32[]{:S(2)}) collective-permute-start(bf16[4,4,24,768]{3,2,1,0:T(8,128)(2,1)S(1)} %pad_maximum_fusion.1.refs_1_), channel_id=1, source_target_pairs={{0,4},{1,5},{2,6},{3,7},{4,0},{5,1},{6,2},{7,3},{8,12},{9,13},{10,... | collective-permute-start | bytes 1769480 | tf_op jit(solution)/shard_map/ppermute | solution.py:530
  49.9 17.7 %collective-permute-start.7 = (bf16[4,4,24,768]{3,2,1,0:T(8,128)(2,1)S(1)}, bf16[4,4,24,768]{3,2,1,0:T(8,128)(2,1)S(1)}, u32[]{:S(2)}, u32[]{:S(2)}) collective-permute-start(bf16[4,4,24,768]{3,2,1,0:T(8,128)(2,1)S(1)} %pad_maximum_fusion.1.refs_1_), channel_id=1, source_target_pairs={{0,1},{1,0},{2,3},{3,2},{4,5},{5,4},{6,7},{7,6},{8,9},{9,8},{10,11... | collective-permute-start | bytes 1769480 | tf_op jit(solution)/shard_map/ppermute | solution.py:522
  113.5 14.4 %collective-permute-start.12 = (bf16[3,1024,768]{2,1,0:T(8,128)(2,1)}, bf16[3,1024,768]{2,1,0:T(8,128)(2,1)}, u32[]{:S(2)}, u32[]{:S(2)}) collective-permute-start(bf16[3,1024,768]{2,1,0:T(8,128)(2,1)} %get-tuple-element.72.a2_ref.dy_ref.refs_0_.refs_1_.refs_7_), channel_id=1, source_target_pairs={{0,1},{1,0},{2,3},{3,2},{4,5},{5,4},{6,7},{7,6},{8,9},{9,8},{10,11... | collective-permute-start | bytes 14155784 | tf_op jit(solution)/shard_map/ppermute | solution.py:522
  114.1 26.8 %collective-permute-start.14 = (bf16[4,1024,768]{2,1,0:T(8,128)(2,1)}, bf16[4,1024,768]{2,1,0:T(8,128)(2,1)}, u32[]{:S(2)}, u32[]{:S(2)}) collective-permute-start(bf16[4,1024,768]{2,1,0:T(8,128)(2,1)} %get-tuple-element.71.refs_3_.refs_5_.refs_1_.refs_2_), channel_id=1, source_target_pairs={{0,1},{1,0},{2,3},{3,2},{4,5},{5,4},{6,7},{7,6},{8,9},{9,8},{10,11... | collective-permute-start | bytes 18874376 | tf_op jit(solution)/shard_map/ppermute | solution.py:522
  127.5 27.9 %collective-permute-start.13 = (bf16[4,1024,768]{2,1,0:T(8,128)(2,1)}, bf16[4,1024,768]{2,1,0:T(8,128)(2,1)}, u32[]{:S(2)}, u32[]{:S(2)}) collective-permute-start(bf16[4,1024,768]{2,1,0:T(8,128)(2,1)} %bitcast.87), channel_id=1, source_target_pairs={{0,1},{1,0},{2,3},{3,2},{4,5},{5,4},{6,7},{7,6},{8,9},{9,8},{10,11... | collective-permute-start | bytes 18874376 | tf_op jit(solution)/shard_map/ppermute | solution.py:522
  140.8 34.6 %collective-permute-start.17 = (bf16[4,1024,768]{2,1,0:T(8,128)(2,1)}, bf16[4,1024,768]{2,1,0:T(8,128)(2,1)}, u32[]{:S(2)}, u32[]{:S(2)}) collective-permute-start(bf16[4,1024,768]{2,1,0:T(8,128)(2,1)} %bitcast.81), channel_id=1, source_target_pairs={{0,1},{1,0},{2,3},{3,2},{4,5},{5,4},{6,7},{7,6},{8,9},{9,8},{10,11... | collective-permute-start | bytes 18874376 | tf_op jit(solution)/shard_map/ppermute | solution.py:522
  152.8 16.0 %collective-permute-start.18 = (bf16[4,2,2,2,24,384]{5,4,3,2,1,0:T(8,128)(2,1)}, bf16[4,2,2,2,24,384]{5,4,3,2,1,0:T(8,128)(2,1)S(1)}, u32[]{:S(2)}, u32[]{:S(2)}) collective-permute-start(bf16[4,2,2,2,24,384]{5,4,3,2,1,0:T(8,128)(2,1)} %get-tuple-element.80), channel_id=1, source_target_pairs={{0,2},{1,3},{2,0},{3,1},{4,6},{5,7},{6,4},{7,5},{8,10},{9,11},{10,... | collective-permute-start | bytes 1769480 | tf_op jit(solution)/shard_map/ppermute | solution.py:526
  154.8 15.9 %collective-permute-start.19 = (bf16[4,2,2,2,24,384]{5,4,3,2,1,0:T(8,128)(2,1)}, bf16[4,2,2,2,24,384]{5,4,3,2,1,0:T(8,128)(2,1)S(1)}, u32[]{:S(2)}, u32[]{:S(2)}) collective-permute-start(bf16[4,2,2,2,24,384]{5,4,3,2,1,0:T(8,128)(2,1)} %get-tuple-element.82), channel_id=1, source_target_pairs={{0,4},{1,5},{2,6},{3,7},{4,0},{5,1},{6,2},{7,3},{8,12},{9,13},{10,... | collective-permute-start | bytes 1769480 | tf_op jit(solution)/shard_map/ppermute | solution.py:530
  167.0 22.9 %collective-permute-start.15 = (bf16[4,2,2,2,24,384]{5,4,3,2,1,0:T(8,128)(2,1)}, bf16[4,2,2,2,24,384]{5,4,3,2,1,0:T(8,128)(2,1)S(1)}, u32[]{:S(2)}, u32[]{:S(2)}) collective-permute-start(bf16[4,2,2,2,24,384]{5,4,3,2,1,0:T(8,128)(2,1)} %get-tuple-element.77), channel_id=1, source_target_pairs={{0,2},{1,3},{2,0},{3,1},{4,6},{5,7},{6,4},{7,5},{8,10},{9,11},{10,... | collective-permute-start | bytes 1769480 | tf_op jit(solution)/shard_map/ppermute | solution.py:526
  167.1 24.4 %collective-permute-start.16 = (bf16[4,2,2,2,24,384]{5,4,3,2,1,0:T(8,128)(2,1)}, bf16[4,2,2,2,24,384]{5,4,3,2,1,0:T(8,128)(2,1)S(1)}, u32[]{:S(2)}, u32[]{:S(2)}) collective-permute-start(bf16[4,2,2,2,24,384]{5,4,3,2,1,0:T(8,128)(2,1)} %get-tuple-element.79), channel_id=1, source_target_pairs={{0,4},{1,5},{2,6},{3,7},{4,0},{5,1},{6,2},{7,3},{8,12},{9,13},{10,... | collective-permute-start | bytes 1769480 | tf_op jit(solution)/shard_map/ppermute | solution.py:530
  175.1 21.1 %collective-permute-start.22 = (bf16[4,2,2,24,384]{4,3,2,1,0:T(8,128)(2,1)}, bf16[4,2,2,24,384]{4,3,2,1,0:T(8,128)(2,1)S(1)}, u32[]{:S(2)}, u32[]{:S(2)}) collective-permute-start(bf16[4,2,2,24,384]{4,3,2,1,0:T(8,128)(2,1)} %get-tuple-element.89), channel_id=1, source_target_pairs={{0,4},{1,5},{2,6},{3,7},{4,0},{5,1},{6,2},{7,3},{8,12},{9,13},{10,... | collective-permute-start | bytes 884744 | tf_op jit(solution)/shard_map/ppermute | solution.py:530
  187.1 22.8 %collective-permute-start.20 = (bf16[4,2,2,2,24,384]{5,4,3,2,1,0:T(8,128)(2,1)}, bf16[4,2,2,2,24,384]{5,4,3,2,1,0:T(8,128)(2,1)S(1)}, u32[]{:S(2)}, u32[]{:S(2)}) collective-permute-start(bf16[4,2,2,2,24,384]{5,4,3,2,1,0:T(8,128)(2,1)} %get-tuple-element.86), channel_id=1, source_target_pairs={{0,2},{1,3},{2,0},{3,1},{4,6},{5,7},{6,4},{7,5},{8,10},{9,11},{10,... | collective-permute-start | bytes 1769480 | tf_op jit(solution)/shard_map/ppermute | solution.py:526
  187.6 22.3 %collective-permute-start.21 = (bf16[4,2,2,2,24,384]{5,4,3,2,1,0:T(8,128)(2,1)}, bf16[4,2,2,2,24,384]{5,4,3,2,1,0:T(8,128)(2,1)S(1)}, u32[]{:S(2)}, u32[]{:S(2)}) collective-permute-start(bf16[4,2,2,2,24,384]{5,4,3,2,1,0:T(8,128)(2,1)} %get-tuple-element.88), channel_id=1, source_target_pairs={{0,4},{1,5},{2,6},{3,7},{4,0},{5,1},{6,2},{7,3},{8,12},{9,13},{10,... | collective-permute-start | bytes 1769480 | tf_op jit(solution)/shard_map/ppermute | solution.py:530
  189.9 20.0 %collective-permute-start.23 = (bf16[4,2,2,24,384]{4,3,2,1,0:T(8,128)(2,1)S(1)}, bf16[4,2,2,24,384]{4,3,2,1,0:T(8,128)(2,1)S(1)}, u32[]{:S(2)}, u32[]{:S(2)}) collective-permute-start(bf16[4,2,2,24,384]{4,3,2,1,0:T(8,128)(2,1)S(1)} %copy-done.43), channel_id=1, source_target_pairs={{0,2},{1,3},{2,0},{3,1},{4,6},{5,7},{6,4},{7,5},{8,10},{9,11},{10,... | collective-permute-start | bytes 884744 | tf_op jit(solution)/shard_map/ppermute | solution.py:526
  196.3 18.0 %collective-permute-start.25 = (bf16[4,2,2,24,384]{4,3,2,1,0:T(8,128)(2,1)}, bf16[4,2,2,24,384]{4,3,2,1,0:T(8,128)(2,1)S(1)}, u32[]{:S(2)}, u32[]{:S(2)}) collective-permute-start(bf16[4,2,2,24,384]{4,3,2,1,0:T(8,128)(2,1)} %get-tuple-element.94), channel_id=1, source_target_pairs={{0,2},{1,3},{2,0},{3,1},{4,6},{5,7},{6,4},{7,5},{8,10},{9,11},{10,... | collective-permute-start | bytes 884744 | tf_op jit(solution)/shard_map/ppermute | solution.py:526
  220.0 17.0 %collective-permute-start.26 = (bf16[4,2,2,24,384]{4,3,2,1,0:T(8,128)(2,1)}, bf16[4,2,2,24,384]{4,3,2,1,0:T(8,128)(2,1)S(1)}, u32[]{:S(2)}, u32[]{:S(2)}) collective-permute-start(bf16[4,2,2,24,384]{4,3,2,1,0:T(8,128)(2,1)} %get-tuple-element.97), channel_id=1, source_target_pairs={{0,4},{1,5},{2,6},{3,7},{4,0},{5,1},{6,2},{7,3},{8,12},{9,13},{10,... | collective-permute-start | bytes 884744 | tf_op jit(solution)/shard_map/ppermute | solution.py:530
  221.3 18.7 %collective-permute-start.27 = (bf16[4,2,2,24,384]{4,3,2,1,0:T(8,128)(2,1)}, bf16[4,2,2,24,384]{4,3,2,1,0:T(8,128)(2,1)S(1)}, u32[]{:S(2)}, u32[]{:S(2)}) collective-permute-start(bf16[4,2,2,24,384]{4,3,2,1,0:T(8,128)(2,1)} %get-tuple-element.99), channel_id=1, source_target_pairs={{0,2},{1,3},{2,0},{3,1},{4,6},{5,7},{6,4},{7,5},{8,10},{9,11},{10,... | collective-permute-start | bytes 884744 | tf_op jit(solution)/shard_map/ppermute | solution.py:526
  222.1 23.0 %collective-permute-start.28 = (bf16[8,24,768]{2,1,0:T(8,128)(2,1)}, bf16[8,24,768]{2,1,0:T(8,128)(2,1)S(1)}, u32[]{:S(2)}, u32[]{:S(2)}) collective-permute-start(bf16[8,24,768]{2,1,0:T(8,128)(2,1)} %bitcast.125), channel_id=1, source_target_pairs={{0,0},{1,16},{2,2},{3,18},{4,4},{5,20},{6,6},{7,22},{8,1},{9,17},{... | collective-permute-start | bytes 884744 | tf_op jit(solution)/shard_map/ppermute | solution.py:660
  223.7 24.8 %collective-permute-start.29 = (bf16[8,24,768]{2,1,0:T(8,128)(2,1)}, bf16[8,24,768]{2,1,0:T(8,128)(2,1)S(1)}, u32[]{:S(2)}, u32[]{:S(2)}) collective-permute-start(bf16[8,24,768]{2,1,0:T(8,128)(2,1)} %bitcast.124), channel_id=1, source_target_pairs={{0,1},{1,17},{2,3},{3,19},{4,5},{5,21},{6,7},{7,23},{8,0},{9,16},{... | collective-permute-start | bytes 884744 | tf_op jit(solution)/shard_map/ppermute | solution.py:660
  227.0 24.2 %collective-permute-start.30 = (bf16[8,24,768]{2,1,0:T(8,128)(2,1)}, bf16[8,24,768]{2,1,0:T(8,128)(2,1)S(1)}, u32[]{:S(2)}, u32[]{:S(2)}) collective-permute-start(bf16[8,24,768]{2,1,0:T(8,128)(2,1)} %bitcast.123), channel_id=1, source_target_pairs={{0,8},{1,24},{2,10},{3,26},{4,12},{5,28},{6,14},{7,30},{8,9},{9,25... | collective-permute-start | bytes 884744 | tf_op jit(solution)/shard_map/ppermute | solution.py:660
  237.1 27.9 %collective-permute-start.31 = (bf16[8,24,768]{2,1,0:T(8,128)(2,1)S(1)}, bf16[8,24,768]{2,1,0:T(8,128)(2,1)S(1)}, u32[]{:S(2)}, u32[]{:S(2)}) collective-permute-start(bf16[8,24,768]{2,1,0:T(8,128)(2,1)S(1)} %bitcast.122), channel_id=1, source_target_pairs={{0,9},{1,25},{2,11},{3,27},{4,13},{5,29},{6,15},{7,31},{8,8},{9,24... | collective-permute-start | bytes 884744 | tf_op jit(solution)/shard_map/ppermute | solution.py:660
  243.6 21.5 %collective-permute-start.32 = (bf16[4,24,768]{2,1,0:T(8,128)(2,1)}, bf16[4,24,768]{2,1,0:T(8,128)(2,1)S(1)}, u32[]{:S(2)}, u32[]{:S(2)}) collective-permute-start(bf16[4,24,768]{2,1,0:T(8,128)(2,1)} %bitcast.128), channel_id=1, source_target_pairs={{0,0},{1,16},{2,2},{3,18},{4,4},{5,20},{6,6},{7,22},{8,1},{9,17},{... | collective-permute-start | bytes 442376 | tf_op jit(solution)/shard_map/ppermute | solution.py:660
  245.1 19.9 %collective-permute-start.33 = (bf16[4,24,768]{2,1,0:T(8,128)(2,1)}, bf16[4,24,768]{2,1,0:T(8,128)(2,1)S(1)}, u32[]{:S(2)}, u32[]{:S(2)}) collective-permute-start(bf16[4,24,768]{2,1,0:T(8,128)(2,1)} %bitcast.127), channel_id=1, source_target_pairs={{0,1},{1,17},{2,3},{3,19},{4,5},{5,21},{6,7},{7,23},{8,0},{9,16},{... | collective-permute-start | bytes 442376 | tf_op jit(solution)/shard_map/ppermute | solution.py:660
  248.5 17.0 %collective-permute-start.34 = (bf16[4,24,768]{2,1,0:T(8,128)(2,1)}, bf16[4,24,768]{2,1,0:T(8,128)(2,1)S(1)}, u32[]{:S(2)}, u32[]{:S(2)}) collective-permute-start(bf16[4,24,768]{2,1,0:T(8,128)(2,1)} %bitcast.126), channel_id=1, source_target_pairs={{0,8},{1,24},{2,10},{3,26},{4,12},{5,28},{6,14},{7,30},{8,9},{9,25... | collective-permute-start | bytes 442376 | tf_op jit(solution)/shard_map/ppermute | solution.py:660
  269.8 35.3 %all-to-all-start.1 = ((bf16[32,24,768]{2,1,0:T(8,128)(2,1)}), bf16[32,24,768]{2,1,0:T(8,128)(2,1)S(1)}, u32[]{:S(2)}, u32[]{:S(2)}) async-start(bf16[32,24,768]{2,1,0:T(8,128)(2,1)} %get-tuple-element.115), calls=%async_computation.1 | async-start | bytes 2359296 | tf_op jit(solution)/shard_map/all_to_all | solution.py:826
  312.6 35.0 %all-to-all-start.2 = ((bf16[32,24,768]{2,1,0:T(8,128)(2,1)}), bf16[32,24,768]{2,1,0:T(8,128)(2,1)S(1)}, u32[]{:S(2)}, u32[]{:S(2)}) async-start(bf16[32,24,768]{2,1,0:T(8,128)(2,1)} %bitcast.105), calls=%async_computation.2 | async-start | bytes 2359296 | tf_op jit(solution)/shard_map/all_to_all | solution.py:826
  (57 other events, 362.0 us)
Sparse Core Ops, SparseCore 0:
  11.0 93.1 all-gather.1

commit v3 on v2

--- a/solution.py
+++ b/solution.py
@@ -147,7 +147,7 @@
 
 def attend_body(
     acts_ref, col_ref, row_ref, q_ref, k_ref, v_ref, do_ref, c_ref, a_ref, b_ref,
-    g_ref, sum_ref, acts_out_ref, mask_ref, dk_acc, dv_acc, *, block,
+    g_ref, sum_ref, acts_out_ref, mask_ref, *, block,
 ):
     length = q_ref.shape[0]
     steps = length // block
@@ -169,9 +169,6 @@
     low = lax.broadcasted_iota(jnp.int32, (1, LANES), 1) < 64
     eighth = jnp.asarray(0.125, bf16)
     zero = jnp.zeros((), bf16)
-    keys, values, grads = k_ref[...], v_ref[...], do_ref[...]
-    queries = q_ref[...] * eighth
-    keys_t, values_t = (keys * eighth).T, values.T
 
     def both(part):
         return jnp.concatenate([jnp.where(low, part, zero), jnp.where(low, zero, part)], axis=0)
@@ -179,48 +176,64 @@
     def unstack(part):
         return jnp.concatenate([part[0:64, 0:block], part[64:, block:]], axis=0).T
 
-    dk_acc[...] = jnp.zeros_like(dk_acc)
-    dv_acc[...] = jnp.zeros_like(dv_acc)
-    q_sum = jnp.zeros((8, LANES), f32)
+    pairs = []
+    for at in range(0, q_ref.shape[1], LANES):
+        lanes = slice(at, at + LANES)
+        keys, values = k_ref[:, lanes], v_ref[:, lanes]
+        pairs.append(
+            (lanes, keys, values, (keys * eighth).T, values.T, q_ref[:, lanes] * eighth, do_ref[:, lanes])
+        )
+    q_sums = [jnp.zeros((8, LANES), f32) for _ in pairs]
+    dks = [[None] * steps for _ in pairs]
+    dvs = [[None] * steps for _ in pairs]
+
+    def add(parts, n, value):
+        parts[n] = value if parts[n] is None else parts[n] + value
+
     for i in range(steps):
         lo, hi = reach(i)
         here = slice(i * block, hi)
-        q2, do2 = both(queries[here]), both(grads[here])
-        scores = mm(keys[lo:hi], q2, NT) + mask_ref[i, 0 : hi - lo, :]
-        raised = jnp.exp(scores - jnp.max(scores, axis=0, keepdims=True))
-        soft = raised * (1.0 / jnp.sum(raised, axis=0, keepdims=True))
-        d_soft = mm(values[lo:hi], do2, NT)
-        inner = jnp.sum(soft * d_soft, axis=0, keepdims=True)
-        soft_low = soft.astype(bf16)
-        d_scores = (soft * (d_soft - inner)).astype(bf16)
-        g_ref[3, here, :] = unstack(mm(values_t[:, lo:hi], soft_low, NN)).astype(bf16)
-        dq = rotate_back(
-            unstack(mm(keys_t[:, lo:hi], d_scores, NN)), c_ref[here, :], a_ref[here, :], b_ref[here, :]
-        ).astype(bf16)
-        g_ref[0, here, :] = dq
-        q_sum = q_sum + sub_sum(dq.astype(f32))
-        dk_acc[lo:hi, :] += mm(d_scores, q2, NN)
-        dv_acc[lo:hi, :] += mm(soft_low, do2, NN)
-    dk = rotate_back(dk_acc[...], c_ref[...], a_ref[...], b_ref[...]).astype(bf16)
-    dv = dv_acc[...].astype(bf16)
-    g_ref[1] = dk
-    g_ref[2] = dv
-    sum_ref[0] = q_sum
-    sum_ref[1] = sub_sum(dk.astype(f32))
-    sum_ref[2] = sub_sum(dv.astype(f32))
-
-
-def attend(segment_ids, q, k, v, do, tables, acts, block=256):
+        for p, (lanes, keys, values, keys_t, values_t, queries, grads) in enumerate(pairs):
+            q2, do2 = both(queries[here]), both(grads[here])
+            scores = mm(keys[lo:hi], q2, NT) + mask_ref[i, 0 : hi - lo, :]
+            d_soft = mm(values[lo:hi], do2, NT)
+            raised = jnp.exp(scores - jnp.max(scores, axis=0, keepdims=True))
+            soft = raised * (1.0 / jnp.sum(raised, axis=0, keepdims=True))
+            inner = jnp.sum(soft * d_soft, axis=0, keepdims=True)
+            soft_low = soft.astype(bf16)
+            d_scores = (soft * (d_soft - inner)).astype(bf16)
+            g_ref[3, here, lanes] = unstack(mm(values_t[:, lo:hi], soft_low, NN)).astype(bf16)
+            dq = rotate_back(
+                unstack(mm(keys_t[:, lo:hi], d_scores, NN)), c_ref[here, :], a_ref[here, :], b_ref[here, :]
+            ).astype(bf16)
+            g_ref[0, here, lanes] = dq
+            q_sums[p] = q_sums[p] + sub_sum(dq.astype(f32))
+            dk, dv = mm(d_scores, q2, NN), mm(soft_low, do2, NN)
+            for n in range(lo // block, i + 1):
+                rows = slice(n * block - lo, (n + 1) * block - lo)
+                add(dks[p], n, dk[rows])
+                add(dvs[p], n, dv[rows])
+    for p, (lanes, *_) in enumerate(pairs):
+        dk = rotate_back(jnp.concatenate(dks[p], axis=0), c_ref[...], a_ref[...], b_ref[...]).astype(bf16)
+        dv = jnp.concatenate(dvs[p], axis=0).astype(bf16)
+        g_ref[1, :, lanes] = dk
+        g_ref[2, :, lanes] = dv
+        sum_ref[0, :, lanes] = q_sums[p]
+        sum_ref[1, :, lanes] = sub_sum(dk.astype(f32))
+        sum_ref[2, :, lanes] = sub_sum(dv.astype(f32))
+
+
+def attend(segment_ids, q, k, v, do, tables, acts, block=256, lanes=3 * LANES):
     rows, length = segment_ids.shape
     count, width = q.shape
     block = min(block, length)
-    token = pl.BlockSpec((length, LANES), lambda r, h: (r, h))
+    token = pl.BlockSpec((length, lanes), lambda r, h: (r, h))
     table = pl.BlockSpec((length, LANES), lambda r, h: (r, 0))
     return call(
         functools.partial(attend_body, block=block),
         24 * count * length * width,
         24 * count * width,
-        grid=(rows, width // LANES),
+        grid=(rows, width // lanes),
         input_output_aliases={0: 2},
         in_specs=[
             pl.BlockSpec(memory_space=pl.ANY),
@@ -235,8 +248,8 @@
             table,
         ],
         out_specs=[
-            pl.BlockSpec((4, length, LANES), lambda r, h: (0, r, h)),
-            pl.BlockSpec((3, 8, LANES), lambda r, h: (0, r, h)),
+            pl.BlockSpec((4, length, lanes), lambda r, h: (0, r, h)),
+            pl.BlockSpec((3, 8, lanes), lambda r, h: (0, r, h)),
             pl.BlockSpec(memory_space=pl.ANY),
         ],
         out_shape=[
@@ -244,11 +257,7 @@
             jax.ShapeDtypeStruct((3, 8 * rows, width), f32),
             jax.ShapeDtypeStruct(acts.shape, acts.dtype),
         ],
-        scratch_shapes=[
-            pltpu.VMEM((length // block, length, 2 * block), f32),
-            pltpu.VMEM((length, LANES), f32),
-            pltpu.VMEM((length, LANES), f32),
-        ],
+        scratch_shapes=[pltpu.VMEM((length // block, length, 2 * block), f32)],
     )(
         acts,
         segment_ids.reshape(-1, 1),
@@ -261,11 +270,10 @@
     )
 
 
-def half_grads_body(place_ref, *refs, first, second, steps):
-    l1o, l1p, l2o, l2p, r1o, r1p, r2o, r2p, ka_ref, sa_ref, kb_ref, sb_ref, acc = refs
+def half_grads_body(place_ref, *refs, first, second, steps, axes):
+    l1o, l1p, l2o, l2p, r1o, r1p, r2o, r2p, *outs, acc = refs
     i = pl.program_id(0)
     y, x = place_ref[1], place_ref[2]
-    half = ka_ref.shape[-1]
 
     @pl.when(i == 0)
     def _():
@@ -281,10 +289,15 @@
     @pl.when(i == steps - 1)
     def _():
         for n in range(first + second):
-            for ref, at in ((ka_ref, x), (sa_ref, 1 - x)):
-                ref[n] = acc[n, :, :, at, :, :, :half].astype(ref.dtype)
-            for ref, at in ((kb_ref, y), (sb_ref, 1 - y)):
-                ref[n] = acc[n, :, at, :, :, :, half:].astype(ref.dtype)
+            for r, axis in enumerate(axes):
+                wide = outs[0].shape[-1]
+                columns = slice(r * wide, (r + 1) * wide)
+                for ref, other in zip(outs[2 * r : 2 * r + 2], (0, 1)):
+                    if axis == "x":
+                        value = acc[n, :, :, x ^ other, :, :, columns]
+                    else:
+                        value = acc[n, :, y ^ other, :, :, :, columns]
+                    ref[n] = value.astype(bf16)
 
 
 def layers(part, step, lanes, half=False):
@@ -292,16 +305,16 @@
     return pl.BlockSpec((count, step, lanes), lambda i, *s: (first // count, i, s[0][3] if half else 0))
 
 
-def half_grads(place, left_one, left_two, right_one, right_two, shard, after=(), step=256):
+def half_grads(place, left_one, left_two, right_one, right_two, shard, axes, after=(), step=256):
     first, second = right_one[2], left_two[2]
     _, count, width = right_two[0][0].shape
     half = width // 2
     blocks = first + second
     steps = count // step
-    shape = (blocks, 2, 2, 2, shard, half)
+    shape = (blocks, 2, 2, 2, shard, width // len(axes))
     out = pl.BlockSpec(shape, lambda i, s: (0, 0, 0, 0, 0, 0))
     return call(
-        functools.partial(half_grads_body, first=first, second=second, steps=steps),
+        functools.partial(half_grads_body, first=first, second=second, steps=steps, axes=axes),
         blocks * 2 * count * width * width,
         blocks * 4 * count * width,
         after=after,
@@ -312,10 +325,10 @@
             + [layers(left_two, step, half, True)] * 2
             + [layers(right_one, step, width)] * 2
             + [layers(right_two, step, width)] * 2,
-            out_specs=[out] * 4,
+            out_specs=[out] * (2 * len(axes)),
             scratch_shapes=[pltpu.VMEM((blocks, 2, 2, 2, 2, shard, width), f32)],
         ),
-        out_shape=[jax.ShapeDtypeStruct(shape, k) for k in (f32, bf16, f32, bf16)],
+        out_shape=[jax.ShapeDtypeStruct(shape, bf16)] * (2 * len(axes)),
     )(place, *left_one[0], *left_two[0], *right_one[0], *right_two[0])
 
 
@@ -589,38 +602,52 @@
     return weights.reshape(blocks, width, width)
 
 
-def chip_pair_body(place_ref, ka_ref, ga_ref, kb_ref, gb_ref, ka2_ref, sa_ref, kb2_ref, sb_ref):
+class Reduction:
+    def __init__(self, axes, made):
+        self.axes, self.made = axes, made[0]
+        self.held = [
+            (keep, over_x(send) if axis == "x" else over_y(send))
+            for axis, keep, send in zip(axes, made[::2], made[1::2])
+        ]
+
+    def second(self, made):
+        self.made = made[0]
+        self.held = [
+            (keep, over_y(send) if axis == "x" else over_x(send))
+            for axis, keep, send in zip(self.axes, made[::2], made[1::2])
+        ]
+
+
+def pair_body(place_ref, r, ins, outs):
     y, x = place_ref[1], place_ref[2]
-    for mine, k_ref, g_ref, k2_ref, s2_ref in (
-        (y, ka_ref, ga_ref, ka2_ref, sa_ref),
-        (x, kb_ref, gb_ref, kb2_ref, sb_ref),
-    ):
-        k2_ref[...] = k_ref[:, :, mine] + g_ref[:, :, mine].astype(f32)
-        s2_ref[...] = (k_ref[:, :, 1 - mine] + g_ref[:, :, 1 - mine].astype(f32)).astype(bf16)
-
-
-def plane_body(place_ref, ka_ref, ga_ref, kb_ref, gb_ref, *out_refs):
-    half = ka_ref.shape[-1]
-    for m, ref in enumerate(out_refs):
+    for n, axis in enumerate(r.axes):
+        keep, got = ins[2 * n : 2 * n + 2]
+        for ref, other in zip(outs[2 * n : 2 * n + 2], (0, 1)):
+            at = (y if axis == "x" else x) ^ other
+            ref[...] = (keep[:, :, at].astype(f32) + got[:, :, at].astype(f32)).astype(bf16)
+
+
+def plane_body(place_ref, r, ins, outs):
+    for m, ref in enumerate(outs):
         at = place_ref[0] ^ m
-        for lo, k_ref, g_ref in ((0, ka_ref, ga_ref), (half, kb_ref, gb_ref)):
-            ref[:, :, lo : lo + half] = (k_ref[:, at >> 1, at & 1] + g_ref[:, at >> 1, at & 1].astype(f32)).astype(
-                bf16
-            )
-
-
-class Reduction:
-    def __init__(self, ka, sa, kb, sb):
-        self.made = ka
-        self.held = (ka, over_x(sa), kb, over_y(sb))
+        for n in range(len(r.axes)):
+            keep, got = ins[2 * n : 2 * n + 2]
+            wide = keep.shape[-1]
+            value = keep[:, at >> 1, at & 1].astype(f32) + got[:, at >> 1, at & 1].astype(f32)
+            ref[:, :, n * wide : (n + 1) * wide] = value.astype(bf16)
 
 
 def advance(place, pairs, planes, after=(), steps=2):
-    blocks, *_, shard, half = (pairs + planes)[0].held[0].shape
-    shapes = [jax.ShapeDtypeStruct((blocks, 2, 2, shard, half), k) for k in (f32, bf16, f32, bf16)] * len(pairs)
+    blocks, *_, shard, wide = (pairs + planes)[0].held[0][0].shape
+    width = wide * len((pairs + planes)[0].axes)
+    shapes, places = [], []
+    for r in pairs:
+        shapes += [jax.ShapeDtypeStruct((blocks, 2, 2, shard, width // len(r.axes)), bf16)] * (2 * len(r.axes))
+    places += [0] * len(shapes)
     if planes:
-        shapes += [jax.ShapeDtypeStruct((len(planes), blocks, shard, 2 * half), bf16)] * 4
-    operands = [v for r in pairs + planes for v in r.held]
+        shapes += [jax.ShapeDtypeStruct((len(planes), blocks, shard, width), bf16)] * 4
+        places += [1] * 4
+    operands = [v for r in pairs + planes for held in r.held for v in held]
 
     def spec(s, at=0):
         n = len(s.shape)
@@ -629,11 +656,14 @@
 
     def body(place_ref, *refs):
         ins, outs = refs[: len(operands)], refs[len(operands) :]
-        for n in range(len(pairs)):
-            chip_pair_body(place_ref, *ins[4 * n : 4 * n + 4], *outs[4 * n : 4 * n + 4])
-        for n in range(len(planes)):
-            m = 4 * (len(pairs) + n)
-            plane_body(place_ref, *ins[m : m + 4], *[ref.at[n] for ref in outs[4 * len(pairs) :]])
+        for r in pairs:
+            count = 2 * len(r.axes)
+            pair_body(place_ref, r, ins[:count], outs[:count])
+            ins, outs = ins[count:], outs[count:]
+        for n, r in enumerate(planes):
+            count = 2 * len(r.axes)
+            plane_body(place_ref, r, ins[:count], [ref.at[n] for ref in outs])
+            ins = ins[count:]
 
     outs = call(
         body,
@@ -644,18 +674,19 @@
             num_scalar_prefetch=1,
             grid=(steps,),
             in_specs=[spec(v) for v in operands],
-            out_specs=[spec(s, n >= 4 * len(pairs)) for n, s in enumerate(shapes)],
+            out_specs=[spec(s, at) for s, at in zip(shapes, places)],
         ),
         out_shape=shapes,
     )(place, *operands)
-    for n, r in enumerate(pairs):
-        ka, sa, kb, sb = outs[4 * n : 4 * n + 4]
-        r.made = ka
-        r.held = (ka, over_y(sa), kb, over_x(sb))
+    for r in pairs:
+        count = 2 * len(r.axes)
+        r.second(outs[:count])
+        outs = outs[count:]
     terms = []
-    for m, v in enumerate(outs[4 * len(pairs) :]):
-        planes[0].made = v
-        v = v.reshape(-1, shard, 2 * half)
+    for m, v in enumerate(outs):
+        for r in planes:
+            r.made = v
+        v = v.reshape(-1, shard, width)
         terms.append(
             lax.ppermute(
                 v, AXES, to_place(lambda z, y, x, c, m=m: (2 * c + ((z ^ m) >> 1), y, x, (z ^ m) & 1))
@@ -724,29 +755,48 @@
     )(slots, *terms)
 
 
-def precondition_body(scale_ref, s_ref, l_ref, r_ref, p_ref, s_low, r_low):
+def to_low_body(l_ref, r_ref, l_low, r_low):
+    l_low[...] = l_ref[...].astype(bf16)
+    r_low[...] = r_ref[...].astype(bf16)
+
+
+def to_low(left, right, after=(), step=384):
+    width = left.shape[0]
+    rows = pl.BlockSpec((step, width), lambda i: (i, 0))
+    return call(
+        to_low_body,
+        0,
+        12 * width**2,
+        after=after,
+        grid=(width // step,),
+        in_specs=[rows, rows],
+        out_specs=[rows, rows],
+        out_shape=[jax.ShapeDtypeStruct((width, width), bf16)] * 2,
+    )(left, right)
+
+
+def precondition_body(scale_ref, s_ref, l_ref, r_ref, p_ref, s_low):
     @pl.when(pl.program_id(0) == 0)
     def _():
         s_low[...] = (s_ref[...].astype(f32) * scale_ref[0]).astype(bf16)
-        r_low[...] = r_ref[...].astype(bf16)
-
-    left = mm(l_ref[...].astype(bf16), s_low[...], NN)
-    p_ref[...] = (scale_ref[1] * mm(left.astype(bf16), r_low[...], NN)).astype(bf16)
-
-
-def precondition(scales, block, left, right, step=256):
+
+    left = mm(l_ref[...], s_low[...], NN)
+    p_ref[...] = (scale_ref[1] * mm(left.astype(bf16), r_ref[...], NN)).astype(bf16)
+
+
+def precondition(scales, block, left, right, step=384):
     width = block.shape[0]
     whole = pl.BlockSpec((width, width), lambda i: (0, 0))
     rows = pl.BlockSpec((step, width), lambda i: (i, 0))
     return call(
         precondition_body,
         4 * width**3,
-        12 * width**2,
+        8 * width**2,
         grid=(width // step,),
         in_specs=[pl.BlockSpec(memory_space=pltpu.SMEM), whole, rows, whole],
         out_specs=rows,
         out_shape=jax.ShapeDtypeStruct((width, width), bf16),
-        scratch_shapes=[pltpu.VMEM((width, width), bf16), pltpu.VMEM((width, width), bf16)],
+        scratch_shapes=[pltpu.VMEM((width, width), bf16)],
     )(scales, block, left, right)
 
 
@@ -881,30 +931,25 @@
         acts_pair, og_pair = (acts, over_c(acts)), (og, over_c(og))
         dys = (acts_pair, 2, 1)
         ed0, up_sum0 = hidden(0, half, acts, mlp_weights, vecs)
-        ed1, up_sum1 = hidden(half, half, acts, mlp_weights, vecs, after=(ed0, acts_pair[1]))
-        pairs = [(v, over_c(v)) for v in (ed0, ed1)]
-        attn = Reduction(
-            *half_grads(place, (acts_pair, 0, 1), (og_pair, 3, 1), (og_pair, 0, 3), dys, shard, after=(ed1,))
-        )
-        low = Reduction(
-            *half_grads(
-                place, (acts_pair, 1, 1), (pairs[0], 0, half), (pairs[0], half, half), dys, shard, after=(attn.made,)
-            )
-        )
-        advance(place, [attn], [], after=(low.made,))
-        high = Reduction(
-            *half_grads(
-                place, (acts_pair, 1, 1), (pairs[1], 0, half), (pairs[1], half, half), dys, shard, after=(attn.made,)
-            )
-        )
-        advance(place, [low], [], after=(high.made,))
+        ed0_pair = (ed0, over_c(ed0))
+
+        def grads(left, two, one, axes, after):
+            operands = ((acts_pair, left, 1), two, one, dys, shard, axes)
+            return Reduction(axes, half_grads(place, *operands, after=after))
+
+        attn = grads(0, (og_pair, 3, 1), (og_pair, 0, 3), "x", (ed0,))
+        low = grads(1, (ed0_pair, 0, half), (ed0_pair, half, half), "y", (attn.made,))
+        ed1, up_sum1 = hidden(half, half, acts, mlp_weights, vecs, after=(low.made,))
+        ed1_pair = (ed1, over_c(ed1))
+        part, one_sums = grad_one(flat_tokens, dy, (og, 0, 3), attn_weights, vecs, after=(ed1,))
+        advance(place, [attn, low], [], after=(part,))
+        high = grads(1, (ed1_pair, 0, half), (ed1_pair, half, half), "xy", (low.made,))
+        terms = [advance(place, [], [attn, low], after=(high.made,))]
         es, dus = [(v, 0, half) for v in (ed0, ed1)], [(v, half, half) for v in (ed0, ed1)]
-        out = output(flat_tokens, (og, 3, 1), es, attn_weights, mlp_weights, vecs, after=(low.made,))
-        terms = [advance(place, [high], [attn, low], after=(out,))]
-        part, one_sums = grad_one(flat_tokens, dy, (og, 0, 3), attn_weights, vecs, after=(high.made,))
-        terms.append(advance(place, [], [high], after=(part,)))
+        grad_in, two_sums = grad_two(flat_tokens, part, dus, mlp_weights, vecs, after=(low.made,))
+        advance(place, [high], [], after=(grad_in,))
+        terms.append(advance(place, [], [high]))
         orders = [orders[0] + orders[1], orders[2]]
-        grad_in, two_sums = grad_two(flat_tokens, part, dus, mlp_weights, vecs, after=(high.made,))
     else:
         ed0, up_sum0 = hidden(0, half, acts, mlp_weights, vecs)
         ed1, up_sum1 = hidden(half, half, acts, mlp_weights, vecs)
@@ -915,7 +960,6 @@
         ]
         terms = [[lax.psum_scatter(v, AXES, scatter_dimension=1, tiled=True)] for v in grads]
         es, dus = [(v, 0, half) for v in (ed0, ed1)], [(v, half, half) for v in (ed0, ed1)]
-        out = output(flat_tokens, (og, 3, 1), es, attn_weights, mlp_weights, vecs)
         part, one_sums = grad_one(flat_tokens, dy, (og, 0, 3), attn_weights, vecs)
         grad_in, two_sums = grad_two(flat_tokens, part, dus, mlp_weights, vecs)
     up_sums = [up_sum0, up_sum1]
@@ -932,6 +976,8 @@
     slots = jnp.sum(jnp.where(match, jnp.arange(1, owners.shape[0] + 1, dtype=jnp.int32)[None], 0), axis=1) - 1
     has_block = jnp.any(owners == my_index)
     shards, outgoing, squares = pack(slots, terms, orders, after=(grad_in,))
+    out = output(flat_tokens, (og, 3, 1), es, attn_weights, mlp_weights, vecs, after=(squares,))
+    left_low, right_low = to_low(root_left[0], root_right[0], after=(out,))
     local = jnp.concatenate([grad_vectors, jnp.sum(squares, axis=0)[None], jnp.zeros((2, width), f32)])
     total = everywhere(local) if paired else lax.psum(local, AXES)
     vector_sums = total[:vec_rows]
@@ -945,7 +991,7 @@
     power = jnp.exp2(jnp.floor(jnp.log2(jnp.maximum(scale, 1e-30)))).astype(bf16).astype(f32)
     scales = jnp.stack([power, scale / power])
     owned = to_all(outgoing).reshape(width, width)
-    precond = precondition(scales, owned, root_left[0], root_right[0])
+    precond = precondition(scales, owned, left_low, right_low)
     returned = to_all(precond.reshape(slot_count, shard, width))
     new_left, new_right = statistics(
         has_block.astype(jnp.int32).reshape(1), scales, owned, stat_left[0], stat_right[0]

time: 362 us -> 394 us (1.088)
  waiting for transfers between devices: 59.8 us -> 113 us
  starting transfers between devices: 61.7 us -> 52.7 us
  local copies, waits for them, and re-layouts: 21.6 us -> 16.7 us
  other arithmetic: 26.7 us -> 22.5 us
    ppermute x9, waiting for transfers between devices: 0.02 us -> 16.8 us  [over_c(): lax.ppermute(value, AXES, to_place(lambda z, y, x, c: (z, y, x, 1 - c)))]
    ppermute x8, waiting for transfers between devices: 3.17 us -> 18.9 us  [advance(): lax.ppermute(v, AXES, to_place(lambda z, y, x, c, m=m: (2 * c + ((z ^ m)...]
    ppermute x8 -> x6, waiting for transfers between devices: 1.9 us -> 14.7 us  [over_y(): lax.ppermute(value, AXES, to_place(lambda z, y, x, c: (z, 1 - y, x, c)))]
    ppermute x8 -> x6, waiting for transfers between devices: 14.4 us -> 23.9 us  [over_x(): lax.ppermute(value, AXES, to_place(lambda z, y, x, c: (z, y, 1 - x, c)))]
    unnamed x95 -> x87, local copies, waits for them, and re-layouts: 13.4 us -> 9.6 us
    ppermute x8 -> x6, starting transfers between devices: 8.47 us -> 5.12 us  [over_y(): lax.ppermute(value, AXES, to_place(lambda z, y, x, c: (z, 1 - y, x, c)))]
    pallas_call x19 -> x20, Pallas kernels: 172 us -> 169 us  [call(): return lambda *operands: made(*operands, *after)]
    ppermute x8 -> x6, starting transfers between devices: 9.57 us -> 7.63 us  [over_x(): lax.ppermute(value, AXES, to_place(lambda z, y, x, c: (z, y, 1 - x, c)))]
  transfers between devices with their start and end apart: 45 -> 41, of which waited for: 14 -> 16; matrix products, arithmetic and copies ran while one was open for 11% -> 7% of each run, Pallas kernels for 43% -> 33%
where the time goes in v3:
time: 394 us; the launch traced here: 393 us
  Pallas kernels  169 us (43%)
  waiting for transfers between devices  113 us (29%)
  starting transfers between devices  52.7 us (13%)
  other arithmetic  22.5 us (6%)
  between operations  18.1 us (5%)
  local copies, waits for them, and re-layouts  16.7 us (4%)
    pallas_call x20, Pallas kernels, call(): return lambda *operands: made(*operands, *after)  169 us
    ppermute x6, waiting for transfers between devices, over_x(): lax.ppermute(value, AXES, to_place(lambda z, y, x, c: (z, y, 1 - x, c)))  23.9 us
    all_to_all x3, waiting for transfers between devices, to_all(): return lax.all_to_all(value, AXES, split_axis=0, concat_axis=0, tiled=True)  19.9 us
    ppermute x5, waiting for transfers between devices, everywhere(): value = value + lax.ppermute(value, AXES, to_place(move))  19.2 us
    ppermute x8, waiting for transfers between devices, advance(): lax.ppermute(v, AXES, to_place(lambda z, y, x, c, m=m: (2 * c + ((z ^ m)...  18.9 us
    ppermute x9, waiting for transfers between devices, over_c(): lax.ppermute(value, AXES, to_place(lambda z, y, x, c: (z, y, x, 1 - c)))  16.8 us
    ppermute x8, starting transfers between devices, advance(): lax.ppermute(v, AXES, to_place(lambda z, y, x, c, m=m: (2 * c + ((z ^ m)...  16.1 us
    ppermute x6, waiting for transfers between devices, over_y(): lax.ppermute(value, AXES, to_place(lambda z, y, x, c: (z, 1 - y, x, c)))  14.7 us
  transfers between devices with their start and end apart: 41, of which 16 were waited for; matrix products, arithmetic and copies ran while one was open for 7% of the time, Pallas kernels for 33%

profile of v3, /device:TPU:0, one launch (start us, length us, event | category | flops | bytes accessed | tf_op | source)
XLA Modules:
  0.0 392.6 jit_solution(8566870125882202507)
XLA Ops:
  9.4 4.1 %collective-permute-start.1 = (bf16[4,24,768]{2,1,0:T(8,128)(2,1)S(1)}, bf16[4,24,768]{2,1,0:T(8,128)(2,1)S(1)}, u32[]{:S(2)}, u32[]{:S(2)}) collective-permute-start(bf16[4,24,768]{2,1,0:T(8,128)(2,1)S(1)} %get-tuple-element.117), channel_id=1, source_target_pairs={{0,16},{1,17},{2,18},{3,19},{4,20},{5,21},{6,22},{7,23},{8,24},{9,... | collective-permute-start | bytes 442376 | tf_op jit(solution)/shard_map/ppermute | solution.py:547
  23.3 5.2 %compare_select_fusion.9 = f32[128]{0:T(128)S(1)} fusion(f32[]{:T(128)} %bitcast.16, f32[]{:T(128)} %bitcast.17, f32[]{:T(128)} %bitcast.18, f32[]{:T(128)} %bitcast.19, f32[]{:T(128)} %bitcast.20, f32[]{:T(128)} %bitcast.22, f32[]{:T(128)} %bitcast.21, f32[]{:T(128)} %bitcast.15), kind=kLoop, calls=%fused_computation.41 | loop fusion | flops 5376 | bytes 544 | tf_op jit(solution)/shard_map/jit(_where)/select_n | solution.py:90
  43.8 9.8 %collective-permute-done.4.refs_3_ = bf16[4,4,24,768]{3,2,1,0:T(8,128)(2,1)} collective-permute-done((bf16[4,4,24,768]{3,2,1,0:T(8,128)(2,1)}, bf16[4,4,24,768]{3,2,1,0:T(8,128)(2,1)}, u32[]{:S(2)}, u32[]{:S(2)}) %collective-permute-start.4) | collective-permute-done | bytes 589856 | tf_op jit(solution)/shard_map/ppermute | solution.py:543
  62.0 3.4 collective-permute-done.6.refs_5_
  70.6 6.5 %shard_map.202 = bf16[4,32,24,768]{3,2,1,0:T(8,128)(2,1)} custom-call(s32[4]{0:T(128)} %pad_add_fusion.refs_0_.place_ref, bf16[4,4,24,768]{3,2,1,0:T(8,128)(2,1)} %pad_maximum_fusion.1.refs_1_, bf16[4,4,24,768]{3,2,1,0:T(8,128)(2,1)} %collective-permute-done.3.refs_2_, bf16[4,4,24,768]{3,2,1,0:T(8,128)(2,1)} %collective-permute-done.4.refs_3_, ...), custom_call_target="tpu_custom_call" | custom-call | bytes 9437184 | tf_op jit(solution)/shard_map/pallas_call | solution.py:74
  77.1 9.8 %shard_map.203 = (bf16[1024,768]{1,0:T(8,128)(2,1)}, bf16[1024,768]{1,0:T(8,128)(2,1)}, bf16[1024,768]{1,0:T(8,128)(2,1)}, bf16[1024,768]{1,0:T(8,128)(2,1)}) custom-call(bf16[3,1024,768]{2,1,0:T(8,128)(2,1)} %pad_maximum_fusion.refs_14_.a1_ref.dy_ref.acts_ref, bf16[3,1024,768]{2,1,0:T(8,128)(2,1)} %pad_maximum_fusion.refs_14_.a1_ref.dy_ref.acts_ref, ...), custom_call_target="tpu_custom_call" | custom-call | flops 4831838208 | bytes 14155776 | tf_op jit(solution)/shard_map/pallas_call | solution.py:74
  86.9 25.6 %shard_map.204 = (bf16[4,1024,768]{2,1,0:T(8,128)(2,1)}, f32[3,16,768]{2,1,0:T(8,128)}, bf16[3,1024,768]{2,1,0:T(8,128)(2,1)}) custom-call(bf16[3,1024,768]{2,1,0:T(8,128)(2,1)} %pad_maximum_fusion.refs_14_.a1_ref.dy_ref.acts_ref, s32[1024,1]{1,0:T(8,128)} %bitcast.109, s32[2,1,512]{2,1,0:T(1,128)} %reshape.482.row_ref, ...), custom_call_target="tpu_custom_call", output_to_operand_aliasing={{2}: (0, {})} | custom-call | flops 9663676416 | bytes 18874368 | tf_op jit(solution)/shard_map/pallas_call | solution.py:74
  112.9 12.6 %shard_map.205 = (bf16[2,2,1024,768]{3,2,1,0:T(8,128)(2,1)}, f32[2,8,768]{2,1,0:T(8,128)}) custom-call(bf16[3,1024,768]{2,1,0:T(8,128)(2,1)} %get-tuple-element.66.a2_ref.dy_ref.refs_1_.refs_7_.refs_0_, bf16[3,1024,768]{2,1,0:T(8,128)(2,1)} %get-tuple-element.66.a2_ref.dy_ref.refs_1_.refs_7_.refs_0_, ...), custom_call_target="tpu_custom_call" | custom-call | flops 4831838208 | bytes 17301504 | tf_op jit(solution)/shard_map/pallas_call | solution.py:74
  126.0 16.7 %collective-permute-done.12.refs_2_.refs_8_ = bf16[3,1024,768]{2,1,0:T(8,128)(2,1)} collective-permute-done((bf16[3,1024,768]{2,1,0:T(8,128)(2,1)}, bf16[3,1024,768]{2,1,0:T(8,128)(2,1)}, u32[]{:S(2)}, u32[]{:S(2)}) %collective-permute-start.12) | collective-permute-done | bytes 4718624 | tf_op jit(solution)/shard_map/ppermute | solution.py:535
  142.7 11.4 %shard_map.206 = (bf16[4,2,2,2,24,768]{5,4,3,2,1,0:T(8,128)(2,1)}, bf16[4,2,2,2,24,768]{5,4,3,2,1,0:T(8,128)(2,1)}) custom-call(s32[4]{0:T(128)} %pad_add_fusion.refs_0_.place_ref, bf16[3,1024,768]{2,1,0:T(8,128)(2,1)} %get-tuple-element.66.a2_ref.dy_ref.refs_1_.refs_7_.refs_0_, bf16[3,1024,768]{2,1,0:T(8,128)(2,1)} %collective-permute-done.12.refs_2_.refs_8_, ...), custom_call_target="tpu_custom_call" | custom-call | flops 4831838208 | bytes 12582912 | tf_op jit(solution)/shard_map/pallas_call | solution.py:74
  154.2 11.2 %shard_map.207 = (bf16[4,2,2,2,24,768]{5,4,3,2,1,0:T(8,128)(2,1)}, bf16[4,2,2,2,24,768]{5,4,3,2,1,0:T(8,128)(2,1)}) custom-call(s32[4]{0:T(128)} %pad_add_fusion.refs_0_.place_ref, bf16[3,1024,768]{2,1,0:T(8,128)(2,1)} %get-tuple-element.66.a2_ref.dy_ref.refs_1_.refs_7_.refs_0_, bf16[3,1024,768]{2,1,0:T(8,128)(2,1)} %collective-permute-done.12.refs_2_.refs_8_, ...), custom_call_target="tpu_custom_call" | custom-call | flops 4831838208 | bytes 12582912 | tf_op jit(solution)/shard_map/pallas_call | solution.py:74
  165.3 12.9 %shard_map.208 = (bf16[2,2,1024,768]{3,2,1,0:T(8,128)(2,1)}, f32[2,8,768]{2,1,0:T(8,128)}) custom-call(bf16[3,1024,768]{2,1,0:T(8,128)(2,1)} %get-tuple-element.66.a2_ref.dy_ref.refs_1_.refs_7_.refs_0_, bf16[3,1024,768]{2,1,0:T(8,128)(2,1)} %get-tuple-element.66.a2_ref.dy_ref.refs_1_.refs_7_.refs_0_, ...), custom_call_target="tpu_custom_call" | custom-call | flops 4831838208 | bytes 17301504 | tf_op jit(solution)/shard_map/pallas_call | solution.py:74
  180.6 9.8 %shard_map.209 = (f32[1024,768]{1,0:T(8,128)}, f32[3,8,768]{2,1,0:T(8,128)}) custom-call(bf16[1024,768]{1,0:T(8,128)(2,1)} %bitcast.93, bf16[1024,768]{1,0:T(8,128)(2,1)} %bitcast.100, bf16[4,1024,768]{2,1,0:T(8,128)(2,1)} %get-tuple-element.65.refs_3_.refs_5_.refs_2_.refs_1_, bf16[4,768,768]{2,1,0:T(8,128)(2,1)} %bitcast.97, ...), custom_call_target="tpu_custom_call" | custom-call | flops 3623878656 | bytes 14548992 | tf_op jit(solution)/shard_map/pallas_call | solution.py:74
  190.4 16.6 %collective-permute-done.15.refs_2_ = bf16[4,2,2,2,24,768]{5,4,3,2,1,0:T(8,128)(2,1)S(1)} collective-permute-done((bf16[4,2,2,2,24,768]{5,4,3,2,1,0:T(8,128)(2,1)S(1)}, bf16[4,2,2,2,24,768]{5,4,3,2,1,0:T(8,128)(2,1)S(1)}, u32[]{:S(2)}, u32[]{:S(2)}) %collective-permute-start.15) | collective-permute-done | bytes 1179680 | tf_op jit(solution)/shard_map/ppermute | solution.py:539
  209.7 4.1 %shard_map.210 = (bf16[4,2,2,24,768]{4,3,2,1,0:T(8,128)(2,1)}, bf16[4,2,2,24,768]{4,3,2,1,0:T(8,128)(2,1)}, bf16[4,2,2,24,768]{4,3,2,1,0:T(8,128)(2,1)}, bf16[4,2,2,24,768]{4,3,2,1,0:T(8,128)(2,1)}) custom-call(s32[4]{0:T(128)} %pad_add_fusion.refs_0_.place_ref, bf16[4,2,2,2,24,768]{5,4,3,2,1,0:T(8,128)(2,1)} %get-tuple-element.68.refs_9_.refs_1_, ...), custom_call_target="tpu_custom_call" | custom-call | bytes 9437184 | tf_op jit(solution)/shard_map/pallas_call | solution.py:74
  214.4 11.2 %shard_map.211 = (bf16[4,2,2,2,24,384]{5,4,3,2,1,0:T(8,128)(2,1)}, bf16[4,2,2,2,24,384]{5,4,3,2,1,0:T(8,128)(2,1)}, bf16[4,2,2,2,24,384]{5,4,3,2,1,0:T(8,128)(2,1)}, bf16[4,2,2,2,24,384]{5,4,3,2,1,0:T(8,128)(2,1)}) custom-call(s32[4]{0:T(128)} %pad_add_fusion.refs_0_.place_ref, bf16[3,1024,768]{2,1,0:T(8,128)(2,1)} %get-tuple-element.66.a2_ref.dy_ref.refs_1_.refs_7_.refs_0_, ...), custom_call_target="tpu_custom_call" | custom-call | flops 4831838208 | bytes 12582912 | tf_op jit(solution)/shard_map/pallas_call | solution.py:74
  233.8 11.0 %shard_map.213 = (bf16[1024,768]{1,0:T(8,128)(2,1)}, f32[2,8,768]{2,1,0:T(8,128)}) custom-call(bf16[1024,768]{1,0:T(8,128)(2,1)} %bitcast.94, f32[1024,768]{1,0:T(8,128)} %get-tuple-element.73.refs_5_.refs_1_, bf16[4,1024,768]{2,1,0:T(8,128)(2,1)} %bitcast.85, bf16[4,1024,768]{2,1,0:T(8,128)(2,1)} %bitcast.91, ...), custom_call_target="tpu_custom_call" | custom-call | flops 4831838208 | bytes 17301504 | tf_op jit(solution)/shard_map/pallas_call | solution.py:74
  251.2 3.3 collective-permute-start.22
  265.1 4.6 %collective-permute-start.30 = (bf16[4,24,768]{2,1,0:T(8,128)(2,1)}, bf16[4,24,768]{2,1,0:T(8,128)(2,1)S(1)}, u32[]{:S(2)}, u32[]{:S(2)}) collective-permute-start(bf16[4,24,768]{2,1,0:T(8,128)(2,1)} %bitcast.126), channel_id=1, source_target_pairs={{0,8},{1,24},{2,10},{3,26},{4,12},{5,28},{6,14},{7,30},{8,9},{9,25... | collective-permute-start | bytes 442376 | tf_op jit(solution)/shard_map/ppermute | solution.py:691
  269.7 11.9 %collective-permute-done.22.refs_3_ = bf16[8,24,768]{2,1,0:T(8,128)(2,1)S(1)} collective-permute-done((bf16[8,24,768]{2,1,0:T(8,128)(2,1)S(1)}, bf16[8,24,768]{2,1,0:T(8,128)(2,1)S(1)}, u32[]{:S(2)}, u32[]{:S(2)}) %collective-permute-start.22) | collective-permute-done | bytes 294944 | tf_op jit(solution)/shard_map/ppermute | solution.py:691
  284.1 7.0 %collective-permute-done.30.refs_7_ = bf16[4,24,768]{2,1,0:T(8,128)(2,1)S(1)} collective-permute-done((bf16[4,24,768]{2,1,0:T(8,128)(2,1)}, bf16[4,24,768]{2,1,0:T(8,128)(2,1)S(1)}, u32[]{:S(2)}, u32[]{:S(2)}) %collective-permute-start.30) | collective-permute-done | bytes 147488 | tf_op jit(solution)/shard_map/ppermute | solution.py:691
  292.4 3.7 shard_map.216
  302.7 8.2 %collective-permute-done.33 = f32[16,768]{1,0:T(8,128)S(1)} collective-permute-done((f32[16,768]{1,0:T(8,128)S(1)}, f32[16,768]{1,0:T(8,128)S(1)}, u32[]{:S(2)}, u32[]{:S(2)}) %collective-permute-start.33) | collective-permute-done | bytes 49184 | tf_op jit(solution)/shard_map/ppermute | solution.py:706
  311.0 4.3 %collective-permute-done.34 = f32[16,768]{1,0:T(8,128)S(1)} collective-permute-done((f32[16,768]{1,0:T(8,128)S(1)}, f32[16,768]{1,0:T(8,128)S(1)}, u32[]{:S(2)}, u32[]{:S(2)}) %collective-permute-start.34) | collective-permute-done | bytes 49184 | tf_op jit(solution)/shard_map/ppermute | solution.py:706
  315.4 5.8 %collective-permute-done.35 = f32[16,768]{1,0:T(8,128)S(1)} collective-permute-done((f32[16,768]{1,0:T(8,128)S(1)}, f32[16,768]{1,0:T(8,128)S(1)}, u32[]{:S(2)}, u32[]{:S(2)}) %collective-permute-start.35) | collective-permute-done | bytes 49184 | tf_op jit(solution)/shard_map/ppermute | solution.py:706
  323.3 11.0 %shard_map.217.refs_2_ = bf16[1024,768]{1,0:T(8,128)(2,1)} custom-call(bf16[1024,768]{1,0:T(8,128)(2,1)} %bitcast.95, bf16[4,1024,768]{2,1,0:T(8,128)(2,1)} %get-tuple-element.65.refs_3_.refs_5_.refs_2_.refs_1_, bf16[4,1024,768]{2,1,0:T(8,128)(2,1)} %bitcast.86, bf16[4,1024,768]{2,1,0:T(8,128)(2,1)} %bitcast.92, bf16[4,768,768]{2,1,0:T(8,128)(2,1)} %bitcast.98, ...), custom_call_target="tpu_custom_call" | custom-call | flops 6039797760 | bytes 16908288 | tf_op jit(solution)/shard_map/pallas_call | solution.py:74
  334.3 3.5 shard_map.218
  342.2 5.3 %shard_map.219 = bf16[768,768]{1,0:T(8,128)(2,1)} custom-call(f32[2]{0:T(128)} %pad_maximum_fusion.2.scale_ref, bf16[768,768]{1,0:T(8,128)(2,1)} %bitcast.106, bf16[768,768]{1,0:T(8,128)(2,1)} %get-tuple-element.102.l_ref, bf16[768,768]{1,0:T(8,128)(2,1)} %get-tuple-element.103.r_ref), custom_call_target="tpu_custom_call" | custom-call | flops 1811939328 | bytes 4718592 | tf_op jit(solution)/shard_map/pallas_call | solution.py:74
  347.5 3.8 all-to-all-start.2
  353.3 7.2 %shard_map.221 = (f32[768,768]{1,0:T(8,128)}, f32[768,768]{1,0:T(8,128)}) custom-call(s32[1]{0:T(128)} %bitcast.45.has_ref, f32[2]{0:T(128)} %pad_maximum_fusion.2.scale_ref, bf16[768,768]{1,0:T(8,128)(2,1)} %bitcast.107, f32[768,768]{1,0:T(8,128)} %bitcast.120, f32[768,768]{1,0:T(8,128)} %bitcast.121), custom_call_target="tpu_custom_call" | custom-call | flops 1811939328 | bytes 10616832 | tf_op jit(solution)/shard_map/pallas_call | solution.py:74
  360.4 19.9 %all-to-all-done.2.p_ref = bf16[32,24,768]{2,1,0:T(8,128)(2,1)S(1)} async-done(((bf16[32,24,768]{2,1,0:T(8,128)(2,1)}), bf16[32,24,768]{2,1,0:T(8,128)(2,1)S(1)}, u32[]{:S(2)}, u32[]{:S(2)}) %all-to-all-start.2) | async-done | bytes 1179680 | tf_op jit(solution)/shard_map/all_to_all | solution.py:876
  381.4 3.3 shard_map.220
  (222 shorter events, 89.8 us)
Async XLA Ops:
  7.2 105.7 %all-gather.2.cloned.1.call-start = ((), (), s32[]{:S(2)}) async-start(), calls=%async_computation.3 | async-start | bytes 9732096 | tf_op jit(solution)/shard_map/all_gather | solution.py:906
  9.4 23.3 %collective-permute-start.1 = (bf16[4,24,768]{2,1,0:T(8,128)(2,1)S(1)}, bf16[4,24,768]{2,1,0:T(8,128)(2,1)S(1)}, u32[]{:S(2)}, u32[]{:S(2)}) collective-permute-start(bf16[4,24,768]{2,1,0:T(8,128)(2,1)S(1)} %get-tuple-element.117), channel_id=1, source_target_pairs={{0,16},{1,17},{2,18},{3,19},{4,20},{5,21},{6,22},{7,23},{8,24},{9,... | collective-permute-start | bytes 442376 | tf_op jit(solution)/shard_map/ppermute | solution.py:547
  13.5 19.2 %collective-permute-start = (bf16[4,24,768]{2,1,0:T(8,128)(2,1)S(1)}, bf16[4,24,768]{2,1,0:T(8,128)(2,1)S(1)}, u32[]{:S(2)}, u32[]{:S(2)}) collective-permute-start(bf16[4,24,768]{2,1,0:T(8,128)(2,1)S(1)} %get-tuple-element.117), channel_id=1, source_target_pairs={{0,8},{1,9},{2,10},{3,11},{4,12},{5,13},{6,14},{7,15},{8,16},{9,17... | collective-permute-start | bytes 442376 | tf_op jit(solution)/shard_map/ppermute | solution.py:547
  15.1 17.6 %collective-permute-start.2 = (bf16[4,24,768]{2,1,0:T(8,128)(2,1)S(1)}, bf16[4,24,768]{2,1,0:T(8,128)(2,1)S(1)}, u32[]{:S(2)}, u32[]{:S(2)}) collective-permute-start(bf16[4,24,768]{2,1,0:T(8,128)(2,1)S(1)} %get-tuple-element.117), channel_id=1, source_target_pairs={{0,24},{1,25},{2,26},{3,27},{4,28},{5,29},{6,30},{7,31},{8,0},{9,1... | collective-permute-start | bytes 442376 | tf_op jit(solution)/shard_map/ppermute | solution.py:547
  19.4 21.6 %all-to-all-start = ((bf16[32,2,156]{2,1,0:T(2,128)(2,1)}), bf16[32,2,156]{2,1,0:T(2,128)(2,1)S(1)}, u32[]{:S(2)}, u32[]{:S(2)}) async-start(bf16[32,2,156]{2,1,0:T(2,128)(2,1)} %reshape.554), calls=%async_computation | async-start | bytes 65536 | tf_op jit(solution)/shard_map/all_to_all | solution.py:876
  33.6 20.0 %collective-permute-start.4 = (bf16[4,4,24,768]{3,2,1,0:T(8,128)(2,1)}, bf16[4,4,24,768]{3,2,1,0:T(8,128)(2,1)}, u32[]{:S(2)}, u32[]{:S(2)}) collective-permute-start(bf16[4,4,24,768]{3,2,1,0:T(8,128)(2,1)} %pad_maximum_fusion.1.refs_1_), channel_id=1, source_target_pairs={{0,4},{1,5},{2,6},{3,7},{4,0},{5,1},{6,2},{7,3},{8,12},{9,13},{10,... | collective-permute-start | bytes 1769480 | tf_op jit(solution)/shard_map/ppermute | solution.py:543
  35.3 24.1 %collective-permute-start.3 = (bf16[4,4,24,768]{3,2,1,0:T(8,128)(2,1)}, bf16[4,4,24,768]{3,2,1,0:T(8,128)(2,1)}, u32[]{:S(2)}, u32[]{:S(2)}) collective-permute-start(bf16[4,4,24,768]{3,2,1,0:T(8,128)(2,1)} %pad_maximum_fusion.1.refs_1_), channel_id=1, source_target_pairs={{0,2},{1,3},{2,0},{3,1},{4,6},{5,7},{6,4},{7,5},{8,10},{9,11},{10,... | collective-permute-start | bytes 1769480 | tf_op jit(solution)/shard_map/ppermute | solution.py:539
  43.7 26.0 %collective-permute-start.7 = (bf16[4,4,24,768]{3,2,1,0:T(8,128)(2,1)}, bf16[4,4,24,768]{3,2,1,0:T(8,128)(2,1)}, u32[]{:S(2)}, u32[]{:S(2)}) collective-permute-start(bf16[4,4,24,768]{3,2,1,0:T(8,128)(2,1)} %pad_maximum_fusion.1.refs_1_), channel_id=1, source_target_pairs={{0,1},{1,0},{2,3},{3,2},{4,5},{5,4},{6,7},{7,6},{8,9},{9,8},{10,11... | collective-permute-start | bytes 1769480 | tf_op jit(solution)/shard_map/ppermute | solution.py:535
  54.6 10.8 %collective-permute-start.6 = (bf16[2,4,24,768]{3,2,1,0:T(8,128)(2,1)S(1)}, bf16[2,4,24,768]{3,2,1,0:T(8,128)(2,1)S(1)}, u32[]{:S(2)}, u32[]{:S(2)}) collective-permute-start(bf16[2,4,24,768]{3,2,1,0:T(8,128)(2,1)S(1)} %slice.67), channel_id=1, source_target_pairs={{0,2},{1,3},{2,0},{3,1},{4,6},{5,7},{6,4},{7,5},{8,10},{9,11},{10,... | collective-permute-start | bytes 884744 | tf_op jit(solution)/shard_map/ppermute | solution.py:539
  60.5 9.2 %collective-permute-start.9 = (bf16[4,4,24,768]{3,2,1,0:T(8,128)(2,1)}, bf16[4,4,24,768]{3,2,1,0:T(8,128)(2,1)}, u32[]{:S(2)}, u32[]{:S(2)}) collective-permute-start(bf16[4,4,24,768]{3,2,1,0:T(8,128)(2,1)} %collective-permute-done.4.refs_3_), channel_id=1, source_target_pairs={{0,1},{1,0},{2,3},{3,2},{4,5},{5,4},{6,7},{7,6},{8,9},{9,8},{10,11... | collective-permute-start | bytes 1769480 | tf_op jit(solution)/shard_map/ppermute | solution.py:535
  112.6 30.2 %collective-permute-start.14 = (bf16[4,1024,768]{2,1,0:T(8,128)(2,1)}, bf16[4,1024,768]{2,1,0:T(8,128)(2,1)}, u32[]{:S(2)}, u32[]{:S(2)}) collective-permute-start(bf16[4,1024,768]{2,1,0:T(8,128)(2,1)} %get-tuple-element.65.refs_3_.refs_5_.refs_2_.refs_1_), channel_id=1, source_target_pairs={{0,1},{1,0},{2,3},{3,2},{4,5},{5,4},{6,7},{7,6},{8,9},{9,8},{10,11... | collective-permute-start | bytes 18874376 | tf_op jit(solution)/shard_map/ppermute | solution.py:535
  125.5 28.7 %collective-permute-start.13 = (bf16[4,1024,768]{2,1,0:T(8,128)(2,1)}, bf16[4,1024,768]{2,1,0:T(8,128)(2,1)}, u32[]{:S(2)}, u32[]{:S(2)}) collective-permute-start(bf16[4,1024,768]{2,1,0:T(8,128)(2,1)} %bitcast.81), channel_id=1, source_target_pairs={{0,1},{1,0},{2,3},{3,2},{4,5},{5,4},{6,7},{7,6},{8,9},{9,8},{10,11... | collective-permute-start | bytes 18874376 | tf_op jit(solution)/shard_map/ppermute | solution.py:535
  125.7 17.0 %collective-permute-start.12 = (bf16[3,1024,768]{2,1,0:T(8,128)(2,1)}, bf16[3,1024,768]{2,1,0:T(8,128)(2,1)}, u32[]{:S(2)}, u32[]{:S(2)}) collective-permute-start(bf16[3,1024,768]{2,1,0:T(8,128)(2,1)} %get-tuple-element.66.a2_ref.dy_ref.refs_1_.refs_7_.refs_0_), channel_id=1, source_target_pairs={{0,1},{1,0},{2,3},{3,2},{4,5},{5,4},{6,7},{7,6},{8,9},{9,8},{10,11... | collective-permute-start | bytes 14155784 | tf_op jit(solution)/shard_map/ppermute | solution.py:535
  178.3 36.1 %collective-permute-start.19 = (bf16[4,1024,768]{2,1,0:T(8,128)(2,1)}, bf16[4,1024,768]{2,1,0:T(8,128)(2,1)}, u32[]{:S(2)}, u32[]{:S(2)}) collective-permute-start(bf16[4,1024,768]{2,1,0:T(8,128)(2,1)} %bitcast.87), channel_id=1, source_target_pairs={{0,1},{1,0},{2,3},{3,2},{4,5},{5,4},{6,7},{7,6},{8,9},{9,8},{10,11... | collective-permute-start | bytes 18874376 | tf_op jit(solution)/shard_map/ppermute | solution.py:535
  178.5 28.5 %collective-permute-start.15 = (bf16[4,2,2,2,24,768]{5,4,3,2,1,0:T(8,128)(2,1)S(1)}, bf16[4,2,2,2,24,768]{5,4,3,2,1,0:T(8,128)(2,1)S(1)}, u32[]{:S(2)}, u32[]{:S(2)}) collective-permute-start(bf16[4,2,2,2,24,768]{5,4,3,2,1,0:T(8,128)(2,1)S(1)} %copy-done.36), channel_id=1, source_target_pairs={{0,2},{1,3},{2,0},{3,1},{4,6},{5,7},{6,4},{7,5},{8,10},{9,11},{10,... | collective-permute-start | bytes 3538952 | tf_op jit(solution)/shard_map/ppermute | solution.py:539
  180.6 28.1 %collective-permute-start.16 = (bf16[4,2,2,2,24,768]{5,4,3,2,1,0:T(8,128)(2,1)}, bf16[4,2,2,2,24,768]{5,4,3,2,1,0:T(8,128)(2,1)S(1)}, u32[]{:S(2)}, u32[]{:S(2)}) collective-permute-start(bf16[4,2,2,2,24,768]{5,4,3,2,1,0:T(8,128)(2,1)} %get-tuple-element.72), channel_id=1, source_target_pairs={{0,4},{1,5},{2,6},{3,7},{4,0},{5,1},{6,2},{7,3},{8,12},{9,13},{10,... | collective-permute-start | bytes 3538952 | tf_op jit(solution)/shard_map/ppermute | solution.py:543
  213.8 15.3 %collective-permute-start.17 = (bf16[4,2,2,24,768]{4,3,2,1,0:T(8,128)(2,1)}, bf16[4,2,2,24,768]{4,3,2,1,0:T(8,128)(2,1)S(1)}, u32[]{:S(2)}, u32[]{:S(2)}) collective-permute-start(bf16[4,2,2,24,768]{4,3,2,1,0:T(8,128)(2,1)} %get-tuple-element.75), channel_id=1, source_target_pairs={{0,4},{1,5},{2,6},{3,7},{4,0},{5,1},{6,2},{7,3},{8,12},{9,13},{10,... | collective-permute-start | bytes 1769480 | tf_op jit(solution)/shard_map/ppermute | solution.py:543
  214.1 15.6 %collective-permute-start.18 = (bf16[4,2,2,24,768]{4,3,2,1,0:T(8,128)(2,1)}, bf16[4,2,2,24,768]{4,3,2,1,0:T(8,128)(2,1)S(1)}, u32[]{:S(2)}, u32[]{:S(2)}) collective-permute-start(bf16[4,2,2,24,768]{4,3,2,1,0:T(8,128)(2,1)} %get-tuple-element.77), channel_id=1, source_target_pairs={{0,2},{1,3},{2,0},{3,1},{4,6},{5,7},{6,4},{7,5},{8,10},{9,11},{10,... | collective-permute-start | bytes 1769480 | tf_op jit(solution)/shard_map/ppermute | solution.py:539
  225.6 19.2 %collective-permute-start.24 = (bf16[4,2,2,2,24,384]{5,4,3,2,1,0:T(8,128)(2,1)}, bf16[4,2,2,2,24,384]{5,4,3,2,1,0:T(8,128)(2,1)S(1)}, u32[]{:S(2)}, u32[]{:S(2)}) collective-permute-start(bf16[4,2,2,2,24,384]{5,4,3,2,1,0:T(8,128)(2,1)} %get-tuple-element.83), channel_id=1, source_target_pairs={{0,2},{1,3},{2,0},{3,1},{4,6},{5,7},{6,4},{7,5},{8,10},{9,11},{10,... | collective-permute-start | bytes 1769480 | tf_op jit(solution)/shard_map/ppermute | solution.py:539
  227.3 17.5 %collective-permute-start.25 = (bf16[4,2,2,2,24,384]{5,4,3,2,1,0:T(8,128)(2,1)}, bf16[4,2,2,2,24,384]{5,4,3,2,1,0:T(8,128)(2,1)S(1)}, u32[]{:S(2)}, u32[]{:S(2)}) collective-permute-start(bf16[4,2,2,2,24,384]{5,4,3,2,1,0:T(8,128)(2,1)} %get-tuple-element.85), channel_id=1, source_target_pairs={{0,4},{1,5},{2,6},{3,7},{4,0},{5,1},{6,2},{7,3},{8,12},{9,13},{10,... | collective-permute-start | bytes 1769480 | tf_op jit(solution)/shard_map/ppermute | solution.py:543
  250.5 13.0 %collective-permute-start.21 = (bf16[8,24,768]{2,1,0:T(8,128)(2,1)S(1)}, bf16[8,24,768]{2,1,0:T(8,128)(2,1)S(1)}, u32[]{:S(2)}, u32[]{:S(2)}) collective-permute-start(bf16[8,24,768]{2,1,0:T(8,128)(2,1)S(1)} %bitcast.124), channel_id=1, source_target_pairs={{0,1},{1,17},{2,3},{3,19},{4,5},{5,21},{6,7},{7,23},{8,0},{9,16},{... | collective-permute-start | bytes 884744 | tf_op jit(solution)/shard_map/ppermute | solution.py:691
  250.5 14.6 %collective-permute-start.20 = (bf16[8,24,768]{2,1,0:T(8,128)(2,1)S(1)}, bf16[8,24,768]{2,1,0:T(8,128)(2,1)S(1)}, u32[]{:S(2)}, u32[]{:S(2)}) collective-permute-start(bf16[8,24,768]{2,1,0:T(8,128)(2,1)S(1)} %bitcast.123), channel_id=1, source_target_pairs={{0,0},{1,16},{2,2},{3,18},{4,4},{5,20},{6,6},{7,22},{8,1},{9,17},{... | collective-permute-start | bytes 884744 | tf_op jit(solution)/shard_map/ppermute | solution.py:691
  251.2 30.4 %collective-permute-start.22 = (bf16[8,24,768]{2,1,0:T(8,128)(2,1)S(1)}, bf16[8,24,768]{2,1,0:T(8,128)(2,1)S(1)}, u32[]{:S(2)}, u32[]{:S(2)}) collective-permute-start(bf16[8,24,768]{2,1,0:T(8,128)(2,1)S(1)} %bitcast.122), channel_id=1, source_target_pairs={{0,8},{1,24},{2,10},{3,26},{4,12},{5,28},{6,14},{7,30},{8,9},{9,25... | collective-permute-start | bytes 884744 | tf_op jit(solution)/shard_map/ppermute | solution.py:691
  255.9 28.2 %collective-permute-start.23 = (bf16[8,24,768]{2,1,0:T(8,128)(2,1)S(1)}, bf16[8,24,768]{2,1,0:T(8,128)(2,1)S(1)}, u32[]{:S(2)}, u32[]{:S(2)}) collective-permute-start(bf16[8,24,768]{2,1,0:T(8,128)(2,1)S(1)} %bitcast.111), channel_id=1, source_target_pairs={{0,9},{1,25},{2,11},{3,27},{4,13},{5,29},{6,15},{7,31},{8,8},{9,24... | collective-permute-start | bytes 884744 | tf_op jit(solution)/shard_map/ppermute | solution.py:691
  261.4 22.7 %collective-permute-start.29 = (bf16[4,24,768]{2,1,0:T(8,128)(2,1)}, bf16[4,24,768]{2,1,0:T(8,128)(2,1)S(1)}, u32[]{:S(2)}, u32[]{:S(2)}) collective-permute-start(bf16[4,24,768]{2,1,0:T(8,128)(2,1)} %bitcast.128), channel_id=1, source_target_pairs={{0,1},{1,17},{2,3},{3,19},{4,5},{5,21},{6,7},{7,23},{8,0},{9,16},{... | collective-permute-start | bytes 442376 | tf_op jit(solution)/shard_map/ppermute | solution.py:691
  263.6 20.6 %collective-permute-start.28 = (bf16[4,24,768]{2,1,0:T(8,128)(2,1)}, bf16[4,24,768]{2,1,0:T(8,128)(2,1)S(1)}, u32[]{:S(2)}, u32[]{:S(2)}) collective-permute-start(bf16[4,24,768]{2,1,0:T(8,128)(2,1)} %bitcast.127), channel_id=1, source_target_pairs={{0,0},{1,16},{2,2},{3,18},{4,4},{5,20},{6,6},{7,22},{8,1},{9,17},{... | collective-permute-start | bytes 442376 | tf_op jit(solution)/shard_map/ppermute | solution.py:691
  265.1 26.0 %collective-permute-start.30 = (bf16[4,24,768]{2,1,0:T(8,128)(2,1)}, bf16[4,24,768]{2,1,0:T(8,128)(2,1)S(1)}, u32[]{:S(2)}, u32[]{:S(2)}) collective-permute-start(bf16[4,24,768]{2,1,0:T(8,128)(2,1)} %bitcast.126), channel_id=1, source_target_pairs={{0,8},{1,24},{2,10},{3,26},{4,12},{5,28},{6,14},{7,30},{8,9},{9,25... | collective-permute-start | bytes 442376 | tf_op jit(solution)/shard_map/ppermute | solution.py:691
  281.6 9.5 %collective-permute-start.31 = (bf16[4,24,768]{2,1,0:T(8,128)(2,1)}, bf16[4,24,768]{2,1,0:T(8,128)(2,1)S(1)}, u32[]{:S(2)}, u32[]{:S(2)}) collective-permute-start(bf16[4,24,768]{2,1,0:T(8,128)(2,1)} %bitcast.125), channel_id=1, source_target_pairs={{0,9},{1,25},{2,11},{3,27},{4,13},{5,29},{6,15},{7,31},{8,8},{9,24... | collective-permute-start | bytes 442376 | tf_op jit(solution)/shard_map/ppermute | solution.py:691
  296.1 45.0 %all-to-all-start.1 = ((bf16[32,24,768]{2,1,0:T(8,128)(2,1)}), bf16[32,24,768]{2,1,0:T(8,128)(2,1)S(1)}, u32[]{:S(2)}, u32[]{:S(2)}) async-start(bf16[32,24,768]{2,1,0:T(8,128)(2,1)} %get-tuple-element.101), calls=%async_computation.1 | async-start | bytes 2359296 | tf_op jit(solution)/shard_map/all_to_all | solution.py:876
  301.0 9.9 %collective-permute-start.33 = (f32[16,768]{1,0:T(8,128)S(1)}, f32[16,768]{1,0:T(8,128)S(1)}, u32[]{:S(2)}, u32[]{:S(2)}) collective-permute-start(f32[16,768]{1,0:T(8,128)S(1)} %add.157), channel_id=1, source_target_pairs={{0,2},{1,3},{2,0},{3,1},{4,6},{5,7},{6,4},{7,5},{8,10},{9,11},{10,... | collective-permute-start | bytes 147464 | tf_op jit(solution)/shard_map/ppermute | solution.py:706
  321.2 16.6 %collective-permute-start.36 = (f32[16,768]{1,0:T(8,128)S(1)}, f32[16,768]{1,0:T(8,128)S(1)}, u32[]{:S(2)}, u32[]{:S(2)}) collective-permute-start(f32[16,768]{1,0:T(8,128)S(1)} %add.160), channel_id=1, source_target_pairs={{0,24},{1,25},{2,26},{3,27},{4,28},{5,29},{6,30},{7,31},{8,16},{9,... | collective-permute-start | bytes 147464 | tf_op jit(solution)/shard_map/ppermute | solution.py:706
  347.5 32.9 %all-to-all-start.2 = ((bf16[32,24,768]{2,1,0:T(8,128)(2,1)}), bf16[32,24,768]{2,1,0:T(8,128)(2,1)S(1)}, u32[]{:S(2)}, u32[]{:S(2)}) async-start(bf16[32,24,768]{2,1,0:T(8,128)(2,1)} %bitcast.108), calls=%async_computation.2 | async-start | bytes 2359296 | tf_op jit(solution)/shard_map/all_to_all | solution.py:876
  (49 other events, 367.5 us)
Sparse Core Ops, SparseCore 0:
  11.0 93.5 all-gather.1

commit v4 on v3

--- a/solution.py
+++ b/solution.py
@@ -114,35 +114,77 @@
     )
 
 
-def project_body(a1_ref, dy_ref, w_ref, vec_ref, c_ref, a_ref, b_ref, q_ref, k_ref, v_ref, do_ref):
-    a1, tables = a1_ref[0], (c_ref[...], a_ref[...], b_ref[...])
+def assemble(place_ref, pieces, w_ref):
+    z, y, x, c = place_ref[0], place_ref[1], place_ref[2], place_ref[3]
+    blocks, rows = w_ref.shape[0], 2 * pieces[0].shape[2]
+
+    def plane(t, carry):
+        apart = lax.rem(z - t + 4, 4)
+
+        def put(here, there, at, ry, rx):
+            chip = (t * 2 + (y ^ ry)) * 2 + (x ^ rx)
+            where = pl.ds(pl.multiple_of(chip * rows, rows), rows)
+            for order, wanted in (((here, there), c == 0), ((there, here), c != 0)):
+
+                @pl.when(wanted)
+                def _(order=order):
+                    for n in range(blocks):
+                        w_ref[n, where, :] = jnp.concatenate([ref[at, n] for ref in order], axis=0)
+
+        for m, (ry, rx) in enumerate(((0, 0), (0, 1), (1, 0))):
+            put(pieces[m], pieces[5 + m], apart, ry, rx)
+        pl.when(apart < 2)(lambda: put(pieces[3], pieces[8], apart, 1, 1))
+        pl.when(apart >= 2)(lambda: put(pieces[4], pieces[9], apart - 2, 1, 1))
+        return carry
+
+    lax.fori_loop(0, 4, plane, 0)
+
+
+def project_body(place_ref, x_ref, dy_ref, vec_ref, c_ref, a_ref, b_ref, *refs):
+    *pieces, q_ref, k_ref, v_ref, do_ref, acts_ref, w_ref = refs
+
+    @pl.when(pl.program_id(0) == 0)
+    def _():
+        if len(pieces) > 1:
+            assemble(place_ref, pieces, w_ref)
+        else:
+            w_ref[...] = pieces[0][...]
+
+    unit, _ = normed(x_ref[...].astype(f32))
+    a1 = (unit * vec_ref[0:1, :] + vec_ref[1:2, :]).astype(bf16)
+    acts_ref[0] = a1
+    acts_ref[1] = (unit * vec_ref[2:3, :] + vec_ref[3:4, :]).astype(bf16)
+    acts_ref[2] = dy_ref[...]
+    tables = (c_ref[...], a_ref[...], b_ref[...])
     q_ref[...] = rotate(mm(a1, w_ref[0], NN) + vec_ref[4:5, :], *tables).astype(bf16)
     k_ref[...] = rotate(mm(a1, w_ref[1], NN) + vec_ref[5:6, :], *tables).astype(bf16)
     v_ref[...] = (mm(a1, w_ref[2], NN) + vec_ref[6:7, :]).astype(bf16)
-    do_ref[...] = mm(dy_ref[0], w_ref[3], NT).astype(bf16)
-
-
-def project(acts, weights, vecs, tables, step=256):
-    _, count, width = acts.shape
-    token = pl.BlockSpec((step, width), lambda i: (i, 0))
-    table = pl.BlockSpec((step, LANES), lambda i: (i, 0))
+    do_ref[...] = mm(dy_ref[...], w_ref[3], NT).astype(bf16)
+
+
+def project(place, x, dy, pieces, vecs, tables, step=256):
+    count, width = x.shape
+    token = pl.BlockSpec((step, width), lambda i, s: (i, 0))
+    table = pl.BlockSpec((step, LANES), lambda i, s: (i, 0))
+    once = pl.Buffered(1)
     return call(
         project_body,
         8 * count * width * width,
-        12 * count * width + 8 * width * width,
-        grid=(count // step,),
-        in_specs=[
-            pl.BlockSpec((1, step, width), lambda i: (0, i, 0)),
-            pl.BlockSpec((1, step, width), lambda i: (2, i, 0)),
-            pl.BlockSpec((4, width, width), lambda i: (0, 0, 0)),
-            pl.BlockSpec(vecs.shape, lambda i: (0, 0)),
-            table,
-            table,
-            table,
-        ],
-        out_specs=[token] * 4,
-        out_shape=[jax.ShapeDtypeStruct((count, width), bf16)] * 4,
-    )(acts, acts, weights, vecs, *tables)
+        20 * count * width + 16 * width * width,
+        grid_spec=pltpu.PrefetchScalarGridSpec(
+            num_scalar_prefetch=1,
+            grid=(count // step,),
+            in_specs=[token, token, pl.BlockSpec(vecs.shape, lambda i, s: (0, 0)), table, table, table]
+            + [pl.BlockSpec(v.shape, lambda i, s, n=v.ndim: (0,) * n, pipeline_mode=once) for v in pieces],
+            out_specs=[token] * 4
+            + [
+                pl.BlockSpec((3, step, width), lambda i, s: (0, i, 0)),
+                pl.BlockSpec((4, width, width), lambda i, s: (0, 0, 0)),
+            ],
+        ),
+        out_shape=[jax.ShapeDtypeStruct((count, width), bf16)] * 4
+        + [jax.ShapeDtypeStruct((3, count, width), bf16), jax.ShapeDtypeStruct((4, width, width), bf16)],
+    )(place, x, dy, vecs, *tables, *pieces)
 
 
 def attend_body(
@@ -547,59 +589,12 @@
     return lax.ppermute(value, AXES, to_place(lambda z, y, x, c: ((z + by) % 4, y, x, c)))
 
 
-def gather_order_body(place_ref, *refs):
-    z, y, x, c = place_ref[0], place_ref[1], place_ref[2], place_ref[3]
-    out_ref = refs[-1]
-    blocks = out_ref.shape[0]
-    near = lax.rem(z - pl.program_id(0) + 4, 4) < 2
-    for rc in range(2):
-        own, by_x, by_y, lower, upper = refs[rc * 5 : rc * 5 + 5]
-        at = (y * 2 + x) * 2 + (c ^ rc)
-        for n in range(blocks):
-            out_ref[n, at] = own[0, n]
-            out_ref[n, at ^ 2] = by_x[0, n]
-            out_ref[n, at ^ 4] = by_y[0, n]
-
-        @pl.when(near)
-        def _(lower=lower, at=at):
-            for n in range(blocks):
-                out_ref[n, at ^ 6] = lower[0, n]
-
-        @pl.when(jnp.logical_not(near))
-        def _(upper=upper, at=at):
-            for n in range(blocks):
-                out_ref[n, at ^ 6] = upper[0, n]
-
-
-def gather_staged(place, shards, after=()):
-    blocks, shard, width = shards.shape
+def gather_staged(shards):
     own = jnp.stack([shards] + [over_z(shards, s) for s in (1, 2, 3)])
     by_x, by_y = over_x(own), over_y(own)
     lower, upper = over_y(by_x[:2]), over_x(by_y[2:])
     here = [own, by_x, by_y, lower, upper]
-    pieces = here + [over_c(v) for v in here]
-
-    def piece(first, count):
-        def index(t, s):
-            apart = lax.rem(s[0] - t + 4, 4)
-            return (jnp.clip(apart - first, 0, count - 1), 0, 0, 0)
-
-        return pl.BlockSpec((1, blocks, shard, width), index)
-
-    weights = call(
-        gather_order_body,
-        0,
-        64 * blocks * shard * width * 2,
-        after=after,
-        grid_spec=pltpu.PrefetchScalarGridSpec(
-            num_scalar_prefetch=1,
-            grid=(4,),
-            in_specs=([piece(0, 4)] * 3 + [piece(0, 2), piece(2, 2)]) * 2,
-            out_specs=pl.BlockSpec((blocks, 8, shard, width), lambda t, s: (0, t, 0, 0)),
-        ),
-        out_shape=jax.ShapeDtypeStruct((blocks, 32, shard, width), bf16),
-    )(place, *pieces)
-    return weights.reshape(blocks, width, width)
+    return here + [over_c(v) for v in here]
 
 
 class Reduction:
@@ -863,15 +858,6 @@
     )(owners, factor, returned, shards, blocks)
 
 
-def layer_inputs(tokens, dy, vecs):
-    values = tokens.astype(f32)
-    centred = values - jnp.mean(values, axis=-1, keepdims=True)
-    spread = jnp.mean(centred * centred, axis=-1, keepdims=True)
-    unit = centred * lax.rsqrt(spread + norm_epsilon)
-    norms = [(unit * vecs[n] + vecs[n + 1]).astype(bf16) for n in (0, 2)]
-    return jnp.stack([*norms, dy])
-
-
 def to_all(value):
     return lax.all_to_all(value, AXES, split_axis=0, concat_axis=0, tiled=True)
 
@@ -908,20 +894,12 @@
     flat_tokens = tokens.reshape(count, width)
     dy = cotangent.reshape(count, width)
     tables = rotary_tables(segment_ids)
-    acts = layer_inputs(flat_tokens, dy, vecs)
     place = jnp.stack(grid_places()).astype(jnp.int32)
     if paired:
-        attn_weights = gather_staged(place, low_blocks[:4], after=(*tables, acts))
+        pieces = gather_staged(low_blocks[:4])
     else:
-        attn_weights = lax.all_gather(low_blocks[:4], AXES, axis=1, tiled=True)
-
-    def pair(v):
-        return (v, over_c(v)) if paired else (v, v)
-
-    def pair(v):
-        return (v, over_c(v)) if paired else (v, v)
-
-    q, k, v, do = project(acts, attn_weights, vecs, tables)
+        pieces = [lax.all_gather(low_blocks[:4], AXES, axis=1, tiled=True)]
+    q, k, v, do, acts, attn_weights = project(place, flat_tokens, dy, pieces, vecs, tables)
     og, attn_sums, acts = attend(segment_ids, q, k, v, do, tables, acts)
     half = splits // 2
     orders = [list(range(4))]
@@ -932,23 +910,23 @@
         dys = (acts_pair, 2, 1)
         ed0, up_sum0 = hidden(0, half, acts, mlp_weights, vecs)
         ed0_pair = (ed0, over_c(ed0))
-
-        def grads(left, two, one, axes, after):
-            operands = ((acts_pair, left, 1), two, one, dys, shard, axes)
-            return Reduction(axes, half_grads(place, *operands, after=after))
-
-        attn = grads(0, (og_pair, 3, 1), (og_pair, 0, 3), "x", (ed0,))
-        low = grads(1, (ed0_pair, 0, half), (ed0_pair, half, half), "y", (attn.made,))
-        ed1, up_sum1 = hidden(half, half, acts, mlp_weights, vecs, after=(low.made,))
+        ed1, up_sum1 = hidden(half, half, acts, mlp_weights, vecs, after=(ed0, acts_pair[1]))
         ed1_pair = (ed1, over_c(ed1))
-        part, one_sums = grad_one(flat_tokens, dy, (og, 0, 3), attn_weights, vecs, after=(ed1,))
-        advance(place, [attn, low], [], after=(part,))
-        high = grads(1, (ed1_pair, 0, half), (ed1_pair, half, half), "xy", (low.made,))
-        terms = [advance(place, [], [attn, low], after=(high.made,))]
+
+        def grads(left, two, one, after):
+            operands = ((acts_pair, left, 1), two, one, dys, shard, "xy")
+            return Reduction("xy", half_grads(place, *operands, after=after))
+
+        attn = grads(0, (og_pair, 3, 1), (og_pair, 0, 3), (ed1,))
+        low = grads(1, (ed0_pair, 0, half), (ed0_pair, half, half), (attn.made,))
+        advance(place, [attn], [], after=(low.made,))
+        high = grads(1, (ed1_pair, 0, half), (ed1_pair, half, half), (attn.made,))
+        advance(place, [low], [], after=(high.made,))
+        part, one_sums = grad_one(flat_tokens, dy, (og, 0, 3), attn_weights, vecs, after=(low.made,))
+        terms = [advance(place, [high], [attn, low], after=(part,))]
         es, dus = [(v, 0, half) for v in (ed0, ed1)], [(v, half, half) for v in (ed0, ed1)]
-        grad_in, two_sums = grad_two(flat_tokens, part, dus, mlp_weights, vecs, after=(low.made,))
-        advance(place, [high], [], after=(grad_in,))
-        terms.append(advance(place, [], [high]))
+        grad_in, two_sums = grad_two(flat_tokens, part, dus, mlp_weights, vecs, after=(high.made,))
+        terms.append(advance(place, [], [high], after=(grad_in,)))
         orders = [orders[0] + orders[1], orders[2]]
     else:
         ed0, up_sum0 = hidden(0, half, acts, mlp_weights, vecs)

time: 394 us -> 358 us (0.909)
  waiting for transfers between devices: 113 us -> 78.3 us
  starting transfers between devices: 52.7 us -> 64.7 us
  other arithmetic: 22.5 us -> 15.4 us
    ppermute x9, waiting for transfers between devices: 16.8 us -> 0.02 us  [over_c(): lax.ppermute(value, AXES, to_place(lambda z, y, x, c: (z, y, x, 1 - c)))]
    ppermute x6 -> x8, waiting for transfers between devices: 14.7 us -> 0.97 us  [over_y(): lax.ppermute(value, AXES, to_place(lambda z, y, x, c: (z, 1 - y, x, c)))]
    ppermute x8, waiting for transfers between devices: 18.9 us -> 12.6 us  [advance(): lax.ppermute(v, AXES, to_place(lambda z, y, x, c, m=m: (2 * c + ((z ^ m)...]
    ppermute x6 -> x8, starting transfers between devices: 5.12 us -> 9.8 us  [over_y(): lax.ppermute(value, AXES, to_place(lambda z, y, x, c: (z, 1 - y, x, c)))]
    ppermute x6 -> x8, starting transfers between devices: 7.63 us -> 10.2 us  [over_x(): lax.ppermute(value, AXES, to_place(lambda z, y, x, c: (z, y, 1 - x, c)))]
    pallas_call x20 -> x19, Pallas kernels: 169 us -> 167 us  [call(): return lambda *operands: made(*operands, *after)]
    ppermute x6 -> x8, waiting for transfers between devices: 23.9 us -> 22.7 us  [over_x(): lax.ppermute(value, AXES, to_place(lambda z, y, x, c: (z, y, 1 - x, c)))]
    unnamed x87 -> x81, local copies, waits for them, and re-layouts: 9.6 us -> 9.07 us
  transfers between devices with their start and end apart: 41 -> 45, of which waited for: 16 -> 16; matrix products, arithmetic and copies ran while one was open for 7% -> 6% of each run, Pallas kernels for 33% -> 42%
where the time goes in v4:
time: 358 us; the launch traced here: 357 us
  Pallas kernels  167 us (47%)
  waiting for transfers between devices  78.3 us (22%)
  starting transfers between devices  64.7 us (18%)
  between operations  18 us (5%)
  other arithmetic  15.4 us (4%)
  local copies, waits for them, and re-layouts  13.6 us (4%)
    pallas_call x19, Pallas kernels, call(): return lambda *operands: made(*operands, *after)  167 us
    ppermute x8, waiting for transfers between devices, over_x(): lax.ppermute(value, AXES, to_place(lambda z, y, x, c: (z, y, 1 - x, c)))  22.7 us
    all_to_all x3, waiting for transfers between devices, to_all(): return lax.all_to_all(value, AXES, split_axis=0, concat_axis=0, tiled=True)  19.9 us
    ppermute x8, starting transfers between devices, advance(): lax.ppermute(v, AXES, to_place(lambda z, y, x, c, m=m: (2 * c + ((z ^ m)...  19.8 us
    ppermute x5, waiting for transfers between devices, everywhere(): value = value + lax.ppermute(value, AXES, to_place(move))  17.8 us
    ppermute x8, waiting for transfers between devices, advance(): lax.ppermute(v, AXES, to_place(lambda z, y, x, c, m=m: (2 * c + ((z ^ m)...  12.6 us
    ppermute x8, starting transfers between devices, over_x(): lax.ppermute(value, AXES, to_place(lambda z, y, x, c: (z, y, 1 - x, c)))  10.2 us
    ppermute x8, starting transfers between devices, over_y(): lax.ppermute(value, AXES, to_place(lambda z, y, x, c: (z, 1 - y, x, c)))  9.8 us
  transfers between devices with their start and end apart: 45, of which 16 were waited for; matrix products, arithmetic and copies ran while one was open for 6% of the time, Pallas kernels for 42%

profile of v4, /device:TPU:0, one launch (start us, length us, event | category | flops | bytes accessed | tf_op | source)
XLA Modules:
  0.0 356.6 jit_solution(13199569164717987288)
XLA Ops:
  21.3 3.3 collective-permute-done.1
  28.8 11.2 %collective-permute-done.3.refs_1_ = bf16[4,4,24,768]{3,2,1,0:T(8,128)(2,1)S(1)} collective-permute-done((bf16[4,4,24,768]{3,2,1,0:T(8,128)(2,1)S(1)}, bf16[4,4,24,768]{3,2,1,0:T(8,128)(2,1)S(1)}, u32[]{:S(2)}, u32[]{:S(2)}) %collective-permute-start.3) | collective-permute-done | bytes 589856 | tf_op jit(solution)/shard_map/ppermute | solution.py:581
  43.2 5.2 %compare_select_fusion.9 = f32[128]{0:T(128)S(1)} fusion(f32[]{:T(128)} %bitcast.10, f32[]{:T(128)} %bitcast.11, f32[]{:T(128)} %bitcast.12, f32[]{:T(128)} %bitcast.13, f32[]{:T(128)} %bitcast.14, f32[]{:T(128)} %bitcast.16, f32[]{:T(128)} %bitcast.15, f32[]{:T(128)} %bitcast.9), kind=kLoop, calls=%fused_computation.32 | loop fusion | flops 5376 | bytes 544 | tf_op jit(solution)/shard_map/jit(_where)/select_n | solution.py:90
  52.8 4.0 %collective-permute-done.6.refs_4_ = bf16[2,4,24,768]{3,2,1,0:T(8,128)(2,1)} collective-permute-done((bf16[2,4,24,768]{3,2,1,0:T(8,128)(2,1)S(1)}, bf16[2,4,24,768]{3,2,1,0:T(8,128)(2,1)}, u32[]{:S(2)}, u32[]{:S(2)}) %collective-permute-start.6) | collective-permute-done | bytes 294944 | tf_op jit(solution)/shard_map/ppermute | solution.py:581
  61.0 14.1 %shard_map.202 = (bf16[1024,768]{1,0:T(8,128)(2,1)}, bf16[1024,768]{1,0:T(8,128)(2,1)}, bf16[1024,768]{1,0:T(8,128)(2,1)}, bf16[1024,768]{1,0:T(8,128)(2,1)}, bf...) custom-call(s32[4]{0:T(128)} %pad_add_fusion.place_ref.refs_0_, bf16[1024,768]{1,0:T(8,128)(2,1)} %bitcast.76, ...), custom_call_target="tpu_custom_call" | custom-call | flops 4831838208 | bytes 25165824 | tf_op jit(solution)/shard_map/pallas_call | solution.py:74
  75.1 25.4 %shard_map.203 = (bf16[4,1024,768]{2,1,0:T(8,128)(2,1)}, f32[3,16,768]{2,1,0:T(8,128)}, bf16[3,1024,768]{2,1,0:T(8,128)(2,1)}) custom-call(bf16[3,1024,768]{2,1,0:T(8,128)(2,1)} %get-tuple-element.71.acts_ref, s32[1024,1]{1,0:T(8,128)} %bitcast.89, s32[2,1,512]{2,1,0:T(1,128)} %broadcast_in_dim.74.row_ref, ...), custom_call_target="tpu_custom_call", output_to_operand_aliasing={{2}: (0, {})} | custom-call | flops 9663676416 | bytes 18874368 | tf_op jit(solution)/shard_map/pallas_call | solution.py:74
  102.9 12.6 %shard_map.204 = (bf16[2,2,1024,768]{3,2,1,0:T(8,128)(2,1)}, f32[2,8,768]{2,1,0:T(8,128)}) custom-call(bf16[3,1024,768]{2,1,0:T(8,128)(2,1)} %get-tuple-element.77.a2_ref.dy_ref.refs_0_.refs_1_.refs_7_, bf16[3,1024,768]{2,1,0:T(8,128)(2,1)} %get-tuple-element.77.a2_ref.dy_ref.refs_0_.refs_1_.refs_7_, ...), custom_call_target="tpu_custom_call" | custom-call | flops 4831838208 | bytes 17301504 | tf_op jit(solution)/shard_map/pallas_call | solution.py:74
  115.8 12.6 %shard_map.205 = (bf16[2,2,1024,768]{3,2,1,0:T(8,128)(2,1)}, f32[2,8,768]{2,1,0:T(8,128)}) custom-call(bf16[3,1024,768]{2,1,0:T(8,128)(2,1)} %get-tuple-element.77.a2_ref.dy_ref.refs_0_.refs_1_.refs_7_, bf16[3,1024,768]{2,1,0:T(8,128)(2,1)} %get-tuple-element.77.a2_ref.dy_ref.refs_0_.refs_1_.refs_7_, ...), custom_call_target="tpu_custom_call" | custom-call | flops 4831838208 | bytes 17301504 | tf_op jit(solution)/shard_map/pallas_call | solution.py:74
  128.6 11.4 %shard_map.206 = (bf16[4,2,2,2,24,384]{5,4,3,2,1,0:T(8,128)(2,1)}, bf16[4,2,2,2,24,384]{5,4,3,2,1,0:T(8,128)(2,1)}, bf16[4,2,2,2,24,384]{5,4,3,2,1,0:T(8,128)(2,1)}, bf16[4,2,2,2,24,384]{5,4,3,2,1,0:T(8,128)(2,1)}) custom-call(s32[4]{0:T(128)} %pad_add_fusion.place_ref.refs_0_, bf16[3,1024,768]{2,1,0:T(8,128)(2,1)} %get-tuple-element.77.a2_ref.dy_ref.refs_0_.refs_1_.refs_7_, ...), custom_call_target="tpu_custom_call" | custom-call | flops 4831838208 | bytes 12582912 | tf_op jit(solution)/shard_map/pallas_call | solution.py:74
  143.0 11.2 %shard_map.207 = (bf16[4,2,2,2,24,384]{5,4,3,2,1,0:T(8,128)(2,1)}, bf16[4,2,2,2,24,384]{5,4,3,2,1,0:T(8,128)(2,1)}, bf16[4,2,2,2,24,384]{5,4,3,2,1,0:T(8,128)(2,1)}, bf16[4,2,2,2,24,384]{5,4,3,2,1,0:T(8,128)(2,1)}) custom-call(s32[4]{0:T(128)} %pad_add_fusion.place_ref.refs_0_, bf16[3,1024,768]{2,1,0:T(8,128)(2,1)} %get-tuple-element.77.a2_ref.dy_ref.refs_0_.refs_1_.refs_7_, ...), custom_call_target="tpu_custom_call" | custom-call | flops 4831838208 | bytes 12582912 | tf_op jit(solution)/shard_map/pallas_call | solution.py:74
  162.9 11.3 %shard_map.209 = (bf16[4,2,2,2,24,384]{5,4,3,2,1,0:T(8,128)(2,1)}, bf16[4,2,2,2,24,384]{5,4,3,2,1,0:T(8,128)(2,1)}, bf16[4,2,2,2,24,384]{5,4,3,2,1,0:T(8,128)(2,1)}, bf16[4,2,2,2,24,384]{5,4,3,2,1,0:T(8,128)(2,1)}) custom-call(s32[4]{0:T(128)} %pad_add_fusion.place_ref.refs_0_, bf16[3,1024,768]{2,1,0:T(8,128)(2,1)} %get-tuple-element.77.a2_ref.dy_ref.refs_0_.refs_1_.refs_7_, ...), custom_call_target="tpu_custom_call" | custom-call | flops 4831838208 | bytes 12582912 | tf_op jit(solution)/shard_map/pallas_call | solution.py:74
  183.8 9.8 %shard_map.211 = (f32[1024,768]{1,0:T(8,128)}, f32[3,8,768]{2,1,0:T(8,128)}) custom-call(bf16[1024,768]{1,0:T(8,128)(2,1)} %bitcast.77, bf16[1024,768]{1,0:T(8,128)(2,1)} %bitcast.85, bf16[4,1024,768]{2,1,0:T(8,128)(2,1)} %get-tuple-element.76.refs_3_.refs_5_.refs_2_.refs_1_, bf16[4,768,768]{2,1,0:T(8,128)(2,1)} %get-tuple-element.80.refs_3_.refs_4_, ...), custom_call_target="tpu_custom_call" | custom-call | flops 3623878656 | bytes 14548992 | tf_op jit(solution)/shard_map/pallas_call | solution.py:74
  193.6 3.4 collective-permute-done.21.refs_8_
  197.0 3.6 %collective-permute-done.25.refs_12_ = bf16[4,2,2,24,384]{4,3,2,1,0:T(8,128)(2,1)S(1)} collective-permute-done((bf16[4,2,2,24,384]{4,3,2,1,0:T(8,128)(2,1)}, bf16[4,2,2,24,384]{4,3,2,1,0:T(8,128)(2,1)S(1)}, u32[]{:S(2)}, u32[]{:S(2)}) %collective-permute-start.25) | collective-permute-done | bytes 294944 | tf_op jit(solution)/shard_map/ppermute | solution.py:581
  201.4 4.3 %shard_map.212 = (bf16[4,2,2,24,384]{4,3,2,1,0:T(8,128)(2,1)}, bf16[4,2,2,24,384]{4,3,2,1,0:T(8,128)(2,1)}, bf16[4,2,2,24,384]{4,3,2,1,0:T(8,128)(2,1)}, bf16[4,...) custom-call(s32[4]{0:T(128)} %pad_add_fusion.place_ref.refs_0_, ...), custom_call_target="tpu_custom_call" | custom-call | bytes 9437184 | tf_op jit(solution)/shard_map/pallas_call | solution.py:74
  209.3 3.6 %collective-permute-start.27 = (bf16[8,24,768]{2,1,0:T(8,128)(2,1)}, bf16[8,24,768]{2,1,0:T(8,128)(2,1)S(1)}, u32[]{:S(2)}, u32[]{:S(2)}) collective-permute-start(bf16[8,24,768]{2,1,0:T(8,128)(2,1)} %bitcast.101), channel_id=1, source_target_pairs={{0,1},{1,17},{2,3},{3,19},{4,5},{5,21},{6,7},{7,23},{8,0},{9,16},{... | collective-permute-start | bytes 884744 | tf_op jit(solution)/shard_map/ppermute | solution.py:686
  212.8 3.8 %collective-permute-start.28 = (bf16[8,24,768]{2,1,0:T(8,128)(2,1)}, bf16[8,24,768]{2,1,0:T(8,128)(2,1)S(1)}, u32[]{:S(2)}, u32[]{:S(2)}) collective-permute-start(bf16[8,24,768]{2,1,0:T(8,128)(2,1)} %bitcast.100), channel_id=1, source_target_pairs={{0,8},{1,24},{2,10},{3,26},{4,12},{5,28},{6,14},{7,30},{8,9},{9,25... | collective-permute-start | bytes 884744 | tf_op jit(solution)/shard_map/ppermute | solution.py:686
  216.6 3.6 %collective-permute-start.29 = (bf16[8,24,768]{2,1,0:T(8,128)(2,1)}, bf16[8,24,768]{2,1,0:T(8,128)(2,1)S(1)}, u32[]{:S(2)}, u32[]{:S(2)}) collective-permute-start(bf16[8,24,768]{2,1,0:T(8,128)(2,1)} %bitcast.99), channel_id=1, source_target_pairs={{0,9},{1,25},{2,11},{3,27},{4,13},{5,29},{6,15},{7,31},{8,8},{9,24... | collective-permute-start | bytes 884744 | tf_op jit(solution)/shard_map/ppermute | solution.py:686
  220.2 11.0 %shard_map.213 = (bf16[1024,768]{1,0:T(8,128)(2,1)}, f32[2,8,768]{2,1,0:T(8,128)}) custom-call(bf16[1024,768]{1,0:T(8,128)(2,1)} %bitcast.78, f32[1024,768]{1,0:T(8,128)} %get-tuple-element.101.refs_13_.refs_1_, bf16[4,1024,768]{2,1,0:T(8,128)(2,1)} %bitcast.74, bf16[4,1024,768]{2,1,0:T(8,128)(2,1)} %bitcast.68, ...), custom_call_target="tpu_custom_call" | custom-call | flops 4831838208 | bytes 17301504 | tf_op jit(solution)/shard_map/pallas_call | solution.py:74
  236.2 3.8 %collective-permute-start.33 = (bf16[4,24,768]{2,1,0:T(8,128)(2,1)}, bf16[4,24,768]{2,1,0:T(8,128)(2,1)S(1)}, u32[]{:S(2)}, u32[]{:S(2)}) collective-permute-start(bf16[4,24,768]{2,1,0:T(8,128)(2,1)} %bitcast.105), channel_id=1, source_target_pairs={{0,1},{1,17},{2,3},{3,19},{4,5},{5,21},{6,7},{7,23},{8,0},{9,16},{... | collective-permute-start | bytes 442376 | tf_op jit(solution)/shard_map/ppermute | solution.py:686
  246.3 8.8 %collective-permute-done.34.refs_7_ = bf16[4,24,768]{2,1,0:T(8,128)(2,1)S(1)} collective-permute-done((bf16[4,24,768]{2,1,0:T(8,128)(2,1)}, bf16[4,24,768]{2,1,0:T(8,128)(2,1)S(1)}, u32[]{:S(2)}, u32[]{:S(2)}) %collective-permute-start.34) | collective-permute-done | bytes 147488 | tf_op jit(solution)/shard_map/ppermute | solution.py:686
  256.4 3.7 %shard_map.215 = (f32[12,24,768]{2,1,0:T(8,128)}, bf16[32,24,768]{2,1,0:T(8,128)(2,1)}, f32[24,768]{1,0:T(8,128)}) custom-call(s32[32]{0:T(128)} %broadcast_add_fusion.refs_0_, bf16[8,24,768]{2,1,0:T(8,128)(2,1)} %copy-done.15, bf16[8,24,768]{2,1,0:T(8,128)(2,1)} %copy-done.16, bf16[8,24,768]{2,1,0:T(8,128)(2,1)} %copy-done.17, ...), custom_call_target="tpu_custom_call" | custom-call | bytes 3538944 | tf_op jit(solution)/shard_map/pallas_call | solution.py:74
  266.3 7.4 %collective-permute-done.37 = f32[16,768]{1,0:T(8,128)S(1)} collective-permute-done((f32[16,768]{1,0:T(8,128)S(1)}, f32[16,768]{1,0:T(8,128)S(1)}, u32[]{:S(2)}, u32[]{:S(2)}) %collective-permute-start.37) | collective-permute-done | bytes 49184 | tf_op jit(solution)/shard_map/ppermute | solution.py:701
  275.0 3.8 %collective-permute-done.38 = f32[16,768]{1,0:T(8,128)S(1)} collective-permute-done((f32[16,768]{1,0:T(8,128)S(1)}, f32[16,768]{1,0:T(8,128)S(1)}, u32[]{:S(2)}, u32[]{:S(2)}) %collective-permute-start.38) | collective-permute-done | bytes 49184 | tf_op jit(solution)/shard_map/ppermute | solution.py:701
  279.2 5.7 %collective-permute-done.39 = f32[16,768]{1,0:T(8,128)S(1)} collective-permute-done((f32[16,768]{1,0:T(8,128)S(1)}, f32[16,768]{1,0:T(8,128)S(1)}, u32[]{:S(2)}, u32[]{:S(2)}) %collective-permute-start.39) | collective-permute-done | bytes 49184 | tf_op jit(solution)/shard_map/ppermute | solution.py:701
  287.3 11.0 %shard_map.216.refs_2_ = bf16[1024,768]{1,0:T(8,128)(2,1)} custom-call(bf16[1024,768]{1,0:T(8,128)(2,1)} %bitcast.79, bf16[4,1024,768]{2,1,0:T(8,128)(2,1)} %get-tuple-element.76.refs_3_.refs_5_.refs_2_.refs_1_, bf16[4,1024,768]{2,1,0:T(8,128)(2,1)} %bitcast.75, bf16[4,1024,768]{2,1,0:T(8,128)(2,1)} %bitcast.69, ...), custom_call_target="tpu_custom_call" | custom-call | flops 6039797760 | bytes 16908288 | tf_op jit(solution)/shard_map/pallas_call | solution.py:74
  298.3 3.5 shard_map.217
  306.2 5.3 %shard_map.218 = bf16[768,768]{1,0:T(8,128)(2,1)} custom-call(f32[2]{0:T(128)} %pad_maximum_fusion.1.scale_ref, bf16[768,768]{1,0:T(8,128)(2,1)} %bitcast.86, bf16[768,768]{1,0:T(8,128)(2,1)} %get-tuple-element.122.l_ref, bf16[768,768]{1,0:T(8,128)(2,1)} %get-tuple-element.123.r_ref), custom_call_target="tpu_custom_call" | custom-call | flops 1811939328 | bytes 4718592 | tf_op jit(solution)/shard_map/pallas_call | solution.py:74
  311.5 3.8 %all-to-all-start.2 = ((bf16[32,24,768]{2,1,0:T(8,128)(2,1)}), bf16[32,24,768]{2,1,0:T(8,128)(2,1)S(1)}, u32[]{:S(2)}, u32[]{:S(2)}) async-start(bf16[32,24,768]{2,1,0:T(8,128)(2,1)} %bitcast.88), calls=%async_computation.2 | async-start | bytes 2359296 | tf_op jit(solution)/shard_map/all_to_all | solution.py:862
  317.3 7.2 %shard_map.220 = (f32[768,768]{1,0:T(8,128)}, f32[768,768]{1,0:T(8,128)}) custom-call(s32[1]{0:T(128)} %bitcast.41.has_ref, f32[2]{0:T(128)} %pad_maximum_fusion.1.scale_ref, bf16[768,768]{1,0:T(8,128)(2,1)} %bitcast.87, f32[768,768]{1,0:T(8,128)} %bitcast.97, f32[768,768]{1,0:T(8,128)} %bitcast.98), custom_call_target="tpu_custom_call" | custom-call | flops 1811939328 | bytes 10616832 | tf_op jit(solution)/shard_map/pallas_call | solution.py:74
  324.5 19.9 %all-to-all-done.2.p_ref = bf16[32,24,768]{2,1,0:T(8,128)(2,1)S(1)} async-done(((bf16[32,24,768]{2,1,0:T(8,128)(2,1)}), bf16[32,24,768]{2,1,0:T(8,128)(2,1)S(1)}, u32[]{:S(2)}, u32[]{:S(2)}) %all-to-all-start.2) | async-done | bytes 1179680 | tf_op jit(solution)/shard_map/all_to_all | solution.py:862
  345.4 3.3 shard_map.219
  (207 shorter events, 86.1 us)
Async XLA Ops:
  7.2 95.7 %all-gather.2.cloned.1.call-start = ((), (), s32[]{:S(2)}) async-start(), calls=%async_computation.3 | async-start | bytes 9732096 | tf_op jit(solution)/shard_map/all_gather | solution.py:892
  9.2 12.1 %collective-permute-start = (bf16[4,24,768]{2,1,0:T(8,128)(2,1)S(1)}, bf16[4,24,768]{2,1,0:T(8,128)(2,1)S(1)}, u32[]{:S(2)}, u32[]{:S(2)}) collective-permute-start(bf16[4,24,768]{2,1,0:T(8,128)(2,1)S(1)} %get-tuple-element.135), channel_id=1, source_target_pairs={{0,8},{1,9},{2,10},{3,11},{4,12},{5,13},{6,14},{7,15},{8,16},{9,17... | collective-permute-start | bytes 442376 | tf_op jit(solution)/shard_map/ppermute | solution.py:589
  12.3 12.3 %collective-permute-start.1 = (bf16[4,24,768]{2,1,0:T(8,128)(2,1)S(1)}, bf16[4,24,768]{2,1,0:T(8,128)(2,1)S(1)}, u32[]{:S(2)}, u32[]{:S(2)}) collective-permute-start(bf16[4,24,768]{2,1,0:T(8,128)(2,1)S(1)} %get-tuple-element.135), channel_id=1, source_target_pairs={{0,16},{1,17},{2,18},{3,19},{4,20},{5,21},{6,22},{7,23},{8,24},{9,... | collective-permute-start | bytes 442376 | tf_op jit(solution)/shard_map/ppermute | solution.py:589
  18.4 40.6 %all-to-all-start = ((bf16[32,2,156]{2,1,0:T(2,128)(2,1)}), bf16[32,2,156]{2,1,0:T(2,128)(2,1)S(1)}, u32[]{:S(2)}, u32[]{:S(2)}) async-start(bf16[32,2,156]{2,1,0:T(2,128)(2,1)} %reshape.296), calls=%async_computation | async-start | bytes 65536 | tf_op jit(solution)/shard_map/all_to_all | solution.py:862
  24.7 15.4 %collective-permute-start.3 = (bf16[4,4,24,768]{3,2,1,0:T(8,128)(2,1)S(1)}, bf16[4,4,24,768]{3,2,1,0:T(8,128)(2,1)S(1)}, u32[]{:S(2)}, u32[]{:S(2)}) collective-permute-start(bf16[4,4,24,768]{3,2,1,0:T(8,128)(2,1)S(1)} %pad_maximum_fusion.refs_0_), channel_id=1, source_target_pairs={{0,2},{1,3},{2,0},{3,1},{4,6},{5,7},{6,4},{7,5},{8,10},{9,11},{10,... | collective-permute-start | bytes 1769480 | tf_op jit(solution)/shard_map/ppermute | solution.py:581
  26.3 15.4 %collective-permute-start.4 = (bf16[4,4,24,768]{3,2,1,0:T(8,128)(2,1)S(1)}, bf16[4,4,24,768]{3,2,1,0:T(8,128)(2,1)S(1)}, u32[]{:S(2)}, u32[]{:S(2)}) collective-permute-start(bf16[4,4,24,768]{3,2,1,0:T(8,128)(2,1)S(1)} %pad_maximum_fusion.refs_0_), channel_id=1, source_target_pairs={{0,4},{1,5},{2,6},{3,7},{4,0},{5,1},{6,2},{7,3},{8,12},{9,13},{10,... | collective-permute-start | bytes 1769480 | tf_op jit(solution)/shard_map/ppermute | solution.py:585
  40.1 12.3 %collective-permute-start.5 = (bf16[2,4,24,768]{3,2,1,0:T(8,128)(2,1)S(1)}, bf16[2,4,24,768]{3,2,1,0:T(8,128)(2,1)S(1)}, u32[]{:S(2)}, u32[]{:S(2)}) collective-permute-start(bf16[2,4,24,768]{3,2,1,0:T(8,128)(2,1)S(1)} %slice.42), channel_id=1, source_target_pairs={{0,4},{1,5},{2,6},{3,7},{4,0},{5,1},{6,2},{7,3},{8,12},{9,13},{10,... | collective-permute-start | bytes 884744 | tf_op jit(solution)/shard_map/ppermute | solution.py:585
  41.7 15.1 %collective-permute-start.6 = (bf16[2,4,24,768]{3,2,1,0:T(8,128)(2,1)S(1)}, bf16[2,4,24,768]{3,2,1,0:T(8,128)(2,1)}, u32[]{:S(2)}, u32[]{:S(2)}) collective-permute-start(bf16[2,4,24,768]{3,2,1,0:T(8,128)(2,1)S(1)} %slice.43), channel_id=1, source_target_pairs={{0,2},{1,3},{2,0},{3,1},{4,6},{5,7},{6,4},{7,5},{8,10},{9,11},{10,... | collective-permute-start | bytes 884744 | tf_op jit(solution)/shard_map/ppermute | solution.py:581
  100.6 15.2 %collective-permute-start.12 = (bf16[3,1024,768]{2,1,0:T(8,128)(2,1)}, bf16[3,1024,768]{2,1,0:T(8,128)(2,1)}, u32[]{:S(2)}, u32[]{:S(2)}) collective-permute-start(bf16[3,1024,768]{2,1,0:T(8,128)(2,1)} %get-tuple-element.77.a2_ref.dy_ref.refs_0_.refs_1_.refs_7_), channel_id=1, source_target_pairs={{0,1},{1,0},{2,3},{3,2},{4,5},{5,4},{6,7},{7,6},{8,9},{9,8},{10,11... | collective-permute-start | bytes 14155784 | tf_op jit(solution)/shard_map/ppermute | solution.py:577
  101.1 27.5 %collective-permute-start.14 = (bf16[4,1024,768]{2,1,0:T(8,128)(2,1)}, bf16[4,1024,768]{2,1,0:T(8,128)(2,1)}, u32[]{:S(2)}, u32[]{:S(2)}) collective-permute-start(bf16[4,1024,768]{2,1,0:T(8,128)(2,1)} %get-tuple-element.76.refs_3_.refs_5_.refs_2_.refs_1_), channel_id=1, source_target_pairs={{0,1},{1,0},{2,3},{3,2},{4,5},{5,4},{6,7},{7,6},{8,9},{9,8},{10,11... | collective-permute-start | bytes 18874376 | tf_op jit(solution)/shard_map/ppermute | solution.py:577
  115.5 27.5 %collective-permute-start.17 = (bf16[4,1024,768]{2,1,0:T(8,128)(2,1)}, bf16[4,1024,768]{2,1,0:T(8,128)(2,1)}, u32[]{:S(2)}, u32[]{:S(2)}) collective-permute-start(bf16[4,1024,768]{2,1,0:T(8,128)(2,1)} %bitcast.70), channel_id=1, source_target_pairs={{0,1},{1,0},{2,3},{3,2},{4,5},{5,4},{6,7},{7,6},{8,9},{9,8},{10,11... | collective-permute-start | bytes 18874376 | tf_op jit(solution)/shard_map/ppermute | solution.py:577
  128.4 34.5 %collective-permute-start.13 = (bf16[4,1024,768]{2,1,0:T(8,128)(2,1)}, bf16[4,1024,768]{2,1,0:T(8,128)(2,1)}, u32[]{:S(2)}, u32[]{:S(2)}) collective-permute-start(bf16[4,1024,768]{2,1,0:T(8,128)(2,1)} %bitcast.64), channel_id=1, source_target_pairs={{0,1},{1,0},{2,3},{3,2},{4,5},{5,4},{6,7},{7,6},{8,9},{9,8},{10,11... | collective-permute-start | bytes 18874376 | tf_op jit(solution)/shard_map/ppermute | solution.py:577
  140.1 15.7 %collective-permute-start.15 = (bf16[4,2,2,2,24,384]{5,4,3,2,1,0:T(8,128)(2,1)}, bf16[4,2,2,2,24,384]{5,4,3,2,1,0:T(8,128)(2,1)S(1)}, u32[]{:S(2)}, u32[]{:S(2)}) collective-permute-start(bf16[4,2,2,2,24,384]{5,4,3,2,1,0:T(8,128)(2,1)} %get-tuple-element.82), channel_id=1, source_target_pairs={{0,2},{1,3},{2,0},{3,1},{4,6},{5,7},{6,4},{7,5},{8,10},{9,11},{10,... | collective-permute-start | bytes 1769480 | tf_op jit(solution)/shard_map/ppermute | solution.py:581
  141.1 15.6 %collective-permute-start.16 = (bf16[4,2,2,2,24,384]{5,4,3,2,1,0:T(8,128)(2,1)}, bf16[4,2,2,2,24,384]{5,4,3,2,1,0:T(8,128)(2,1)S(1)}, u32[]{:S(2)}, u32[]{:S(2)}) collective-permute-start(bf16[4,2,2,2,24,384]{5,4,3,2,1,0:T(8,128)(2,1)} %get-tuple-element.84), channel_id=1, source_target_pairs={{0,4},{1,5},{2,6},{3,7},{4,0},{5,1},{6,2},{7,3},{8,12},{9,13},{10,... | collective-permute-start | bytes 1769480 | tf_op jit(solution)/shard_map/ppermute | solution.py:585
  154.2 21.5 %collective-permute-start.22 = (bf16[4,2,2,2,24,384]{5,4,3,2,1,0:T(8,128)(2,1)}, bf16[4,2,2,2,24,384]{5,4,3,2,1,0:T(8,128)(2,1)S(1)}, u32[]{:S(2)}, u32[]{:S(2)}) collective-permute-start(bf16[4,2,2,2,24,384]{5,4,3,2,1,0:T(8,128)(2,1)} %get-tuple-element.94), channel_id=1, source_target_pairs={{0,2},{1,3},{2,0},{3,1},{4,6},{5,7},{6,4},{7,5},{8,10},{9,11},{10,... | collective-permute-start | bytes 1769480 | tf_op jit(solution)/shard_map/ppermute | solution.py:581
  155.4 21.0 %collective-permute-start.23 = (bf16[4,2,2,2,24,384]{5,4,3,2,1,0:T(8,128)(2,1)}, bf16[4,2,2,2,24,384]{5,4,3,2,1,0:T(8,128)(2,1)S(1)}, u32[]{:S(2)}, u32[]{:S(2)}) collective-permute-start(bf16[4,2,2,2,24,384]{5,4,3,2,1,0:T(8,128)(2,1)} %get-tuple-element.96), channel_id=1, source_target_pairs={{0,4},{1,5},{2,6},{3,7},{4,0},{5,1},{6,2},{7,3},{8,12},{9,13},{10,... | collective-permute-start | bytes 1769480 | tf_op jit(solution)/shard_map/ppermute | solution.py:585
  160.6 21.7 %collective-permute-start.20 = (bf16[4,2,2,24,384]{4,3,2,1,0:T(8,128)(2,1)}, bf16[4,2,2,24,384]{4,3,2,1,0:T(8,128)(2,1)S(1)}, u32[]{:S(2)}, u32[]{:S(2)}) collective-permute-start(bf16[4,2,2,24,384]{4,3,2,1,0:T(8,128)(2,1)} %get-tuple-element.91), channel_id=1, source_target_pairs={{0,4},{1,5},{2,6},{3,7},{4,0},{5,1},{6,2},{7,3},{8,12},{9,13},{10,... | collective-permute-start | bytes 884744 | tf_op jit(solution)/shard_map/ppermute | solution.py:585
  174.2 22.8 %collective-permute-start.18 = (bf16[4,2,2,2,24,384]{5,4,3,2,1,0:T(8,128)(2,1)}, bf16[4,2,2,2,24,384]{5,4,3,2,1,0:T(8,128)(2,1)S(1)}, u32[]{:S(2)}, u32[]{:S(2)}) collective-permute-start(bf16[4,2,2,2,24,384]{5,4,3,2,1,0:T(8,128)(2,1)} %get-tuple-element.88), channel_id=1, source_target_pairs={{0,2},{1,3},{2,0},{3,1},{4,6},{5,7},{6,4},{7,5},{8,10},{9,11},{10,... | collective-permute-start | bytes 1769480 | tf_op jit(solution)/shard_map/ppermute | solution.py:581
  175.7 21.3 %collective-permute-start.19 = (bf16[4,2,2,2,24,384]{5,4,3,2,1,0:T(8,128)(2,1)}, bf16[4,2,2,2,24,384]{5,4,3,2,1,0:T(8,128)(2,1)S(1)}, u32[]{:S(2)}, u32[]{:S(2)}) collective-permute-start(bf16[4,2,2,2,24,384]{5,4,3,2,1,0:T(8,128)(2,1)} %get-tuple-element.90), channel_id=1, source_target_pairs={{0,4},{1,5},{2,6},{3,7},{4,0},{5,1},{6,2},{7,3},{8,12},{9,13},{10,... | collective-permute-start | bytes 1769480 | tf_op jit(solution)/shard_map/ppermute | solution.py:585
  175.7 21.3 %collective-permute-start.21 = (bf16[4,2,2,24,384]{4,3,2,1,0:T(8,128)(2,1)S(1)}, bf16[4,2,2,24,384]{4,3,2,1,0:T(8,128)(2,1)S(1)}, u32[]{:S(2)}, u32[]{:S(2)}) collective-permute-start(bf16[4,2,2,24,384]{4,3,2,1,0:T(8,128)(2,1)S(1)} %copy-done.37), channel_id=1, source_target_pairs={{0,2},{1,3},{2,0},{3,1},{4,6},{5,7},{6,4},{7,5},{8,10},{9,11},{10,... | collective-permute-start | bytes 884744 | tf_op jit(solution)/shard_map/ppermute | solution.py:581
  180.4 16.7 %collective-permute-start.24 = (bf16[4,2,2,24,384]{4,3,2,1,0:T(8,128)(2,1)}, bf16[4,2,2,24,384]{4,3,2,1,0:T(8,128)(2,1)S(1)}, u32[]{:S(2)}, u32[]{:S(2)}) collective-permute-start(bf16[4,2,2,24,384]{4,3,2,1,0:T(8,128)(2,1)} %get-tuple-element.98), channel_id=1, source_target_pairs={{0,4},{1,5},{2,6},{3,7},{4,0},{5,1},{6,2},{7,3},{8,12},{9,13},{10,... | collective-permute-start | bytes 884744 | tf_op jit(solution)/shard_map/ppermute | solution.py:585
  182.4 18.3 %collective-permute-start.25 = (bf16[4,2,2,24,384]{4,3,2,1,0:T(8,128)(2,1)}, bf16[4,2,2,24,384]{4,3,2,1,0:T(8,128)(2,1)S(1)}, u32[]{:S(2)}, u32[]{:S(2)}) collective-permute-start(bf16[4,2,2,24,384]{4,3,2,1,0:T(8,128)(2,1)} %get-tuple-element.100), channel_id=1, source_target_pairs={{0,2},{1,3},{2,0},{3,1},{4,6},{5,7},{6,4},{7,5},{8,10},{9,11},{10,... | collective-permute-start | bytes 884744 | tf_op jit(solution)/shard_map/ppermute | solution.py:581
  206.3 24.9 %collective-permute-start.31 = (bf16[4,2,2,24,384]{4,3,2,1,0:T(8,128)(2,1)}, bf16[4,2,2,24,384]{4,3,2,1,0:T(8,128)(2,1)S(1)}, u32[]{:S(2)}, u32[]{:S(2)}) collective-permute-start(bf16[4,2,2,24,384]{4,3,2,1,0:T(8,128)(2,1)} %get-tuple-element.109), channel_id=1, source_target_pairs={{0,2},{1,3},{2,0},{3,1},{4,6},{5,7},{6,4},{7,5},{8,10},{9,11},{10,... | collective-permute-start | bytes 884744 | tf_op jit(solution)/shard_map/ppermute | solution.py:581
  207.6 28.6 %collective-permute-start.26 = (bf16[8,24,768]{2,1,0:T(8,128)(2,1)}, bf16[8,24,768]{2,1,0:T(8,128)(2,1)S(1)}, u32[]{:S(2)}, u32[]{:S(2)}) collective-permute-start(bf16[8,24,768]{2,1,0:T(8,128)(2,1)} %bitcast.102), channel_id=1, source_target_pairs={{0,0},{1,16},{2,2},{3,18},{4,4},{5,20},{6,6},{7,22},{8,1},{9,17},{... | collective-permute-start | bytes 884744 | tf_op jit(solution)/shard_map/ppermute | solution.py:686
  209.3 30.8 %collective-permute-start.27 = (bf16[8,24,768]{2,1,0:T(8,128)(2,1)}, bf16[8,24,768]{2,1,0:T(8,128)(2,1)S(1)}, u32[]{:S(2)}, u32[]{:S(2)}) collective-permute-start(bf16[8,24,768]{2,1,0:T(8,128)(2,1)} %bitcast.101), channel_id=1, source_target_pairs={{0,1},{1,17},{2,3},{3,19},{4,5},{5,21},{6,7},{7,23},{8,0},{9,16},{... | collective-permute-start | bytes 884744 | tf_op jit(solution)/shard_map/ppermute | solution.py:686
  212.8 28.1 %collective-permute-start.28 = (bf16[8,24,768]{2,1,0:T(8,128)(2,1)}, bf16[8,24,768]{2,1,0:T(8,128)(2,1)S(1)}, u32[]{:S(2)}, u32[]{:S(2)}) collective-permute-start(bf16[8,24,768]{2,1,0:T(8,128)(2,1)} %bitcast.100), channel_id=1, source_target_pairs={{0,8},{1,24},{2,10},{3,26},{4,12},{5,28},{6,14},{7,30},{8,9},{9,25... | collective-permute-start | bytes 884744 | tf_op jit(solution)/shard_map/ppermute | solution.py:686
  216.6 26.8 %collective-permute-start.29 = (bf16[8,24,768]{2,1,0:T(8,128)(2,1)}, bf16[8,24,768]{2,1,0:T(8,128)(2,1)S(1)}, u32[]{:S(2)}, u32[]{:S(2)}) collective-permute-start(bf16[8,24,768]{2,1,0:T(8,128)(2,1)} %bitcast.99), channel_id=1, source_target_pairs={{0,9},{1,25},{2,11},{3,27},{4,13},{5,29},{6,15},{7,31},{8,8},{9,24... | collective-permute-start | bytes 884744 | tf_op jit(solution)/shard_map/ppermute | solution.py:686
  240.0 15.1 %collective-permute-start.34 = (bf16[4,24,768]{2,1,0:T(8,128)(2,1)}, bf16[4,24,768]{2,1,0:T(8,128)(2,1)S(1)}, u32[]{:S(2)}, u32[]{:S(2)}) collective-permute-start(bf16[4,24,768]{2,1,0:T(8,128)(2,1)} %bitcast.104), channel_id=1, source_target_pairs={{0,8},{1,24},{2,10},{3,26},{4,12},{5,28},{6,14},{7,30},{8,9},{9,25... | collective-permute-start | bytes 442376 | tf_op jit(solution)/shard_map/ppermute | solution.py:686
  240.9 14.2 %collective-permute-start.35 = (bf16[4,24,768]{2,1,0:T(8,128)(2,1)}, bf16[4,24,768]{2,1,0:T(8,128)(2,1)S(1)}, u32[]{:S(2)}, u32[]{:S(2)}) collective-permute-start(bf16[4,24,768]{2,1,0:T(8,128)(2,1)} %bitcast.103), channel_id=1, source_target_pairs={{0,9},{1,25},{2,11},{3,27},{4,13},{5,29},{6,15},{7,31},{8,8},{9,24... | collective-permute-start | bytes 442376 | tf_op jit(solution)/shard_map/ppermute | solution.py:686
  260.2 45.0 %all-to-all-start.1 = ((bf16[32,24,768]{2,1,0:T(8,128)(2,1)}), bf16[32,24,768]{2,1,0:T(8,128)(2,1)S(1)}, u32[]{:S(2)}, u32[]{:S(2)}) async-start(bf16[32,24,768]{2,1,0:T(8,128)(2,1)} %get-tuple-element.121), calls=%async_computation.1 | async-start | bytes 2359296 | tf_op jit(solution)/shard_map/all_to_all | solution.py:862
  284.9 16.9 %collective-permute-start.40 = (f32[16,768]{1,0:T(8,128)S(1)}, f32[16,768]{1,0:T(8,128)S(1)}, u32[]{:S(2)}, u32[]{:S(2)}) collective-permute-start(f32[16,768]{1,0:T(8,128)S(1)} %add.106), channel_id=1, source_target_pairs={{0,24},{1,25},{2,26},{3,27},{4,28},{5,29},{6,30},{7,31},{8,16},{9,... | collective-permute-start | bytes 147464 | tf_op jit(solution)/shard_map/ppermute | solution.py:701
  311.5 32.9 %all-to-all-start.2 = ((bf16[32,24,768]{2,1,0:T(8,128)(2,1)}), bf16[32,24,768]{2,1,0:T(8,128)(2,1)S(1)}, u32[]{:S(2)}, u32[]{:S(2)}) async-start(bf16[32,24,768]{2,1,0:T(8,128)(2,1)} %bitcast.88), calls=%async_computation.2 | async-start | bytes 2359296 | tf_op jit(solution)/shard_map/all_to_all | solution.py:862
  (51 other events, 473.5 us)
Sparse Core Ops, SparseCore 0:
  11.0 91.9 all-gather.1

commit v5 on v4

--- a/solution.py
+++ b/solution.py
@@ -3,6 +3,7 @@
 
 import jax
 import jax.numpy as jnp
+import numpy as np
 from jax import lax
 from jax.experimental import pallas as pl
 from jax.experimental.pallas import tpu as pltpu
@@ -35,7 +36,7 @@
     return lax.dot_general(left, right, dims, preferred_element_type=f32)
 
 
-def call(body, flops, moved, vmem=60, after=(), **rest):
+def call(body, flops, moved, vmem=63, after=(), **rest):
     spec = rest.pop("grid_spec", None)
     grid = spec.grid if spec is not None else rest.get("grid", ())
     later = len(after)
@@ -85,12 +86,12 @@
     )
     offset = (jnp.arange(length, dtype=jnp.int32)[None] - start).astype(f32).reshape(-1, 1)
     half = ROT // 2
-    lane = jnp.arange(LANES) % 64
-    rates = jnp.power(10000.0, -2.0 * jnp.arange(half, dtype=f32) / ROT)
-    angle = offset * jnp.where(lane < ROT, rates[lane % half], 0.0)[None]
+    lane = np.arange(LANES) % 64
+    rates = np.where(lane < ROT, 10000.0 ** (-2.0 * (lane % half) / ROT), 0.0)
+    angle = offset * jnp.asarray(rates, f32)[None]
     cosine, sine = jnp.cos(angle), jnp.sin(angle)
-    first = jnp.where(lane[None] < half, -sine, 0.0)
-    second = jnp.where((lane[None] >= half) & (lane[None] < ROT), sine, 0.0)
+    first = sine * jnp.asarray(np.where(lane < half, -1.0, 0.0), f32)[None]
+    second = sine * jnp.asarray(np.where((lane >= half) & (lane < ROT), 1.0, 0.0), f32)[None]
     return cosine, first, second
 
 
@@ -409,9 +410,9 @@
         sum_ref[0] += part
 
 
-def hidden(first, blocks, acts, weights, vecs, after=(), step=512):
+def hidden(first, acts, weights, vecs, after=(), step=512):
     _, count, width = acts.shape
-    splits = weights.shape[0] // 2
+    blocks = weights.shape[0] // 2
     both, sums = call(
         hidden_body,
         blocks * 4 * count * width * width,
@@ -421,9 +422,9 @@
         in_specs=[
             pl.BlockSpec((1, step, width), lambda j, i: (1, i, 0)),
             pl.BlockSpec((1, step, width), lambda j, i: (2, i, 0)),
-            pl.BlockSpec((1, width, width), lambda j, i: (first + j, 0, 0)),
-            pl.BlockSpec((1, width, width), lambda j, i: (splits + first + j, 0, 0)),
-            pl.BlockSpec((1, 1, width), lambda j, i: (8 + first + j, 0, 0)),
+            pl.BlockSpec((1, width, width), lambda j, i: (j, 0, 0)),
+            pl.BlockSpec((1, width, width), lambda j, i: (blocks + j, 0, 0)),
+            pl.BlockSpec((1, 1, width), lambda j, i: (first + j, 0, 0)),
         ],
         out_specs=[
             pl.BlockSpec((2, 1, step, width), lambda j, i: (0, j, i, 0)),
@@ -444,18 +445,17 @@
     return scale * (grad - first - unit * second)
 
 
-def hidden_sum(hidden_refs, w_ref, at, dims, acc):
-    for ref in hidden_refs:
+def hidden_sum(hidden_refs, w_refs, dims, acc):
+    for ref, w_ref in zip(hidden_refs, w_refs):
         for m in range(ref.shape[0]):
-            part = mm(ref[m], w_ref[at], dims)
+            part = mm(ref[m], w_ref[m], dims)
             acc = part if acc is None else acc + part
-            at += 1
     return acc
 
 
-def output_body(x_ref, o_ref, *refs, splits):
-    *e_refs, wo_ref, wm_ref, vec_ref, out_ref = refs
-    acc = hidden_sum(e_refs, wm_ref, 0, NN, mm(o_ref[0], wo_ref[0], NN))
+def output_body(x_ref, o_ref, *refs, parts, splits):
+    e_refs, wo_ref, w_refs, (vec_ref, out_ref) = refs[:parts], refs[parts], refs[parts + 1 : -2], refs[-2:]
+    acc = hidden_sum(e_refs, w_refs, NN, mm(o_ref[0], wo_ref[0], NN))
     bias = vec_ref[7:8, :] + vec_ref[8 + splits : 9 + splits, :]
     out_ref[...] = (x_ref[...].astype(f32) + acc + bias).astype(bf16)
 
@@ -466,20 +466,23 @@
 
 def output(x, o, es, wa, wm, vecs, after=(), step=256):
     count, width = x.shape
-    splits = wm.shape[0] // 2
+    half = wm[0].shape[0] // 2
+    splits = half * len(wm)
     token = pl.BlockSpec((step, width), lambda i: (i, 0))
     return call(
-        functools.partial(output_body, splits=splits),
+        functools.partial(output_body, parts=len(es), splits=splits),
         10 * count * width * width,
         14 * count * width + 10 * width * width,
         after=after,
         grid=(count // step,),
         in_specs=[token]
         + [layers(v, step, width) for v in (o, *es)]
-        + [resident(1, width, 3), resident(splits, width, 1), pl.BlockSpec(vecs.shape, lambda i: (0, 0))],
+        + [resident(1, width, 3)]
+        + [resident(half, width, 1)] * len(wm)
+        + [pl.BlockSpec(vecs.shape, lambda i: (0, 0))],
         out_specs=token,
         out_shape=jax.ShapeDtypeStruct((count, width), bf16),
-    )(x, *[v[0] for v in (o, *es)], wa, wm, vecs)
+    )(x, *[v[0] for v in (o, *es)], wa, *wm, vecs)
 
 
 def normed(x):
@@ -532,8 +535,9 @@
 
 
 def grad_two_body(x_ref, part_ref, *refs):
-    *du_refs, wm_ref, vec_ref, grad_ref, sum_ref = refs
-    grad = hidden_sum(du_refs, wm_ref, 0, NT, None)
+    parts = (len(refs) - 3) // 2
+    vec_ref, grad_ref, sum_ref = refs[2 * parts :]
+    grad = hidden_sum(refs[:parts], refs[parts : 2 * parts], NT, None)
     unit, scale = normed(x_ref[...].astype(f32))
     grad_ref[...] = (part_ref[...] + norm_back(grad, unit, scale, vec_ref[2:3, :])).astype(bf16)
     add_sums(sum_ref, (grad * unit, grad))
@@ -541,7 +545,6 @@
 
 def grad_two(x, part, dus, wm, vecs, after=(), step=256):
     count, width = x.shape
-    splits = wm.shape[0] // 2
     token = pl.BlockSpec((step, width), lambda i: (i, 0))
     return call(
         grad_two_body,
@@ -551,10 +554,11 @@
         grid=(count // step,),
         in_specs=[token, token]
         + [layers(v, step, width) for v in dus]
-        + [resident(splits, width, 0), pl.BlockSpec(vecs.shape, lambda i: (0, 0))],
+        + [resident(w.shape[0] // 2, width, 0) for w in wm]
+        + [pl.BlockSpec(vecs.shape, lambda i: (0, 0))],
         out_specs=[token, pl.BlockSpec((2, 8, width), lambda i: (0, 0, 0))],
         out_shape=[jax.ShapeDtypeStruct((count, width), bf16), jax.ShapeDtypeStruct((2, 8, width), f32)],
-    )(x, part, *[v[0] for v in dus], wm, vecs)
+    )(x, part, *[v[0] for v in dus], *wm, vecs)
 
 
 def grid_places():
@@ -691,15 +695,17 @@
 
 
 def everywhere(value):
-    for move in (
-        lambda z, y, x, c: (z, y, x, 1 - c),
-        lambda z, y, x, c: (z, y, 1 - x, c),
-        lambda z, y, x, c: (z, 1 - y, x, c),
-        lambda z, y, x, c: (z ^ 1, y, x, c),
-        lambda z, y, x, c: (3 - z, y, x, c),
-    ):
-        value = value + lax.ppermute(value, AXES, to_place(move))
-    return value
+    def get(move):
+        return lax.ppermute(value, AXES, to_place(move))
+
+    value = value + over_c(value)
+    by_x, by_y = over_x(value), over_y(value)
+    across = get(lambda z, y, x, c: (z, 1 - y, 1 - x, c))
+    value = (value + by_x) + (by_y + across)
+    near = get(lambda z, y, x, c: (z ^ 1, y, x, c))
+    far = get(lambda z, y, x, c: (z ^ 2, y, x, c))
+    last = get(lambda z, y, x, c: (z ^ 3, y, x, c))
+    return (value + near) + (far + last)
 
 
 def pack_body(slot_ref, *refs, orders, per):
@@ -889,7 +895,11 @@
     everyone = jnp.broadcast_to(low_vectors.reshape(1, -1), (slot_count, vec_rows * shard))
     vecs = to_all(everyone).reshape(slot_count, vec_rows, shard)
     vecs = vecs.transpose(1, 0, 2).reshape(vec_rows, width).astype(f32)
-    mlp_weights = lax.all_gather(low_blocks[4:], AXES, axis=1, tiled=True)
+    half = splits // 2
+    mlp_weights = []
+    for first in (4, 4 + half):
+        part = jnp.concatenate([low_blocks[first : first + half], low_blocks[first + splits : first + splits + half]])
+        mlp_weights.append(lax.all_gather(part, AXES, axis=1, tiled=True))
 
     flat_tokens = tokens.reshape(count, width)
     dy = cotangent.reshape(count, width)
@@ -901,16 +911,15 @@
         pieces = [lax.all_gather(low_blocks[:4], AXES, axis=1, tiled=True)]
     q, k, v, do, acts, attn_weights = project(place, flat_tokens, dy, pieces, vecs, tables)
     og, attn_sums, acts = attend(segment_ids, q, k, v, do, tables, acts)
-    half = splits // 2
     orders = [list(range(4))]
     for first in (0, half):
         orders.append([base + first + j for base in (4, 4 + splits) for j in range(half)])
     if paired:
         acts_pair, og_pair = (acts, over_c(acts)), (og, over_c(og))
         dys = (acts_pair, 2, 1)
-        ed0, up_sum0 = hidden(0, half, acts, mlp_weights, vecs)
+        ed0, up_sum0 = hidden(8, acts, mlp_weights[0], vecs)
         ed0_pair = (ed0, over_c(ed0))
-        ed1, up_sum1 = hidden(half, half, acts, mlp_weights, vecs, after=(ed0, acts_pair[1]))
+        ed1, up_sum1 = hidden(8 + half, acts, mlp_weights[1], vecs, after=(ed0, acts_pair[1]))
         ed1_pair = (ed1, over_c(ed1))
 
         def grads(left, two, one, after):
@@ -927,10 +936,11 @@
         es, dus = [(v, 0, half) for v in (ed0, ed1)], [(v, half, half) for v in (ed0, ed1)]
         grad_in, two_sums = grad_two(flat_tokens, part, dus, mlp_weights, vecs, after=(high.made,))
         terms.append(advance(place, [], [high], after=(grad_in,)))
+        last = high.made
         orders = [orders[0] + orders[1], orders[2]]
     else:
-        ed0, up_sum0 = hidden(0, half, acts, mlp_weights, vecs)
-        ed1, up_sum1 = hidden(half, half, acts, mlp_weights, vecs)
+        ed0, up_sum0 = hidden(8, acts, mlp_weights[0], vecs)
+        ed1, up_sum1 = hidden(8 + half, acts, mlp_weights[1], vecs)
         grads = [
             full_grads(acts[0], og[3:], og[:3], dy),
             full_grads(acts[1], ed0[:half], ed0[half:], dy),
@@ -940,6 +950,7 @@
         es, dus = [(v, 0, half) for v in (ed0, ed1)], [(v, half, half) for v in (ed0, ed1)]
         part, one_sums = grad_one(flat_tokens, dy, (og, 0, 3), attn_weights, vecs)
         grad_in, two_sums = grad_two(flat_tokens, part, dus, mlp_weights, vecs)
+        last = grad_in
     up_sums = [up_sum0, up_sum1]
 
     one_sums, two_sums = jnp.sum(one_sums, axis=1), jnp.sum(two_sums, axis=1)
@@ -953,9 +964,9 @@
     match = owners[None, :] == slot_ids[:, None]
     slots = jnp.sum(jnp.where(match, jnp.arange(1, owners.shape[0] + 1, dtype=jnp.int32)[None], 0), axis=1) - 1
     has_block = jnp.any(owners == my_index)
-    shards, outgoing, squares = pack(slots, terms, orders, after=(grad_in,))
-    out = output(flat_tokens, (og, 3, 1), es, attn_weights, mlp_weights, vecs, after=(squares,))
-    left_low, right_low = to_low(root_left[0], root_right[0], after=(out,))
+    out = output(flat_tokens, (og, 3, 1), es, attn_weights, mlp_weights, vecs, after=(last,))
+    shards, outgoing, squares = pack(slots, terms, orders, after=(out,))
+    left_low, right_low = to_low(root_left[0], root_right[0], after=(squares,))
     local = jnp.concatenate([grad_vectors, jnp.sum(squares, axis=0)[None], jnp.zeros((2, width), f32)])
     total = everywhere(local) if paired else lax.psum(local, AXES)
     vector_sums = total[:vec_rows]

time: 358 us -> 380 us (1.061)
  waiting for transfers between devices: 78.3 us -> 106 us
  local copies, waits for them, and re-layouts: 13.6 us -> 8.79 us
    all_gather x1 -> x2, waiting for transfers between devices: 0.98 us -> 33.8 us  [per_device(): mlp_weights.append(lax.all_gather(part, AXES, axis=1, tiled=True))]
    ppermute x8 -> x9, waiting for transfers between devices: 0.97 us -> 18.9 us  [over_y(): lax.ppermute(value, AXES, to_place(lambda z, y, x, c: (z, 1 - y, x, c)))]
    ppermute x8, waiting for transfers between devices: 12.6 us -> 0.02 us  [advance(): lax.ppermute(v, AXES, to_place(lambda z, y, x, c, m=m: (2 * c + ((z ^ m)...]
    ppermute x8 -> x9, waiting for transfers between devices: 22.7 us -> 11.3 us  [over_x(): lax.ppermute(value, AXES, to_place(lambda z, y, x, c: (z, y, 1 - x, c)))]
    select_n x2 -> x0, other arithmetic: 8.39 us -> none  [the longest x1 5.18 us: rotary_tables(): angle = offset * jnp.where(lane < ROT, rates[lane % half], 0.0)[None]]
    ppermute x5 -> x4, waiting for transfers between devices: 17.8 us -> 11.2 us  [get(): return lax.ppermute(value, AXES, to_place(move))]
    ppermute x3, waiting for transfers between devices: 3.27 us -> 9.35 us  [over_z(): lax.ppermute(value, AXES, to_place(lambda z, y, x, c: ((z + by) % 4, y, x...]
    all_to_all x3, starting transfers between devices: 9.54 us -> 13.8 us  [to_all(): return lax.all_to_all(value, AXES, split_axis=0, concat_axis=0, tiled=True)]
  transfers between devices with their start and end apart: 45 -> 48, of which waited for: 16 -> 14; matrix products, arithmetic and copies ran while one was open for 6% -> 4% of each run, Pallas kernels for 42% -> 40%
where the time goes in v5:
time: 380 us; the launch traced here: 379 us
  Pallas kernels  167 us (44%)
  waiting for transfers between devices  106 us (28%)
  starting transfers between devices  67.4 us (18%)
  between operations  17.9 us (5%)
  other arithmetic  12.4 us (3%)
  local copies, waits for them, and re-layouts  8.79 us (2%)
    pallas_call x19, Pallas kernels, call(): return lambda *operands: made(*operands, *after)  167 us
    all_gather x2, waiting for transfers between devices, per_device(): mlp_weights.append(lax.all_gather(part, AXES, axis=1, tiled=True))  33.8 us
    all_to_all x3, waiting for transfers between devices, to_all(): return lax.all_to_all(value, AXES, split_axis=0, concat_axis=0, tiled=True)  19.9 us
    ppermute x9, waiting for transfers between devices, over_y(): lax.ppermute(value, AXES, to_place(lambda z, y, x, c: (z, 1 - y, x, c)))  18.9 us
    ppermute x8, starting transfers between devices, advance(): lax.ppermute(v, AXES, to_place(lambda z, y, x, c, m=m: (2 * c + ((z ^ m)...  16.7 us
    all_to_all x3, starting transfers between devices, to_all(): return lax.all_to_all(value, AXES, split_axis=0, concat_axis=0, tiled=True)  13.8 us
    ppermute x9, starting transfers between devices, over_x(): lax.ppermute(value, AXES, to_place(lambda z, y, x, c: (z, y, 1 - x, c)))  12.7 us
    ppermute x9, waiting for transfers between devices, over_x(): lax.ppermute(value, AXES, to_place(lambda z, y, x, c: (z, y, 1 - x, c)))  11.3 us
  transfers between devices with their start and end apart: 48, of which 14 were waited for; matrix products, arithmetic and copies ran while one was open for 4% of the time, Pallas kernels for 40%

profile of v5, /device:TPU:0, one launch (start us, length us, event | category | flops | bytes accessed | tf_op | source)
XLA Modules:
  0.0 378.8 jit_solution(15185515965730097153)
XLA Ops:
  10.0 4.1 %collective-permute-start.1 = (bf16[4,24,768]{2,1,0:T(8,128)(2,1)S(1)}, bf16[4,24,768]{2,1,0:T(8,128)(2,1)S(1)}, u32[]{:S(2)}, u32[]{:S(2)}) collective-permute-start(bf16[4,24,768]{2,1,0:T(8,128)(2,1)S(1)} %get-tuple-element.139), channel_id=1, source_target_pairs={{0,16},{1,17},{2,18},{3,19},{4,20},{5,21},{6,22},{7,23},{8,24},{9,... | collective-permute-start | bytes 442376 | tf_op jit(solution)/shard_map/ppermute | solution.py:593
  16.1 6.6 %collective-permute-done.1 = bf16[4,24,768]{2,1,0:T(8,128)(2,1)S(1)} collective-permute-done((bf16[4,24,768]{2,1,0:T(8,128)(2,1)S(1)}, bf16[4,24,768]{2,1,0:T(8,128)(2,1)S(1)}, u32[]{:S(2)}, u32[]{:S(2)}) %collective-permute-start.1) | collective-permute-done | bytes 147488 | tf_op jit(solution)/shard_map/ppermute | solution.py:593
  30.8 6.6 %all-to-all-start = ((bf16[32,2,156]{2,1,0:T(2,128)(2,1)}), bf16[32,2,156]{2,1,0:T(2,128)(2,1)S(1)}, u32[]{:S(2)}, u32[]{:S(2)}) async-start(bf16[32,2,156]{2,1,0:T(2,128)(2,1)} %reshape.167), calls=%async_computation | async-start | bytes 65536 | tf_op jit(solution)/shard_map/all_to_all | solution.py:868
  43.6 3.2 fusion
  57.0 14.3 %shard_map.229 = (bf16[1024,768]{1,0:T(8,128)(2,1)}, bf16[1024,768]{1,0:T(8,128)(2,1)}, bf16[1024,768]{1,0:T(8,128)(2,1)}, bf16[1024,768]{1,0:T(8,128)(2,1)}, bf...) custom-call(s32[4]{0:T(128)} %pad_add_fusion.place_ref.refs_0_, bf16[1024,768]{1,0:T(8,128)(2,1)} %bitcast.58, ...), custom_call_target="tpu_custom_call" | custom-call | flops 4831838208 | bytes 25165824 | tf_op jit(solution)/shard_map/pallas_call | solution.py:75
  71.3 25.5 %shard_map.230 = (bf16[4,1024,768]{2,1,0:T(8,128)(2,1)}, f32[3,16,768]{2,1,0:T(8,128)}, bf16[3,1024,768]{2,1,0:T(8,128)(2,1)}) custom-call(bf16[3,1024,768]{2,1,0:T(8,128)(2,1)} %get-tuple-element.71.acts_ref, s32[1024,1]{1,0:T(8,128)} %bitcast.69, s32[2,1,512]{2,1,0:T(1,128)} %broadcast_in_dim.46.row_ref, ...), custom_call_target="tpu_custom_call", output_to_operand_aliasing={{2}: (0, {})} | custom-call | flops 9663676416 | bytes 18874368 | tf_op jit(solution)/shard_map/pallas_call | solution.py:75
  98.3 12.7 %shard_map.231 = (bf16[2,2,1024,768]{3,2,1,0:T(8,128)(2,1)}, f32[2,8,768]{2,1,0:T(8,128)}) custom-call(bf16[3,1024,768]{2,1,0:T(8,128)(2,1)} %get-tuple-element.77.a2_ref.dy_ref.refs_0_.refs_1_.refs_7_, bf16[3,1024,768]{2,1,0:T(8,128)(2,1)} %get-tuple-element.77.a2_ref.dy_ref.refs_0_.refs_1_.refs_7_, ...), custom_call_target="tpu_custom_call" | custom-call | flops 4831838208 | bytes 17301504 | tf_op jit(solution)/shard_map/pallas_call | solution.py:75
  111.4 33.8 %all-gather.5.cloned.1.call-done.refs_2_.refs_3_.refs_5_.refs_6_ = bf16[4,768,768]{2,1,0:T(8,128)(2,1)} async-done(((bf16[4,24,768]{2,1,0:T(8,128)(2,1)}), bf16[4,768,768]{2,1,0:T(8,128)(2,1)}) %all-gather.5.cloned.1.call-update) | async-done | bytes 4718608 | tf_op jit(solution)/shard_map/all_gather | solution.py:902
  145.2 12.5 %shard_map.232 = (bf16[2,2,1024,768]{3,2,1,0:T(8,128)(2,1)}, f32[2,8,768]{2,1,0:T(8,128)}) custom-call(bf16[3,1024,768]{2,1,0:T(8,128)(2,1)} %get-tuple-element.77.a2_ref.dy_ref.refs_0_.refs_1_.refs_7_, bf16[3,1024,768]{2,1,0:T(8,128)(2,1)} %get-tuple-element.77.a2_ref.dy_ref.refs_0_.refs_1_.refs_7_, ...), custom_call_target="tpu_custom_call" | custom-call | flops 4831838208 | bytes 17301504 | tf_op jit(solution)/shard_map/pallas_call | solution.py:75
  158.0 11.4 %shard_map.233 = (bf16[4,2,2,2,24,384]{5,4,3,2,1,0:T(8,128)(2,1)}, bf16[4,2,2,2,24,384]{5,4,3,2,1,0:T(8,128)(2,1)}, bf16[4,2,2,2,24,384]{5,4,3,2,1,0:T(8,128)(2,1)}, bf16[4,2,2,2,24,384]{5,4,3,2,1,0:T(8,128)(2,1)}) custom-call(s32[4]{0:T(128)} %pad_add_fusion.place_ref.refs_0_, bf16[3,1024,768]{2,1,0:T(8,128)(2,1)} %get-tuple-element.77.a2_ref.dy_ref.refs_0_.refs_1_.refs_7_, ...), custom_call_target="tpu_custom_call" | custom-call | flops 4831838208 | bytes 12582912 | tf_op jit(solution)/shard_map/pallas_call | solution.py:75
  171.5 11.2 %shard_map.234 = (bf16[4,2,2,2,24,384]{5,4,3,2,1,0:T(8,128)(2,1)}, bf16[4,2,2,2,24,384]{5,4,3,2,1,0:T(8,128)(2,1)}, bf16[4,2,2,2,24,384]{5,4,3,2,1,0:T(8,128)(2,1)}, bf16[4,2,2,2,24,384]{5,4,3,2,1,0:T(8,128)(2,1)}) custom-call(s32[4]{0:T(128)} %pad_add_fusion.place_ref.refs_0_, bf16[3,1024,768]{2,1,0:T(8,128)(2,1)} %get-tuple-element.77.a2_ref.dy_ref.refs_0_.refs_1_.refs_7_, ...), custom_call_target="tpu_custom_call" | custom-call | flops 4831838208 | bytes 12582912 | tf_op jit(solution)/shard_map/pallas_call | solution.py:75
  189.6 11.2 %shard_map.236 = (bf16[4,2,2,2,24,384]{5,4,3,2,1,0:T(8,128)(2,1)}, bf16[4,2,2,2,24,384]{5,4,3,2,1,0:T(8,128)(2,1)}, bf16[4,2,2,2,24,384]{5,4,3,2,1,0:T(8,128)(2,1)}, bf16[4,2,2,2,24,384]{5,4,3,2,1,0:T(8,128)(2,1)}) custom-call(s32[4]{0:T(128)} %pad_add_fusion.place_ref.refs_0_, bf16[3,1024,768]{2,1,0:T(8,128)(2,1)} %get-tuple-element.77.a2_ref.dy_ref.refs_0_.refs_1_.refs_7_, ...), custom_call_target="tpu_custom_call" | custom-call | flops 4831838208 | bytes 12582912 | tf_op jit(solution)/shard_map/pallas_call | solution.py:75
  205.4 3.1 shard_map.237
  209.4 14.7 %collective-permute-done.20.refs_6_ = bf16[4,2,2,24,384]{4,3,2,1,0:T(8,128)(2,1)S(1)} collective-permute-done((bf16[4,2,2,24,384]{4,3,2,1,0:T(8,128)(2,1)}, bf16[4,2,2,24,384]{4,3,2,1,0:T(8,128)(2,1)S(1)}, u32[]{:S(2)}, u32[]{:S(2)}) %collective-permute-start.20) | collective-permute-done | bytes 294944 | tf_op jit(solution)/shard_map/ppermute | solution.py:589
  225.6 9.7 %shard_map.238 = (f32[1024,768]{1,0:T(8,128)}, f32[3,8,768]{2,1,0:T(8,128)}) custom-call(bf16[1024,768]{1,0:T(8,128)(2,1)} %bitcast.59, bf16[1024,768]{1,0:T(8,128)(2,1)} %bitcast.67, bf16[4,1024,768]{2,1,0:T(8,128)(2,1)} %get-tuple-element.76.refs_3_.refs_5_.refs_2_.refs_1_, bf16[4,768,768]{2,1,0:T(8,128)(2,1)} %get-tuple-element.80.refs_3_.refs_4_, ...), custom_call_target="tpu_custom_call" | custom-call | flops 3623878656 | bytes 14548992 | tf_op jit(solution)/shard_map/pallas_call | solution.py:75
  236.2 4.2 %shard_map.239 = (bf16[4,2,2,24,384]{4,3,2,1,0:T(8,128)(2,1)}, bf16[4,2,2,24,384]{4,3,2,1,0:T(8,128)(2,1)}, bf16[4,2,2,24,384]{4,3,2,1,0:T(8,128)(2,1)}, bf16[4,...) custom-call(s32[4]{0:T(128)} %pad_add_fusion.place_ref.refs_0_, ...), custom_call_target="tpu_custom_call" | custom-call | bytes 9437184 | tf_op jit(solution)/shard_map/pallas_call | solution.py:75
  246.7 11.0 %shard_map.240 = (bf16[1024,768]{1,0:T(8,128)(2,1)}, f32[2,8,768]{2,1,0:T(8,128)}) custom-call(bf16[1024,768]{1,0:T(8,128)(2,1)} %bitcast.60, f32[1024,768]{1,0:T(8,128)} %get-tuple-element.101.refs_13_.refs_1_, bf16[4,1024,768]{2,1,0:T(8,128)(2,1)} %bitcast.56, bf16[4,1024,768]{2,1,0:T(8,128)(2,1)} %bitcast.50, ...), custom_call_target="tpu_custom_call" | custom-call | flops 4831838208 | bytes 17301504 | tf_op jit(solution)/shard_map/pallas_call | solution.py:75
  257.7 3.3 collective-permute-start.31
  266.1 3.8 collective-permute-start.33
  269.9 3.9 %collective-permute-start.35 = (bf16[4,24,768]{2,1,0:T(8,128)(2,1)}, bf16[4,24,768]{2,1,0:T(8,128)(2,1)S(1)}, u32[]{:S(2)}, u32[]{:S(2)}) collective-permute-start(bf16[4,24,768]{2,1,0:T(8,128)(2,1)} %bitcast.71), channel_id=1, source_target_pairs={{0,9},{1,25},{2,11},{3,27},{4,13},{5,29},{6,15},{7,31},{8,8},{9,24... | collective-permute-start | bytes 442376 | tf_op jit(solution)/shard_map/ppermute | solution.py:690
  273.8 11.2 %shard_map.242.refs_9_ = bf16[1024,768]{1,0:T(8,128)(2,1)} custom-call(bf16[1024,768]{1,0:T(8,128)(2,1)} %bitcast.61, bf16[4,1024,768]{2,1,0:T(8,128)(2,1)} %get-tuple-element.76.refs_3_.refs_5_.refs_2_.refs_1_, bf16[4,1024,768]{2,1,0:T(8,128)(2,1)} %bitcast.57, bf16[4,1024,768]{2,1,0:T(8,128)(2,1)} %bitcast.51, ...), custom_call_target="tpu_custom_call" | custom-call | flops 6039797760 | bytes 16908288 | tf_op jit(solution)/shard_map/pallas_call | solution.py:75
  286.4 3.7 shard_map.243
  290.1 3.6 all-to-all-start.1
  299.7 5.9 %collective-permute-done.37 = f32[16,768]{1,0:T(8,128)S(1)} collective-permute-done((f32[16,768]{1,0:T(8,128)S(1)}, f32[16,768]{1,0:T(8,128)S(1)}, u32[]{:S(2)}, u32[]{:S(2)}) %collective-permute-start.37) | collective-permute-done | bytes 49184 | tf_op jit(solution)/shard_map/ppermute | solution.py:585
  307.7 5.7 %collective-permute-start.41 = (f32[16,768]{1,0:T(8,128)S(1)}, f32[16,768]{1,0:T(8,128)S(1)}, u32[]{:S(2)}, u32[]{:S(2)}) collective-permute-start(f32[16,768]{1,0:T(8,128)S(1)} %add_add_fusion.1), channel_id=1, source_target_pairs={{0,16},{1,17},{2,18},{3,19},{4,20},{5,21},{6,22},{7,23},{8,24},{9,... | collective-permute-start | bytes 147464 | tf_op jit(solution)/shard_map/ppermute | solution.py:699
  313.3 3.5 shard_map.244
  316.8 9.5 %collective-permute-done.41 = f32[16,768]{1,0:T(8,128)S(1)} collective-permute-done((f32[16,768]{1,0:T(8,128)S(1)}, f32[16,768]{1,0:T(8,128)S(1)}, u32[]{:S(2)}, u32[]{:S(2)}) %collective-permute-start.41) | collective-permute-done | bytes 49184 | tf_op jit(solution)/shard_map/ppermute | solution.py:699
  329.7 5.3 %shard_map.245 = bf16[768,768]{1,0:T(8,128)(2,1)} custom-call(f32[2]{0:T(128)} %pad_maximum_fusion.3.scale_ref, bf16[768,768]{1,0:T(8,128)(2,1)} %bitcast.27.s_ref, bf16[768,768]{1,0:T(8,128)(2,1)} %get-tuple-element.122.l_ref, bf16[768,768]{1,0:T(8,128)(2,1)} %get-tuple-element.123.r_ref), custom_call_target="tpu_custom_call" | custom-call | flops 1811939328 | bytes 4718592 | tf_op jit(solution)/shard_map/pallas_call | solution.py:75
  335.0 3.5 all-to-all-start.2
  340.5 7.1 %shard_map.247 = (f32[768,768]{1,0:T(8,128)}, f32[768,768]{1,0:T(8,128)}) custom-call(s32[1]{0:T(128)} %bitcast.31.has_ref, f32[2]{0:T(128)} %pad_maximum_fusion.3.scale_ref, bf16[768,768]{1,0:T(8,128)(2,1)} %bitcast.27.s_ref, f32[768,768]{1,0:T(8,128)} %bitcast.78, f32[768,768]{1,0:T(8,128)} %bitcast.79), custom_call_target="tpu_custom_call" | custom-call | flops 1811939328 | bytes 10616832 | tf_op jit(solution)/shard_map/pallas_call | solution.py:75
  347.6 19.9 %all-to-all-done.2.p_ref = bf16[32,24,768]{2,1,0:T(8,128)(2,1)} async-done(((bf16[32,24,768]{2,1,0:T(8,128)(2,1)}), bf16[32,24,768]{2,1,0:T(8,128)(2,1)}, u32[]{:S(2)}, u32[]{:S(2)}) %all-to-all-start.2) | async-done | bytes 1179680 | tf_op jit(solution)/shard_map/all_to_all | solution.py:868
  367.5 3.3 shard_map.246
  (188 shorter events, 71.8 us)
Async XLA Ops:
  7.2 91.1 %all-gather.3.cloned.1.call-start = ((), (), s32[]{:S(2)}) async-start(), calls=%async_computation.3 | async-start | bytes 4866048 | tf_op jit(solution)/shard_map/all_gather | solution.py:902
  9.2 136.0 %all-gather.5.cloned.1.call-start = ((), (), s32[]{:S(2)}) async-start(), calls=%async_computation.4 | async-start | bytes 4866048 | tf_op jit(solution)/shard_map/all_gather | solution.py:902
  25.6 14.2 %collective-permute-start.3 = (bf16[4,4,24,768]{3,2,1,0:T(8,128)(2,1)S(1)}, bf16[4,4,24,768]{3,2,1,0:T(8,128)(2,1)S(1)}, u32[]{:S(2)}, u32[]{:S(2)}) collective-permute-start(bf16[4,4,24,768]{3,2,1,0:T(8,128)(2,1)S(1)} %pad_maximum_fusion.refs_0_), channel_id=1, source_target_pairs={{0,2},{1,3},{2,0},{3,1},{4,6},{5,7},{6,4},{7,5},{8,10},{9,11},{10,... | collective-permute-start | bytes 1769480 | tf_op jit(solution)/shard_map/ppermute | solution.py:585
  27.1 14.3 %collective-permute-start.4 = (bf16[4,4,24,768]{3,2,1,0:T(8,128)(2,1)S(1)}, bf16[4,4,24,768]{3,2,1,0:T(8,128)(2,1)S(1)}, u32[]{:S(2)}, u32[]{:S(2)}) collective-permute-start(bf16[4,4,24,768]{3,2,1,0:T(8,128)(2,1)S(1)} %pad_maximum_fusion.refs_0_), channel_id=1, source_target_pairs={{0,4},{1,5},{2,6},{3,7},{4,0},{5,1},{6,2},{7,3},{8,12},{9,13},{10,... | collective-permute-start | bytes 1769480 | tf_op jit(solution)/shard_map/ppermute | solution.py:589
  30.8 24.2 %all-to-all-start = ((bf16[32,2,156]{2,1,0:T(2,128)(2,1)}), bf16[32,2,156]{2,1,0:T(2,128)(2,1)S(1)}, u32[]{:S(2)}, u32[]{:S(2)}) async-start(bf16[32,2,156]{2,1,0:T(2,128)(2,1)} %reshape.167), calls=%async_computation | async-start | bytes 65536 | tf_op jit(solution)/shard_map/all_to_all | solution.py:868
  43.0 13.2 %collective-permute-start.8 = (bf16[4,4,24,768]{3,2,1,0:T(8,128)(2,1)S(1)}, bf16[4,4,24,768]{3,2,1,0:T(8,128)(2,1)}, u32[]{:S(2)}, u32[]{:S(2)}) collective-permute-start(bf16[4,4,24,768]{3,2,1,0:T(8,128)(2,1)S(1)} %collective-permute-done.3.refs_1_), channel_id=1, source_target_pairs={{0,1},{1,0},{2,3},{3,2},{4,5},{5,4},{6,7},{7,6},{8,9},{9,8},{10,11... | collective-permute-start | bytes 1769480 | tf_op jit(solution)/shard_map/ppermute | solution.py:581
  96.8 14.6 %collective-permute-start.12 = (bf16[3,1024,768]{2,1,0:T(8,128)(2,1)}, bf16[3,1024,768]{2,1,0:T(8,128)(2,1)}, u32[]{:S(2)}, u32[]{:S(2)}) collective-permute-start(bf16[3,1024,768]{2,1,0:T(8,128)(2,1)} %get-tuple-element.77.a2_ref.dy_ref.refs_0_.refs_1_.refs_7_), channel_id=1, source_target_pairs={{0,1},{1,0},{2,3},{3,2},{4,5},{5,4},{6,7},{7,6},{8,9},{9,8},{10,11... | collective-permute-start | bytes 14155784 | tf_op jit(solution)/shard_map/ppermute | solution.py:581
  97.5 60.6 %collective-permute-start.14 = (bf16[4,1024,768]{2,1,0:T(8,128)(2,1)}, bf16[4,1024,768]{2,1,0:T(8,128)(2,1)}, u32[]{:S(2)}, u32[]{:S(2)}) collective-permute-start(bf16[4,1024,768]{2,1,0:T(8,128)(2,1)} %get-tuple-element.76.refs_3_.refs_5_.refs_2_.refs_1_), channel_id=1, source_target_pairs={{0,1},{1,0},{2,3},{3,2},{4,5},{5,4},{6,7},{7,6},{8,9},{9,8},{10,11... | collective-permute-start | bytes 18874376 | tf_op jit(solution)/shard_map/ppermute | solution.py:581
  111.0 60.5 %collective-permute-start.17 = (bf16[4,1024,768]{2,1,0:T(8,128)(2,1)}, bf16[4,1024,768]{2,1,0:T(8,128)(2,1)}, u32[]{:S(2)}, u32[]{:S(2)}) collective-permute-start(bf16[4,1024,768]{2,1,0:T(8,128)(2,1)} %bitcast.52), channel_id=1, source_target_pairs={{0,1},{1,0},{2,3},{3,2},{4,5},{5,4},{6,7},{7,6},{8,9},{9,8},{10,11... | collective-permute-start | bytes 18874376 | tf_op jit(solution)/shard_map/ppermute | solution.py:581
  157.8 31.8 %collective-permute-start.13 = (bf16[4,1024,768]{2,1,0:T(8,128)(2,1)}, bf16[4,1024,768]{2,1,0:T(8,128)(2,1)}, u32[]{:S(2)}, u32[]{:S(2)}) collective-permute-start(bf16[4,1024,768]{2,1,0:T(8,128)(2,1)} %bitcast.46), channel_id=1, source_target_pairs={{0,1},{1,0},{2,3},{3,2},{4,5},{5,4},{6,7},{7,6},{8,9},{9,8},{10,11... | collective-permute-start | bytes 18874376 | tf_op jit(solution)/shard_map/ppermute | solution.py:581
  169.5 15.8 %collective-permute-start.15 = (bf16[4,2,2,2,24,384]{5,4,3,2,1,0:T(8,128)(2,1)}, bf16[4,2,2,2,24,384]{5,4,3,2,1,0:T(8,128)(2,1)}, u32[]{:S(2)}, u32[]{:S(2)}) collective-permute-start(bf16[4,2,2,2,24,384]{5,4,3,2,1,0:T(8,128)(2,1)} %get-tuple-element.82), channel_id=1, source_target_pairs={{0,2},{1,3},{2,0},{3,1},{4,6},{5,7},{6,4},{7,5},{8,10},{9,11},{10,... | collective-permute-start | bytes 1769480 | tf_op jit(solution)/shard_map/ppermute | solution.py:585
  170.9 15.5 %collective-permute-start.16 = (bf16[4,2,2,2,24,384]{5,4,3,2,1,0:T(8,128)(2,1)}, bf16[4,2,2,2,24,384]{5,4,3,2,1,0:T(8,128)(2,1)}, u32[]{:S(2)}, u32[]{:S(2)}) collective-permute-start(bf16[4,2,2,2,24,384]{5,4,3,2,1,0:T(8,128)(2,1)} %get-tuple-element.84), channel_id=1, source_target_pairs={{0,4},{1,5},{2,6},{3,7},{4,0},{5,1},{6,2},{7,3},{8,12},{9,13},{10,... | collective-permute-start | bytes 1769480 | tf_op jit(solution)/shard_map/ppermute | solution.py:589
  182.7 21.3 %collective-permute-start.22 = (bf16[4,2,2,2,24,384]{5,4,3,2,1,0:T(8,128)(2,1)}, bf16[4,2,2,2,24,384]{5,4,3,2,1,0:T(8,128)(2,1)S(1)}, u32[]{:S(2)}, u32[]{:S(2)}) collective-permute-start(bf16[4,2,2,2,24,384]{5,4,3,2,1,0:T(8,128)(2,1)} %get-tuple-element.94), channel_id=1, source_target_pairs={{0,2},{1,3},{2,0},{3,1},{4,6},{5,7},{6,4},{7,5},{8,10},{9,11},{10,... | collective-permute-start | bytes 1769480 | tf_op jit(solution)/shard_map/ppermute | solution.py:585
  184.1 21.3 %collective-permute-start.23 = (bf16[4,2,2,2,24,384]{5,4,3,2,1,0:T(8,128)(2,1)}, bf16[4,2,2,2,24,384]{5,4,3,2,1,0:T(8,128)(2,1)}, u32[]{:S(2)}, u32[]{:S(2)}) collective-permute-start(bf16[4,2,2,2,24,384]{5,4,3,2,1,0:T(8,128)(2,1)} %get-tuple-element.96), channel_id=1, source_target_pairs={{0,4},{1,5},{2,6},{3,7},{4,0},{5,1},{6,2},{7,3},{8,12},{9,13},{10,... | collective-permute-start | bytes 1769480 | tf_op jit(solution)/shard_map/ppermute | solution.py:589
  200.8 34.6 %collective-permute-start.18 = (bf16[4,2,2,2,24,384]{5,4,3,2,1,0:T(8,128)(2,1)}, bf16[4,2,2,2,24,384]{5,4,3,2,1,0:T(8,128)(2,1)}, u32[]{:S(2)}, u32[]{:S(2)}) collective-permute-start(bf16[4,2,2,2,24,384]{5,4,3,2,1,0:T(8,128)(2,1)} %get-tuple-element.88), channel_id=1, source_target_pairs={{0,2},{1,3},{2,0},{3,1},{4,6},{5,7},{6,4},{7,5},{8,10},{9,11},{10,... | collective-permute-start | bytes 1769480 | tf_op jit(solution)/shard_map/ppermute | solution.py:585
  201.4 34.0 %collective-permute-start.19 = (bf16[4,2,2,2,24,384]{5,4,3,2,1,0:T(8,128)(2,1)}, bf16[4,2,2,2,24,384]{5,4,3,2,1,0:T(8,128)(2,1)}, u32[]{:S(2)}, u32[]{:S(2)}) collective-permute-start(bf16[4,2,2,2,24,384]{5,4,3,2,1,0:T(8,128)(2,1)} %get-tuple-element.90), channel_id=1, source_target_pairs={{0,4},{1,5},{2,6},{3,7},{4,0},{5,1},{6,2},{7,3},{8,12},{9,13},{10,... | collective-permute-start | bytes 1769480 | tf_op jit(solution)/shard_map/ppermute | solution.py:589
  202.8 21.3 %collective-permute-start.20 = (bf16[4,2,2,24,384]{4,3,2,1,0:T(8,128)(2,1)}, bf16[4,2,2,24,384]{4,3,2,1,0:T(8,128)(2,1)S(1)}, u32[]{:S(2)}, u32[]{:S(2)}) collective-permute-start(bf16[4,2,2,24,384]{4,3,2,1,0:T(8,128)(2,1)} %get-tuple-element.91), channel_id=1, source_target_pairs={{0,4},{1,5},{2,6},{3,7},{4,0},{5,1},{6,2},{7,3},{8,12},{9,13},{10,... | collective-permute-start | bytes 884744 | tf_op jit(solution)/shard_map/ppermute | solution.py:589
  204.0 31.3 %collective-permute-start.21 = (bf16[4,2,2,24,384]{4,3,2,1,0:T(8,128)(2,1)}, bf16[4,2,2,24,384]{4,3,2,1,0:T(8,128)(2,1)}, u32[]{:S(2)}, u32[]{:S(2)}) collective-permute-start(bf16[4,2,2,24,384]{4,3,2,1,0:T(8,128)(2,1)} %get-tuple-element.93), channel_id=1, source_target_pairs={{0,2},{1,3},{2,0},{3,1},{4,6},{5,7},{6,4},{7,5},{8,10},{9,11},{10,... | collective-permute-start | bytes 884744 | tf_op jit(solution)/shard_map/ppermute | solution.py:585
  208.6 26.8 %collective-permute-start.24 = (bf16[4,2,2,24,384]{4,3,2,1,0:T(8,128)(2,1)}, bf16[4,2,2,24,384]{4,3,2,1,0:T(8,128)(2,1)S(1)}, u32[]{:S(2)}, u32[]{:S(2)}) collective-permute-start(bf16[4,2,2,24,384]{4,3,2,1,0:T(8,128)(2,1)} %get-tuple-element.98), channel_id=1, source_target_pairs={{0,4},{1,5},{2,6},{3,7},{4,0},{5,1},{6,2},{7,3},{8,12},{9,13},{10,... | collective-permute-start | bytes 884744 | tf_op jit(solution)/shard_map/ppermute | solution.py:589
  240.3 17.4 %collective-permute-start.26 = (bf16[4,2,2,24,384]{4,3,2,1,0:T(8,128)(2,1)}, bf16[4,2,2,24,384]{4,3,2,1,0:T(8,128)(2,1)S(1)}, u32[]{:S(2)}, u32[]{:S(2)}) collective-permute-start(bf16[4,2,2,24,384]{4,3,2,1,0:T(8,128)(2,1)} %get-tuple-element.103), channel_id=1, source_target_pairs={{0,4},{1,5},{2,6},{3,7},{4,0},{5,1},{6,2},{7,3},{8,12},{9,13},{10,... | collective-permute-start | bytes 884744 | tf_op jit(solution)/shard_map/ppermute | solution.py:589
  241.0 20.0 %collective-permute-start.27 = (bf16[4,2,2,24,384]{4,3,2,1,0:T(8,128)(2,1)}, bf16[4,2,2,24,384]{4,3,2,1,0:T(8,128)(2,1)S(1)}, u32[]{:S(2)}, u32[]{:S(2)}) collective-permute-start(bf16[4,2,2,24,384]{4,3,2,1,0:T(8,128)(2,1)} %get-tuple-element.105), channel_id=1, source_target_pairs={{0,2},{1,3},{2,0},{3,1},{4,6},{5,7},{6,4},{7,5},{8,10},{9,11},{10,... | collective-permute-start | bytes 884744 | tf_op jit(solution)/shard_map/ppermute | solution.py:585
  242.5 23.6 %collective-permute-start.28 = (bf16[8,24,768]{2,1,0:T(8,128)(2,1)}, bf16[8,24,768]{2,1,0:T(8,128)(2,1)S(1)}, u32[]{:S(2)}, u32[]{:S(2)}) collective-permute-start(bf16[8,24,768]{2,1,0:T(8,128)(2,1)} %bitcast.83), channel_id=1, source_target_pairs={{0,0},{1,16},{2,2},{3,18},{4,4},{5,20},{6,6},{7,22},{8,1},{9,17},{... | collective-permute-start | bytes 884744 | tf_op jit(solution)/shard_map/ppermute | solution.py:690
  244.1 25.8 %collective-permute-start.29 = (bf16[8,24,768]{2,1,0:T(8,128)(2,1)}, bf16[8,24,768]{2,1,0:T(8,128)(2,1)}, u32[]{:S(2)}, u32[]{:S(2)}) collective-permute-start(bf16[8,24,768]{2,1,0:T(8,128)(2,1)} %bitcast.82), channel_id=1, source_target_pairs={{0,1},{1,17},{2,3},{3,19},{4,5},{5,21},{6,7},{7,23},{8,0},{9,16},{... | collective-permute-start | bytes 884744 | tf_op jit(solution)/shard_map/ppermute | solution.py:690
  246.7 23.2 %collective-permute-start.30 = (bf16[8,24,768]{2,1,0:T(8,128)(2,1)}, bf16[8,24,768]{2,1,0:T(8,128)(2,1)}, u32[]{:S(2)}, u32[]{:S(2)}) collective-permute-start(bf16[8,24,768]{2,1,0:T(8,128)(2,1)} %bitcast.81), channel_id=1, source_target_pairs={{0,8},{1,24},{2,10},{3,26},{4,12},{5,28},{6,14},{7,30},{8,9},{9,25... | collective-permute-start | bytes 884744 | tf_op jit(solution)/shard_map/ppermute | solution.py:690
  257.7 27.2 %collective-permute-start.31 = (bf16[8,24,768]{2,1,0:T(8,128)(2,1)}, bf16[8,24,768]{2,1,0:T(8,128)(2,1)}, u32[]{:S(2)}, u32[]{:S(2)}) collective-permute-start(bf16[8,24,768]{2,1,0:T(8,128)(2,1)} %bitcast.80), channel_id=1, source_target_pairs={{0,9},{1,25},{2,11},{3,27},{4,13},{5,29},{6,15},{7,31},{8,8},{9,24... | collective-permute-start | bytes 884744 | tf_op jit(solution)/shard_map/ppermute | solution.py:690
  264.5 20.5 %collective-permute-start.32 = (bf16[4,24,768]{2,1,0:T(8,128)(2,1)}, bf16[4,24,768]{2,1,0:T(8,128)(2,1)S(1)}, u32[]{:S(2)}, u32[]{:S(2)}) collective-permute-start(bf16[4,24,768]{2,1,0:T(8,128)(2,1)} %bitcast.86), channel_id=1, source_target_pairs={{0,0},{1,16},{2,2},{3,18},{4,4},{5,20},{6,6},{7,22},{8,1},{9,17},{... | collective-permute-start | bytes 442376 | tf_op jit(solution)/shard_map/ppermute | solution.py:690
  266.1 18.9 %collective-permute-start.33 = (bf16[4,24,768]{2,1,0:T(8,128)(2,1)}, bf16[4,24,768]{2,1,0:T(8,128)(2,1)S(1)}, u32[]{:S(2)}, u32[]{:S(2)}) collective-permute-start(bf16[4,24,768]{2,1,0:T(8,128)(2,1)} %bitcast.85), channel_id=1, source_target_pairs={{0,1},{1,17},{2,3},{3,19},{4,5},{5,21},{6,7},{7,23},{8,0},{9,16},{... | collective-permute-start | bytes 442376 | tf_op jit(solution)/shard_map/ppermute | solution.py:690
  269.9 15.2 %collective-permute-start.34 = (bf16[4,24,768]{2,1,0:T(8,128)(2,1)}, bf16[4,24,768]{2,1,0:T(8,128)(2,1)S(1)}, u32[]{:S(2)}, u32[]{:S(2)}) collective-permute-start(bf16[4,24,768]{2,1,0:T(8,128)(2,1)} %bitcast.84), channel_id=1, source_target_pairs={{0,8},{1,24},{2,10},{3,26},{4,12},{5,28},{6,14},{7,30},{8,9},{9,25... | collective-permute-start | bytes 442376 | tf_op jit(solution)/shard_map/ppermute | solution.py:690
  269.9 15.2 %collective-permute-start.35 = (bf16[4,24,768]{2,1,0:T(8,128)(2,1)}, bf16[4,24,768]{2,1,0:T(8,128)(2,1)S(1)}, u32[]{:S(2)}, u32[]{:S(2)}) collective-permute-start(bf16[4,24,768]{2,1,0:T(8,128)(2,1)} %bitcast.71), channel_id=1, source_target_pairs={{0,9},{1,25},{2,11},{3,27},{4,13},{5,29},{6,15},{7,31},{8,8},{9,24... | collective-permute-start | bytes 442376 | tf_op jit(solution)/shard_map/ppermute | solution.py:690
  290.1 39.6 %all-to-all-start.1 = ((bf16[32,24,768]{2,1,0:T(8,128)(2,1)}), bf16[32,24,768]{2,1,0:T(8,128)(2,1)}, u32[]{:S(2)}, u32[]{:S(2)}) async-start(bf16[32,24,768]{2,1,0:T(8,128)(2,1)} %get-tuple-element.121), calls=%async_computation.1 | async-start | bytes 2359296 | tf_op jit(solution)/shard_map/all_to_all | solution.py:868
  307.7 18.7 %collective-permute-start.41 = (f32[16,768]{1,0:T(8,128)S(1)}, f32[16,768]{1,0:T(8,128)S(1)}, u32[]{:S(2)}, u32[]{:S(2)}) collective-permute-start(f32[16,768]{1,0:T(8,128)S(1)} %add_add_fusion.1), channel_id=1, source_target_pairs={{0,16},{1,17},{2,18},{3,19},{4,20},{5,21},{6,22},{7,23},{8,24},{9,... | collective-permute-start | bytes 147464 | tf_op jit(solution)/shard_map/ppermute | solution.py:699
  335.0 32.6 %all-to-all-start.2 = ((bf16[32,24,768]{2,1,0:T(8,128)(2,1)}), bf16[32,24,768]{2,1,0:T(8,128)(2,1)}, u32[]{:S(2)}, u32[]{:S(2)}) async-start(bf16[32,24,768]{2,1,0:T(8,128)(2,1)} %bitcast.68), calls=%async_computation.2 | async-start | bytes 2359296 | tf_op jit(solution)/shard_map/all_to_all | solution.py:868
  (43 other events, 468.4 us)
Sparse Core Ops, SparseCore 0:
  11.5 68.1 all-gather.2
  82.7 62.4 all-gather.4

commit v6 on v4

--- a/solution.py
+++ b/solution.py
@@ -3,6 +3,7 @@
 
 import jax
 import jax.numpy as jnp
+import numpy as np
 from jax import lax
 from jax.experimental import pallas as pl
 from jax.experimental.pallas import tpu as pltpu
@@ -35,7 +36,7 @@
     return lax.dot_general(left, right, dims, preferred_element_type=f32)
 
 
-def call(body, flops, moved, vmem=60, after=(), **rest):
+def call(body, flops, moved, vmem=64, after=(), **rest):
     spec = rest.pop("grid_spec", None)
     grid = spec.grid if spec is not None else rest.get("grid", ())
     later = len(after)
@@ -85,12 +86,12 @@
     )
     offset = (jnp.arange(length, dtype=jnp.int32)[None] - start).astype(f32).reshape(-1, 1)
     half = ROT // 2
-    lane = jnp.arange(LANES) % 64
-    rates = jnp.power(10000.0, -2.0 * jnp.arange(half, dtype=f32) / ROT)
-    angle = offset * jnp.where(lane < ROT, rates[lane % half], 0.0)[None]
+    lane = np.arange(LANES) % 64
+    rates = np.where(lane < ROT, 10000.0 ** (-2.0 * (lane % half) / ROT), 0.0)
+    angle = offset * jnp.asarray(rates, f32)[None]
     cosine, sine = jnp.cos(angle), jnp.sin(angle)
-    first = jnp.where(lane[None] < half, -sine, 0.0)
-    second = jnp.where((lane[None] >= half) & (lane[None] < ROT), sine, 0.0)
+    first = sine * jnp.asarray(np.where(lane < half, -1.0, 0.0), f32)[None]
+    second = sine * jnp.asarray(np.where((lane >= half) & (lane < ROT), 1.0, 0.0), f32)[None]
     return cosine, first, second
 
 
@@ -409,9 +410,10 @@
         sum_ref[0] += part
 
 
-def hidden(first, blocks, acts, weights, vecs, after=(), step=512):
+def hidden(first, acts, weights, vecs, after=(), step=512):
     _, count, width = acts.shape
     splits = weights.shape[0] // 2
+    blocks = splits // 2
     both, sums = call(
         hidden_body,
         blocks * 4 * count * width * width,
@@ -444,7 +446,8 @@
     return scale * (grad - first - unit * second)
 
 
-def hidden_sum(hidden_refs, w_ref, at, dims, acc):
+def hidden_sum(hidden_refs, w_ref, dims, acc):
+    at = 0
     for ref in hidden_refs:
         for m in range(ref.shape[0]):
             part = mm(ref[m], w_ref[at], dims)
@@ -454,8 +457,8 @@
 
 
 def output_body(x_ref, o_ref, *refs, splits):
-    *e_refs, wo_ref, wm_ref, vec_ref, out_ref = refs
-    acc = hidden_sum(e_refs, wm_ref, 0, NN, mm(o_ref[0], wo_ref[0], NN))
+    *e_refs, wo_ref, w_ref, vec_ref, out_ref = refs
+    acc = hidden_sum(e_refs, w_ref, NN, mm(o_ref[0], wo_ref[0], NN))
     bias = vec_ref[7:8, :] + vec_ref[8 + splits : 9 + splits, :]
     out_ref[...] = (x_ref[...].astype(f32) + acc + bias).astype(bf16)
 
@@ -532,8 +535,8 @@
 
 
 def grad_two_body(x_ref, part_ref, *refs):
-    *du_refs, wm_ref, vec_ref, grad_ref, sum_ref = refs
-    grad = hidden_sum(du_refs, wm_ref, 0, NT, None)
+    *du_refs, w_ref, vec_ref, grad_ref, sum_ref = refs
+    grad = hidden_sum(du_refs, w_ref, NT, None)
     unit, scale = normed(x_ref[...].astype(f32))
     grad_ref[...] = (part_ref[...] + norm_back(grad, unit, scale, vec_ref[2:3, :])).astype(bf16)
     add_sums(sum_ref, (grad * unit, grad))
@@ -541,7 +544,6 @@
 
 def grad_two(x, part, dus, wm, vecs, after=(), step=256):
     count, width = x.shape
-    splits = wm.shape[0] // 2
     token = pl.BlockSpec((step, width), lambda i: (i, 0))
     return call(
         grad_two_body,
@@ -551,7 +553,7 @@
         grid=(count // step,),
         in_specs=[token, token]
         + [layers(v, step, width) for v in dus]
-        + [resident(splits, width, 0), pl.BlockSpec(vecs.shape, lambda i: (0, 0))],
+        + [resident(wm.shape[0] // 2, width, 0), pl.BlockSpec(vecs.shape, lambda i: (0, 0))],
         out_specs=[token, pl.BlockSpec((2, 8, width), lambda i: (0, 0, 0))],
         out_shape=[jax.ShapeDtypeStruct((count, width), bf16), jax.ShapeDtypeStruct((2, 8, width), f32)],
     )(x, part, *[v[0] for v in dus], wm, vecs)
@@ -691,15 +693,17 @@
 
 
 def everywhere(value):
-    for move in (
-        lambda z, y, x, c: (z, y, x, 1 - c),
-        lambda z, y, x, c: (z, y, 1 - x, c),
-        lambda z, y, x, c: (z, 1 - y, x, c),
-        lambda z, y, x, c: (z ^ 1, y, x, c),
-        lambda z, y, x, c: (3 - z, y, x, c),
-    ):
-        value = value + lax.ppermute(value, AXES, to_place(move))
-    return value
+    def get(move):
+        return lax.ppermute(value, AXES, to_place(move))
+
+    near = get(lambda z, y, x, c: (z ^ 1, y, x, c))
+    far = get(lambda z, y, x, c: (z ^ 2, y, x, c))
+    last = get(lambda z, y, x, c: (z ^ 3, y, x, c))
+    value = (value + near) + (far + last)
+    by_x, by_y = over_x(value), over_y(value)
+    across = get(lambda z, y, x, c: (z, 1 - y, 1 - x, c))
+    value = (value + by_x) + (by_y + across)
+    return value + over_c(value)
 
 
 def pack_body(slot_ref, *refs, orders, per):
@@ -889,6 +893,7 @@
     everyone = jnp.broadcast_to(low_vectors.reshape(1, -1), (slot_count, vec_rows * shard))
     vecs = to_all(everyone).reshape(slot_count, vec_rows, shard)
     vecs = vecs.transpose(1, 0, 2).reshape(vec_rows, width).astype(f32)
+    half = splits // 2
     mlp_weights = lax.all_gather(low_blocks[4:], AXES, axis=1, tiled=True)
 
     flat_tokens = tokens.reshape(count, width)
@@ -901,16 +906,15 @@
         pieces = [lax.all_gather(low_blocks[:4], AXES, axis=1, tiled=True)]
     q, k, v, do, acts, attn_weights = project(place, flat_tokens, dy, pieces, vecs, tables)
     og, attn_sums, acts = attend(segment_ids, q, k, v, do, tables, acts)
-    half = splits // 2
     orders = [list(range(4))]
     for first in (0, half):
         orders.append([base + first + j for base in (4, 4 + splits) for j in range(half)])
     if paired:
         acts_pair, og_pair = (acts, over_c(acts)), (og, over_c(og))
         dys = (acts_pair, 2, 1)
-        ed0, up_sum0 = hidden(0, half, acts, mlp_weights, vecs)
+        ed0, up_sum0 = hidden(0, acts, mlp_weights, vecs)
         ed0_pair = (ed0, over_c(ed0))
-        ed1, up_sum1 = hidden(half, half, acts, mlp_weights, vecs, after=(ed0, acts_pair[1]))
+        ed1, up_sum1 = hidden(half, acts, mlp_weights, vecs, after=(ed0, acts_pair[1]))
         ed1_pair = (ed1, over_c(ed1))
 
         def grads(left, two, one, after):
@@ -921,16 +925,17 @@
         low = grads(1, (ed0_pair, 0, half), (ed0_pair, half, half), (attn.made,))
         advance(place, [attn], [], after=(low.made,))
         high = grads(1, (ed1_pair, 0, half), (ed1_pair, half, half), (attn.made,))
-        advance(place, [low], [], after=(high.made,))
+        advance(place, [low], [], after=(high.made, *[got for _, got in attn.held]))
         part, one_sums = grad_one(flat_tokens, dy, (og, 0, 3), attn_weights, vecs, after=(low.made,))
         terms = [advance(place, [high], [attn, low], after=(part,))]
         es, dus = [(v, 0, half) for v in (ed0, ed1)], [(v, half, half) for v in (ed0, ed1)]
         grad_in, two_sums = grad_two(flat_tokens, part, dus, mlp_weights, vecs, after=(high.made,))
         terms.append(advance(place, [], [high], after=(grad_in,)))
+        last = high.made
         orders = [orders[0] + orders[1], orders[2]]
     else:
-        ed0, up_sum0 = hidden(0, half, acts, mlp_weights, vecs)
-        ed1, up_sum1 = hidden(half, half, acts, mlp_weights, vecs)
+        ed0, up_sum0 = hidden(0, acts, mlp_weights, vecs)
+        ed1, up_sum1 = hidden(half, acts, mlp_weights, vecs)
         grads = [
             full_grads(acts[0], og[3:], og[:3], dy),
             full_grads(acts[1], ed0[:half], ed0[half:], dy),
@@ -940,6 +945,7 @@
         es, dus = [(v, 0, half) for v in (ed0, ed1)], [(v, half, half) for v in (ed0, ed1)]
         part, one_sums = grad_one(flat_tokens, dy, (og, 0, 3), attn_weights, vecs)
         grad_in, two_sums = grad_two(flat_tokens, part, dus, mlp_weights, vecs)
+        last = grad_in
     up_sums = [up_sum0, up_sum1]
 
     one_sums, two_sums = jnp.sum(one_sums, axis=1), jnp.sum(two_sums, axis=1)
@@ -953,9 +959,9 @@
     match = owners[None, :] == slot_ids[:, None]
     slots = jnp.sum(jnp.where(match, jnp.arange(1, owners.shape[0] + 1, dtype=jnp.int32)[None], 0), axis=1) - 1
     has_block = jnp.any(owners == my_index)
-    shards, outgoing, squares = pack(slots, terms, orders, after=(grad_in,))
-    out = output(flat_tokens, (og, 3, 1), es, attn_weights, mlp_weights, vecs, after=(squares,))
-    left_low, right_low = to_low(root_left[0], root_right[0], after=(out,))
+    out = output(flat_tokens, (og, 3, 1), es, attn_weights, mlp_weights, vecs, after=(last,))
+    shards, outgoing, squares = pack(slots, terms, orders, after=(out,))
+    left_low, right_low = to_low(root_left[0], root_right[0], after=(squares,))
     local = jnp.concatenate([grad_vectors, jnp.sum(squares, axis=0)[None], jnp.zeros((2, width), f32)])
     total = everywhere(local) if paired else lax.psum(local, AXES)
     vector_sums = total[:vec_rows]

time: 358 us -> 365 us (1.020)
  starting transfers between devices: 64.7 us -> 74.1 us
  local copies, waits for them, and re-layouts: 13.6 us -> 9.02 us
    ppermute x8, waiting for transfers between devices: 12.6 us -> 0.02 us  [advance(): lax.ppermute(v, AXES, to_place(lambda z, y, x, c, m=m: (2 * c + ((z ^ m)...]
    ppermute x5 -> x4, waiting for transfers between devices: 17.8 us -> 29.7 us  [get(): return lax.ppermute(value, AXES, to_place(move))]
    ppermute x8 -> x9, waiting for transfers between devices: 0.97 us -> 9.74 us  [over_y(): lax.ppermute(value, AXES, to_place(lambda z, y, x, c: (z, 1 - y, x, c)))]
    ppermute x8 -> x9, waiting for transfers between devices: 22.7 us -> 14 us  [over_x(): lax.ppermute(value, AXES, to_place(lambda z, y, x, c: (z, y, 1 - x, c)))]
    select_n x2 -> x0, other arithmetic: 8.39 us -> none  [the longest x1 5.18 us: rotary_tables(): angle = offset * jnp.where(lane < ROT, rates[lane % half], 0.0)[None]]
    all_to_all x3, starting transfers between devices: 9.54 us -> 17.9 us  [to_all(): return lax.all_to_all(value, AXES, split_axis=0, concat_axis=0, tiled=True)]
    ppermute x3, waiting for transfers between devices: 3.27 us -> 9.35 us  [over_z(): lax.ppermute(value, AXES, to_place(lambda z, y, x, c: ((z + by) % 4, y, x...]
    unnamed x81 -> x47, local copies, waits for them, and re-layouts: 9.07 us -> 4.18 us
  transfers between devices with their start and end apart: 45 -> 47, of which waited for: 16 -> 15; matrix products, arithmetic and copies ran while one was open for 6% -> 5% of each run, Pallas kernels for 42% -> 41%
where the time goes in v6:
time: 365 us; the launch traced here: 364 us
  Pallas kernels  167 us (46%)
  waiting for transfers between devices  81.9 us (22%)
  starting transfers between devices  74.1 us (20%)
  between operations  17.9 us (5%)
  other arithmetic  14.2 us (4%)
  local copies, waits for them, and re-layouts  9.02 us (2%)
    pallas_call x19, Pallas kernels, call(): return lambda *operands: made(*operands, *after)  167 us
    ppermute x4, waiting for transfers between devices, get(): return lax.ppermute(value, AXES, to_place(move))  29.7 us
    ppermute x8, starting transfers between devices, advance(): lax.ppermute(v, AXES, to_place(lambda z, y, x, c, m=m: (2 * c + ((z ^ m)...  21.8 us
    all_to_all x3, waiting for transfers between devices, to_all(): return lax.all_to_all(value, AXES, split_axis=0, concat_axis=0, tiled=True)  19.1 us
    all_to_all x3, starting transfers between devices, to_all(): return lax.all_to_all(value, AXES, split_axis=0, concat_axis=0, tiled=True)  17.9 us
    ppermute x9, waiting for transfers between devices, over_x(): lax.ppermute(value, AXES, to_place(lambda z, y, x, c: (z, y, 1 - x, c)))  14 us
    ppermute x9, starting transfers between devices, over_x(): lax.ppermute(value, AXES, to_place(lambda z, y, x, c: (z, y, 1 - x, c)))  11.5 us
    ppermute x9, starting transfers between devices, over_y(): lax.ppermute(value, AXES, to_place(lambda z, y, x, c: (z, 1 - y, x, c)))  9.91 us
  transfers between devices with their start and end apart: 47, of which 15 were waited for; matrix products, arithmetic and copies ran while one was open for 5% of the time, Pallas kernels for 41%

profile of v6, /device:TPU:0, one launch (start us, length us, event | category | flops | bytes accessed | tf_op | source)
XLA Modules:
  0.0 363.8 jit_solution(1297529326971062982)
XLA Ops:
  9.3 4.1 %collective-permute-start.1 = (bf16[4,24,768]{2,1,0:T(8,128)(2,1)S(1)}, bf16[4,24,768]{2,1,0:T(8,128)(2,1)S(1)}, u32[]{:S(2)}, u32[]{:S(2)}) collective-permute-start(bf16[4,24,768]{2,1,0:T(8,128)(2,1)S(1)} %get-tuple-element.135), channel_id=1, source_target_pairs={{0,16},{1,17},{2,18},{3,19},{4,20},{5,21},{6,22},{7,23},{8,24},{9,... | collective-permute-start | bytes 442376 | tf_op jit(solution)/shard_map/ppermute | solution.py:591
  15.4 6.6 %collective-permute-done.1 = bf16[4,24,768]{2,1,0:T(8,128)(2,1)S(1)} collective-permute-done((bf16[4,24,768]{2,1,0:T(8,128)(2,1)S(1)}, bf16[4,24,768]{2,1,0:T(8,128)(2,1)S(1)}, u32[]{:S(2)}, u32[]{:S(2)}) %collective-permute-start.1) | collective-permute-done | bytes 147488 | tf_op jit(solution)/shard_map/ppermute | solution.py:591
  30.1 9.6 %all-to-all-start = ((bf16[32,2,156]{2,1,0:T(2,128)(2,1)}), bf16[32,2,156]{2,1,0:T(2,128)(2,1)S(1)}, u32[]{:S(2)}, u32[]{:S(2)}) async-start(bf16[32,2,156]{2,1,0:T(2,128)(2,1)} %reshape.167), calls=%async_computation | async-start | bytes 65536 | tf_op jit(solution)/shard_map/all_to_all | solution.py:866
  44.2 3.2 fusion
  47.4 6.6 %collective-permute-done.5.refs_3_ = bf16[2,4,24,768]{3,2,1,0:T(8,128)(2,1)S(1)} collective-permute-done((bf16[2,4,24,768]{3,2,1,0:T(8,128)(2,1)S(1)}, bf16[2,4,24,768]{3,2,1,0:T(8,128)(2,1)S(1)}, u32[]{:S(2)}, u32[]{:S(2)}) %collective-permute-start.5) | collective-permute-done | bytes 294944 | tf_op jit(solution)/shard_map/ppermute | solution.py:587
  54.1 3.9 %collective-permute-done.6.refs_4_ = bf16[2,4,24,768]{3,2,1,0:T(8,128)(2,1)} collective-permute-done((bf16[2,4,24,768]{3,2,1,0:T(8,128)(2,1)S(1)}, bf16[2,4,24,768]{3,2,1,0:T(8,128)(2,1)}, u32[]{:S(2)}, u32[]{:S(2)}) %collective-permute-start.6) | collective-permute-done | bytes 294944 | tf_op jit(solution)/shard_map/ppermute | solution.py:583
  63.7 14.2 %shard_map.229 = (bf16[1024,768]{1,0:T(8,128)(2,1)}, bf16[1024,768]{1,0:T(8,128)(2,1)}, bf16[1024,768]{1,0:T(8,128)(2,1)}, bf16[1024,768]{1,0:T(8,128)(2,1)}, bf...) custom-call(s32[4]{0:T(128)} %pad_add_fusion.place_ref.refs_0_, bf16[1024,768]{1,0:T(8,128)(2,1)} %bitcast.58, ...), custom_call_target="tpu_custom_call" | custom-call | flops 4831838208 | bytes 25165824 | tf_op jit(solution)/shard_map/pallas_call | solution.py:75
  78.0 25.4 %shard_map.230 = (bf16[4,1024,768]{2,1,0:T(8,128)(2,1)}, f32[3,16,768]{2,1,0:T(8,128)}, bf16[3,1024,768]{2,1,0:T(8,128)(2,1)}) custom-call(bf16[3,1024,768]{2,1,0:T(8,128)(2,1)} %get-tuple-element.71.acts_ref, s32[1024,1]{1,0:T(8,128)} %bitcast.69, s32[2,1,512]{2,1,0:T(1,128)} %broadcast_in_dim.46.row_ref, ...), custom_call_target="tpu_custom_call", output_to_operand_aliasing={{2}: (0, {})} | custom-call | flops 9663676416 | bytes 18874368 | tf_op jit(solution)/shard_map/pallas_call | solution.py:75
  105.8 12.8 %shard_map.231 = (bf16[2,2,1024,768]{3,2,1,0:T(8,128)(2,1)}, f32[2,8,768]{2,1,0:T(8,128)}) custom-call(bf16[3,1024,768]{2,1,0:T(8,128)(2,1)} %get-tuple-element.77.a2_ref.dy_ref.refs_0_.refs_1_.refs_7_, bf16[3,1024,768]{2,1,0:T(8,128)(2,1)} %get-tuple-element.77.a2_ref.dy_ref.refs_0_.refs_1_.refs_7_, ...), custom_call_target="tpu_custom_call" | custom-call | flops 4831838208 | bytes 17301504 | tf_op jit(solution)/shard_map/pallas_call | solution.py:75
  119.0 12.6 %shard_map.232 = (bf16[2,2,1024,768]{3,2,1,0:T(8,128)(2,1)}, f32[2,8,768]{2,1,0:T(8,128)}) custom-call(bf16[3,1024,768]{2,1,0:T(8,128)(2,1)} %get-tuple-element.77.a2_ref.dy_ref.refs_0_.refs_1_.refs_7_, bf16[3,1024,768]{2,1,0:T(8,128)(2,1)} %get-tuple-element.77.a2_ref.dy_ref.refs_0_.refs_1_.refs_7_, ...), custom_call_target="tpu_custom_call" | custom-call | flops 4831838208 | bytes 17301504 | tf_op jit(solution)/shard_map/pallas_call | solution.py:75
  131.7 11.4 %shard_map.233 = (bf16[4,2,2,2,24,384]{5,4,3,2,1,0:T(8,128)(2,1)}, bf16[4,2,2,2,24,384]{5,4,3,2,1,0:T(8,128)(2,1)}, bf16[4,2,2,2,24,384]{5,4,3,2,1,0:T(8,128)(2,1)}, bf16[4,2,2,2,24,384]{5,4,3,2,1,0:T(8,128)(2,1)}) custom-call(s32[4]{0:T(128)} %pad_add_fusion.place_ref.refs_0_, bf16[3,1024,768]{2,1,0:T(8,128)(2,1)} %get-tuple-element.77.a2_ref.dy_ref.refs_0_.refs_1_.refs_7_, ...), custom_call_target="tpu_custom_call" | custom-call | flops 4831838208 | bytes 12582912 | tf_op jit(solution)/shard_map/pallas_call | solution.py:75
  145.6 11.2 %shard_map.234 = (bf16[4,2,2,2,24,384]{5,4,3,2,1,0:T(8,128)(2,1)}, bf16[4,2,2,2,24,384]{5,4,3,2,1,0:T(8,128)(2,1)}, bf16[4,2,2,2,24,384]{5,4,3,2,1,0:T(8,128)(2,1)}, bf16[4,2,2,2,24,384]{5,4,3,2,1,0:T(8,128)(2,1)}) custom-call(s32[4]{0:T(128)} %pad_add_fusion.place_ref.refs_0_, bf16[3,1024,768]{2,1,0:T(8,128)(2,1)} %get-tuple-element.77.a2_ref.dy_ref.refs_0_.refs_1_.refs_7_, ...), custom_call_target="tpu_custom_call" | custom-call | flops 4831838208 | bytes 12582912 | tf_op jit(solution)/shard_map/pallas_call | solution.py:75
  166.6 11.2 %shard_map.236 = (bf16[4,2,2,2,24,384]{5,4,3,2,1,0:T(8,128)(2,1)}, bf16[4,2,2,2,24,384]{5,4,3,2,1,0:T(8,128)(2,1)}, bf16[4,2,2,2,24,384]{5,4,3,2,1,0:T(8,128)(2,1)}, bf16[4,2,2,2,24,384]{5,4,3,2,1,0:T(8,128)(2,1)}) custom-call(s32[4]{0:T(128)} %pad_add_fusion.place_ref.refs_0_, bf16[3,1024,768]{2,1,0:T(8,128)(2,1)} %get-tuple-element.77.a2_ref.dy_ref.refs_0_.refs_1_.refs_7_, ...), custom_call_target="tpu_custom_call" | custom-call | flops 4831838208 | bytes 12582912 | tf_op jit(solution)/shard_map/pallas_call | solution.py:75
  180.8 6.0 %collective-permute-done.22.refs_2_ = bf16[4,2,2,2,24,384]{5,4,3,2,1,0:T(8,128)(2,1)} collective-permute-done((bf16[4,2,2,2,24,384]{5,4,3,2,1,0:T(8,128)(2,1)}, bf16[4,2,2,2,24,384]{5,4,3,2,1,0:T(8,128)(2,1)}, u32[]{:S(2)}, u32[]{:S(2)}) %collective-permute-start.22) | collective-permute-done | bytes 589856 | tf_op jit(solution)/shard_map/ppermute | solution.py:583
  186.9 3.1 shard_map.237
  192.1 9.8 %shard_map.238 = (f32[1024,768]{1,0:T(8,128)}, f32[3,8,768]{2,1,0:T(8,128)}) custom-call(bf16[1024,768]{1,0:T(8,128)(2,1)} %bitcast.59, bf16[1024,768]{1,0:T(8,128)(2,1)} %bitcast.67, bf16[4,1024,768]{2,1,0:T(8,128)(2,1)} %get-tuple-element.76.refs_3_.refs_5_.refs_2_.refs_1_, bf16[4,768,768]{2,1,0:T(8,128)(2,1)} %get-tuple-element.80.refs_3_.refs_4_, ...), custom_call_target="tpu_custom_call" | custom-call | flops 3623878656 | bytes 14548992 | tf_op jit(solution)/shard_map/pallas_call | solution.py:75
  203.8 4.1 %shard_map.239 = (bf16[4,2,2,24,384]{4,3,2,1,0:T(8,128)(2,1)}, bf16[4,2,2,24,384]{4,3,2,1,0:T(8,128)(2,1)}, bf16[4,2,2,24,384]{4,3,2,1,0:T(8,128)(2,1)}, bf16[4,...) custom-call(s32[4]{0:T(128)} %pad_add_fusion.place_ref.refs_0_, ...), custom_call_target="tpu_custom_call" | custom-call | bytes 9437184 | tf_op jit(solution)/shard_map/pallas_call | solution.py:75
  210.1 3.7 %collective-permute-start.28 = (bf16[8,24,768]{2,1,0:T(8,128)(2,1)}, bf16[8,24,768]{2,1,0:T(8,128)(2,1)}, u32[]{:S(2)}, u32[]{:S(2)}) collective-permute-start(bf16[8,24,768]{2,1,0:T(8,128)(2,1)} %bitcast.83), channel_id=1, source_target_pairs={{0,0},{1,16},{2,2},{3,18},{4,4},{5,20},{6,6},{7,22},{8,1},{9,17},{... | collective-permute-start | bytes 884744 | tf_op jit(solution)/shard_map/ppermute | solution.py:688
  213.9 5.7 %collective-permute-start.29 = (bf16[8,24,768]{2,1,0:T(8,128)(2,1)}, bf16[8,24,768]{2,1,0:T(8,128)(2,1)}, u32[]{:S(2)}, u32[]{:S(2)}) collective-permute-start(bf16[8,24,768]{2,1,0:T(8,128)(2,1)} %bitcast.82), channel_id=1, source_target_pairs={{0,1},{1,17},{2,3},{3,19},{4,5},{5,21},{6,7},{7,23},{8,0},{9,16},{... | collective-permute-start | bytes 884744 | tf_op jit(solution)/shard_map/ppermute | solution.py:688
  219.6 11.0 %shard_map.240 = (bf16[1024,768]{1,0:T(8,128)(2,1)}, f32[2,8,768]{2,1,0:T(8,128)}) custom-call(bf16[1024,768]{1,0:T(8,128)(2,1)} %bitcast.60, f32[1024,768]{1,0:T(8,128)} %get-tuple-element.101.refs_13_.refs_1_, bf16[4,1024,768]{2,1,0:T(8,128)(2,1)} %bitcast.56, bf16[4,1024,768]{2,1,0:T(8,128)(2,1)} %bitcast.50, ...), custom_call_target="tpu_custom_call" | custom-call | flops 4831838208 | bytes 17301504 | tf_op jit(solution)/shard_map/pallas_call | solution.py:75
  240.3 5.4 %collective-permute-start.35 = (bf16[4,24,768]{2,1,0:T(8,128)(2,1)}, bf16[4,24,768]{2,1,0:T(8,128)(2,1)}, u32[]{:S(2)}, u32[]{:S(2)}) collective-permute-start(bf16[4,24,768]{2,1,0:T(8,128)(2,1)} %bitcast.71), channel_id=1, source_target_pairs={{0,9},{1,25},{2,11},{3,27},{4,13},{5,29},{6,15},{7,31},{8,8},{9,24... | collective-permute-start | bytes 442376 | tf_op jit(solution)/shard_map/ppermute | solution.py:688
  245.7 11.1 %shard_map.242.refs_9_ = bf16[1024,768]{1,0:T(8,128)(2,1)} custom-call(bf16[1024,768]{1,0:T(8,128)(2,1)} %bitcast.61, bf16[4,1024,768]{2,1,0:T(8,128)(2,1)} %get-tuple-element.76.refs_3_.refs_5_.refs_2_.refs_1_, bf16[4,1024,768]{2,1,0:T(8,128)(2,1)} %bitcast.57, bf16[4,1024,768]{2,1,0:T(8,128)(2,1)} %bitcast.51, ...), custom_call_target="tpu_custom_call" | custom-call | flops 6039797760 | bytes 16908288 | tf_op jit(solution)/shard_map/pallas_call | solution.py:75
  256.8 3.7 %shard_map.243 = (f32[12,24,768]{2,1,0:T(8,128)}, bf16[32,24,768]{2,1,0:T(8,128)(2,1)}, f32[24,768]{1,0:T(8,128)}) custom-call(s32[32]{0:T(128)} %broadcast_add_fusion.refs_0_, bf16[8,24,768]{2,1,0:T(8,128)(2,1)} %collective-permute-done.28.refs_1_, bf16[8,24,768]{2,1,0:T(8,128)(2,1)} %collective-permute-done.29.refs_2_, ...), custom_call_target="tpu_custom_call" | custom-call | bytes 3538944 | tf_op jit(solution)/shard_map/pallas_call | solution.py:75
  260.5 4.7 %all-to-all-start.1 = ((bf16[32,24,768]{2,1,0:T(8,128)(2,1)}), bf16[32,24,768]{2,1,0:T(8,128)(2,1)}, u32[]{:S(2)}, u32[]{:S(2)}) async-start(bf16[32,24,768]{2,1,0:T(8,128)(2,1)} %get-tuple-element.121), calls=%async_computation.1 | async-start | bytes 2359296 | tf_op jit(solution)/shard_map/all_to_all | solution.py:866
  270.0 16.2 %collective-permute-done.36 = f32[16,768]{1,0:T(8,128)S(1)} collective-permute-done((f32[16,768]{1,0:T(8,128)S(1)}, f32[16,768]{1,0:T(8,128)S(1)}, u32[]{:S(2)}, u32[]{:S(2)}) %collective-permute-start.36) | collective-permute-done | bytes 49184 | tf_op jit(solution)/shard_map/ppermute | solution.py:697
  286.2 11.6 %collective-permute-done.37 = f32[16,768]{1,0:T(8,128)S(1)} collective-permute-done((f32[16,768]{1,0:T(8,128)S(1)}, f32[16,768]{1,0:T(8,128)S(1)}, u32[]{:S(2)}, u32[]{:S(2)}) %collective-permute-start.37) | collective-permute-done | bytes 49184 | tf_op jit(solution)/shard_map/ppermute | solution.py:697
  306.4 3.5 shard_map.244
  314.7 5.3 %shard_map.245 = bf16[768,768]{1,0:T(8,128)(2,1)} custom-call(f32[2]{0:T(128)} %pad_maximum_fusion.1.scale_ref, bf16[768,768]{1,0:T(8,128)(2,1)} %bitcast.27.s_ref, bf16[768,768]{1,0:T(8,128)(2,1)} %get-tuple-element.122.l_ref, bf16[768,768]{1,0:T(8,128)(2,1)} %get-tuple-element.123.r_ref), custom_call_target="tpu_custom_call" | custom-call | flops 1811939328 | bytes 4718592 | tf_op jit(solution)/shard_map/pallas_call | solution.py:75
  320.0 3.5 all-to-all-start.2
  326.2 7.2 %shard_map.247 = (f32[768,768]{1,0:T(8,128)}, f32[768,768]{1,0:T(8,128)}) custom-call(s32[1]{0:T(128)} %bitcast.31.has_ref, f32[2]{0:T(128)} %pad_maximum_fusion.1.scale_ref, bf16[768,768]{1,0:T(8,128)(2,1)} %bitcast.27.s_ref, f32[768,768]{1,0:T(8,128)} %bitcast.78, f32[768,768]{1,0:T(8,128)} %bitcast.79), custom_call_target="tpu_custom_call" | custom-call | flops 1811939328 | bytes 10616832 | tf_op jit(solution)/shard_map/pallas_call | solution.py:75
  333.4 19.1 %all-to-all-done.2.p_ref = bf16[32,24,768]{2,1,0:T(8,128)(2,1)} async-done(((bf16[32,24,768]{2,1,0:T(8,128)(2,1)}), bf16[32,24,768]{2,1,0:T(8,128)(2,1)}, u32[]{:S(2)}, u32[]{:S(2)}) %all-to-all-start.2) | async-done | bytes 1179680 | tf_op jit(solution)/shard_map/all_to_all | solution.py:866
  352.5 3.3 shard_map.246
  (171 shorter events, 75.0 us)
Async XLA Ops:
  7.2 98.6 %all-gather.2.cloned.1.call-start = ((), (), s32[]{:S(2)}) async-start(), calls=%async_computation.3 | async-start | bytes 9732096 | tf_op jit(solution)/shard_map/all_gather | solution.py:897
  30.1 30.2 %all-to-all-start = ((bf16[32,2,156]{2,1,0:T(2,128)(2,1)}), bf16[32,2,156]{2,1,0:T(2,128)(2,1)S(1)}, u32[]{:S(2)}, u32[]{:S(2)}) async-start(bf16[32,2,156]{2,1,0:T(2,128)(2,1)} %reshape.167), calls=%async_computation | async-start | bytes 65536 | tf_op jit(solution)/shard_map/all_to_all | solution.py:866
  42.0 16.0 %collective-permute-start.6 = (bf16[2,4,24,768]{3,2,1,0:T(8,128)(2,1)S(1)}, bf16[2,4,24,768]{3,2,1,0:T(8,128)(2,1)}, u32[]{:S(2)}, u32[]{:S(2)}) collective-permute-start(bf16[2,4,24,768]{3,2,1,0:T(8,128)(2,1)S(1)} %slice.34), channel_id=1, source_target_pairs={{0,2},{1,3},{2,0},{3,1},{4,6},{5,7},{6,4},{7,5},{8,10},{9,11},{10,... | collective-permute-start | bytes 884744 | tf_op jit(solution)/shard_map/ppermute | solution.py:583
  43.6 18.6 %collective-permute-start.7 = (bf16[4,4,24,768]{3,2,1,0:T(8,128)(2,1)S(1)}, bf16[4,4,24,768]{3,2,1,0:T(8,128)(2,1)S(1)}, u32[]{:S(2)}, u32[]{:S(2)}) collective-permute-start(bf16[4,4,24,768]{3,2,1,0:T(8,128)(2,1)S(1)} %pad_maximum_fusion.refs_0_), channel_id=1, source_target_pairs={{0,1},{1,0},{2,3},{3,2},{4,5},{5,4},{6,7},{7,6},{8,9},{9,8},{10,11... | collective-permute-start | bytes 1769480 | tf_op jit(solution)/shard_map/ppermute | solution.py:579
  43.6 18.6 %collective-permute-start.8 = (bf16[4,4,24,768]{3,2,1,0:T(8,128)(2,1)S(1)}, bf16[4,4,24,768]{3,2,1,0:T(8,128)(2,1)}, u32[]{:S(2)}, u32[]{:S(2)}) collective-permute-start(bf16[4,4,24,768]{3,2,1,0:T(8,128)(2,1)S(1)} %collective-permute-done.3.refs_1_), channel_id=1, source_target_pairs={{0,1},{1,0},{2,3},{3,2},{4,5},{5,4},{6,7},{7,6},{8,9},{9,8},{10,11... | collective-permute-start | bytes 1769480 | tf_op jit(solution)/shard_map/ppermute | solution.py:579
  44.1 18.1 %collective-permute-start.9 = (bf16[4,4,24,768]{3,2,1,0:T(8,128)(2,1)S(1)}, bf16[4,4,24,768]{3,2,1,0:T(8,128)(2,1)}, u32[]{:S(2)}, u32[]{:S(2)}) collective-permute-start(bf16[4,4,24,768]{3,2,1,0:T(8,128)(2,1)S(1)} %collective-permute-done.4.refs_2_), channel_id=1, source_target_pairs={{0,1},{1,0},{2,3},{3,2},{4,5},{5,4},{6,7},{7,6},{8,9},{9,8},{10,11... | collective-permute-start | bytes 1769480 | tf_op jit(solution)/shard_map/ppermute | solution.py:579
  104.0 27.7 %collective-permute-start.14 = (bf16[4,1024,768]{2,1,0:T(8,128)(2,1)}, bf16[4,1024,768]{2,1,0:T(8,128)(2,1)}, u32[]{:S(2)}, u32[]{:S(2)}) collective-permute-start(bf16[4,1024,768]{2,1,0:T(8,128)(2,1)} %get-tuple-element.76.refs_3_.refs_5_.refs_2_.refs_1_), channel_id=1, source_target_pairs={{0,1},{1,0},{2,3},{3,2},{4,5},{5,4},{6,7},{7,6},{8,9},{9,8},{10,11... | collective-permute-start | bytes 18874376 | tf_op jit(solution)/shard_map/ppermute | solution.py:579
  118.6 27.0 %collective-permute-start.17 = (bf16[4,1024,768]{2,1,0:T(8,128)(2,1)}, bf16[4,1024,768]{2,1,0:T(8,128)(2,1)}, u32[]{:S(2)}, u32[]{:S(2)}) collective-permute-start(bf16[4,1024,768]{2,1,0:T(8,128)(2,1)} %bitcast.52), channel_id=1, source_target_pairs={{0,1},{1,0},{2,3},{3,2},{4,5},{5,4},{6,7},{7,6},{8,9},{9,8},{10,11... | collective-permute-start | bytes 18874376 | tf_op jit(solution)/shard_map/ppermute | solution.py:579
  131.6 35.0 %collective-permute-start.13 = (bf16[4,1024,768]{2,1,0:T(8,128)(2,1)}, bf16[4,1024,768]{2,1,0:T(8,128)(2,1)}, u32[]{:S(2)}, u32[]{:S(2)}) collective-permute-start(bf16[4,1024,768]{2,1,0:T(8,128)(2,1)} %bitcast.46), channel_id=1, source_target_pairs={{0,1},{1,0},{2,3},{3,2},{4,5},{5,4},{6,7},{7,6},{8,9},{9,8},{10,11... | collective-permute-start | bytes 18874376 | tf_op jit(solution)/shard_map/ppermute | solution.py:579
  143.1 16.0 %collective-permute-start.15 = (bf16[4,2,2,2,24,384]{5,4,3,2,1,0:T(8,128)(2,1)}, bf16[4,2,2,2,24,384]{5,4,3,2,1,0:T(8,128)(2,1)}, u32[]{:S(2)}, u32[]{:S(2)}) collective-permute-start(bf16[4,2,2,2,24,384]{5,4,3,2,1,0:T(8,128)(2,1)} %get-tuple-element.82), channel_id=1, source_target_pairs={{0,2},{1,3},{2,0},{3,1},{4,6},{5,7},{6,4},{7,5},{8,10},{9,11},{10,... | collective-permute-start | bytes 1769480 | tf_op jit(solution)/shard_map/ppermute | solution.py:583
  143.7 15.7 %collective-permute-start.16 = (bf16[4,2,2,2,24,384]{5,4,3,2,1,0:T(8,128)(2,1)}, bf16[4,2,2,2,24,384]{5,4,3,2,1,0:T(8,128)(2,1)}, u32[]{:S(2)}, u32[]{:S(2)}) collective-permute-start(bf16[4,2,2,2,24,384]{5,4,3,2,1,0:T(8,128)(2,1)} %get-tuple-element.84), channel_id=1, source_target_pairs={{0,4},{1,5},{2,6},{3,7},{4,0},{5,1},{6,2},{7,3},{8,12},{9,13},{10,... | collective-permute-start | bytes 1769480 | tf_op jit(solution)/shard_map/ppermute | solution.py:587
  162.5 16.7 %collective-permute-start.20 = (bf16[4,2,2,24,384]{4,3,2,1,0:T(8,128)(2,1)}, bf16[4,2,2,24,384]{4,3,2,1,0:T(8,128)(2,1)}, u32[]{:S(2)}, u32[]{:S(2)}) collective-permute-start(bf16[4,2,2,24,384]{4,3,2,1,0:T(8,128)(2,1)} %get-tuple-element.91), channel_id=1, source_target_pairs={{0,4},{1,5},{2,6},{3,7},{4,0},{5,1},{6,2},{7,3},{8,12},{9,13},{10,... | collective-permute-start | bytes 884744 | tf_op jit(solution)/shard_map/ppermute | solution.py:587
  164.0 16.9 %collective-permute-start.21 = (bf16[4,2,2,24,384]{4,3,2,1,0:T(8,128)(2,1)}, bf16[4,2,2,24,384]{4,3,2,1,0:T(8,128)(2,1)}, u32[]{:S(2)}, u32[]{:S(2)}) collective-permute-start(bf16[4,2,2,24,384]{4,3,2,1,0:T(8,128)(2,1)} %get-tuple-element.93), channel_id=1, source_target_pairs={{0,2},{1,3},{2,0},{3,1},{4,6},{5,7},{6,4},{7,5},{8,10},{9,11},{10,... | collective-permute-start | bytes 884744 | tf_op jit(solution)/shard_map/ppermute | solution.py:583
  164.3 22.6 %collective-permute-start.22 = (bf16[4,2,2,2,24,384]{5,4,3,2,1,0:T(8,128)(2,1)}, bf16[4,2,2,2,24,384]{5,4,3,2,1,0:T(8,128)(2,1)}, u32[]{:S(2)}, u32[]{:S(2)}) collective-permute-start(bf16[4,2,2,2,24,384]{5,4,3,2,1,0:T(8,128)(2,1)} %get-tuple-element.94), channel_id=1, source_target_pairs={{0,2},{1,3},{2,0},{3,1},{4,6},{5,7},{6,4},{7,5},{8,10},{9,11},{10,... | collective-permute-start | bytes 1769480 | tf_op jit(solution)/shard_map/ppermute | solution.py:583
  166.0 20.9 %collective-permute-start.23 = (bf16[4,2,2,2,24,384]{5,4,3,2,1,0:T(8,128)(2,1)}, bf16[4,2,2,2,24,384]{5,4,3,2,1,0:T(8,128)(2,1)}, u32[]{:S(2)}, u32[]{:S(2)}) collective-permute-start(bf16[4,2,2,2,24,384]{5,4,3,2,1,0:T(8,128)(2,1)} %get-tuple-element.96), channel_id=1, source_target_pairs={{0,4},{1,5},{2,6},{3,7},{4,0},{5,1},{6,2},{7,3},{8,12},{9,13},{10,... | collective-permute-start | bytes 1769480 | tf_op jit(solution)/shard_map/ppermute | solution.py:587
  177.7 24.1 %collective-permute-start.18 = (bf16[4,2,2,2,24,384]{5,4,3,2,1,0:T(8,128)(2,1)}, bf16[4,2,2,2,24,384]{5,4,3,2,1,0:T(8,128)(2,1)}, u32[]{:S(2)}, u32[]{:S(2)}) collective-permute-start(bf16[4,2,2,2,24,384]{5,4,3,2,1,0:T(8,128)(2,1)} %get-tuple-element.88), channel_id=1, source_target_pairs={{0,2},{1,3},{2,0},{3,1},{4,6},{5,7},{6,4},{7,5},{8,10},{9,11},{10,... | collective-permute-start | bytes 1769480 | tf_op jit(solution)/shard_map/ppermute | solution.py:583
  179.2 22.6 %collective-permute-start.19 = (bf16[4,2,2,2,24,384]{5,4,3,2,1,0:T(8,128)(2,1)}, bf16[4,2,2,2,24,384]{5,4,3,2,1,0:T(8,128)(2,1)}, u32[]{:S(2)}, u32[]{:S(2)}) collective-permute-start(bf16[4,2,2,2,24,384]{5,4,3,2,1,0:T(8,128)(2,1)} %get-tuple-element.90), channel_id=1, source_target_pairs={{0,4},{1,5},{2,6},{3,7},{4,0},{5,1},{6,2},{7,3},{8,12},{9,13},{10,... | collective-permute-start | bytes 1769480 | tf_op jit(solution)/shard_map/ppermute | solution.py:587
  208.0 22.6 %collective-permute-start.26 = (bf16[4,2,2,24,384]{4,3,2,1,0:T(8,128)(2,1)}, bf16[4,2,2,24,384]{4,3,2,1,0:T(8,128)(2,1)}, u32[]{:S(2)}, u32[]{:S(2)}) collective-permute-start(bf16[4,2,2,24,384]{4,3,2,1,0:T(8,128)(2,1)} %get-tuple-element.103), channel_id=1, source_target_pairs={{0,4},{1,5},{2,6},{3,7},{4,0},{5,1},{6,2},{7,3},{8,12},{9,13},{10,... | collective-permute-start | bytes 884744 | tf_op jit(solution)/shard_map/ppermute | solution.py:587
  208.7 24.0 %collective-permute-start.27 = (bf16[4,2,2,24,384]{4,3,2,1,0:T(8,128)(2,1)}, bf16[4,2,2,24,384]{4,3,2,1,0:T(8,128)(2,1)}, u32[]{:S(2)}, u32[]{:S(2)}) collective-permute-start(bf16[4,2,2,24,384]{4,3,2,1,0:T(8,128)(2,1)} %get-tuple-element.105), channel_id=1, source_target_pairs={{0,2},{1,3},{2,0},{3,1},{4,6},{5,7},{6,4},{7,5},{8,10},{9,11},{10,... | collective-permute-start | bytes 884744 | tf_op jit(solution)/shard_map/ppermute | solution.py:583
  210.1 28.2 %collective-permute-start.28 = (bf16[8,24,768]{2,1,0:T(8,128)(2,1)}, bf16[8,24,768]{2,1,0:T(8,128)(2,1)}, u32[]{:S(2)}, u32[]{:S(2)}) collective-permute-start(bf16[8,24,768]{2,1,0:T(8,128)(2,1)} %bitcast.83), channel_id=1, source_target_pairs={{0,0},{1,16},{2,2},{3,18},{4,4},{5,20},{6,6},{7,22},{8,1},{9,17},{... | collective-permute-start | bytes 884744 | tf_op jit(solution)/shard_map/ppermute | solution.py:688
  213.9 26.4 %collective-permute-start.29 = (bf16[8,24,768]{2,1,0:T(8,128)(2,1)}, bf16[8,24,768]{2,1,0:T(8,128)(2,1)}, u32[]{:S(2)}, u32[]{:S(2)}) collective-permute-start(bf16[8,24,768]{2,1,0:T(8,128)(2,1)} %bitcast.82), channel_id=1, source_target_pairs={{0,1},{1,17},{2,3},{3,19},{4,5},{5,21},{6,7},{7,23},{8,0},{9,16},{... | collective-permute-start | bytes 884744 | tf_op jit(solution)/shard_map/ppermute | solution.py:688
  219.6 20.7 %collective-permute-start.30 = (bf16[8,24,768]{2,1,0:T(8,128)(2,1)}, bf16[8,24,768]{2,1,0:T(8,128)(2,1)}, u32[]{:S(2)}, u32[]{:S(2)}) collective-permute-start(bf16[8,24,768]{2,1,0:T(8,128)(2,1)} %bitcast.81), channel_id=1, source_target_pairs={{0,8},{1,24},{2,10},{3,26},{4,12},{5,28},{6,14},{7,30},{8,9},{9,25... | collective-permute-start | bytes 884744 | tf_op jit(solution)/shard_map/ppermute | solution.py:688
  230.6 26.2 %collective-permute-start.31 = (bf16[8,24,768]{2,1,0:T(8,128)(2,1)}, bf16[8,24,768]{2,1,0:T(8,128)(2,1)}, u32[]{:S(2)}, u32[]{:S(2)}) collective-permute-start(bf16[8,24,768]{2,1,0:T(8,128)(2,1)} %bitcast.80), channel_id=1, source_target_pairs={{0,9},{1,25},{2,11},{3,27},{4,13},{5,29},{6,15},{7,31},{8,8},{9,24... | collective-permute-start | bytes 884744 | tf_op jit(solution)/shard_map/ppermute | solution.py:688
  235.5 21.3 %collective-permute-start.32 = (bf16[4,24,768]{2,1,0:T(8,128)(2,1)}, bf16[4,24,768]{2,1,0:T(8,128)(2,1)}, u32[]{:S(2)}, u32[]{:S(2)}) collective-permute-start(bf16[4,24,768]{2,1,0:T(8,128)(2,1)} %bitcast.86), channel_id=1, source_target_pairs={{0,0},{1,16},{2,2},{3,18},{4,4},{5,20},{6,6},{7,22},{8,1},{9,17},{... | collective-permute-start | bytes 442376 | tf_op jit(solution)/shard_map/ppermute | solution.py:688
  238.3 18.5 %collective-permute-start.33 = (bf16[4,24,768]{2,1,0:T(8,128)(2,1)}, bf16[4,24,768]{2,1,0:T(8,128)(2,1)}, u32[]{:S(2)}, u32[]{:S(2)}) collective-permute-start(bf16[4,24,768]{2,1,0:T(8,128)(2,1)} %bitcast.85), channel_id=1, source_target_pairs={{0,1},{1,17},{2,3},{3,19},{4,5},{5,21},{6,7},{7,23},{8,0},{9,16},{... | collective-permute-start | bytes 442376 | tf_op jit(solution)/shard_map/ppermute | solution.py:688
  240.3 16.5 %collective-permute-start.34 = (bf16[4,24,768]{2,1,0:T(8,128)(2,1)}, bf16[4,24,768]{2,1,0:T(8,128)(2,1)}, u32[]{:S(2)}, u32[]{:S(2)}) collective-permute-start(bf16[4,24,768]{2,1,0:T(8,128)(2,1)} %bitcast.84), channel_id=1, source_target_pairs={{0,8},{1,24},{2,10},{3,26},{4,12},{5,28},{6,14},{7,30},{8,9},{9,25... | collective-permute-start | bytes 442376 | tf_op jit(solution)/shard_map/ppermute | solution.py:688
  240.3 16.5 %collective-permute-start.35 = (bf16[4,24,768]{2,1,0:T(8,128)(2,1)}, bf16[4,24,768]{2,1,0:T(8,128)(2,1)}, u32[]{:S(2)}, u32[]{:S(2)}) collective-permute-start(bf16[4,24,768]{2,1,0:T(8,128)(2,1)} %bitcast.71), channel_id=1, source_target_pairs={{0,9},{1,25},{2,11},{3,27},{4,13},{5,29},{6,15},{7,31},{8,8},{9,24... | collective-permute-start | bytes 442376 | tf_op jit(solution)/shard_map/ppermute | solution.py:688
  260.5 54.2 %all-to-all-start.1 = ((bf16[32,24,768]{2,1,0:T(8,128)(2,1)}), bf16[32,24,768]{2,1,0:T(8,128)(2,1)}, u32[]{:S(2)}, u32[]{:S(2)}) async-start(bf16[32,24,768]{2,1,0:T(8,128)(2,1)} %get-tuple-element.121), calls=%async_computation.1 | async-start | bytes 2359296 | tf_op jit(solution)/shard_map/all_to_all | solution.py:866
  265.5 20.7 %collective-permute-start.36 = (f32[16,768]{1,0:T(8,128)S(1)}, f32[16,768]{1,0:T(8,128)S(1)}, u32[]{:S(2)}, u32[]{:S(2)}) collective-permute-start(f32[16,768]{1,0:T(8,128)S(1)} %concatenate.7), channel_id=1, source_target_pairs={{0,8},{1,9},{2,10},{3,11},{4,12},{5,13},{6,14},{7,15},{8,0},{9,1},... | collective-permute-start | bytes 147464 | tf_op jit(solution)/shard_map/ppermute | solution.py:697
  267.3 30.5 %collective-permute-start.37 = (f32[16,768]{1,0:T(8,128)S(1)}, f32[16,768]{1,0:T(8,128)S(1)}, u32[]{:S(2)}, u32[]{:S(2)}) collective-permute-start(f32[16,768]{1,0:T(8,128)S(1)} %concatenate.7), channel_id=1, source_target_pairs={{0,16},{1,17},{2,18},{3,19},{4,20},{5,21},{6,22},{7,23},{8,24},{9,... | collective-permute-start | bytes 147464 | tf_op jit(solution)/shard_map/ppermute | solution.py:697
  269.7 28.1 %collective-permute-start.38 = (f32[16,768]{1,0:T(8,128)S(1)}, f32[16,768]{1,0:T(8,128)S(1)}, u32[]{:S(2)}, u32[]{:S(2)}) collective-permute-start(f32[16,768]{1,0:T(8,128)S(1)} %concatenate.7), channel_id=1, source_target_pairs={{0,24},{1,25},{2,26},{3,27},{4,28},{5,29},{6,30},{7,31},{8,16},{9,... | collective-permute-start | bytes 147464 | tf_op jit(solution)/shard_map/ppermute | solution.py:697
  320.0 32.6 %all-to-all-start.2 = ((bf16[32,24,768]{2,1,0:T(8,128)(2,1)}), bf16[32,24,768]{2,1,0:T(8,128)(2,1)}, u32[]{:S(2)}, u32[]{:S(2)}) async-start(bf16[32,24,768]{2,1,0:T(8,128)(2,1)} %bitcast.68), calls=%async_computation.2 | async-start | bytes 2359296 | tf_op jit(solution)/shard_map/all_to_all | solution.py:866
  (36 other events, 442.5 us)
Sparse Core Ops, SparseCore 0:
  11.0 91.7 all-gather.1

commit v7 on v6

--- a/solution.py
+++ b/solution.py
@@ -318,16 +318,22 @@
     i = pl.program_id(0)
     y, x = place_ref[1], place_ref[2]
 
+    def part(n):
+        if n < first:
+            value = mm(l1o[0], r1o[n], TN) + mm(l1p[0], r1p[n], TN)
+        else:
+            value = mm(l2o[n - first], r2o[0], TN) + mm(l2p[n - first], r2p[0], TN)
+        return value.reshape(acc.shape[1:])
+
     @pl.when(i == 0)
     def _():
-        acc[...] = jnp.zeros_like(acc)
-
-    for n in range(first + second):
-        if n < first:
-            part = mm(l1o[0], r1o[n], TN) + mm(l1p[0], r1p[n], TN)
-        else:
-            part = mm(l2o[n - first], r2o[0], TN) + mm(l2p[n - first], r2p[0], TN)
-        acc[n] += part.reshape(acc.shape[1:])
+        for n in range(first + second):
+            acc[n] = part(n)
+
+    @pl.when(i > 0)
+    def _():
+        for n in range(first + second):
+            acc[n] += part(n)
 
     @pl.when(i == steps - 1)
     def _():
@@ -392,8 +398,9 @@
     return jnp.where(u < 0, tail, 1.0 - tail), raised * (1.0 / math.sqrt(2.0 * math.pi))
 
 
-def hidden_body(a2_ref, dy_ref, wu_ref, wd_ref, bu_ref, out_ref, sum_ref):
-    u = mm(a2_ref[0], wu_ref[0], NN) + bu_ref[0]
+def hidden_body(a2_ref, dy_ref, wu_ref, wd_ref, vec_ref, out_ref, sum_ref, *, first):
+    row = first + pl.program_id(0)
+    u = mm(a2_ref[0], wu_ref[0], NN) + vec_ref[pl.ds(row, 1), :]
     de = mm(dy_ref[0], wd_ref[0], NT)
     dist, density = gelu_parts(u)
     out_ref[0, 0] = (u * dist).astype(bf16)
@@ -415,7 +422,7 @@
     splits = weights.shape[0] // 2
     blocks = splits // 2
     both, sums = call(
-        hidden_body,
+        functools.partial(hidden_body, first=8 + first),
         blocks * 4 * count * width * width,
         blocks * (8 * count * width + 4 * width * width),
         after=after,
@@ -425,7 +432,7 @@
             pl.BlockSpec((1, step, width), lambda j, i: (2, i, 0)),
             pl.BlockSpec((1, width, width), lambda j, i: (first + j, 0, 0)),
             pl.BlockSpec((1, width, width), lambda j, i: (splits + first + j, 0, 0)),
-            pl.BlockSpec((1, 1, width), lambda j, i: (8 + first + j, 0, 0)),
+            pl.BlockSpec(vecs.shape, lambda j, i: (0, 0)),
         ],
         out_specs=[
             pl.BlockSpec((2, 1, step, width), lambda j, i: (0, j, i, 0)),
@@ -435,7 +442,7 @@
             jax.ShapeDtypeStruct((2, blocks, count, width), bf16),
             jax.ShapeDtypeStruct((blocks, 8, width), f32),
         ],
-    )(acts, acts, weights, weights, vecs[:, None, :])
+    )(acts, acts, weights, weights, vecs)
     return both.reshape(2 * blocks, count, width), sums
 
 
@@ -696,14 +703,14 @@
     def get(move):
         return lax.ppermute(value, AXES, to_place(move))
 
+    value = value + over_c(value)
+    by_x, by_y = over_x(value), over_y(value)
+    across = get(lambda z, y, x, c: (z, 1 - y, 1 - x, c))
+    value = (value + by_x) + (by_y + across)
     near = get(lambda z, y, x, c: (z ^ 1, y, x, c))
     far = get(lambda z, y, x, c: (z ^ 2, y, x, c))
     last = get(lambda z, y, x, c: (z ^ 3, y, x, c))
-    value = (value + near) + (far + last)
-    by_x, by_y = over_x(value), over_y(value)
-    across = get(lambda z, y, x, c: (z, 1 - y, 1 - x, c))
-    value = (value + by_x) + (by_y + across)
-    return value + over_c(value)
+    return (value + near) + (far + last)
 
 
 def pack_body(slot_ref, *refs, orders, per):
@@ -931,7 +938,6 @@
         es, dus = [(v, 0, half) for v in (ed0, ed1)], [(v, half, half) for v in (ed0, ed1)]
         grad_in, two_sums = grad_two(flat_tokens, part, dus, mlp_weights, vecs, after=(high.made,))
         terms.append(advance(place, [], [high], after=(grad_in,)))
-        last = high.made
         orders = [orders[0] + orders[1], orders[2]]
     else:
         ed0, up_sum0 = hidden(0, acts, mlp_weights, vecs)
@@ -945,7 +951,6 @@
         es, dus = [(v, 0, half) for v in (ed0, ed1)], [(v, half, half) for v in (ed0, ed1)]
         part, one_sums = grad_one(flat_tokens, dy, (og, 0, 3), attn_weights, vecs)
         grad_in, two_sums = grad_two(flat_tokens, part, dus, mlp_weights, vecs)
-        last = grad_in
     up_sums = [up_sum0, up_sum1]
 
     one_sums, two_sums = jnp.sum(one_sums, axis=1), jnp.sum(two_sums, axis=1)
@@ -959,9 +964,9 @@
     match = owners[None, :] == slot_ids[:, None]
     slots = jnp.sum(jnp.where(match, jnp.arange(1, owners.shape[0] + 1, dtype=jnp.int32)[None], 0), axis=1) - 1
     has_block = jnp.any(owners == my_index)
-    out = output(flat_tokens, (og, 3, 1), es, attn_weights, mlp_weights, vecs, after=(last,))
-    shards, outgoing, squares = pack(slots, terms, orders, after=(out,))
+    shards, outgoing, squares = pack(slots, terms, orders, after=(grad_in,))
     left_low, right_low = to_low(root_left[0], root_right[0], after=(squares,))
+    out = output(flat_tokens, (og, 3, 1), es, attn_weights, mlp_weights, vecs, after=(left_low,))
     local = jnp.concatenate([grad_vectors, jnp.sum(squares, axis=0)[None], jnp.zeros((2, width), f32)])
     total = everywhere(local) if paired else lax.psum(local, AXES)
     vector_sums = total[:vec_rows]

time: 365 us -> 351 us (0.962)
  waiting for transfers between devices: 81.9 us -> 68.1 us
    ppermute x4, waiting for transfers between devices: 29.7 us -> 10.7 us  [get(): return lax.ppermute(value, AXES, to_place(move))]
    all_to_all x3, waiting for transfers between devices: 19.1 us -> 8.09 us  [to_all(): return lax.all_to_all(value, AXES, split_axis=0, concat_axis=0, tiled=True)]
    ppermute x8, waiting for transfers between devices: 0.02 us -> 9 us  [advance(): lax.ppermute(v, AXES, to_place(lambda z, y, x, c, m=m: (2 * c + ((z ^ m)...]
    ppermute x9, waiting for transfers between devices: 14 us -> 21.7 us  [over_x(): lax.ppermute(value, AXES, to_place(lambda z, y, x, c: (z, y, 1 - x, c)))]
  transfers between devices with their start and end apart: 47 -> 47, of which waited for: 15 -> 17; matrix products, arithmetic and copies ran while one was open for 5% -> 5% of each run, Pallas kernels for 41% -> 43%
where the time goes in v7:
time: 351 us; the launch traced here: 350 us
  Pallas kernels  166 us (47%)
  starting transfers between devices  76 us (22%)
  waiting for transfers between devices  68.1 us (19%)
  between operations  17.8 us (5%)
  other arithmetic  14.9 us (4%)
  local copies, waits for them, and re-layouts  6.61 us (2%)
    pallas_call x19, Pallas kernels, call(): return lambda *operands: made(*operands, *after)  166 us
    ppermute x9, waiting for transfers between devices, over_x(): lax.ppermute(value, AXES, to_place(lambda z, y, x, c: (z, y, 1 - x, c)))  21.7 us
    ppermute x8, starting transfers between devices, advance(): lax.ppermute(v, AXES, to_place(lambda z, y, x, c, m=m: (2 * c + ((z ^ m)...  20.5 us
    all_to_all x3, starting transfers between devices, to_all(): return lax.all_to_all(value, AXES, split_axis=0, concat_axis=0, tiled=True)  19 us
    ppermute x9, starting transfers between devices, over_x(): lax.ppermute(value, AXES, to_place(lambda z, y, x, c: (z, y, 1 - x, c)))  11.6 us
    ppermute x4, waiting for transfers between devices, get(): return lax.ppermute(value, AXES, to_place(move))  10.7 us
    ppermute x9, starting transfers between devices, over_y(): lax.ppermute(value, AXES, to_place(lambda z, y, x, c: (z, 1 - y, x, c)))  10.3 us
    ppermute x3, waiting for transfers between devices, over_z(): lax.ppermute(value, AXES, to_place(lambda z, y, x, c: ((z + by) % 4, y, x...  9.35 us
  transfers between devices with their start and end apart: 47, of which 17 were waited for; matrix products, arithmetic and copies ran while one was open for 5% of the time, Pallas kernels for 43%

profile of v7, /device:TPU:0, one launch (start us, length us, event | category | flops | bytes accessed | tf_op | source)
XLA Modules:
  0.0 349.8 jit_solution(4897446562911792294)
XLA Ops:
  9.3 4.1 %collective-permute-start.1 = (bf16[4,24,768]{2,1,0:T(8,128)(2,1)S(1)}, bf16[4,24,768]{2,1,0:T(8,128)(2,1)S(1)}, u32[]{:S(2)}, u32[]{:S(2)}) collective-permute-start(bf16[4,24,768]{2,1,0:T(8,128)(2,1)S(1)} %get-tuple-element.135), channel_id=1, source_target_pairs={{0,16},{1,17},{2,18},{3,19},{4,20},{5,21},{6,22},{7,23},{8,24},{9,... | collective-permute-start | bytes 442376 | tf_op jit(solution)/shard_map/ppermute | solution.py:598
  15.4 6.6 %collective-permute-done.1 = bf16[4,24,768]{2,1,0:T(8,128)(2,1)S(1)} collective-permute-done((bf16[4,24,768]{2,1,0:T(8,128)(2,1)S(1)}, bf16[4,24,768]{2,1,0:T(8,128)(2,1)S(1)}, u32[]{:S(2)}, u32[]{:S(2)}) %collective-permute-start.1) | collective-permute-done | bytes 147488 | tf_op jit(solution)/shard_map/ppermute | solution.py:598
  30.1 9.6 %all-to-all-start = ((bf16[32,2,156]{2,1,0:T(2,128)(2,1)}), bf16[32,2,156]{2,1,0:T(2,128)(2,1)S(1)}, u32[]{:S(2)}, u32[]{:S(2)}) async-start(bf16[32,2,156]{2,1,0:T(2,128)(2,1)} %reshape.150), calls=%async_computation | async-start | bytes 65536 | tf_op jit(solution)/shard_map/all_to_all | solution.py:873
  47.4 6.5 %collective-permute-done.5.refs_3_ = bf16[2,4,24,768]{3,2,1,0:T(8,128)(2,1)S(1)} collective-permute-done((bf16[2,4,24,768]{3,2,1,0:T(8,128)(2,1)S(1)}, bf16[2,4,24,768]{3,2,1,0:T(8,128)(2,1)S(1)}, u32[]{:S(2)}, u32[]{:S(2)}) %collective-permute-start.5) | collective-permute-done | bytes 294944 | tf_op jit(solution)/shard_map/ppermute | solution.py:594
  54.2 3.9 %collective-permute-done.6.refs_4_ = bf16[2,4,24,768]{3,2,1,0:T(8,128)(2,1)} collective-permute-done((bf16[2,4,24,768]{3,2,1,0:T(8,128)(2,1)S(1)}, bf16[2,4,24,768]{3,2,1,0:T(8,128)(2,1)}, u32[]{:S(2)}, u32[]{:S(2)}) %collective-permute-start.6) | collective-permute-done | bytes 294944 | tf_op jit(solution)/shard_map/ppermute | solution.py:590
  63.1 14.1 %shard_map.229 = (bf16[1024,768]{1,0:T(8,128)(2,1)}, bf16[1024,768]{1,0:T(8,128)(2,1)}, bf16[1024,768]{1,0:T(8,128)(2,1)}, bf16[1024,768]{1,0:T(8,128)(2,1)}, bf...) custom-call(s32[4]{0:T(128)} %pad_add_fusion.place_ref.refs_0_, bf16[1024,768]{1,0:T(8,128)(2,1)} %bitcast.58, ...), custom_call_target="tpu_custom_call" | custom-call | flops 4831838208 | bytes 25165824 | tf_op jit(solution)/shard_map/pallas_call | solution.py:75
  77.2 25.4 %shard_map.230 = (bf16[4,1024,768]{2,1,0:T(8,128)(2,1)}, f32[3,16,768]{2,1,0:T(8,128)}, bf16[3,1024,768]{2,1,0:T(8,128)(2,1)}) custom-call(bf16[3,1024,768]{2,1,0:T(8,128)(2,1)} %get-tuple-element.71.acts_ref, s32[1024,1]{1,0:T(8,128)} %bitcast.69, s32[2,1,512]{2,1,0:T(1,128)} %broadcast_in_dim.44.row_ref, ...), custom_call_target="tpu_custom_call", output_to_operand_aliasing={{2}: (0, {})} | custom-call | flops 9663676416 | bytes 18874368 | tf_op jit(solution)/shard_map/pallas_call | solution.py:75
  103.3 13.0 %shard_map.231 = (bf16[2,2,1024,768]{3,2,1,0:T(8,128)(2,1)}, f32[2,8,768]{2,1,0:T(8,128)}) custom-call(bf16[3,1024,768]{2,1,0:T(8,128)(2,1)} %get-tuple-element.77.a2_ref.dy_ref.refs_0_.refs_1_.refs_7_, bf16[3,1024,768]{2,1,0:T(8,128)(2,1)} %get-tuple-element.77.a2_ref.dy_ref.refs_0_.refs_1_.refs_7_, ...), custom_call_target="tpu_custom_call" | custom-call | flops 4831838208 | bytes 17301504 | tf_op jit(solution)/shard_map/pallas_call | solution.py:75
  116.6 13.1 %shard_map.232 = (bf16[2,2,1024,768]{3,2,1,0:T(8,128)(2,1)}, f32[2,8,768]{2,1,0:T(8,128)}) custom-call(bf16[3,1024,768]{2,1,0:T(8,128)(2,1)} %get-tuple-element.77.a2_ref.dy_ref.refs_0_.refs_1_.refs_7_, bf16[3,1024,768]{2,1,0:T(8,128)(2,1)} %get-tuple-element.77.a2_ref.dy_ref.refs_0_.refs_1_.refs_7_, ...), custom_call_target="tpu_custom_call" | custom-call | flops 4831838208 | bytes 17301504 | tf_op jit(solution)/shard_map/pallas_call | solution.py:75
  129.8 11.2 %shard_map.233 = (bf16[4,2,2,2,24,384]{5,4,3,2,1,0:T(8,128)(2,1)}, bf16[4,2,2,2,24,384]{5,4,3,2,1,0:T(8,128)(2,1)}, bf16[4,2,2,2,24,384]{5,4,3,2,1,0:T(8,128)(2,1)}, bf16[4,2,2,2,24,384]{5,4,3,2,1,0:T(8,128)(2,1)}) custom-call(s32[4]{0:T(128)} %pad_add_fusion.place_ref.refs_0_, bf16[3,1024,768]{2,1,0:T(8,128)(2,1)} %get-tuple-element.77.a2_ref.dy_ref.refs_0_.refs_1_.refs_7_, ...), custom_call_target="tpu_custom_call" | custom-call | flops 4831838208 | bytes 12582912 | tf_op jit(solution)/shard_map/pallas_call | solution.py:75
  143.1 10.9 %shard_map.234 = (bf16[4,2,2,2,24,384]{5,4,3,2,1,0:T(8,128)(2,1)}, bf16[4,2,2,2,24,384]{5,4,3,2,1,0:T(8,128)(2,1)}, bf16[4,2,2,2,24,384]{5,4,3,2,1,0:T(8,128)(2,1)}, bf16[4,2,2,2,24,384]{5,4,3,2,1,0:T(8,128)(2,1)}) custom-call(s32[4]{0:T(128)} %pad_add_fusion.place_ref.refs_0_, bf16[3,1024,768]{2,1,0:T(8,128)(2,1)} %get-tuple-element.77.a2_ref.dy_ref.refs_0_.refs_1_.refs_7_, ...), custom_call_target="tpu_custom_call" | custom-call | flops 4831838208 | bytes 12582912 | tf_op jit(solution)/shard_map/pallas_call | solution.py:75
  164.7 10.9 %shard_map.236 = (bf16[4,2,2,2,24,384]{5,4,3,2,1,0:T(8,128)(2,1)}, bf16[4,2,2,2,24,384]{5,4,3,2,1,0:T(8,128)(2,1)}, bf16[4,2,2,2,24,384]{5,4,3,2,1,0:T(8,128)(2,1)}, bf16[4,2,2,2,24,384]{5,4,3,2,1,0:T(8,128)(2,1)}) custom-call(s32[4]{0:T(128)} %pad_add_fusion.place_ref.refs_0_, bf16[3,1024,768]{2,1,0:T(8,128)(2,1)} %get-tuple-element.77.a2_ref.dy_ref.refs_0_.refs_1_.refs_7_, ...), custom_call_target="tpu_custom_call" | custom-call | flops 4831838208 | bytes 12582912 | tf_op jit(solution)/shard_map/pallas_call | solution.py:75
  177.7 7.1 %collective-permute-done.22.refs_2_ = bf16[4,2,2,2,24,384]{5,4,3,2,1,0:T(8,128)(2,1)} collective-permute-done((bf16[4,2,2,2,24,384]{5,4,3,2,1,0:T(8,128)(2,1)}, bf16[4,2,2,2,24,384]{5,4,3,2,1,0:T(8,128)(2,1)}, u32[]{:S(2)}, u32[]{:S(2)}) %collective-permute-start.22) | collective-permute-done | bytes 589856 | tf_op jit(solution)/shard_map/ppermute | solution.py:590
  189.9 9.8 %shard_map.238 = (f32[1024,768]{1,0:T(8,128)}, f32[3,8,768]{2,1,0:T(8,128)}) custom-call(bf16[1024,768]{1,0:T(8,128)(2,1)} %bitcast.59, bf16[1024,768]{1,0:T(8,128)(2,1)} %bitcast.67, bf16[4,1024,768]{2,1,0:T(8,128)(2,1)} %get-tuple-element.76.refs_3_.refs_5_.refs_2_.refs_1_, bf16[4,768,768]{2,1,0:T(8,128)(2,1)} %get-tuple-element.80.refs_3_.refs_4_, ...), custom_call_target="tpu_custom_call" | custom-call | flops 3623878656 | bytes 14548992 | tf_op jit(solution)/shard_map/pallas_call | solution.py:75
  201.8 4.2 %shard_map.239 = (bf16[4,2,2,24,384]{4,3,2,1,0:T(8,128)(2,1)}, bf16[4,2,2,24,384]{4,3,2,1,0:T(8,128)(2,1)}, bf16[4,2,2,24,384]{4,3,2,1,0:T(8,128)(2,1)}, bf16[4,...) custom-call(s32[4]{0:T(128)} %pad_add_fusion.place_ref.refs_0_, ...), custom_call_target="tpu_custom_call" | custom-call | bytes 9437184 | tf_op jit(solution)/shard_map/pallas_call | solution.py:75
  209.2 3.8 %collective-permute-start.26 = (bf16[8,24,768]{2,1,0:T(8,128)(2,1)}, bf16[8,24,768]{2,1,0:T(8,128)(2,1)}, u32[]{:S(2)}, u32[]{:S(2)}) collective-permute-start(bf16[8,24,768]{2,1,0:T(8,128)(2,1)} %bitcast.82), channel_id=1, source_target_pairs={{0,0},{1,16},{2,2},{3,18},{4,4},{5,20},{6,6},{7,22},{8,1},{9,17},{... | collective-permute-start | bytes 884744 | tf_op jit(solution)/shard_map/ppermute | solution.py:695
  213.0 5.0 %collective-permute-start.27 = (bf16[8,24,768]{2,1,0:T(8,128)(2,1)}, bf16[8,24,768]{2,1,0:T(8,128)(2,1)}, u32[]{:S(2)}, u32[]{:S(2)}) collective-permute-start(bf16[8,24,768]{2,1,0:T(8,128)(2,1)} %bitcast.81), channel_id=1, source_target_pairs={{0,1},{1,17},{2,3},{3,19},{4,5},{5,21},{6,7},{7,23},{8,0},{9,16},{... | collective-permute-start | bytes 884744 | tf_op jit(solution)/shard_map/ppermute | solution.py:695
  220.1 11.0 %shard_map.240 = (bf16[1024,768]{1,0:T(8,128)(2,1)}, f32[2,8,768]{2,1,0:T(8,128)}) custom-call(bf16[1024,768]{1,0:T(8,128)(2,1)} %bitcast.60, f32[1024,768]{1,0:T(8,128)} %get-tuple-element.101.refs_13_.refs_1_, bf16[4,1024,768]{2,1,0:T(8,128)(2,1)} %bitcast.56, bf16[4,1024,768]{2,1,0:T(8,128)(2,1)} %bitcast.50, ...), custom_call_target="tpu_custom_call" | custom-call | flops 4831838208 | bytes 17301504 | tf_op jit(solution)/shard_map/pallas_call | solution.py:75
  239.4 4.7 %collective-permute-start.35 = (bf16[4,24,768]{2,1,0:T(8,128)(2,1)}, bf16[4,24,768]{2,1,0:T(8,128)(2,1)}, u32[]{:S(2)}, u32[]{:S(2)}) collective-permute-start(bf16[4,24,768]{2,1,0:T(8,128)(2,1)} %bitcast.83), channel_id=1, source_target_pairs={{0,9},{1,25},{2,11},{3,27},{4,13},{5,29},{6,15},{7,31},{8,8},{9,24... | collective-permute-start | bytes 442376 | tf_op jit(solution)/shard_map/ppermute | solution.py:695
  245.7 7.9 %collective-permute-done.34.refs_7_ = bf16[4,24,768]{2,1,0:T(8,128)(2,1)} collective-permute-done((bf16[4,24,768]{2,1,0:T(8,128)(2,1)}, bf16[4,24,768]{2,1,0:T(8,128)(2,1)}, u32[]{:S(2)}, u32[]{:S(2)}) %collective-permute-start.34) | collective-permute-done | bytes 147488 | tf_op jit(solution)/shard_map/ppermute | solution.py:695
  253.6 3.7 %shard_map.242 = (f32[12,24,768]{2,1,0:T(8,128)}, bf16[32,24,768]{2,1,0:T(8,128)(2,1)}, f32[24,768]{1,0:T(8,128)}) custom-call(s32[32]{0:T(128)} %broadcast_add_fusion.refs_0_, bf16[8,24,768]{2,1,0:T(8,128)(2,1)} %collective-permute-done.26.refs_1_, bf16[8,24,768]{2,1,0:T(8,128)(2,1)} %collective-permute-done.27.refs_2_, ...), custom_call_target="tpu_custom_call" | custom-call | bytes 3538944 | tf_op jit(solution)/shard_map/pallas_call | solution.py:75
  257.4 5.8 %all-to-all-start.1 = ((bf16[32,24,768]{2,1,0:T(8,128)(2,1)}), bf16[32,24,768]{2,1,0:T(8,128)(2,1)}, u32[]{:S(2)}, u32[]{:S(2)}) async-start(bf16[32,24,768]{2,1,0:T(8,128)(2,1)} %get-tuple-element.122), calls=%async_computation.1 | async-start | bytes 2359296 | tf_op jit(solution)/shard_map/all_to_all | solution.py:873
  268.4 6.7 %collective-permute-done.37 = f32[16,768]{1,0:T(8,128)S(1)} collective-permute-done((f32[16,768]{1,0:T(8,128)S(1)}, f32[16,768]{1,0:T(8,128)S(1)}, u32[]{:S(2)}, u32[]{:S(2)}) %collective-permute-start.37) | collective-permute-done | bytes 49184 | tf_op jit(solution)/shard_map/ppermute | solution.py:590
  277.6 5.7 %collective-permute-start.41 = (f32[16,768]{1,0:T(8,128)}, f32[16,768]{1,0:T(8,128)}, u32[]{:S(2)}, u32[]{:S(2)}) collective-permute-start(f32[16,768]{1,0:T(8,128)} %add_add_fusion.1), channel_id=1, source_target_pairs={{0,16},{1,17},{2,18},{3,19},{4,20},{5,21},{6,22},{7,23},{8,24},{9,... | collective-permute-start | bytes 147464 | tf_op jit(solution)/shard_map/ppermute | solution.py:704
  283.3 3.5 shard_map.243
  286.8 9.1 %collective-permute-done.41 = f32[16,768]{1,0:T(8,128)} collective-permute-done((f32[16,768]{1,0:T(8,128)}, f32[16,768]{1,0:T(8,128)}, u32[]{:S(2)}, u32[]{:S(2)}) %collective-permute-start.41) | collective-permute-done | bytes 49184 | tf_op jit(solution)/shard_map/ppermute | solution.py:704
  300.7 5.3 %shard_map.245 = bf16[768,768]{1,0:T(8,128)(2,1)} custom-call(f32[2]{0:T(128)} %pad_maximum_fusion.1.scale_ref, bf16[768,768]{1,0:T(8,128)(2,1)} %bitcast.29.s_ref, bf16[768,768]{1,0:T(8,128)(2,1)} %get-tuple-element.116.refs_7_.l_ref, bf16[768,768]{1,0:T(8,128)(2,1)} %get-tuple-element.123.r_ref), custom_call_target="tpu_custom_call" | custom-call | flops 1811939328 | bytes 4718592 | tf_op jit(solution)/shard_map/pallas_call | solution.py:75
  306.0 3.5 %all-to-all-start.2 = ((bf16[32,24,768]{2,1,0:T(8,128)(2,1)}), bf16[32,24,768]{2,1,0:T(8,128)(2,1)}, u32[]{:S(2)}, u32[]{:S(2)}) async-start(bf16[32,24,768]{2,1,0:T(8,128)(2,1)} %bitcast.68), calls=%async_computation.2 | async-start | bytes 2359296 | tf_op jit(solution)/shard_map/all_to_all | solution.py:873
  310.8 11.1 %shard_map.244 = bf16[1024,768]{1,0:T(8,128)(2,1)} custom-call(bf16[1024,768]{1,0:T(8,128)(2,1)} %bitcast.61, bf16[4,1024,768]{2,1,0:T(8,128)(2,1)} %get-tuple-element.76.refs_3_.refs_5_.refs_2_.refs_1_, bf16[4,1024,768]{2,1,0:T(8,128)(2,1)} %bitcast.57, bf16[4,1024,768]{2,1,0:T(8,128)(2,1)} %bitcast.51, ...), custom_call_target="tpu_custom_call" | custom-call | flops 6039797760 | bytes 16908288 | tf_op jit(solution)/shard_map/pallas_call | solution.py:75
  323.3 7.2 %shard_map.247 = (f32[768,768]{1,0:T(8,128)}, f32[768,768]{1,0:T(8,128)}) custom-call(s32[1]{0:T(128)} %bitcast.31.has_ref, f32[2]{0:T(128)} %pad_maximum_fusion.1.scale_ref, bf16[768,768]{1,0:T(8,128)(2,1)} %bitcast.29.s_ref, f32[768,768]{1,0:T(8,128)} %bitcast.77, f32[768,768]{1,0:T(8,128)} %bitcast.78), custom_call_target="tpu_custom_call" | custom-call | flops 1811939328 | bytes 10616832 | tf_op jit(solution)/shard_map/pallas_call | solution.py:75
  330.5 8.1 %all-to-all-done.2.p_ref = bf16[32,24,768]{2,1,0:T(8,128)(2,1)} async-done(((bf16[32,24,768]{2,1,0:T(8,128)(2,1)}), bf16[32,24,768]{2,1,0:T(8,128)(2,1)}, u32[]{:S(2)}, u32[]{:S(2)}) %all-to-all-start.2) | async-done | bytes 1179680 | tf_op jit(solution)/shard_map/all_to_all | solution.py:873
  338.6 3.3 shard_map.246
  (164 shorter events, 76.5 us)
Async XLA Ops:
  7.2 96.1 %all-gather.2.cloned.1.call-start = ((), (), s32[]{:S(2)}) async-start(), calls=%async_computation.3 | async-start | bytes 9732096 | tf_op jit(solution)/shard_map/all_gather | solution.py:904
  24.9 15.3 %collective-permute-start.3 = (bf16[4,4,24,768]{3,2,1,0:T(8,128)(2,1)S(1)}, bf16[4,4,24,768]{3,2,1,0:T(8,128)(2,1)S(1)}, u32[]{:S(2)}, u32[]{:S(2)}) collective-permute-start(bf16[4,4,24,768]{3,2,1,0:T(8,128)(2,1)S(1)} %pad_maximum_fusion.refs_0_), channel_id=1, source_target_pairs={{0,2},{1,3},{2,0},{3,1},{4,6},{5,7},{6,4},{7,5},{8,10},{9,11},{10,... | collective-permute-start | bytes 1769480 | tf_op jit(solution)/shard_map/ppermute | solution.py:590
  26.4 15.6 %collective-permute-start.4 = (bf16[4,4,24,768]{3,2,1,0:T(8,128)(2,1)S(1)}, bf16[4,4,24,768]{3,2,1,0:T(8,128)(2,1)S(1)}, u32[]{:S(2)}, u32[]{:S(2)}) collective-permute-start(bf16[4,4,24,768]{3,2,1,0:T(8,128)(2,1)S(1)} %pad_maximum_fusion.refs_0_), channel_id=1, source_target_pairs={{0,4},{1,5},{2,6},{3,7},{4,0},{5,1},{6,2},{7,3},{8,12},{9,13},{10,... | collective-permute-start | bytes 1769480 | tf_op jit(solution)/shard_map/ppermute | solution.py:594
  30.1 30.2 %all-to-all-start = ((bf16[32,2,156]{2,1,0:T(2,128)(2,1)}), bf16[32,2,156]{2,1,0:T(2,128)(2,1)S(1)}, u32[]{:S(2)}, u32[]{:S(2)}) async-start(bf16[32,2,156]{2,1,0:T(2,128)(2,1)} %reshape.150), calls=%async_computation | async-start | bytes 65536 | tf_op jit(solution)/shard_map/all_to_all | solution.py:873
  40.2 13.8 %collective-permute-start.5 = (bf16[2,4,24,768]{3,2,1,0:T(8,128)(2,1)S(1)}, bf16[2,4,24,768]{3,2,1,0:T(8,128)(2,1)S(1)}, u32[]{:S(2)}, u32[]{:S(2)}) collective-permute-start(bf16[2,4,24,768]{3,2,1,0:T(8,128)(2,1)S(1)} %slice.33), channel_id=1, source_target_pairs={{0,4},{1,5},{2,6},{3,7},{4,0},{5,1},{6,2},{7,3},{8,12},{9,13},{10,... | collective-permute-start | bytes 884744 | tf_op jit(solution)/shard_map/ppermute | solution.py:594
  42.1 16.0 %collective-permute-start.6 = (bf16[2,4,24,768]{3,2,1,0:T(8,128)(2,1)S(1)}, bf16[2,4,24,768]{3,2,1,0:T(8,128)(2,1)}, u32[]{:S(2)}, u32[]{:S(2)}) collective-permute-start(bf16[2,4,24,768]{3,2,1,0:T(8,128)(2,1)S(1)} %slice.34), channel_id=1, source_target_pairs={{0,2},{1,3},{2,0},{3,1},{4,6},{5,7},{6,4},{7,5},{8,10},{9,11},{10,... | collective-permute-start | bytes 884744 | tf_op jit(solution)/shard_map/ppermute | solution.py:590
  43.6 17.9 %collective-permute-start.7 = (bf16[4,4,24,768]{3,2,1,0:T(8,128)(2,1)S(1)}, bf16[4,4,24,768]{3,2,1,0:T(8,128)(2,1)S(1)}, u32[]{:S(2)}, u32[]{:S(2)}) collective-permute-start(bf16[4,4,24,768]{3,2,1,0:T(8,128)(2,1)S(1)} %pad_maximum_fusion.refs_0_), channel_id=1, source_target_pairs={{0,1},{1,0},{2,3},{3,2},{4,5},{5,4},{6,7},{7,6},{8,9},{9,8},{10,11... | collective-permute-start | bytes 1769480 | tf_op jit(solution)/shard_map/ppermute | solution.py:586
  43.6 17.9 %collective-permute-start.8 = (bf16[4,4,24,768]{3,2,1,0:T(8,128)(2,1)S(1)}, bf16[4,4,24,768]{3,2,1,0:T(8,128)(2,1)}, u32[]{:S(2)}, u32[]{:S(2)}) collective-permute-start(bf16[4,4,24,768]{3,2,1,0:T(8,128)(2,1)S(1)} %collective-permute-done.3.refs_1_), channel_id=1, source_target_pairs={{0,1},{1,0},{2,3},{3,2},{4,5},{5,4},{6,7},{7,6},{8,9},{9,8},{10,11... | collective-permute-start | bytes 1769480 | tf_op jit(solution)/shard_map/ppermute | solution.py:586
  44.1 17.4 %collective-permute-start.9 = (bf16[4,4,24,768]{3,2,1,0:T(8,128)(2,1)S(1)}, bf16[4,4,24,768]{3,2,1,0:T(8,128)(2,1)}, u32[]{:S(2)}, u32[]{:S(2)}) collective-permute-start(bf16[4,4,24,768]{3,2,1,0:T(8,128)(2,1)S(1)} %collective-permute-done.4.refs_2_), channel_id=1, source_target_pairs={{0,1},{1,0},{2,3},{3,2},{4,5},{5,4},{6,7},{7,6},{8,9},{9,8},{10,11... | collective-permute-start | bytes 1769480 | tf_op jit(solution)/shard_map/ppermute | solution.py:586
  102.7 14.0 %collective-permute-start.12 = (bf16[3,1024,768]{2,1,0:T(8,128)(2,1)}, bf16[3,1024,768]{2,1,0:T(8,128)(2,1)}, u32[]{:S(2)}, u32[]{:S(2)}) collective-permute-start(bf16[3,1024,768]{2,1,0:T(8,128)(2,1)} %get-tuple-element.77.a2_ref.dy_ref.refs_0_.refs_1_.refs_7_), channel_id=1, source_target_pairs={{0,1},{1,0},{2,3},{3,2},{4,5},{5,4},{6,7},{7,6},{8,9},{9,8},{10,11... | collective-permute-start | bytes 14155784 | tf_op jit(solution)/shard_map/ppermute | solution.py:586
  103.2 26.6 %collective-permute-start.14 = (bf16[4,1024,768]{2,1,0:T(8,128)(2,1)}, bf16[4,1024,768]{2,1,0:T(8,128)(2,1)}, u32[]{:S(2)}, u32[]{:S(2)}) collective-permute-start(bf16[4,1024,768]{2,1,0:T(8,128)(2,1)} %get-tuple-element.76.refs_3_.refs_5_.refs_2_.refs_1_), channel_id=1, source_target_pairs={{0,1},{1,0},{2,3},{3,2},{4,5},{5,4},{6,7},{7,6},{8,9},{9,8},{10,11... | collective-permute-start | bytes 18874376 | tf_op jit(solution)/shard_map/ppermute | solution.py:586
  116.2 26.8 %collective-permute-start.17 = (bf16[4,1024,768]{2,1,0:T(8,128)(2,1)}, bf16[4,1024,768]{2,1,0:T(8,128)(2,1)}, u32[]{:S(2)}, u32[]{:S(2)}) collective-permute-start(bf16[4,1024,768]{2,1,0:T(8,128)(2,1)} %bitcast.52), channel_id=1, source_target_pairs={{0,1},{1,0},{2,3},{3,2},{4,5},{5,4},{6,7},{7,6},{8,9},{9,8},{10,11... | collective-permute-start | bytes 18874376 | tf_op jit(solution)/shard_map/ppermute | solution.py:586
  129.7 35.0 %collective-permute-start.13 = (bf16[4,1024,768]{2,1,0:T(8,128)(2,1)}, bf16[4,1024,768]{2,1,0:T(8,128)(2,1)}, u32[]{:S(2)}, u32[]{:S(2)}) collective-permute-start(bf16[4,1024,768]{2,1,0:T(8,128)(2,1)} %bitcast.46), channel_id=1, source_target_pairs={{0,1},{1,0},{2,3},{3,2},{4,5},{5,4},{6,7},{7,6},{8,9},{9,8},{10,11... | collective-permute-start | bytes 18874376 | tf_op jit(solution)/shard_map/ppermute | solution.py:586
  141.0 16.0 %collective-permute-start.15 = (bf16[4,2,2,2,24,384]{5,4,3,2,1,0:T(8,128)(2,1)}, bf16[4,2,2,2,24,384]{5,4,3,2,1,0:T(8,128)(2,1)}, u32[]{:S(2)}, u32[]{:S(2)}) collective-permute-start(bf16[4,2,2,2,24,384]{5,4,3,2,1,0:T(8,128)(2,1)} %get-tuple-element.82), channel_id=1, source_target_pairs={{0,2},{1,3},{2,0},{3,1},{4,6},{5,7},{6,4},{7,5},{8,10},{9,11},{10,... | collective-permute-start | bytes 1769480 | tf_op jit(solution)/shard_map/ppermute | solution.py:590
  142.0 15.5 %collective-permute-start.16 = (bf16[4,2,2,2,24,384]{5,4,3,2,1,0:T(8,128)(2,1)}, bf16[4,2,2,2,24,384]{5,4,3,2,1,0:T(8,128)(2,1)}, u32[]{:S(2)}, u32[]{:S(2)}) collective-permute-start(bf16[4,2,2,2,24,384]{5,4,3,2,1,0:T(8,128)(2,1)} %get-tuple-element.84), channel_id=1, source_target_pairs={{0,4},{1,5},{2,6},{3,7},{4,0},{5,1},{6,2},{7,3},{8,12},{9,13},{10,... | collective-permute-start | bytes 1769480 | tf_op jit(solution)/shard_map/ppermute | solution.py:594
  160.7 16.1 %collective-permute-start.20 = (bf16[4,2,2,24,384]{4,3,2,1,0:T(8,128)(2,1)}, bf16[4,2,2,24,384]{4,3,2,1,0:T(8,128)(2,1)}, u32[]{:S(2)}, u32[]{:S(2)}) collective-permute-start(bf16[4,2,2,24,384]{4,3,2,1,0:T(8,128)(2,1)} %get-tuple-element.91), channel_id=1, source_target_pairs={{0,4},{1,5},{2,6},{3,7},{4,0},{5,1},{6,2},{7,3},{8,12},{9,13},{10,... | collective-permute-start | bytes 884744 | tf_op jit(solution)/shard_map/ppermute | solution.py:594
  161.9 15.8 %collective-permute-start.21 = (bf16[4,2,2,24,384]{4,3,2,1,0:T(8,128)(2,1)}, bf16[4,2,2,24,384]{4,3,2,1,0:T(8,128)(2,1)}, u32[]{:S(2)}, u32[]{:S(2)}) collective-permute-start(bf16[4,2,2,24,384]{4,3,2,1,0:T(8,128)(2,1)} %get-tuple-element.93), channel_id=1, source_target_pairs={{0,2},{1,3},{2,0},{3,1},{4,6},{5,7},{6,4},{7,5},{8,10},{9,11},{10,... | collective-permute-start | bytes 884744 | tf_op jit(solution)/shard_map/ppermute | solution.py:590
  162.8 22.0 %collective-permute-start.22 = (bf16[4,2,2,2,24,384]{5,4,3,2,1,0:T(8,128)(2,1)}, bf16[4,2,2,2,24,384]{5,4,3,2,1,0:T(8,128)(2,1)}, u32[]{:S(2)}, u32[]{:S(2)}) collective-permute-start(bf16[4,2,2,2,24,384]{5,4,3,2,1,0:T(8,128)(2,1)} %get-tuple-element.94), channel_id=1, source_target_pairs={{0,2},{1,3},{2,0},{3,1},{4,6},{5,7},{6,4},{7,5},{8,10},{9,11},{10,... | collective-permute-start | bytes 1769480 | tf_op jit(solution)/shard_map/ppermute | solution.py:590
  163.9 20.9 %collective-permute-start.23 = (bf16[4,2,2,2,24,384]{5,4,3,2,1,0:T(8,128)(2,1)}, bf16[4,2,2,2,24,384]{5,4,3,2,1,0:T(8,128)(2,1)}, u32[]{:S(2)}, u32[]{:S(2)}) collective-permute-start(bf16[4,2,2,2,24,384]{5,4,3,2,1,0:T(8,128)(2,1)} %get-tuple-element.96), channel_id=1, source_target_pairs={{0,4},{1,5},{2,6},{3,7},{4,0},{5,1},{6,2},{7,3},{8,12},{9,13},{10,... | collective-permute-start | bytes 1769480 | tf_op jit(solution)/shard_map/ppermute | solution.py:594
  175.6 24.1 %collective-permute-start.18 = (bf16[4,2,2,2,24,384]{5,4,3,2,1,0:T(8,128)(2,1)}, bf16[4,2,2,2,24,384]{5,4,3,2,1,0:T(8,128)(2,1)}, u32[]{:S(2)}, u32[]{:S(2)}) collective-permute-start(bf16[4,2,2,2,24,384]{5,4,3,2,1,0:T(8,128)(2,1)} %get-tuple-element.88), channel_id=1, source_target_pairs={{0,2},{1,3},{2,0},{3,1},{4,6},{5,7},{6,4},{7,5},{8,10},{9,11},{10,... | collective-permute-start | bytes 1769480 | tf_op jit(solution)/shard_map/ppermute | solution.py:590
  176.8 22.9 %collective-permute-start.19 = (bf16[4,2,2,2,24,384]{5,4,3,2,1,0:T(8,128)(2,1)}, bf16[4,2,2,2,24,384]{5,4,3,2,1,0:T(8,128)(2,1)}, u32[]{:S(2)}, u32[]{:S(2)}) collective-permute-start(bf16[4,2,2,2,24,384]{5,4,3,2,1,0:T(8,128)(2,1)} %get-tuple-element.90), channel_id=1, source_target_pairs={{0,4},{1,5},{2,6},{3,7},{4,0},{5,1},{6,2},{7,3},{8,12},{9,13},{10,... | collective-permute-start | bytes 1769480 | tf_op jit(solution)/shard_map/ppermute | solution.py:594
  188.8 13.0 %collective-permute-start.25 = (bf16[4,2,2,24,384]{4,3,2,1,0:T(8,128)(2,1)}, bf16[4,2,2,24,384]{4,3,2,1,0:T(8,128)(2,1)}, u32[]{:S(2)}, u32[]{:S(2)}) collective-permute-start(bf16[4,2,2,24,384]{4,3,2,1,0:T(8,128)(2,1)} %get-tuple-element.100), channel_id=1, source_target_pairs={{0,2},{1,3},{2,0},{3,1},{4,6},{5,7},{6,4},{7,5},{8,10},{9,11},{10,... | collective-permute-start | bytes 884744 | tf_op jit(solution)/shard_map/ppermute | solution.py:590
  207.9 23.2 %collective-permute-start.31 = (bf16[4,2,2,24,384]{4,3,2,1,0:T(8,128)(2,1)}, bf16[4,2,2,24,384]{4,3,2,1,0:T(8,128)(2,1)}, u32[]{:S(2)}, u32[]{:S(2)}) collective-permute-start(bf16[4,2,2,24,384]{4,3,2,1,0:T(8,128)(2,1)} %get-tuple-element.109), channel_id=1, source_target_pairs={{0,2},{1,3},{2,0},{3,1},{4,6},{5,7},{6,4},{7,5},{8,10},{9,11},{10,... | collective-permute-start | bytes 884744 | tf_op jit(solution)/shard_map/ppermute | solution.py:590
  209.2 27.5 %collective-permute-start.26 = (bf16[8,24,768]{2,1,0:T(8,128)(2,1)}, bf16[8,24,768]{2,1,0:T(8,128)(2,1)}, u32[]{:S(2)}, u32[]{:S(2)}) collective-permute-start(bf16[8,24,768]{2,1,0:T(8,128)(2,1)} %bitcast.82), channel_id=1, source_target_pairs={{0,0},{1,16},{2,2},{3,18},{4,4},{5,20},{6,6},{7,22},{8,1},{9,17},{... | collective-permute-start | bytes 884744 | tf_op jit(solution)/shard_map/ppermute | solution.py:695
  213.0 25.8 %collective-permute-start.27 = (bf16[8,24,768]{2,1,0:T(8,128)(2,1)}, bf16[8,24,768]{2,1,0:T(8,128)(2,1)}, u32[]{:S(2)}, u32[]{:S(2)}) collective-permute-start(bf16[8,24,768]{2,1,0:T(8,128)(2,1)} %bitcast.81), channel_id=1, source_target_pairs={{0,1},{1,17},{2,3},{3,19},{4,5},{5,21},{6,7},{7,23},{8,0},{9,16},{... | collective-permute-start | bytes 884744 | tf_op jit(solution)/shard_map/ppermute | solution.py:695
  218.0 21.4 %collective-permute-start.28 = (bf16[8,24,768]{2,1,0:T(8,128)(2,1)}, bf16[8,24,768]{2,1,0:T(8,128)(2,1)}, u32[]{:S(2)}, u32[]{:S(2)}) collective-permute-start(bf16[8,24,768]{2,1,0:T(8,128)(2,1)} %bitcast.80), channel_id=1, source_target_pairs={{0,8},{1,24},{2,10},{3,26},{4,12},{5,28},{6,14},{7,30},{8,9},{9,25... | collective-permute-start | bytes 884744 | tf_op jit(solution)/shard_map/ppermute | solution.py:695
  218.0 27.3 %collective-permute-start.29 = (bf16[8,24,768]{2,1,0:T(8,128)(2,1)}, bf16[8,24,768]{2,1,0:T(8,128)(2,1)}, u32[]{:S(2)}, u32[]{:S(2)}) collective-permute-start(bf16[8,24,768]{2,1,0:T(8,128)(2,1)} %bitcast.79), channel_id=1, source_target_pairs={{0,9},{1,25},{2,11},{3,27},{4,13},{5,29},{6,15},{7,31},{8,8},{9,24... | collective-permute-start | bytes 884744 | tf_op jit(solution)/shard_map/ppermute | solution.py:695
  238.8 14.9 %collective-permute-start.34 = (bf16[4,24,768]{2,1,0:T(8,128)(2,1)}, bf16[4,24,768]{2,1,0:T(8,128)(2,1)}, u32[]{:S(2)}, u32[]{:S(2)}) collective-permute-start(bf16[4,24,768]{2,1,0:T(8,128)(2,1)} %bitcast.84), channel_id=1, source_target_pairs={{0,8},{1,24},{2,10},{3,26},{4,12},{5,28},{6,14},{7,30},{8,9},{9,25... | collective-permute-start | bytes 442376 | tf_op jit(solution)/shard_map/ppermute | solution.py:695
  239.4 14.3 %collective-permute-start.35 = (bf16[4,24,768]{2,1,0:T(8,128)(2,1)}, bf16[4,24,768]{2,1,0:T(8,128)(2,1)}, u32[]{:S(2)}, u32[]{:S(2)}) collective-permute-start(bf16[4,24,768]{2,1,0:T(8,128)(2,1)} %bitcast.83), channel_id=1, source_target_pairs={{0,9},{1,25},{2,11},{3,27},{4,13},{5,29},{6,15},{7,31},{8,8},{9,24... | collective-permute-start | bytes 442376 | tf_op jit(solution)/shard_map/ppermute | solution.py:695
  257.4 43.3 %all-to-all-start.1 = ((bf16[32,24,768]{2,1,0:T(8,128)(2,1)}), bf16[32,24,768]{2,1,0:T(8,128)(2,1)}, u32[]{:S(2)}, u32[]{:S(2)}) async-start(bf16[32,24,768]{2,1,0:T(8,128)(2,1)} %get-tuple-element.122), calls=%async_computation.1 | async-start | bytes 2359296 | tf_op jit(solution)/shard_map/all_to_all | solution.py:873
  277.6 18.2 %collective-permute-start.41 = (f32[16,768]{1,0:T(8,128)}, f32[16,768]{1,0:T(8,128)}, u32[]{:S(2)}, u32[]{:S(2)}) collective-permute-start(f32[16,768]{1,0:T(8,128)} %add_add_fusion.1), channel_id=1, source_target_pairs={{0,16},{1,17},{2,18},{3,19},{4,20},{5,21},{6,22},{7,23},{8,24},{9,... | collective-permute-start | bytes 147464 | tf_op jit(solution)/shard_map/ppermute | solution.py:704
  306.0 32.6 %all-to-all-start.2 = ((bf16[32,24,768]{2,1,0:T(8,128)(2,1)}), bf16[32,24,768]{2,1,0:T(8,128)(2,1)}, u32[]{:S(2)}, u32[]{:S(2)}) async-start(bf16[32,24,768]{2,1,0:T(8,128)(2,1)} %bitcast.68), calls=%async_computation.2 | async-start | bytes 2359296 | tf_op jit(solution)/shard_map/all_to_all | solution.py:873
  (33 other events, 427.1 us)
Sparse Core Ops, SparseCore 0:
  11.0 91.8 all-gather.1

commit v8 on v7

--- a/solution.py
+++ b/solution.py
@@ -710,7 +710,7 @@
     near = get(lambda z, y, x, c: (z ^ 1, y, x, c))
     far = get(lambda z, y, x, c: (z ^ 2, y, x, c))
     last = get(lambda z, y, x, c: (z ^ 3, y, x, c))
-    return (value + near) + (far + last)
+    return [value, near, far, last]
 
 
 def pack_body(slot_ref, *refs, orders, per):
@@ -781,29 +781,48 @@
     )(left, right)
 
 
-def precondition_body(scale_ref, s_ref, l_ref, r_ref, p_ref, s_low):
+def scale_parts(total, rows):
+    vectors = total[:rows]
+    squares = jnp.sum(vectors * vectors, keepdims=True) + jnp.sum(total[rows : rows + 1], keepdims=True)
+    scale = jnp.minimum(1.0, clip_level / jnp.sqrt(squares)) * math.sqrt(NPARAM)
+    power = jnp.exp2(jnp.floor(jnp.log2(jnp.maximum(scale, 1e-30)))).astype(bf16).astype(f32)
+    return power, scale / power
+
+
+def precondition_body(s_ref, l_ref, r_ref, *refs, rows):
+    *part_refs, p_ref, s_low, rest = refs
+
     @pl.when(pl.program_id(0) == 0)
     def _():
-        s_low[...] = (s_ref[...].astype(f32) * scale_ref[0]).astype(bf16)
+        parts = [ref[...] for ref in part_refs]
+        power, left = scale_parts(sum_parts(parts), rows)
+        s_low[...] = (s_ref[...].astype(f32) * power).astype(bf16)
+        rest[...] = jnp.broadcast_to(left, rest.shape)
 
     left = mm(l_ref[...], s_low[...], NN)
-    p_ref[...] = (scale_ref[1] * mm(left.astype(bf16), r_ref[...], NN)).astype(bf16)
-
-
-def precondition(scales, block, left, right, step=384):
+    p_ref[...] = (rest[0:1, 0:1] * mm(left.astype(bf16), r_ref[...], NN)).astype(bf16)
+
+
+def sum_parts(parts):
+    if len(parts) == 1:
+        return parts[0]
+    return (parts[0] + parts[1]) + (parts[2] + parts[3])
+
+
+def precondition(parts, rows, block, left, right, step=384):
     width = block.shape[0]
     whole = pl.BlockSpec((width, width), lambda i: (0, 0))
-    rows = pl.BlockSpec((step, width), lambda i: (i, 0))
+    some = pl.BlockSpec((step, width), lambda i: (i, 0))
     return call(
-        precondition_body,
+        functools.partial(precondition_body, rows=rows),
         4 * width**3,
         8 * width**2,
         grid=(width // step,),
-        in_specs=[pl.BlockSpec(memory_space=pltpu.SMEM), whole, rows, whole],
-        out_specs=rows,
+        in_specs=[whole, some, whole] + [pl.BlockSpec(v.shape, lambda i: (0, 0)) for v in parts],
+        out_specs=some,
         out_shape=jax.ShapeDtypeStruct((width, width), bf16),
-        scratch_shapes=[pltpu.VMEM((width, width), bf16)],
-    )(scales, block, left, right)
+        scratch_shapes=[pltpu.VMEM((width, width), bf16), pltpu.VMEM((8, LANES), f32)],
+    )(block, left, right, *parts)
 
 
 def statistics_body(has_ref, scale_ref, s_ref, l_ref, r_ref, nl_ref, nr_ref, s_low, *, step):
@@ -968,7 +987,8 @@
     left_low, right_low = to_low(root_left[0], root_right[0], after=(squares,))
     out = output(flat_tokens, (og, 3, 1), es, attn_weights, mlp_weights, vecs, after=(left_low,))
     local = jnp.concatenate([grad_vectors, jnp.sum(squares, axis=0)[None], jnp.zeros((2, width), f32)])
-    total = everywhere(local) if paired else lax.psum(local, AXES)
+    parts = everywhere(local) if paired else [lax.psum(local, AXES)]
+    total = sum_parts(parts)
     vector_sums = total[:vec_rows]
     square_sum = jnp.sum(total[vec_rows]) + jnp.sum(vector_sums * vector_sums)
     shard_vectors = lax.dynamic_slice_in_dim(vector_sums, my_index * shard, shard, axis=1)
@@ -980,7 +1000,7 @@
     power = jnp.exp2(jnp.floor(jnp.log2(jnp.maximum(scale, 1e-30)))).astype(bf16).astype(f32)
     scales = jnp.stack([power, scale / power])
     owned = to_all(outgoing).reshape(width, width)
-    precond = precondition(scales, owned, left_low, right_low)
+    precond = precondition(parts, vec_rows, owned, left_low, right_low)
     returned = to_all(precond.reshape(slot_count, shard, width))
     new_left, new_right = statistics(
         has_block.astype(jnp.int32).reshape(1), scales, owned, stat_left[0], stat_right[0]

time: 351 us -> 361 us (1.028); the launches traced: 350 us -> 354 us
  Pallas kernels: 166 us -> 175 us
  waiting for transfers between devices: 68.1 us -> 63.9 us
    pallas_call x19, Pallas kernels: 166 us -> 175 us  [call(): return lambda *operands: made(*operands, *after)]
    all_to_all x3, waiting for transfers between devices: 8.09 us -> 3.93 us  [to_all(): return lax.all_to_all(value, AXES, split_axis=0, concat_axis=0, tiled=True)]
  transfers between devices with their start and end apart: 47 -> 47, of which waited for: 17 -> 17; matrix products, arithmetic and copies ran while one was open for 5% -> 5% of each run, Pallas kernels for 43% -> 45%
where the time goes in v8:
time: 361 us; the launch traced here: 354 us
  Pallas kernels  175 us (48%)
  starting transfers between devices  76 us (21%)
  waiting for transfers between devices  63.9 us (18%)
  between operations  18.2 us (5%)
  other arithmetic  14.3 us (4%)
  local copies, waits for them, and re-layouts  6.61 us (2%)
    pallas_call x19, Pallas kernels, call(): return lambda *operands: made(*operands, *after)  175 us
    ppermute x9, waiting for transfers between devices, over_x(): lax.ppermute(value, AXES, to_place(lambda z, y, x, c: (z, y, 1 - x, c)))  21.8 us
    ppermute x8, starting transfers between devices, advance(): lax.ppermute(v, AXES, to_place(lambda z, y, x, c, m=m: (2 * c + ((z ^ m)...  20.5 us
    all_to_all x3, starting transfers between devices, to_all(): return lax.all_to_all(value, AXES, split_axis=0, concat_axis=0, tiled=True)  19 us
    ppermute x9, starting transfers between devices, over_x(): lax.ppermute(value, AXES, to_place(lambda z, y, x, c: (z, y, 1 - x, c)))  11.6 us
    ppermute x4, waiting for transfers between devices, get(): return lax.ppermute(value, AXES, to_place(move))  10.7 us
    ppermute x9, starting transfers between devices, over_y(): lax.ppermute(value, AXES, to_place(lambda z, y, x, c: (z, 1 - y, x, c)))  10.3 us
    ppermute x3, waiting for transfers between devices, over_z(): lax.ppermute(value, AXES, to_place(lambda z, y, x, c: ((z + by) % 4, y, x...  9.35 us
  transfers between devices with their start and end apart: 47, of which 17 were waited for; matrix products, arithmetic and copies ran while one was open for 5% of the time, Pallas kernels for 45%

profile of v8, /device:TPU:0, one launch (start us, length us, event | category | flops | bytes accessed | tf_op | source)
XLA Modules:
  0.0 354.2 jit_solution(15983218896982629806)
XLA Ops:
  9.3 4.1 %collective-permute-start.1 = (bf16[4,24,768]{2,1,0:T(8,128)(2,1)S(1)}, bf16[4,24,768]{2,1,0:T(8,128)(2,1)S(1)}, u32[]{:S(2)}, u32[]{:S(2)}) collective-permute-start(bf16[4,24,768]{2,1,0:T(8,128)(2,1)S(1)} %get-tuple-element.135), channel_id=1, source_target_pairs={{0,16},{1,17},{2,18},{3,19},{4,20},{5,21},{6,22},{7,23},{8,24},{9,... | collective-permute-start | bytes 442376 | tf_op jit(solution)/shard_map/ppermute | solution.py:598
  15.4 6.6 %collective-permute-done.1 = bf16[4,24,768]{2,1,0:T(8,128)(2,1)S(1)} collective-permute-done((bf16[4,24,768]{2,1,0:T(8,128)(2,1)S(1)}, bf16[4,24,768]{2,1,0:T(8,128)(2,1)S(1)}, u32[]{:S(2)}, u32[]{:S(2)}) %collective-permute-start.1) | collective-permute-done | bytes 147488 | tf_op jit(solution)/shard_map/ppermute | solution.py:598
  30.1 9.6 %all-to-all-start = ((bf16[32,2,156]{2,1,0:T(2,128)(2,1)}), bf16[32,2,156]{2,1,0:T(2,128)(2,1)S(1)}, u32[]{:S(2)}, u32[]{:S(2)}) async-start(bf16[32,2,156]{2,1,0:T(2,128)(2,1)} %reshape.150), calls=%async_computation | async-start | bytes 65536 | tf_op jit(solution)/shard_map/all_to_all | solution.py:892
  47.4 6.5 %collective-permute-done.5.refs_3_ = bf16[2,4,24,768]{3,2,1,0:T(8,128)(2,1)S(1)} collective-permute-done((bf16[2,4,24,768]{3,2,1,0:T(8,128)(2,1)S(1)}, bf16[2,4,24,768]{3,2,1,0:T(8,128)(2,1)S(1)}, u32[]{:S(2)}, u32[]{:S(2)}) %collective-permute-start.5) | collective-permute-done | bytes 294944 | tf_op jit(solution)/shard_map/ppermute | solution.py:594
  54.2 3.9 %collective-permute-done.6.refs_4_ = bf16[2,4,24,768]{3,2,1,0:T(8,128)(2,1)} collective-permute-done((bf16[2,4,24,768]{3,2,1,0:T(8,128)(2,1)S(1)}, bf16[2,4,24,768]{3,2,1,0:T(8,128)(2,1)}, u32[]{:S(2)}, u32[]{:S(2)}) %collective-permute-start.6) | collective-permute-done | bytes 294944 | tf_op jit(solution)/shard_map/ppermute | solution.py:590
  63.1 14.1 %shard_map.229 = (bf16[1024,768]{1,0:T(8,128)(2,1)}, bf16[1024,768]{1,0:T(8,128)(2,1)}, bf16[1024,768]{1,0:T(8,128)(2,1)}, bf16[1024,768]{1,0:T(8,128)(2,1)}, bf...) custom-call(s32[4]{0:T(128)} %pad_add_fusion.place_ref.refs_0_, bf16[1024,768]{1,0:T(8,128)(2,1)} %bitcast.58, ...), custom_call_target="tpu_custom_call" | custom-call | flops 4831838208 | bytes 25165824 | tf_op jit(solution)/shard_map/pallas_call | solution.py:75
  77.2 25.4 %shard_map.230 = (bf16[4,1024,768]{2,1,0:T(8,128)(2,1)}, f32[3,16,768]{2,1,0:T(8,128)}, bf16[3,1024,768]{2,1,0:T(8,128)(2,1)}) custom-call(bf16[3,1024,768]{2,1,0:T(8,128)(2,1)} %get-tuple-element.71.acts_ref, s32[1024,1]{1,0:T(8,128)} %bitcast.69, s32[2,1,512]{2,1,0:T(1,128)} %broadcast_in_dim.44.row_ref, ...), custom_call_target="tpu_custom_call", output_to_operand_aliasing={{2}: (0, {})} | custom-call | flops 9663676416 | bytes 18874368 | tf_op jit(solution)/shard_map/pallas_call | solution.py:75
  103.3 13.0 %shard_map.231 = (bf16[2,2,1024,768]{3,2,1,0:T(8,128)(2,1)}, f32[2,8,768]{2,1,0:T(8,128)}) custom-call(bf16[3,1024,768]{2,1,0:T(8,128)(2,1)} %get-tuple-element.77.a2_ref.dy_ref.refs_0_.refs_1_.refs_7_, bf16[3,1024,768]{2,1,0:T(8,128)(2,1)} %get-tuple-element.77.a2_ref.dy_ref.refs_0_.refs_1_.refs_7_, ...), custom_call_target="tpu_custom_call" | custom-call | flops 4831838208 | bytes 17301504 | tf_op jit(solution)/shard_map/pallas_call | solution.py:75
  116.6 21.5 %shard_map.232 = (bf16[2,2,1024,768]{3,2,1,0:T(8,128)(2,1)}, f32[2,8,768]{2,1,0:T(8,128)}) custom-call(bf16[3,1024,768]{2,1,0:T(8,128)(2,1)} %get-tuple-element.77.a2_ref.dy_ref.refs_0_.refs_1_.refs_7_, bf16[3,1024,768]{2,1,0:T(8,128)(2,1)} %get-tuple-element.77.a2_ref.dy_ref.refs_0_.refs_1_.refs_7_, ...), custom_call_target="tpu_custom_call" | custom-call | flops 4831838208 | bytes 17301504 | tf_op jit(solution)/shard_map/pallas_call | solution.py:75
  138.3 11.2 %shard_map.233 = (bf16[4,2,2,2,24,384]{5,4,3,2,1,0:T(8,128)(2,1)}, bf16[4,2,2,2,24,384]{5,4,3,2,1,0:T(8,128)(2,1)}, bf16[4,2,2,2,24,384]{5,4,3,2,1,0:T(8,128)(2,1)}, bf16[4,2,2,2,24,384]{5,4,3,2,1,0:T(8,128)(2,1)}) custom-call(s32[4]{0:T(128)} %pad_add_fusion.place_ref.refs_0_, bf16[3,1024,768]{2,1,0:T(8,128)(2,1)} %get-tuple-element.77.a2_ref.dy_ref.refs_0_.refs_1_.refs_7_, ...), custom_call_target="tpu_custom_call" | custom-call | flops 4831838208 | bytes 12582912 | tf_op jit(solution)/shard_map/pallas_call | solution.py:75
  151.5 10.9 %shard_map.234 = (bf16[4,2,2,2,24,384]{5,4,3,2,1,0:T(8,128)(2,1)}, bf16[4,2,2,2,24,384]{5,4,3,2,1,0:T(8,128)(2,1)}, bf16[4,2,2,2,24,384]{5,4,3,2,1,0:T(8,128)(2,1)}, bf16[4,2,2,2,24,384]{5,4,3,2,1,0:T(8,128)(2,1)}) custom-call(s32[4]{0:T(128)} %pad_add_fusion.place_ref.refs_0_, bf16[3,1024,768]{2,1,0:T(8,128)(2,1)} %get-tuple-element.77.a2_ref.dy_ref.refs_0_.refs_1_.refs_7_, ...), custom_call_target="tpu_custom_call" | custom-call | flops 4831838208 | bytes 12582912 | tf_op jit(solution)/shard_map/pallas_call | solution.py:75
  173.2 10.9 %shard_map.236 = (bf16[4,2,2,2,24,384]{5,4,3,2,1,0:T(8,128)(2,1)}, bf16[4,2,2,2,24,384]{5,4,3,2,1,0:T(8,128)(2,1)}, bf16[4,2,2,2,24,384]{5,4,3,2,1,0:T(8,128)(2,1)}, bf16[4,2,2,2,24,384]{5,4,3,2,1,0:T(8,128)(2,1)}) custom-call(s32[4]{0:T(128)} %pad_add_fusion.place_ref.refs_0_, bf16[3,1024,768]{2,1,0:T(8,128)(2,1)} %get-tuple-element.77.a2_ref.dy_ref.refs_0_.refs_1_.refs_7_, ...), custom_call_target="tpu_custom_call" | custom-call | flops 4831838208 | bytes 12582912 | tf_op jit(solution)/shard_map/pallas_call | solution.py:75
  186.2 7.1 %collective-permute-done.22.refs_2_ = bf16[4,2,2,2,24,384]{5,4,3,2,1,0:T(8,128)(2,1)} collective-permute-done((bf16[4,2,2,2,24,384]{5,4,3,2,1,0:T(8,128)(2,1)}, bf16[4,2,2,2,24,384]{5,4,3,2,1,0:T(8,128)(2,1)}, u32[]{:S(2)}, u32[]{:S(2)}) %collective-permute-start.22) | collective-permute-done | bytes 589856 | tf_op jit(solution)/shard_map/ppermute | solution.py:590
  198.4 9.8 %shard_map.238 = (f32[1024,768]{1,0:T(8,128)}, f32[3,8,768]{2,1,0:T(8,128)}) custom-call(bf16[1024,768]{1,0:T(8,128)(2,1)} %bitcast.59, bf16[1024,768]{1,0:T(8,128)(2,1)} %bitcast.67, bf16[4,1024,768]{2,1,0:T(8,128)(2,1)} %get-tuple-element.76.refs_3_.refs_5_.refs_2_.refs_1_, bf16[4,768,768]{2,1,0:T(8,128)(2,1)} %get-tuple-element.80.refs_3_.refs_4_, ...), custom_call_target="tpu_custom_call" | custom-call | flops 3623878656 | bytes 14548992 | tf_op jit(solution)/shard_map/pallas_call | solution.py:75
  210.2 4.2 %shard_map.239 = (bf16[4,2,2,24,384]{4,3,2,1,0:T(8,128)(2,1)}, bf16[4,2,2,24,384]{4,3,2,1,0:T(8,128)(2,1)}, bf16[4,2,2,24,384]{4,3,2,1,0:T(8,128)(2,1)}, bf16[4,...) custom-call(s32[4]{0:T(128)} %pad_add_fusion.place_ref.refs_0_, ...), custom_call_target="tpu_custom_call" | custom-call | bytes 9437184 | tf_op jit(solution)/shard_map/pallas_call | solution.py:75
  217.7 3.8 %collective-permute-start.26 = (bf16[8,24,768]{2,1,0:T(8,128)(2,1)}, bf16[8,24,768]{2,1,0:T(8,128)(2,1)}, u32[]{:S(2)}, u32[]{:S(2)}) collective-permute-start(bf16[8,24,768]{2,1,0:T(8,128)(2,1)} %bitcast.82), channel_id=1, source_target_pairs={{0,0},{1,16},{2,2},{3,18},{4,4},{5,20},{6,6},{7,22},{8,1},{9,17},{... | collective-permute-start | bytes 884744 | tf_op jit(solution)/shard_map/ppermute | solution.py:695
  221.4 5.0 %collective-permute-start.27 = (bf16[8,24,768]{2,1,0:T(8,128)(2,1)}, bf16[8,24,768]{2,1,0:T(8,128)(2,1)}, u32[]{:S(2)}, u32[]{:S(2)}) collective-permute-start(bf16[8,24,768]{2,1,0:T(8,128)(2,1)} %bitcast.81), channel_id=1, source_target_pairs={{0,1},{1,17},{2,3},{3,19},{4,5},{5,21},{6,7},{7,23},{8,0},{9,16},{... | collective-permute-start | bytes 884744 | tf_op jit(solution)/shard_map/ppermute | solution.py:695
  228.6 11.0 %shard_map.240 = (bf16[1024,768]{1,0:T(8,128)(2,1)}, f32[2,8,768]{2,1,0:T(8,128)}) custom-call(bf16[1024,768]{1,0:T(8,128)(2,1)} %bitcast.60, f32[1024,768]{1,0:T(8,128)} %get-tuple-element.101.refs_13_.refs_1_, bf16[4,1024,768]{2,1,0:T(8,128)(2,1)} %bitcast.56, bf16[4,1024,768]{2,1,0:T(8,128)(2,1)} %bitcast.50, ...), custom_call_target="tpu_custom_call" | custom-call | flops 4831838208 | bytes 17301504 | tf_op jit(solution)/shard_map/pallas_call | solution.py:75
  247.8 4.7 %collective-permute-start.35 = (bf16[4,24,768]{2,1,0:T(8,128)(2,1)}, bf16[4,24,768]{2,1,0:T(8,128)(2,1)}, u32[]{:S(2)}, u32[]{:S(2)}) collective-permute-start(bf16[4,24,768]{2,1,0:T(8,128)(2,1)} %bitcast.83), channel_id=1, source_target_pairs={{0,9},{1,25},{2,11},{3,27},{4,13},{5,29},{6,15},{7,31},{8,8},{9,24... | collective-permute-start | bytes 442376 | tf_op jit(solution)/shard_map/ppermute | solution.py:695
  254.2 7.9 %collective-permute-done.34.refs_7_ = bf16[4,24,768]{2,1,0:T(8,128)(2,1)} collective-permute-done((bf16[4,24,768]{2,1,0:T(8,128)(2,1)}, bf16[4,24,768]{2,1,0:T(8,128)(2,1)}, u32[]{:S(2)}, u32[]{:S(2)}) %collective-permute-start.34) | collective-permute-done | bytes 147488 | tf_op jit(solution)/shard_map/ppermute | solution.py:695
  262.1 3.7 %shard_map.242 = (f32[12,24,768]{2,1,0:T(8,128)}, bf16[32,24,768]{2,1,0:T(8,128)(2,1)}, f32[24,768]{1,0:T(8,128)}) custom-call(s32[32]{0:T(128)} %broadcast_add_fusion.refs_0_, bf16[8,24,768]{2,1,0:T(8,128)(2,1)} %collective-permute-done.26.refs_1_, bf16[8,24,768]{2,1,0:T(8,128)(2,1)} %collective-permute-done.27.refs_2_, ...), custom_call_target="tpu_custom_call" | custom-call | bytes 3538944 | tf_op jit(solution)/shard_map/pallas_call | solution.py:75
  265.8 5.8 %all-to-all-start.1 = ((bf16[32,24,768]{2,1,0:T(8,128)(2,1)}), bf16[32,24,768]{2,1,0:T(8,128)(2,1)}, u32[]{:S(2)}, u32[]{:S(2)}) async-start(bf16[32,24,768]{2,1,0:T(8,128)(2,1)} %get-tuple-element.122), calls=%async_computation.1 | async-start | bytes 2359296 | tf_op jit(solution)/shard_map/all_to_all | solution.py:892
  276.8 6.7 %collective-permute-done.37 = f32[16,768]{1,0:T(8,128)S(1)} collective-permute-done((f32[16,768]{1,0:T(8,128)S(1)}, f32[16,768]{1,0:T(8,128)S(1)}, u32[]{:S(2)}, u32[]{:S(2)}) %collective-permute-start.37) | collective-permute-done | bytes 49184 | tf_op jit(solution)/shard_map/ppermute | solution.py:590
  286.1 5.7 %collective-permute-start.41 = (f32[16,768]{1,0:T(8,128)}, f32[16,768]{1,0:T(8,128)}, u32[]{:S(2)}, u32[]{:S(2)}) collective-permute-start(f32[16,768]{1,0:T(8,128)} %add_add_fusion.1.refs_0_), channel_id=1, source_target_pairs={{0,16},{1,17},{2,18},{3,19},{4,20},{5,21},{6,22},{7,23},{8,24},{9,... | collective-permute-start | bytes 147464 | tf_op jit(solution)/shard_map/ppermute | solution.py:704
  291.8 3.5 shard_map.243
  295.2 9.1 %collective-permute-done.41.refs_2_ = f32[16,768]{1,0:T(8,128)} collective-permute-done((f32[16,768]{1,0:T(8,128)}, f32[16,768]{1,0:T(8,128)}, u32[]{:S(2)}, u32[]{:S(2)}) %collective-permute-start.41) | collective-permute-done | bytes 49184 | tf_op jit(solution)/shard_map/ppermute | solution.py:704
  304.3 5.7 %shard_map.245 = bf16[768,768]{1,0:T(8,128)(2,1)} custom-call(bf16[768,768]{1,0:T(8,128)(2,1)} %bitcast.27.s_ref, bf16[768,768]{1,0:T(8,128)(2,1)} %get-tuple-element.116.refs_7_.l_ref, bf16[768,768]{1,0:T(8,128)(2,1)} %get-tuple-element.123.r_ref, f32[16,768]{1,0:T(8,128)} %add_add_fusion.1.refs_0_, f32[16,768]{1,0:T(8,128)} %collective-permute-done.40.refs_1_, ...), custom_call_target="tpu_custom_call" | custom-call | flops 1811939328 | bytes 4718592 | tf_op jit(solution)/shard_map/pallas_call | solution.py:75
  310.0 3.5 all-to-all-start.2
  314.8 11.1 %shard_map.244 = bf16[1024,768]{1,0:T(8,128)(2,1)} custom-call(bf16[1024,768]{1,0:T(8,128)(2,1)} %bitcast.61, bf16[4,1024,768]{2,1,0:T(8,128)(2,1)} %get-tuple-element.76.refs_3_.refs_5_.refs_2_.refs_1_, bf16[4,1024,768]{2,1,0:T(8,128)(2,1)} %bitcast.57, bf16[4,1024,768]{2,1,0:T(8,128)(2,1)} %bitcast.51, ...), custom_call_target="tpu_custom_call" | custom-call | flops 6039797760 | bytes 16908288 | tf_op jit(solution)/shard_map/pallas_call | solution.py:75
  331.5 7.2 %shard_map.247 = (f32[768,768]{1,0:T(8,128)}, f32[768,768]{1,0:T(8,128)}) custom-call(s32[1]{0:T(128)} %bitcast.29.has_ref, f32[2]{0:T(128)} %pad_maximum_fusion.1.scale_ref, bf16[768,768]{1,0:T(8,128)(2,1)} %bitcast.27.s_ref, f32[768,768]{1,0:T(8,128)} %bitcast.77, f32[768,768]{1,0:T(8,128)} %bitcast.78), custom_call_target="tpu_custom_call" | custom-call | flops 1811939328 | bytes 10616832 | tf_op jit(solution)/shard_map/pallas_call | solution.py:75
  338.7 3.9 %all-to-all-done.2.p_ref = bf16[32,24,768]{2,1,0:T(8,128)(2,1)} async-done(((bf16[32,24,768]{2,1,0:T(8,128)(2,1)}), bf16[32,24,768]{2,1,0:T(8,128)(2,1)}, u32[]{:S(2)}, u32[]{:S(2)}) %all-to-all-start.2) | async-done | bytes 1179680 | tf_op jit(solution)/shard_map/all_to_all | solution.py:892
  342.6 3.3 shard_map.246
  (164 shorter events, 75.8 us)
Async XLA Ops:
  7.2 96.1 %all-gather.2.cloned.1.call-start = ((), (), s32[]{:S(2)}) async-start(), calls=%async_computation.3 | async-start | bytes 9732096 | tf_op jit(solution)/shard_map/all_gather | solution.py:923
  24.9 15.3 %collective-permute-start.3 = (bf16[4,4,24,768]{3,2,1,0:T(8,128)(2,1)S(1)}, bf16[4,4,24,768]{3,2,1,0:T(8,128)(2,1)S(1)}, u32[]{:S(2)}, u32[]{:S(2)}) collective-permute-start(bf16[4,4,24,768]{3,2,1,0:T(8,128)(2,1)S(1)} %pad_maximum_fusion.refs_0_), channel_id=1, source_target_pairs={{0,2},{1,3},{2,0},{3,1},{4,6},{5,7},{6,4},{7,5},{8,10},{9,11},{10,... | collective-permute-start | bytes 1769480 | tf_op jit(solution)/shard_map/ppermute | solution.py:590
  26.4 15.6 %collective-permute-start.4 = (bf16[4,4,24,768]{3,2,1,0:T(8,128)(2,1)S(1)}, bf16[4,4,24,768]{3,2,1,0:T(8,128)(2,1)S(1)}, u32[]{:S(2)}, u32[]{:S(2)}) collective-permute-start(bf16[4,4,24,768]{3,2,1,0:T(8,128)(2,1)S(1)} %pad_maximum_fusion.refs_0_), channel_id=1, source_target_pairs={{0,4},{1,5},{2,6},{3,7},{4,0},{5,1},{6,2},{7,3},{8,12},{9,13},{10,... | collective-permute-start | bytes 1769480 | tf_op jit(solution)/shard_map/ppermute | solution.py:594
  30.1 30.2 %all-to-all-start = ((bf16[32,2,156]{2,1,0:T(2,128)(2,1)}), bf16[32,2,156]{2,1,0:T(2,128)(2,1)S(1)}, u32[]{:S(2)}, u32[]{:S(2)}) async-start(bf16[32,2,156]{2,1,0:T(2,128)(2,1)} %reshape.150), calls=%async_computation | async-start | bytes 65536 | tf_op jit(solution)/shard_map/all_to_all | solution.py:892
  40.2 13.8 %collective-permute-start.5 = (bf16[2,4,24,768]{3,2,1,0:T(8,128)(2,1)S(1)}, bf16[2,4,24,768]{3,2,1,0:T(8,128)(2,1)S(1)}, u32[]{:S(2)}, u32[]{:S(2)}) collective-permute-start(bf16[2,4,24,768]{3,2,1,0:T(8,128)(2,1)S(1)} %slice.33), channel_id=1, source_target_pairs={{0,4},{1,5},{2,6},{3,7},{4,0},{5,1},{6,2},{7,3},{8,12},{9,13},{10,... | collective-permute-start | bytes 884744 | tf_op jit(solution)/shard_map/ppermute | solution.py:594
  42.1 16.0 %collective-permute-start.6 = (bf16[2,4,24,768]{3,2,1,0:T(8,128)(2,1)S(1)}, bf16[2,4,24,768]{3,2,1,0:T(8,128)(2,1)}, u32[]{:S(2)}, u32[]{:S(2)}) collective-permute-start(bf16[2,4,24,768]{3,2,1,0:T(8,128)(2,1)S(1)} %slice.34), channel_id=1, source_target_pairs={{0,2},{1,3},{2,0},{3,1},{4,6},{5,7},{6,4},{7,5},{8,10},{9,11},{10,... | collective-permute-start | bytes 884744 | tf_op jit(solution)/shard_map/ppermute | solution.py:590
  43.6 17.9 %collective-permute-start.7 = (bf16[4,4,24,768]{3,2,1,0:T(8,128)(2,1)S(1)}, bf16[4,4,24,768]{3,2,1,0:T(8,128)(2,1)S(1)}, u32[]{:S(2)}, u32[]{:S(2)}) collective-permute-start(bf16[4,4,24,768]{3,2,1,0:T(8,128)(2,1)S(1)} %pad_maximum_fusion.refs_0_), channel_id=1, source_target_pairs={{0,1},{1,0},{2,3},{3,2},{4,5},{5,4},{6,7},{7,6},{8,9},{9,8},{10,11... | collective-permute-start | bytes 1769480 | tf_op jit(solution)/shard_map/ppermute | solution.py:586
  43.6 17.9 %collective-permute-start.8 = (bf16[4,4,24,768]{3,2,1,0:T(8,128)(2,1)S(1)}, bf16[4,4,24,768]{3,2,1,0:T(8,128)(2,1)}, u32[]{:S(2)}, u32[]{:S(2)}) collective-permute-start(bf16[4,4,24,768]{3,2,1,0:T(8,128)(2,1)S(1)} %collective-permute-done.3.refs_1_), channel_id=1, source_target_pairs={{0,1},{1,0},{2,3},{3,2},{4,5},{5,4},{6,7},{7,6},{8,9},{9,8},{10,11... | collective-permute-start | bytes 1769480 | tf_op jit(solution)/shard_map/ppermute | solution.py:586
  44.1 17.4 %collective-permute-start.9 = (bf16[4,4,24,768]{3,2,1,0:T(8,128)(2,1)S(1)}, bf16[4,4,24,768]{3,2,1,0:T(8,128)(2,1)}, u32[]{:S(2)}, u32[]{:S(2)}) collective-permute-start(bf16[4,4,24,768]{3,2,1,0:T(8,128)(2,1)S(1)} %collective-permute-done.4.refs_2_), channel_id=1, source_target_pairs={{0,1},{1,0},{2,3},{3,2},{4,5},{5,4},{6,7},{7,6},{8,9},{9,8},{10,11... | collective-permute-start | bytes 1769480 | tf_op jit(solution)/shard_map/ppermute | solution.py:586
  102.7 14.0 %collective-permute-start.12 = (bf16[3,1024,768]{2,1,0:T(8,128)(2,1)}, bf16[3,1024,768]{2,1,0:T(8,128)(2,1)}, u32[]{:S(2)}, u32[]{:S(2)}) collective-permute-start(bf16[3,1024,768]{2,1,0:T(8,128)(2,1)} %get-tuple-element.77.a2_ref.dy_ref.refs_0_.refs_1_.refs_7_), channel_id=1, source_target_pairs={{0,1},{1,0},{2,3},{3,2},{4,5},{5,4},{6,7},{7,6},{8,9},{9,8},{10,11... | collective-permute-start | bytes 14155784 | tf_op jit(solution)/shard_map/ppermute | solution.py:586
  103.2 35.1 %collective-permute-start.14 = (bf16[4,1024,768]{2,1,0:T(8,128)(2,1)}, bf16[4,1024,768]{2,1,0:T(8,128)(2,1)}, u32[]{:S(2)}, u32[]{:S(2)}) collective-permute-start(bf16[4,1024,768]{2,1,0:T(8,128)(2,1)} %get-tuple-element.76.refs_3_.refs_5_.refs_2_.refs_1_), channel_id=1, source_target_pairs={{0,1},{1,0},{2,3},{3,2},{4,5},{5,4},{6,7},{7,6},{8,9},{9,8},{10,11... | collective-permute-start | bytes 18874376 | tf_op jit(solution)/shard_map/ppermute | solution.py:586
  116.2 35.3 %collective-permute-start.17 = (bf16[4,1024,768]{2,1,0:T(8,128)(2,1)}, bf16[4,1024,768]{2,1,0:T(8,128)(2,1)}, u32[]{:S(2)}, u32[]{:S(2)}) collective-permute-start(bf16[4,1024,768]{2,1,0:T(8,128)(2,1)} %bitcast.52), channel_id=1, source_target_pairs={{0,1},{1,0},{2,3},{3,2},{4,5},{5,4},{6,7},{7,6},{8,9},{9,8},{10,11... | collective-permute-start | bytes 18874376 | tf_op jit(solution)/shard_map/ppermute | solution.py:586
  138.2 35.0 %collective-permute-start.13 = (bf16[4,1024,768]{2,1,0:T(8,128)(2,1)}, bf16[4,1024,768]{2,1,0:T(8,128)(2,1)}, u32[]{:S(2)}, u32[]{:S(2)}) collective-permute-start(bf16[4,1024,768]{2,1,0:T(8,128)(2,1)} %bitcast.46), channel_id=1, source_target_pairs={{0,1},{1,0},{2,3},{3,2},{4,5},{5,4},{6,7},{7,6},{8,9},{9,8},{10,11... | collective-permute-start | bytes 18874376 | tf_op jit(solution)/shard_map/ppermute | solution.py:586
  149.4 16.0 %collective-permute-start.15 = (bf16[4,2,2,2,24,384]{5,4,3,2,1,0:T(8,128)(2,1)}, bf16[4,2,2,2,24,384]{5,4,3,2,1,0:T(8,128)(2,1)}, u32[]{:S(2)}, u32[]{:S(2)}) collective-permute-start(bf16[4,2,2,2,24,384]{5,4,3,2,1,0:T(8,128)(2,1)} %get-tuple-element.82), channel_id=1, source_target_pairs={{0,2},{1,3},{2,0},{3,1},{4,6},{5,7},{6,4},{7,5},{8,10},{9,11},{10,... | collective-permute-start | bytes 1769480 | tf_op jit(solution)/shard_map/ppermute | solution.py:590
  150.4 15.5 %collective-permute-start.16 = (bf16[4,2,2,2,24,384]{5,4,3,2,1,0:T(8,128)(2,1)}, bf16[4,2,2,2,24,384]{5,4,3,2,1,0:T(8,128)(2,1)}, u32[]{:S(2)}, u32[]{:S(2)}) collective-permute-start(bf16[4,2,2,2,24,384]{5,4,3,2,1,0:T(8,128)(2,1)} %get-tuple-element.84), channel_id=1, source_target_pairs={{0,4},{1,5},{2,6},{3,7},{4,0},{5,1},{6,2},{7,3},{8,12},{9,13},{10,... | collective-permute-start | bytes 1769480 | tf_op jit(solution)/shard_map/ppermute | solution.py:594
  169.1 16.1 %collective-permute-start.20 = (bf16[4,2,2,24,384]{4,3,2,1,0:T(8,128)(2,1)}, bf16[4,2,2,24,384]{4,3,2,1,0:T(8,128)(2,1)}, u32[]{:S(2)}, u32[]{:S(2)}) collective-permute-start(bf16[4,2,2,24,384]{4,3,2,1,0:T(8,128)(2,1)} %get-tuple-element.91), channel_id=1, source_target_pairs={{0,4},{1,5},{2,6},{3,7},{4,0},{5,1},{6,2},{7,3},{8,12},{9,13},{10,... | collective-permute-start | bytes 884744 | tf_op jit(solution)/shard_map/ppermute | solution.py:594
  170.4 15.8 %collective-permute-start.21 = (bf16[4,2,2,24,384]{4,3,2,1,0:T(8,128)(2,1)}, bf16[4,2,2,24,384]{4,3,2,1,0:T(8,128)(2,1)}, u32[]{:S(2)}, u32[]{:S(2)}) collective-permute-start(bf16[4,2,2,24,384]{4,3,2,1,0:T(8,128)(2,1)} %get-tuple-element.93), channel_id=1, source_target_pairs={{0,2},{1,3},{2,0},{3,1},{4,6},{5,7},{6,4},{7,5},{8,10},{9,11},{10,... | collective-permute-start | bytes 884744 | tf_op jit(solution)/shard_map/ppermute | solution.py:590
  171.2 22.1 %collective-permute-start.22 = (bf16[4,2,2,2,24,384]{5,4,3,2,1,0:T(8,128)(2,1)}, bf16[4,2,2,2,24,384]{5,4,3,2,1,0:T(8,128)(2,1)}, u32[]{:S(2)}, u32[]{:S(2)}) collective-permute-start(bf16[4,2,2,2,24,384]{5,4,3,2,1,0:T(8,128)(2,1)} %get-tuple-element.94), channel_id=1, source_target_pairs={{0,2},{1,3},{2,0},{3,1},{4,6},{5,7},{6,4},{7,5},{8,10},{9,11},{10,... | collective-permute-start | bytes 1769480 | tf_op jit(solution)/shard_map/ppermute | solution.py:590
  172.4 20.9 %collective-permute-start.23 = (bf16[4,2,2,2,24,384]{5,4,3,2,1,0:T(8,128)(2,1)}, bf16[4,2,2,2,24,384]{5,4,3,2,1,0:T(8,128)(2,1)}, u32[]{:S(2)}, u32[]{:S(2)}) collective-permute-start(bf16[4,2,2,2,24,384]{5,4,3,2,1,0:T(8,128)(2,1)} %get-tuple-element.96), channel_id=1, source_target_pairs={{0,4},{1,5},{2,6},{3,7},{4,0},{5,1},{6,2},{7,3},{8,12},{9,13},{10,... | collective-permute-start | bytes 1769480 | tf_op jit(solution)/shard_map/ppermute | solution.py:594
  184.1 24.1 %collective-permute-start.18 = (bf16[4,2,2,2,24,384]{5,4,3,2,1,0:T(8,128)(2,1)}, bf16[4,2,2,2,24,384]{5,4,3,2,1,0:T(8,128)(2,1)}, u32[]{:S(2)}, u32[]{:S(2)}) collective-permute-start(bf16[4,2,2,2,24,384]{5,4,3,2,1,0:T(8,128)(2,1)} %get-tuple-element.88), channel_id=1, source_target_pairs={{0,2},{1,3},{2,0},{3,1},{4,6},{5,7},{6,4},{7,5},{8,10},{9,11},{10,... | collective-permute-start | bytes 1769480 | tf_op jit(solution)/shard_map/ppermute | solution.py:590
  185.3 22.9 %collective-permute-start.19 = (bf16[4,2,2,2,24,384]{5,4,3,2,1,0:T(8,128)(2,1)}, bf16[4,2,2,2,24,384]{5,4,3,2,1,0:T(8,128)(2,1)}, u32[]{:S(2)}, u32[]{:S(2)}) collective-permute-start(bf16[4,2,2,2,24,384]{5,4,3,2,1,0:T(8,128)(2,1)} %get-tuple-element.90), channel_id=1, source_target_pairs={{0,4},{1,5},{2,6},{3,7},{4,0},{5,1},{6,2},{7,3},{8,12},{9,13},{10,... | collective-permute-start | bytes 1769480 | tf_op jit(solution)/shard_map/ppermute | solution.py:594
  197.2 13.0 %collective-permute-start.25 = (bf16[4,2,2,24,384]{4,3,2,1,0:T(8,128)(2,1)}, bf16[4,2,2,24,384]{4,3,2,1,0:T(8,128)(2,1)}, u32[]{:S(2)}, u32[]{:S(2)}) collective-permute-start(bf16[4,2,2,24,384]{4,3,2,1,0:T(8,128)(2,1)} %get-tuple-element.100), channel_id=1, source_target_pairs={{0,2},{1,3},{2,0},{3,1},{4,6},{5,7},{6,4},{7,5},{8,10},{9,11},{10,... | collective-permute-start | bytes 884744 | tf_op jit(solution)/shard_map/ppermute | solution.py:590
  216.3 23.3 %collective-permute-start.31 = (bf16[4,2,2,24,384]{4,3,2,1,0:T(8,128)(2,1)}, bf16[4,2,2,24,384]{4,3,2,1,0:T(8,128)(2,1)}, u32[]{:S(2)}, u32[]{:S(2)}) collective-permute-start(bf16[4,2,2,24,384]{4,3,2,1,0:T(8,128)(2,1)} %get-tuple-element.109), channel_id=1, source_target_pairs={{0,2},{1,3},{2,0},{3,1},{4,6},{5,7},{6,4},{7,5},{8,10},{9,11},{10,... | collective-permute-start | bytes 884744 | tf_op jit(solution)/shard_map/ppermute | solution.py:590
  217.7 27.5 %collective-permute-start.26 = (bf16[8,24,768]{2,1,0:T(8,128)(2,1)}, bf16[8,24,768]{2,1,0:T(8,128)(2,1)}, u32[]{:S(2)}, u32[]{:S(2)}) collective-permute-start(bf16[8,24,768]{2,1,0:T(8,128)(2,1)} %bitcast.82), channel_id=1, source_target_pairs={{0,0},{1,16},{2,2},{3,18},{4,4},{5,20},{6,6},{7,22},{8,1},{9,17},{... | collective-permute-start | bytes 884744 | tf_op jit(solution)/shard_map/ppermute | solution.py:695
  221.4 25.8 %collective-permute-start.27 = (bf16[8,24,768]{2,1,0:T(8,128)(2,1)}, bf16[8,24,768]{2,1,0:T(8,128)(2,1)}, u32[]{:S(2)}, u32[]{:S(2)}) collective-permute-start(bf16[8,24,768]{2,1,0:T(8,128)(2,1)} %bitcast.81), channel_id=1, source_target_pairs={{0,1},{1,17},{2,3},{3,19},{4,5},{5,21},{6,7},{7,23},{8,0},{9,16},{... | collective-permute-start | bytes 884744 | tf_op jit(solution)/shard_map/ppermute | solution.py:695
  226.5 21.4 %collective-permute-start.28 = (bf16[8,24,768]{2,1,0:T(8,128)(2,1)}, bf16[8,24,768]{2,1,0:T(8,128)(2,1)}, u32[]{:S(2)}, u32[]{:S(2)}) collective-permute-start(bf16[8,24,768]{2,1,0:T(8,128)(2,1)} %bitcast.80), channel_id=1, source_target_pairs={{0,8},{1,24},{2,10},{3,26},{4,12},{5,28},{6,14},{7,30},{8,9},{9,25... | collective-permute-start | bytes 884744 | tf_op jit(solution)/shard_map/ppermute | solution.py:695
  226.5 27.3 %collective-permute-start.29 = (bf16[8,24,768]{2,1,0:T(8,128)(2,1)}, bf16[8,24,768]{2,1,0:T(8,128)(2,1)}, u32[]{:S(2)}, u32[]{:S(2)}) collective-permute-start(bf16[8,24,768]{2,1,0:T(8,128)(2,1)} %bitcast.79), channel_id=1, source_target_pairs={{0,9},{1,25},{2,11},{3,27},{4,13},{5,29},{6,15},{7,31},{8,8},{9,24... | collective-permute-start | bytes 884744 | tf_op jit(solution)/shard_map/ppermute | solution.py:695
  247.2 14.9 %collective-permute-start.34 = (bf16[4,24,768]{2,1,0:T(8,128)(2,1)}, bf16[4,24,768]{2,1,0:T(8,128)(2,1)}, u32[]{:S(2)}, u32[]{:S(2)}) collective-permute-start(bf16[4,24,768]{2,1,0:T(8,128)(2,1)} %bitcast.84), channel_id=1, source_target_pairs={{0,8},{1,24},{2,10},{3,26},{4,12},{5,28},{6,14},{7,30},{8,9},{9,25... | collective-permute-start | bytes 442376 | tf_op jit(solution)/shard_map/ppermute | solution.py:695
  247.8 14.3 %collective-permute-start.35 = (bf16[4,24,768]{2,1,0:T(8,128)(2,1)}, bf16[4,24,768]{2,1,0:T(8,128)(2,1)}, u32[]{:S(2)}, u32[]{:S(2)}) collective-permute-start(bf16[4,24,768]{2,1,0:T(8,128)(2,1)} %bitcast.83), channel_id=1, source_target_pairs={{0,9},{1,25},{2,11},{3,27},{4,13},{5,29},{6,15},{7,31},{8,8},{9,24... | collective-permute-start | bytes 442376 | tf_op jit(solution)/shard_map/ppermute | solution.py:695
  265.8 38.5 %all-to-all-start.1 = ((bf16[32,24,768]{2,1,0:T(8,128)(2,1)}), bf16[32,24,768]{2,1,0:T(8,128)(2,1)}, u32[]{:S(2)}, u32[]{:S(2)}) async-start(bf16[32,24,768]{2,1,0:T(8,128)(2,1)} %get-tuple-element.122), calls=%async_computation.1 | async-start | bytes 2359296 | tf_op jit(solution)/shard_map/all_to_all | solution.py:892
  286.1 18.2 %collective-permute-start.41 = (f32[16,768]{1,0:T(8,128)}, f32[16,768]{1,0:T(8,128)}, u32[]{:S(2)}, u32[]{:S(2)}) collective-permute-start(f32[16,768]{1,0:T(8,128)} %add_add_fusion.1.refs_0_), channel_id=1, source_target_pairs={{0,16},{1,17},{2,18},{3,19},{4,20},{5,21},{6,22},{7,23},{8,24},{9,... | collective-permute-start | bytes 147464 | tf_op jit(solution)/shard_map/ppermute | solution.py:704
  310.0 32.6 %all-to-all-start.2 = ((bf16[32,24,768]{2,1,0:T(8,128)(2,1)}), bf16[32,24,768]{2,1,0:T(8,128)(2,1)}, u32[]{:S(2)}, u32[]{:S(2)}) async-start(bf16[32,24,768]{2,1,0:T(8,128)(2,1)} %bitcast.68), calls=%async_computation.2 | async-start | bytes 2359296 | tf_op jit(solution)/shard_map/all_to_all | solution.py:892
  (33 other events, 427.0 us)
Sparse Core Ops, SparseCore 0:
  11.0 91.8 all-gather.1

commit v9 on v8

--- a/solution.py
+++ b/solution.py
@@ -985,7 +985,6 @@
     has_block = jnp.any(owners == my_index)
     shards, outgoing, squares = pack(slots, terms, orders, after=(grad_in,))
     left_low, right_low = to_low(root_left[0], root_right[0], after=(squares,))
-    out = output(flat_tokens, (og, 3, 1), es, attn_weights, mlp_weights, vecs, after=(left_low,))
     local = jnp.concatenate([grad_vectors, jnp.sum(squares, axis=0)[None], jnp.zeros((2, width), f32)])
     parts = everywhere(local) if paired else [lax.psum(local, AXES)]
     total = sum_parts(parts)
@@ -999,6 +998,7 @@
     scale = factor * root_count
     power = jnp.exp2(jnp.floor(jnp.log2(jnp.maximum(scale, 1e-30)))).astype(bf16).astype(f32)
     scales = jnp.stack([power, scale / power])
+    out = output(flat_tokens, (og, 3, 1), es, attn_weights, mlp_weights, vecs, after=(left_low, scales, factor.reshape(1)))
     owned = to_all(outgoing).reshape(width, width)
     precond = precondition(parts, vec_rows, owned, left_low, right_low)
     returned = to_all(precond.reshape(slot_count, shard, width))

time: 361 us -> 361 us (level)
  no operation moved by 1% of the time
where the time goes in v9:
time: 361 us; the launch traced here: 354 us
  Pallas kernels  175 us (48%)
  starting transfers between devices  76 us (21%)
  waiting for transfers between devices  64.7 us (18%)
  between operations  18.2 us (5%)
  other arithmetic  13.5 us (4%)
  local copies, waits for them, and re-layouts  6.61 us (2%)
    pallas_call x19, Pallas kernels, call(): return lambda *operands: made(*operands, *after)  175 us
    ppermute x9, waiting for transfers between devices, over_x(): lax.ppermute(value, AXES, to_place(lambda z, y, x, c: (z, y, 1 - x, c)))  22.1 us
    ppermute x8, starting transfers between devices, advance(): lax.ppermute(v, AXES, to_place(lambda z, y, x, c, m=m: (2 * c + ((z ^ m)...  20.5 us
    all_to_all x3, starting transfers between devices, to_all(): return lax.all_to_all(value, AXES, split_axis=0, concat_axis=0, tiled=True)  19 us
    ppermute x9, starting transfers between devices, over_x(): lax.ppermute(value, AXES, to_place(lambda z, y, x, c: (z, y, 1 - x, c)))  11.8 us
    ppermute x4, waiting for transfers between devices, get(): return lax.ppermute(value, AXES, to_place(move))  10.7 us
    ppermute x9, starting transfers between devices, over_y(): lax.ppermute(value, AXES, to_place(lambda z, y, x, c: (z, 1 - y, x, c)))  10.1 us
    ppermute x3, waiting for transfers between devices, over_z(): lax.ppermute(value, AXES, to_place(lambda z, y, x, c: ((z + by) % 4, y, x...  9.35 us
  transfers between devices with their start and end apart: 47, of which 17 were waited for; matrix products, arithmetic and copies ran while one was open for 5% of the time, Pallas kernels for 45%

profile of v9, /device:TPU:0, one launch (start us, length us, event | category | flops | bytes accessed | tf_op | source)
XLA Modules:
  0.0 354.3 jit_solution(6299572174410047369)
XLA Ops:
  9.3 4.1 %collective-permute-start.1 = (bf16[4,24,768]{2,1,0:T(8,128)(2,1)S(1)}, bf16[4,24,768]{2,1,0:T(8,128)(2,1)S(1)}, u32[]{:S(2)}, u32[]{:S(2)}) collective-permute-start(bf16[4,24,768]{2,1,0:T(8,128)(2,1)S(1)} %get-tuple-element.135), channel_id=1, source_target_pairs={{0,16},{1,17},{2,18},{3,19},{4,20},{5,21},{6,22},{7,23},{8,24},{9,... | collective-permute-start | bytes 442376 | tf_op jit(solution)/shard_map/ppermute | solution.py:598
  15.4 6.6 %collective-permute-done.1 = bf16[4,24,768]{2,1,0:T(8,128)(2,1)S(1)} collective-permute-done((bf16[4,24,768]{2,1,0:T(8,128)(2,1)S(1)}, bf16[4,24,768]{2,1,0:T(8,128)(2,1)S(1)}, u32[]{:S(2)}, u32[]{:S(2)}) %collective-permute-start.1) | collective-permute-done | bytes 147488 | tf_op jit(solution)/shard_map/ppermute | solution.py:598
  30.1 9.6 %all-to-all-start = ((bf16[32,2,156]{2,1,0:T(2,128)(2,1)}), bf16[32,2,156]{2,1,0:T(2,128)(2,1)S(1)}, u32[]{:S(2)}, u32[]{:S(2)}) async-start(bf16[32,2,156]{2,1,0:T(2,128)(2,1)} %reshape.151), calls=%async_computation | async-start | bytes 65536 | tf_op jit(solution)/shard_map/all_to_all | solution.py:892
  47.4 6.6 %collective-permute-done.5.refs_3_ = bf16[2,4,24,768]{3,2,1,0:T(8,128)(2,1)S(1)} collective-permute-done((bf16[2,4,24,768]{3,2,1,0:T(8,128)(2,1)S(1)}, bf16[2,4,24,768]{3,2,1,0:T(8,128)(2,1)S(1)}, u32[]{:S(2)}, u32[]{:S(2)}) %collective-permute-start.5) | collective-permute-done | bytes 294944 | tf_op jit(solution)/shard_map/ppermute | solution.py:594
  54.1 3.9 %collective-permute-done.6.refs_4_ = bf16[2,4,24,768]{3,2,1,0:T(8,128)(2,1)} collective-permute-done((bf16[2,4,24,768]{3,2,1,0:T(8,128)(2,1)S(1)}, bf16[2,4,24,768]{3,2,1,0:T(8,128)(2,1)}, u32[]{:S(2)}, u32[]{:S(2)}) %collective-permute-start.6) | collective-permute-done | bytes 294944 | tf_op jit(solution)/shard_map/ppermute | solution.py:590
  63.1 14.2 %shard_map.229 = (bf16[1024,768]{1,0:T(8,128)(2,1)}, bf16[1024,768]{1,0:T(8,128)(2,1)}, bf16[1024,768]{1,0:T(8,128)(2,1)}, bf16[1024,768]{1,0:T(8,128)(2,1)}, bf...) custom-call(s32[4]{0:T(128)} %pad_add_fusion.place_ref.refs_0_, bf16[1024,768]{1,0:T(8,128)(2,1)} %bitcast.58, ...), custom_call_target="tpu_custom_call" | custom-call | flops 4831838208 | bytes 25165824 | tf_op jit(solution)/shard_map/pallas_call | solution.py:75
  77.3 25.5 %shard_map.230 = (bf16[4,1024,768]{2,1,0:T(8,128)(2,1)}, f32[3,16,768]{2,1,0:T(8,128)}, bf16[3,1024,768]{2,1,0:T(8,128)(2,1)}) custom-call(bf16[3,1024,768]{2,1,0:T(8,128)(2,1)} %get-tuple-element.71.acts_ref, s32[1024,1]{1,0:T(8,128)} %bitcast.69, s32[2,1,512]{2,1,0:T(1,128)} %broadcast_in_dim.44.row_ref, ...), custom_call_target="tpu_custom_call", output_to_operand_aliasing={{2}: (0, {})} | custom-call | flops 9663676416 | bytes 18874368 | tf_op jit(solution)/shard_map/pallas_call | solution.py:75
  103.3 13.0 %shard_map.231 = (bf16[2,2,1024,768]{3,2,1,0:T(8,128)(2,1)}, f32[2,8,768]{2,1,0:T(8,128)}) custom-call(bf16[3,1024,768]{2,1,0:T(8,128)(2,1)} %get-tuple-element.77.a2_ref.dy_ref.refs_0_.refs_1_.refs_7_, bf16[3,1024,768]{2,1,0:T(8,128)(2,1)} %get-tuple-element.77.a2_ref.dy_ref.refs_0_.refs_1_.refs_7_, ...), custom_call_target="tpu_custom_call" | custom-call | flops 4831838208 | bytes 17301504 | tf_op jit(solution)/shard_map/pallas_call | solution.py:75
  116.7 21.5 %shard_map.232 = (bf16[2,2,1024,768]{3,2,1,0:T(8,128)(2,1)}, f32[2,8,768]{2,1,0:T(8,128)}) custom-call(bf16[3,1024,768]{2,1,0:T(8,128)(2,1)} %get-tuple-element.77.a2_ref.dy_ref.refs_0_.refs_1_.refs_7_, bf16[3,1024,768]{2,1,0:T(8,128)(2,1)} %get-tuple-element.77.a2_ref.dy_ref.refs_0_.refs_1_.refs_7_, ...), custom_call_target="tpu_custom_call" | custom-call | flops 4831838208 | bytes 17301504 | tf_op jit(solution)/shard_map/pallas_call | solution.py:75
  138.4 11.2 %shard_map.233 = (bf16[4,2,2,2,24,384]{5,4,3,2,1,0:T(8,128)(2,1)}, bf16[4,2,2,2,24,384]{5,4,3,2,1,0:T(8,128)(2,1)}, bf16[4,2,2,2,24,384]{5,4,3,2,1,0:T(8,128)(2,1)}, bf16[4,2,2,2,24,384]{5,4,3,2,1,0:T(8,128)(2,1)}) custom-call(s32[4]{0:T(128)} %pad_add_fusion.place_ref.refs_0_, bf16[3,1024,768]{2,1,0:T(8,128)(2,1)} %get-tuple-element.77.a2_ref.dy_ref.refs_0_.refs_1_.refs_7_, ...), custom_call_target="tpu_custom_call" | custom-call | flops 4831838208 | bytes 12582912 | tf_op jit(solution)/shard_map/pallas_call | solution.py:75
  151.6 10.9 %shard_map.234 = (bf16[4,2,2,2,24,384]{5,4,3,2,1,0:T(8,128)(2,1)}, bf16[4,2,2,2,24,384]{5,4,3,2,1,0:T(8,128)(2,1)}, bf16[4,2,2,2,24,384]{5,4,3,2,1,0:T(8,128)(2,1)}, bf16[4,2,2,2,24,384]{5,4,3,2,1,0:T(8,128)(2,1)}) custom-call(s32[4]{0:T(128)} %pad_add_fusion.place_ref.refs_0_, bf16[3,1024,768]{2,1,0:T(8,128)(2,1)} %get-tuple-element.77.a2_ref.dy_ref.refs_0_.refs_1_.refs_7_, ...), custom_call_target="tpu_custom_call" | custom-call | flops 4831838208 | bytes 12582912 | tf_op jit(solution)/shard_map/pallas_call | solution.py:75
  173.1 10.9 %shard_map.236 = (bf16[4,2,2,2,24,384]{5,4,3,2,1,0:T(8,128)(2,1)}, bf16[4,2,2,2,24,384]{5,4,3,2,1,0:T(8,128)(2,1)}, bf16[4,2,2,2,24,384]{5,4,3,2,1,0:T(8,128)(2,1)}, bf16[4,2,2,2,24,384]{5,4,3,2,1,0:T(8,128)(2,1)}) custom-call(s32[4]{0:T(128)} %pad_add_fusion.place_ref.refs_0_, bf16[3,1024,768]{2,1,0:T(8,128)(2,1)} %get-tuple-element.77.a2_ref.dy_ref.refs_0_.refs_1_.refs_7_, ...), custom_call_target="tpu_custom_call" | custom-call | flops 4831838208 | bytes 12582912 | tf_op jit(solution)/shard_map/pallas_call | solution.py:75
  186.1 7.3 %collective-permute-done.22.refs_2_ = bf16[4,2,2,2,24,384]{5,4,3,2,1,0:T(8,128)(2,1)} collective-permute-done((bf16[4,2,2,2,24,384]{5,4,3,2,1,0:T(8,128)(2,1)}, bf16[4,2,2,2,24,384]{5,4,3,2,1,0:T(8,128)(2,1)}, u32[]{:S(2)}, u32[]{:S(2)}) %collective-permute-start.22) | collective-permute-done | bytes 589856 | tf_op jit(solution)/shard_map/ppermute | solution.py:590
  198.5 9.8 %shard_map.238 = (f32[1024,768]{1,0:T(8,128)}, f32[3,8,768]{2,1,0:T(8,128)}) custom-call(bf16[1024,768]{1,0:T(8,128)(2,1)} %bitcast.59, bf16[1024,768]{1,0:T(8,128)(2,1)} %bitcast.67, bf16[4,1024,768]{2,1,0:T(8,128)(2,1)} %get-tuple-element.76.refs_3_.refs_5_.refs_2_.refs_1_, bf16[4,768,768]{2,1,0:T(8,128)(2,1)} %get-tuple-element.80.refs_3_.refs_4_, ...), custom_call_target="tpu_custom_call" | custom-call | flops 3623878656 | bytes 14548992 | tf_op jit(solution)/shard_map/pallas_call | solution.py:75
  210.3 4.1 %shard_map.239 = (bf16[4,2,2,24,384]{4,3,2,1,0:T(8,128)(2,1)}, bf16[4,2,2,24,384]{4,3,2,1,0:T(8,128)(2,1)}, bf16[4,2,2,24,384]{4,3,2,1,0:T(8,128)(2,1)}, bf16[4,...) custom-call(s32[4]{0:T(128)} %pad_add_fusion.place_ref.refs_0_, ...), custom_call_target="tpu_custom_call" | custom-call | bytes 9437184 | tf_op jit(solution)/shard_map/pallas_call | solution.py:75
  217.8 3.8 %collective-permute-start.26 = (bf16[8,24,768]{2,1,0:T(8,128)(2,1)}, bf16[8,24,768]{2,1,0:T(8,128)(2,1)}, u32[]{:S(2)}, u32[]{:S(2)}) collective-permute-start(bf16[8,24,768]{2,1,0:T(8,128)(2,1)} %bitcast.82), channel_id=1, source_target_pairs={{0,0},{1,16},{2,2},{3,18},{4,4},{5,20},{6,6},{7,22},{8,1},{9,17},{... | collective-permute-start | bytes 884744 | tf_op jit(solution)/shard_map/ppermute | solution.py:695
  221.5 5.0 %collective-permute-start.27 = (bf16[8,24,768]{2,1,0:T(8,128)(2,1)}, bf16[8,24,768]{2,1,0:T(8,128)(2,1)}, u32[]{:S(2)}, u32[]{:S(2)}) collective-permute-start(bf16[8,24,768]{2,1,0:T(8,128)(2,1)} %bitcast.81), channel_id=1, source_target_pairs={{0,1},{1,17},{2,3},{3,19},{4,5},{5,21},{6,7},{7,23},{8,0},{9,16},{... | collective-permute-start | bytes 884744 | tf_op jit(solution)/shard_map/ppermute | solution.py:695
  228.6 11.0 %shard_map.240 = (bf16[1024,768]{1,0:T(8,128)(2,1)}, f32[2,8,768]{2,1,0:T(8,128)}) custom-call(bf16[1024,768]{1,0:T(8,128)(2,1)} %bitcast.60, f32[1024,768]{1,0:T(8,128)} %get-tuple-element.101.refs_13_.refs_1_, bf16[4,1024,768]{2,1,0:T(8,128)(2,1)} %bitcast.56, bf16[4,1024,768]{2,1,0:T(8,128)(2,1)} %bitcast.50, ...), custom_call_target="tpu_custom_call" | custom-call | flops 4831838208 | bytes 17301504 | tf_op jit(solution)/shard_map/pallas_call | solution.py:75
  247.9 4.7 %collective-permute-start.35 = (bf16[4,24,768]{2,1,0:T(8,128)(2,1)}, bf16[4,24,768]{2,1,0:T(8,128)(2,1)}, u32[]{:S(2)}, u32[]{:S(2)}) collective-permute-start(bf16[4,24,768]{2,1,0:T(8,128)(2,1)} %bitcast.83), channel_id=1, source_target_pairs={{0,9},{1,25},{2,11},{3,27},{4,13},{5,29},{6,15},{7,31},{8,8},{9,24... | collective-permute-start | bytes 442376 | tf_op jit(solution)/shard_map/ppermute | solution.py:695
  254.2 7.9 %collective-permute-done.34.refs_7_ = bf16[4,24,768]{2,1,0:T(8,128)(2,1)} collective-permute-done((bf16[4,24,768]{2,1,0:T(8,128)(2,1)}, bf16[4,24,768]{2,1,0:T(8,128)(2,1)}, u32[]{:S(2)}, u32[]{:S(2)}) %collective-permute-start.34) | collective-permute-done | bytes 147488 | tf_op jit(solution)/shard_map/ppermute | solution.py:695
  262.2 3.7 %shard_map.242 = (f32[12,24,768]{2,1,0:T(8,128)}, bf16[32,24,768]{2,1,0:T(8,128)(2,1)}, f32[24,768]{1,0:T(8,128)}) custom-call(s32[32]{0:T(128)} %broadcast_add_fusion.refs_0_, bf16[8,24,768]{2,1,0:T(8,128)(2,1)} %collective-permute-done.26.refs_1_, bf16[8,24,768]{2,1,0:T(8,128)(2,1)} %collective-permute-done.27.refs_2_, ...), custom_call_target="tpu_custom_call" | custom-call | bytes 3538944 | tf_op jit(solution)/shard_map/pallas_call | solution.py:75
  265.9 5.9 %all-to-all-start.1 = ((bf16[32,24,768]{2,1,0:T(8,128)(2,1)}), bf16[32,24,768]{2,1,0:T(8,128)(2,1)}, u32[]{:S(2)}, u32[]{:S(2)}) async-start(bf16[32,24,768]{2,1,0:T(8,128)(2,1)} %get-tuple-element.122), calls=%async_computation.1 | async-start | bytes 2359296 | tf_op jit(solution)/shard_map/all_to_all | solution.py:892
  277.0 6.7 %collective-permute-done.37 = f32[16,768]{1,0:T(8,128)S(1)} collective-permute-done((f32[16,768]{1,0:T(8,128)S(1)}, f32[16,768]{1,0:T(8,128)S(1)}, u32[]{:S(2)}, u32[]{:S(2)}) %collective-permute-start.37) | collective-permute-done | bytes 49184 | tf_op jit(solution)/shard_map/ppermute | solution.py:590
  286.2 5.7 %collective-permute-start.41 = (f32[16,768]{1,0:T(8,128)}, f32[16,768]{1,0:T(8,128)}, u32[]{:S(2)}, u32[]{:S(2)}) collective-permute-start(f32[16,768]{1,0:T(8,128)} %add_add_fusion.1.refs_0_), channel_id=1, source_target_pairs={{0,16},{1,17},{2,18},{3,19},{4,20},{5,21},{6,22},{7,23},{8,24},{9,... | collective-permute-start | bytes 147464 | tf_op jit(solution)/shard_map/ppermute | solution.py:704
  291.9 3.5 shard_map.243
  295.4 9.1 %collective-permute-done.41.refs_2_ = f32[16,768]{1,0:T(8,128)} collective-permute-done((f32[16,768]{1,0:T(8,128)}, f32[16,768]{1,0:T(8,128)}, u32[]{:S(2)}, u32[]{:S(2)}) %collective-permute-start.41) | collective-permute-done | bytes 49184 | tf_op jit(solution)/shard_map/ppermute | solution.py:704
  304.5 5.7 %shard_map.245 = bf16[768,768]{1,0:T(8,128)(2,1)} custom-call(bf16[768,768]{1,0:T(8,128)(2,1)} %bitcast.29.s_ref, bf16[768,768]{1,0:T(8,128)(2,1)} %get-tuple-element.116.refs_7_.l_ref, bf16[768,768]{1,0:T(8,128)(2,1)} %get-tuple-element.123.r_ref, f32[16,768]{1,0:T(8,128)} %add_add_fusion.1.refs_0_, f32[16,768]{1,0:T(8,128)} %collective-permute-done.40.refs_1_, ...), custom_call_target="tpu_custom_call" | custom-call | flops 1811939328 | bytes 4718592 | tf_op jit(solution)/shard_map/pallas_call | solution.py:75
  310.1 3.5 all-to-all-start.2
  319.9 11.0 %shard_map.244 = bf16[1024,768]{1,0:T(8,128)(2,1)} custom-call(bf16[1024,768]{1,0:T(8,128)(2,1)} %bitcast.61, bf16[4,1024,768]{2,1,0:T(8,128)(2,1)} %get-tuple-element.76.refs_3_.refs_5_.refs_2_.refs_1_, bf16[4,1024,768]{2,1,0:T(8,128)(2,1)} %bitcast.57, bf16[4,1024,768]{2,1,0:T(8,128)(2,1)} %bitcast.51, ...), custom_call_target="tpu_custom_call" | custom-call | flops 6039797760 | bytes 16908288 | tf_op jit(solution)/shard_map/pallas_call | solution.py:75
  330.9 7.2 %shard_map.247 = (f32[768,768]{1,0:T(8,128)}, f32[768,768]{1,0:T(8,128)}) custom-call(s32[1]{0:T(128)} %bitcast.31.has_ref, f32[2]{0:T(128)} %pad_maximum_fusion.1.refs_8_.scale_ref, bf16[768,768]{1,0:T(8,128)(2,1)} %bitcast.29.s_ref, f32[768,768]{1,0:T(8,128)} %bitcast.77, f32[768,768]{1,0:T(8,128)} %bitcast.78), custom_call_target="tpu_custom_call" | custom-call | flops 1811939328 | bytes 10616832 | tf_op jit(solution)/shard_map/pallas_call | solution.py:75
  338.1 4.6 %all-to-all-done.2.p_ref = bf16[32,24,768]{2,1,0:T(8,128)(2,1)} async-done(((bf16[32,24,768]{2,1,0:T(8,128)(2,1)}), bf16[32,24,768]{2,1,0:T(8,128)(2,1)}, u32[]{:S(2)}, u32[]{:S(2)}) %all-to-all-start.2) | async-done | bytes 1179680 | tf_op jit(solution)/shard_map/all_to_all | solution.py:892
  342.7 3.3 shard_map.246
  (168 shorter events, 74.9 us)
Async XLA Ops:
  7.2 96.1 %all-gather.2.cloned.1.call-start = ((), (), s32[]{:S(2)}) async-start(), calls=%async_computation.3 | async-start | bytes 9732096 | tf_op jit(solution)/shard_map/all_gather | solution.py:923
  24.9 15.3 %collective-permute-start.3 = (bf16[4,4,24,768]{3,2,1,0:T(8,128)(2,1)S(1)}, bf16[4,4,24,768]{3,2,1,0:T(8,128)(2,1)S(1)}, u32[]{:S(2)}, u32[]{:S(2)}) collective-permute-start(bf16[4,4,24,768]{3,2,1,0:T(8,128)(2,1)S(1)} %pad_maximum_fusion.refs_0_), channel_id=1, source_target_pairs={{0,2},{1,3},{2,0},{3,1},{4,6},{5,7},{6,4},{7,5},{8,10},{9,11},{10,... | collective-permute-start | bytes 1769480 | tf_op jit(solution)/shard_map/ppermute | solution.py:590
  26.4 15.6 %collective-permute-start.4 = (bf16[4,4,24,768]{3,2,1,0:T(8,128)(2,1)S(1)}, bf16[4,4,24,768]{3,2,1,0:T(8,128)(2,1)S(1)}, u32[]{:S(2)}, u32[]{:S(2)}) collective-permute-start(bf16[4,4,24,768]{3,2,1,0:T(8,128)(2,1)S(1)} %pad_maximum_fusion.refs_0_), channel_id=1, source_target_pairs={{0,4},{1,5},{2,6},{3,7},{4,0},{5,1},{6,2},{7,3},{8,12},{9,13},{10,... | collective-permute-start | bytes 1769480 | tf_op jit(solution)/shard_map/ppermute | solution.py:594
  30.1 30.2 %all-to-all-start = ((bf16[32,2,156]{2,1,0:T(2,128)(2,1)}), bf16[32,2,156]{2,1,0:T(2,128)(2,1)S(1)}, u32[]{:S(2)}, u32[]{:S(2)}) async-start(bf16[32,2,156]{2,1,0:T(2,128)(2,1)} %reshape.151), calls=%async_computation | async-start | bytes 65536 | tf_op jit(solution)/shard_map/all_to_all | solution.py:892
  40.2 13.8 %collective-permute-start.5 = (bf16[2,4,24,768]{3,2,1,0:T(8,128)(2,1)S(1)}, bf16[2,4,24,768]{3,2,1,0:T(8,128)(2,1)S(1)}, u32[]{:S(2)}, u32[]{:S(2)}) collective-permute-start(bf16[2,4,24,768]{3,2,1,0:T(8,128)(2,1)S(1)} %slice.33), channel_id=1, source_target_pairs={{0,4},{1,5},{2,6},{3,7},{4,0},{5,1},{6,2},{7,3},{8,12},{9,13},{10,... | collective-permute-start | bytes 884744 | tf_op jit(solution)/shard_map/ppermute | solution.py:594
  42.0 16.0 %collective-permute-start.6 = (bf16[2,4,24,768]{3,2,1,0:T(8,128)(2,1)S(1)}, bf16[2,4,24,768]{3,2,1,0:T(8,128)(2,1)}, u32[]{:S(2)}, u32[]{:S(2)}) collective-permute-start(bf16[2,4,24,768]{3,2,1,0:T(8,128)(2,1)S(1)} %slice.34), channel_id=1, source_target_pairs={{0,2},{1,3},{2,0},{3,1},{4,6},{5,7},{6,4},{7,5},{8,10},{9,11},{10,... | collective-permute-start | bytes 884744 | tf_op jit(solution)/shard_map/ppermute | solution.py:590
  43.6 17.9 %collective-permute-start.7 = (bf16[4,4,24,768]{3,2,1,0:T(8,128)(2,1)S(1)}, bf16[4,4,24,768]{3,2,1,0:T(8,128)(2,1)S(1)}, u32[]{:S(2)}, u32[]{:S(2)}) collective-permute-start(bf16[4,4,24,768]{3,2,1,0:T(8,128)(2,1)S(1)} %pad_maximum_fusion.refs_0_), channel_id=1, source_target_pairs={{0,1},{1,0},{2,3},{3,2},{4,5},{5,4},{6,7},{7,6},{8,9},{9,8},{10,11... | collective-permute-start | bytes 1769480 | tf_op jit(solution)/shard_map/ppermute | solution.py:586
  43.6 17.9 %collective-permute-start.8 = (bf16[4,4,24,768]{3,2,1,0:T(8,128)(2,1)S(1)}, bf16[4,4,24,768]{3,2,1,0:T(8,128)(2,1)}, u32[]{:S(2)}, u32[]{:S(2)}) collective-permute-start(bf16[4,4,24,768]{3,2,1,0:T(8,128)(2,1)S(1)} %collective-permute-done.3.refs_1_), channel_id=1, source_target_pairs={{0,1},{1,0},{2,3},{3,2},{4,5},{5,4},{6,7},{7,6},{8,9},{9,8},{10,11... | collective-permute-start | bytes 1769480 | tf_op jit(solution)/shard_map/ppermute | solution.py:586
  44.1 17.4 %collective-permute-start.9 = (bf16[4,4,24,768]{3,2,1,0:T(8,128)(2,1)S(1)}, bf16[4,4,24,768]{3,2,1,0:T(8,128)(2,1)}, u32[]{:S(2)}, u32[]{:S(2)}) collective-permute-start(bf16[4,4,24,768]{3,2,1,0:T(8,128)(2,1)S(1)} %collective-permute-done.4.refs_2_), channel_id=1, source_target_pairs={{0,1},{1,0},{2,3},{3,2},{4,5},{5,4},{6,7},{7,6},{8,9},{9,8},{10,11... | collective-permute-start | bytes 1769480 | tf_op jit(solution)/shard_map/ppermute | solution.py:586
  102.7 14.0 %collective-permute-start.12 = (bf16[3,1024,768]{2,1,0:T(8,128)(2,1)}, bf16[3,1024,768]{2,1,0:T(8,128)(2,1)}, u32[]{:S(2)}, u32[]{:S(2)}) collective-permute-start(bf16[3,1024,768]{2,1,0:T(8,128)(2,1)} %get-tuple-element.77.a2_ref.dy_ref.refs_0_.refs_1_.refs_7_), channel_id=1, source_target_pairs={{0,1},{1,0},{2,3},{3,2},{4,5},{5,4},{6,7},{7,6},{8,9},{9,8},{10,11... | collective-permute-start | bytes 14155784 | tf_op jit(solution)/shard_map/ppermute | solution.py:586
  103.3 35.1 %collective-permute-start.14 = (bf16[4,1024,768]{2,1,0:T(8,128)(2,1)}, bf16[4,1024,768]{2,1,0:T(8,128)(2,1)}, u32[]{:S(2)}, u32[]{:S(2)}) collective-permute-start(bf16[4,1024,768]{2,1,0:T(8,128)(2,1)} %get-tuple-element.76.refs_3_.refs_5_.refs_2_.refs_1_), channel_id=1, source_target_pairs={{0,1},{1,0},{2,3},{3,2},{4,5},{5,4},{6,7},{7,6},{8,9},{9,8},{10,11... | collective-permute-start | bytes 18874376 | tf_op jit(solution)/shard_map/ppermute | solution.py:586
  116.3 35.3 %collective-permute-start.17 = (bf16[4,1024,768]{2,1,0:T(8,128)(2,1)}, bf16[4,1024,768]{2,1,0:T(8,128)(2,1)}, u32[]{:S(2)}, u32[]{:S(2)}) collective-permute-start(bf16[4,1024,768]{2,1,0:T(8,128)(2,1)} %bitcast.52), channel_id=1, source_target_pairs={{0,1},{1,0},{2,3},{3,2},{4,5},{5,4},{6,7},{7,6},{8,9},{9,8},{10,11... | collective-permute-start | bytes 18874376 | tf_op jit(solution)/shard_map/ppermute | solution.py:586
  138.3 34.8 %collective-permute-start.13 = (bf16[4,1024,768]{2,1,0:T(8,128)(2,1)}, bf16[4,1024,768]{2,1,0:T(8,128)(2,1)}, u32[]{:S(2)}, u32[]{:S(2)}) collective-permute-start(bf16[4,1024,768]{2,1,0:T(8,128)(2,1)} %bitcast.46), channel_id=1, source_target_pairs={{0,1},{1,0},{2,3},{3,2},{4,5},{5,4},{6,7},{7,6},{8,9},{9,8},{10,11... | collective-permute-start | bytes 18874376 | tf_op jit(solution)/shard_map/ppermute | solution.py:586
  149.5 16.0 %collective-permute-start.15 = (bf16[4,2,2,2,24,384]{5,4,3,2,1,0:T(8,128)(2,1)}, bf16[4,2,2,2,24,384]{5,4,3,2,1,0:T(8,128)(2,1)}, u32[]{:S(2)}, u32[]{:S(2)}) collective-permute-start(bf16[4,2,2,2,24,384]{5,4,3,2,1,0:T(8,128)(2,1)} %get-tuple-element.82), channel_id=1, source_target_pairs={{0,2},{1,3},{2,0},{3,1},{4,6},{5,7},{6,4},{7,5},{8,10},{9,11},{10,... | collective-permute-start | bytes 1769480 | tf_op jit(solution)/shard_map/ppermute | solution.py:590
  150.3 15.6 %collective-permute-start.16 = (bf16[4,2,2,2,24,384]{5,4,3,2,1,0:T(8,128)(2,1)}, bf16[4,2,2,2,24,384]{5,4,3,2,1,0:T(8,128)(2,1)}, u32[]{:S(2)}, u32[]{:S(2)}) collective-permute-start(bf16[4,2,2,2,24,384]{5,4,3,2,1,0:T(8,128)(2,1)} %get-tuple-element.84), channel_id=1, source_target_pairs={{0,4},{1,5},{2,6},{3,7},{4,0},{5,1},{6,2},{7,3},{8,12},{9,13},{10,... | collective-permute-start | bytes 1769480 | tf_op jit(solution)/shard_map/ppermute | solution.py:594
  169.0 16.3 %collective-permute-start.20 = (bf16[4,2,2,24,384]{4,3,2,1,0:T(8,128)(2,1)}, bf16[4,2,2,24,384]{4,3,2,1,0:T(8,128)(2,1)}, u32[]{:S(2)}, u32[]{:S(2)}) collective-permute-start(bf16[4,2,2,24,384]{4,3,2,1,0:T(8,128)(2,1)} %get-tuple-element.91), channel_id=1, source_target_pairs={{0,4},{1,5},{2,6},{3,7},{4,0},{5,1},{6,2},{7,3},{8,12},{9,13},{10,... | collective-permute-start | bytes 884744 | tf_op jit(solution)/shard_map/ppermute | solution.py:594
  170.4 15.6 %collective-permute-start.21 = (bf16[4,2,2,24,384]{4,3,2,1,0:T(8,128)(2,1)}, bf16[4,2,2,24,384]{4,3,2,1,0:T(8,128)(2,1)}, u32[]{:S(2)}, u32[]{:S(2)}) collective-permute-start(bf16[4,2,2,24,384]{4,3,2,1,0:T(8,128)(2,1)} %get-tuple-element.93), channel_id=1, source_target_pairs={{0,2},{1,3},{2,0},{3,1},{4,6},{5,7},{6,4},{7,5},{8,10},{9,11},{10,... | collective-permute-start | bytes 884744 | tf_op jit(solution)/shard_map/ppermute | solution.py:590
  171.1 22.2 %collective-permute-start.22 = (bf16[4,2,2,2,24,384]{5,4,3,2,1,0:T(8,128)(2,1)}, bf16[4,2,2,2,24,384]{5,4,3,2,1,0:T(8,128)(2,1)}, u32[]{:S(2)}, u32[]{:S(2)}) collective-permute-start(bf16[4,2,2,2,24,384]{5,4,3,2,1,0:T(8,128)(2,1)} %get-tuple-element.94), channel_id=1, source_target_pairs={{0,2},{1,3},{2,0},{3,1},{4,6},{5,7},{6,4},{7,5},{8,10},{9,11},{10,... | collective-permute-start | bytes 1769480 | tf_op jit(solution)/shard_map/ppermute | solution.py:590
  172.5 20.9 %collective-permute-start.23 = (bf16[4,2,2,2,24,384]{5,4,3,2,1,0:T(8,128)(2,1)}, bf16[4,2,2,2,24,384]{5,4,3,2,1,0:T(8,128)(2,1)}, u32[]{:S(2)}, u32[]{:S(2)}) collective-permute-start(bf16[4,2,2,2,24,384]{5,4,3,2,1,0:T(8,128)(2,1)} %get-tuple-element.96), channel_id=1, source_target_pairs={{0,4},{1,5},{2,6},{3,7},{4,0},{5,1},{6,2},{7,3},{8,12},{9,13},{10,... | collective-permute-start | bytes 1769480 | tf_op jit(solution)/shard_map/ppermute | solution.py:594
  184.0 24.3 %collective-permute-start.18 = (bf16[4,2,2,2,24,384]{5,4,3,2,1,0:T(8,128)(2,1)}, bf16[4,2,2,2,24,384]{5,4,3,2,1,0:T(8,128)(2,1)}, u32[]{:S(2)}, u32[]{:S(2)}) collective-permute-start(bf16[4,2,2,2,24,384]{5,4,3,2,1,0:T(8,128)(2,1)} %get-tuple-element.88), channel_id=1, source_target_pairs={{0,2},{1,3},{2,0},{3,1},{4,6},{5,7},{6,4},{7,5},{8,10},{9,11},{10,... | collective-permute-start | bytes 1769480 | tf_op jit(solution)/shard_map/ppermute | solution.py:590
  185.4 22.9 %collective-permute-start.19 = (bf16[4,2,2,2,24,384]{5,4,3,2,1,0:T(8,128)(2,1)}, bf16[4,2,2,2,24,384]{5,4,3,2,1,0:T(8,128)(2,1)}, u32[]{:S(2)}, u32[]{:S(2)}) collective-permute-start(bf16[4,2,2,2,24,384]{5,4,3,2,1,0:T(8,128)(2,1)} %get-tuple-element.90), channel_id=1, source_target_pairs={{0,4},{1,5},{2,6},{3,7},{4,0},{5,1},{6,2},{7,3},{8,12},{9,13},{10,... | collective-permute-start | bytes 1769480 | tf_op jit(solution)/shard_map/ppermute | solution.py:594
  197.1 13.2 %collective-permute-start.25 = (bf16[4,2,2,24,384]{4,3,2,1,0:T(8,128)(2,1)}, bf16[4,2,2,24,384]{4,3,2,1,0:T(8,128)(2,1)}, u32[]{:S(2)}, u32[]{:S(2)}) collective-permute-start(bf16[4,2,2,24,384]{4,3,2,1,0:T(8,128)(2,1)} %get-tuple-element.100), channel_id=1, source_target_pairs={{0,2},{1,3},{2,0},{3,1},{4,6},{5,7},{6,4},{7,5},{8,10},{9,11},{10,... | collective-permute-start | bytes 884744 | tf_op jit(solution)/shard_map/ppermute | solution.py:590
  216.4 23.3 %collective-permute-start.31 = (bf16[4,2,2,24,384]{4,3,2,1,0:T(8,128)(2,1)}, bf16[4,2,2,24,384]{4,3,2,1,0:T(8,128)(2,1)}, u32[]{:S(2)}, u32[]{:S(2)}) collective-permute-start(bf16[4,2,2,24,384]{4,3,2,1,0:T(8,128)(2,1)} %get-tuple-element.109), channel_id=1, source_target_pairs={{0,2},{1,3},{2,0},{3,1},{4,6},{5,7},{6,4},{7,5},{8,10},{9,11},{10,... | collective-permute-start | bytes 884744 | tf_op jit(solution)/shard_map/ppermute | solution.py:590
  217.8 27.4 %collective-permute-start.26 = (bf16[8,24,768]{2,1,0:T(8,128)(2,1)}, bf16[8,24,768]{2,1,0:T(8,128)(2,1)}, u32[]{:S(2)}, u32[]{:S(2)}) collective-permute-start(bf16[8,24,768]{2,1,0:T(8,128)(2,1)} %bitcast.82), channel_id=1, source_target_pairs={{0,0},{1,16},{2,2},{3,18},{4,4},{5,20},{6,6},{7,22},{8,1},{9,17},{... | collective-permute-start | bytes 884744 | tf_op jit(solution)/shard_map/ppermute | solution.py:695
  221.5 25.8 %collective-permute-start.27 = (bf16[8,24,768]{2,1,0:T(8,128)(2,1)}, bf16[8,24,768]{2,1,0:T(8,128)(2,1)}, u32[]{:S(2)}, u32[]{:S(2)}) collective-permute-start(bf16[8,24,768]{2,1,0:T(8,128)(2,1)} %bitcast.81), channel_id=1, source_target_pairs={{0,1},{1,17},{2,3},{3,19},{4,5},{5,21},{6,7},{7,23},{8,0},{9,16},{... | collective-permute-start | bytes 884744 | tf_op jit(solution)/shard_map/ppermute | solution.py:695
  226.5 21.4 %collective-permute-start.28 = (bf16[8,24,768]{2,1,0:T(8,128)(2,1)}, bf16[8,24,768]{2,1,0:T(8,128)(2,1)}, u32[]{:S(2)}, u32[]{:S(2)}) collective-permute-start(bf16[8,24,768]{2,1,0:T(8,128)(2,1)} %bitcast.80), channel_id=1, source_target_pairs={{0,8},{1,24},{2,10},{3,26},{4,12},{5,28},{6,14},{7,30},{8,9},{9,25... | collective-permute-start | bytes 884744 | tf_op jit(solution)/shard_map/ppermute | solution.py:695
  226.5 27.3 %collective-permute-start.29 = (bf16[8,24,768]{2,1,0:T(8,128)(2,1)}, bf16[8,24,768]{2,1,0:T(8,128)(2,1)}, u32[]{:S(2)}, u32[]{:S(2)}) collective-permute-start(bf16[8,24,768]{2,1,0:T(8,128)(2,1)} %bitcast.79), channel_id=1, source_target_pairs={{0,9},{1,25},{2,11},{3,27},{4,13},{5,29},{6,15},{7,31},{8,8},{9,24... | collective-permute-start | bytes 884744 | tf_op jit(solution)/shard_map/ppermute | solution.py:695
  247.3 14.9 %collective-permute-start.34 = (bf16[4,24,768]{2,1,0:T(8,128)(2,1)}, bf16[4,24,768]{2,1,0:T(8,128)(2,1)}, u32[]{:S(2)}, u32[]{:S(2)}) collective-permute-start(bf16[4,24,768]{2,1,0:T(8,128)(2,1)} %bitcast.84), channel_id=1, source_target_pairs={{0,8},{1,24},{2,10},{3,26},{4,12},{5,28},{6,14},{7,30},{8,9},{9,25... | collective-permute-start | bytes 442376 | tf_op jit(solution)/shard_map/ppermute | solution.py:695
  247.9 14.3 %collective-permute-start.35 = (bf16[4,24,768]{2,1,0:T(8,128)(2,1)}, bf16[4,24,768]{2,1,0:T(8,128)(2,1)}, u32[]{:S(2)}, u32[]{:S(2)}) collective-permute-start(bf16[4,24,768]{2,1,0:T(8,128)(2,1)} %bitcast.83), channel_id=1, source_target_pairs={{0,9},{1,25},{2,11},{3,27},{4,13},{5,29},{6,15},{7,31},{8,8},{9,24... | collective-permute-start | bytes 442376 | tf_op jit(solution)/shard_map/ppermute | solution.py:695
  265.9 38.6 %all-to-all-start.1 = ((bf16[32,24,768]{2,1,0:T(8,128)(2,1)}), bf16[32,24,768]{2,1,0:T(8,128)(2,1)}, u32[]{:S(2)}, u32[]{:S(2)}) async-start(bf16[32,24,768]{2,1,0:T(8,128)(2,1)} %get-tuple-element.122), calls=%async_computation.1 | async-start | bytes 2359296 | tf_op jit(solution)/shard_map/all_to_all | solution.py:892
  286.2 18.2 %collective-permute-start.41 = (f32[16,768]{1,0:T(8,128)}, f32[16,768]{1,0:T(8,128)}, u32[]{:S(2)}, u32[]{:S(2)}) collective-permute-start(f32[16,768]{1,0:T(8,128)} %add_add_fusion.1.refs_0_), channel_id=1, source_target_pairs={{0,16},{1,17},{2,18},{3,19},{4,20},{5,21},{6,22},{7,23},{8,24},{9,... | collective-permute-start | bytes 147464 | tf_op jit(solution)/shard_map/ppermute | solution.py:704
  310.1 32.6 %all-to-all-start.2 = ((bf16[32,24,768]{2,1,0:T(8,128)(2,1)}), bf16[32,24,768]{2,1,0:T(8,128)(2,1)}, u32[]{:S(2)}, u32[]{:S(2)}) async-start(bf16[32,24,768]{2,1,0:T(8,128)(2,1)} %bitcast.68), calls=%async_computation.2 | async-start | bytes 2359296 | tf_op jit(solution)/shard_map/all_to_all | solution.py:892
  (35 other events, 445.4 us)
Sparse Core Ops, SparseCore 0:
  11.0 91.7 all-gather.1

commit v10 on v9

--- a/solution.py
+++ b/solution.py
@@ -318,22 +318,16 @@
     i = pl.program_id(0)
     y, x = place_ref[1], place_ref[2]
 
-    def part(n):
+    @pl.when(i == 0)
+    def _():
+        acc[...] = jnp.zeros_like(acc)
+
+    for n in range(first + second):
         if n < first:
-            value = mm(l1o[0], r1o[n], TN) + mm(l1p[0], r1p[n], TN)
+            part = mm(l1o[0], r1o[n], TN) + mm(l1p[0], r1p[n], TN)
         else:
-            value = mm(l2o[n - first], r2o[0], TN) + mm(l2p[n - first], r2p[0], TN)
-        return value.reshape(acc.shape[1:])
-
-    @pl.when(i == 0)
-    def _():
-        for n in range(first + second):
-            acc[n] = part(n)
-
-    @pl.when(i > 0)
-    def _():
-        for n in range(first + second):
-            acc[n] += part(n)
+            part = mm(l2o[n - first], r2o[0], TN) + mm(l2p[n - first], r2p[0], TN)
+        acc[n] += part.reshape(acc.shape[1:])
 
     @pl.when(i == steps - 1)
     def _():

time: 361 us -> 347 us (0.961); the launches traced: 354 us -> 346 us
  Pallas kernels: 175 us -> 168 us
    pallas_call x19, Pallas kernels: 175 us -> 168 us  [call(): return lambda *operands: made(*operands, *after)]
  transfers between devices with their start and end apart: 47 -> 47, of which waited for: 17 -> 17; matrix products, arithmetic and copies ran while one was open for 5% -> 5% of each run, Pallas kernels for 45% -> 44%
where the time goes in v10:
time: 347 us; the launch traced here: 346 us
  Pallas kernels  168 us (48%)
  starting transfers between devices  76.3 us (22%)
  waiting for transfers between devices  63.6 us (18%)
  between operations  17.8 us (5%)
  other arithmetic  13.5 us (4%)
  local copies, waits for them, and re-layouts  6.61 us (2%)
    pallas_call x19, Pallas kernels, call(): return lambda *operands: made(*operands, *after)  168 us
    ppermute x9, waiting for transfers between devices, over_x(): lax.ppermute(value, AXES, to_place(lambda z, y, x, c: (z, y, 1 - x, c)))  21.5 us
    ppermute x8, starting transfers between devices, advance(): lax.ppermute(v, AXES, to_place(lambda z, y, x, c, m=m: (2 * c + ((z ^ m)...  20.8 us
    all_to_all x3, starting transfers between devices, to_all(): return lax.all_to_all(value, AXES, split_axis=0, concat_axis=0, tiled=True)  19.1 us
    ppermute x9, starting transfers between devices, over_x(): lax.ppermute(value, AXES, to_place(lambda z, y, x, c: (z, y, 1 - x, c)))  11.9 us
    ppermute x4, waiting for transfers between devices, get(): return lax.ppermute(value, AXES, to_place(move))  10.7 us
    ppermute x9, starting transfers between devices, over_y(): lax.ppermute(value, AXES, to_place(lambda z, y, x, c: (z, 1 - y, x, c)))  9.98 us
    ppermute x3, waiting for transfers between devices, over_z(): lax.ppermute(value, AXES, to_place(lambda z, y, x, c: ((z + by) % 4, y, x...  9.35 us
  transfers between devices with their start and end apart: 47, of which 17 were waited for; matrix products, arithmetic and copies ran while one was open for 5% of the time, Pallas kernels for 44%

profile of v10, /device:TPU:0, one launch (start us, length us, event | category | flops | bytes accessed | tf_op | source)
XLA Modules:
  0.0 345.8 jit_solution(3789873894102263507)
XLA Ops:
  9.3 4.1 %collective-permute-start.1 = (bf16[4,24,768]{2,1,0:T(8,128)(2,1)S(1)}, bf16[4,24,768]{2,1,0:T(8,128)(2,1)S(1)}, u32[]{:S(2)}, u32[]{:S(2)}) collective-permute-start(bf16[4,24,768]{2,1,0:T(8,128)(2,1)S(1)} %get-tuple-element.135), channel_id=1, source_target_pairs={{0,16},{1,17},{2,18},{3,19},{4,20},{5,21},{6,22},{7,23},{8,24},{9,... | collective-permute-start | bytes 442376 | tf_op jit(solution)/shard_map/ppermute | solution.py:592
  15.4 6.6 %collective-permute-done.1 = bf16[4,24,768]{2,1,0:T(8,128)(2,1)S(1)} collective-permute-done((bf16[4,24,768]{2,1,0:T(8,128)(2,1)S(1)}, bf16[4,24,768]{2,1,0:T(8,128)(2,1)S(1)}, u32[]{:S(2)}, u32[]{:S(2)}) %collective-permute-start.1) | collective-permute-done | bytes 147488 | tf_op jit(solution)/shard_map/ppermute | solution.py:592
  30.1 9.6 %all-to-all-start = ((bf16[32,2,156]{2,1,0:T(2,128)(2,1)}), bf16[32,2,156]{2,1,0:T(2,128)(2,1)S(1)}, u32[]{:S(2)}, u32[]{:S(2)}) async-start(bf16[32,2,156]{2,1,0:T(2,128)(2,1)} %reshape.151), calls=%async_computation | async-start | bytes 65536 | tf_op jit(solution)/shard_map/all_to_all | solution.py:886
  47.4 6.6 %collective-permute-done.5.refs_3_ = bf16[2,4,24,768]{3,2,1,0:T(8,128)(2,1)S(1)} collective-permute-done((bf16[2,4,24,768]{3,2,1,0:T(8,128)(2,1)S(1)}, bf16[2,4,24,768]{3,2,1,0:T(8,128)(2,1)S(1)}, u32[]{:S(2)}, u32[]{:S(2)}) %collective-permute-start.5) | collective-permute-done | bytes 294944 | tf_op jit(solution)/shard_map/ppermute | solution.py:588
  54.1 3.9 %collective-permute-done.6.refs_4_ = bf16[2,4,24,768]{3,2,1,0:T(8,128)(2,1)} collective-permute-done((bf16[2,4,24,768]{3,2,1,0:T(8,128)(2,1)S(1)}, bf16[2,4,24,768]{3,2,1,0:T(8,128)(2,1)}, u32[]{:S(2)}, u32[]{:S(2)}) %collective-permute-start.6) | collective-permute-done | bytes 294944 | tf_op jit(solution)/shard_map/ppermute | solution.py:584
  63.1 14.2 %shard_map.229 = (bf16[1024,768]{1,0:T(8,128)(2,1)}, bf16[1024,768]{1,0:T(8,128)(2,1)}, bf16[1024,768]{1,0:T(8,128)(2,1)}, bf16[1024,768]{1,0:T(8,128)(2,1)}, bf...) custom-call(s32[4]{0:T(128)} %pad_add_fusion.place_ref.refs_0_, bf16[1024,768]{1,0:T(8,128)(2,1)} %bitcast.58, ...), custom_call_target="tpu_custom_call" | custom-call | flops 4831838208 | bytes 25165824 | tf_op jit(solution)/shard_map/pallas_call | solution.py:75
  77.3 25.5 %shard_map.230 = (bf16[4,1024,768]{2,1,0:T(8,128)(2,1)}, f32[3,16,768]{2,1,0:T(8,128)}, bf16[3,1024,768]{2,1,0:T(8,128)(2,1)}) custom-call(bf16[3,1024,768]{2,1,0:T(8,128)(2,1)} %get-tuple-element.71.acts_ref, s32[1024,1]{1,0:T(8,128)} %bitcast.69, s32[2,1,512]{2,1,0:T(1,128)} %broadcast_in_dim.44.row_ref, ...), custom_call_target="tpu_custom_call", output_to_operand_aliasing={{2}: (0, {})} | custom-call | flops 9663676416 | bytes 18874368 | tf_op jit(solution)/shard_map/pallas_call | solution.py:75
  103.3 13.0 %shard_map.231 = (bf16[2,2,1024,768]{3,2,1,0:T(8,128)(2,1)}, f32[2,8,768]{2,1,0:T(8,128)}) custom-call(bf16[3,1024,768]{2,1,0:T(8,128)(2,1)} %get-tuple-element.77.a2_ref.dy_ref.refs_0_.refs_1_.refs_7_, bf16[3,1024,768]{2,1,0:T(8,128)(2,1)} %get-tuple-element.77.a2_ref.dy_ref.refs_0_.refs_1_.refs_7_, ...), custom_call_target="tpu_custom_call" | custom-call | flops 4831838208 | bytes 17301504 | tf_op jit(solution)/shard_map/pallas_call | solution.py:75
  116.7 13.1 %shard_map.232 = (bf16[2,2,1024,768]{3,2,1,0:T(8,128)(2,1)}, f32[2,8,768]{2,1,0:T(8,128)}) custom-call(bf16[3,1024,768]{2,1,0:T(8,128)(2,1)} %get-tuple-element.77.a2_ref.dy_ref.refs_0_.refs_1_.refs_7_, bf16[3,1024,768]{2,1,0:T(8,128)(2,1)} %get-tuple-element.77.a2_ref.dy_ref.refs_0_.refs_1_.refs_7_, ...), custom_call_target="tpu_custom_call" | custom-call | flops 4831838208 | bytes 17301504 | tf_op jit(solution)/shard_map/pallas_call | solution.py:75
  129.9 11.4 %shard_map.233 = (bf16[4,2,2,2,24,384]{5,4,3,2,1,0:T(8,128)(2,1)}, bf16[4,2,2,2,24,384]{5,4,3,2,1,0:T(8,128)(2,1)}, bf16[4,2,2,2,24,384]{5,4,3,2,1,0:T(8,128)(2,1)}, bf16[4,2,2,2,24,384]{5,4,3,2,1,0:T(8,128)(2,1)}) custom-call(s32[4]{0:T(128)} %pad_add_fusion.place_ref.refs_0_, bf16[3,1024,768]{2,1,0:T(8,128)(2,1)} %get-tuple-element.77.a2_ref.dy_ref.refs_0_.refs_1_.refs_7_, ...), custom_call_target="tpu_custom_call" | custom-call | flops 4831838208 | bytes 12582912 | tf_op jit(solution)/shard_map/pallas_call | solution.py:75
  143.4 11.2 %shard_map.234 = (bf16[4,2,2,2,24,384]{5,4,3,2,1,0:T(8,128)(2,1)}, bf16[4,2,2,2,24,384]{5,4,3,2,1,0:T(8,128)(2,1)}, bf16[4,2,2,2,24,384]{5,4,3,2,1,0:T(8,128)(2,1)}, bf16[4,2,2,2,24,384]{5,4,3,2,1,0:T(8,128)(2,1)}) custom-call(s32[4]{0:T(128)} %pad_add_fusion.place_ref.refs_0_, bf16[3,1024,768]{2,1,0:T(8,128)(2,1)} %get-tuple-element.77.a2_ref.dy_ref.refs_0_.refs_1_.refs_7_, ...), custom_call_target="tpu_custom_call" | custom-call | flops 4831838208 | bytes 12582912 | tf_op jit(solution)/shard_map/pallas_call | solution.py:75
  164.9 11.2 %shard_map.236 = (bf16[4,2,2,2,24,384]{5,4,3,2,1,0:T(8,128)(2,1)}, bf16[4,2,2,2,24,384]{5,4,3,2,1,0:T(8,128)(2,1)}, bf16[4,2,2,2,24,384]{5,4,3,2,1,0:T(8,128)(2,1)}, bf16[4,2,2,2,24,384]{5,4,3,2,1,0:T(8,128)(2,1)}) custom-call(s32[4]{0:T(128)} %pad_add_fusion.place_ref.refs_0_, bf16[3,1024,768]{2,1,0:T(8,128)(2,1)} %get-tuple-element.77.a2_ref.dy_ref.refs_0_.refs_1_.refs_7_, ...), custom_call_target="tpu_custom_call" | custom-call | flops 4831838208 | bytes 12582912 | tf_op jit(solution)/shard_map/pallas_call | solution.py:75
  178.1 7.0 %collective-permute-done.22.refs_2_ = bf16[4,2,2,2,24,384]{5,4,3,2,1,0:T(8,128)(2,1)} collective-permute-done((bf16[4,2,2,2,24,384]{5,4,3,2,1,0:T(8,128)(2,1)}, bf16[4,2,2,2,24,384]{5,4,3,2,1,0:T(8,128)(2,1)}, u32[]{:S(2)}, u32[]{:S(2)}) %collective-permute-start.22) | collective-permute-done | bytes 589856 | tf_op jit(solution)/shard_map/ppermute | solution.py:584
  190.3 9.8 %shard_map.238 = (f32[1024,768]{1,0:T(8,128)}, f32[3,8,768]{2,1,0:T(8,128)}) custom-call(bf16[1024,768]{1,0:T(8,128)(2,1)} %bitcast.59, bf16[1024,768]{1,0:T(8,128)(2,1)} %bitcast.67, bf16[4,1024,768]{2,1,0:T(8,128)(2,1)} %get-tuple-element.76.refs_3_.refs_5_.refs_2_.refs_1_, bf16[4,768,768]{2,1,0:T(8,128)(2,1)} %get-tuple-element.80.refs_3_.refs_4_, ...), custom_call_target="tpu_custom_call" | custom-call | flops 3623878656 | bytes 14548992 | tf_op jit(solution)/shard_map/pallas_call | solution.py:75
  202.1 4.1 %shard_map.239 = (bf16[4,2,2,24,384]{4,3,2,1,0:T(8,128)(2,1)}, bf16[4,2,2,24,384]{4,3,2,1,0:T(8,128)(2,1)}, bf16[4,2,2,24,384]{4,3,2,1,0:T(8,128)(2,1)}, bf16[4,...) custom-call(s32[4]{0:T(128)} %pad_add_fusion.place_ref.refs_0_, ...), custom_call_target="tpu_custom_call" | custom-call | bytes 9437184 | tf_op jit(solution)/shard_map/pallas_call | solution.py:75
  209.6 3.8 %collective-permute-start.26 = (bf16[8,24,768]{2,1,0:T(8,128)(2,1)}, bf16[8,24,768]{2,1,0:T(8,128)(2,1)}, u32[]{:S(2)}, u32[]{:S(2)}) collective-permute-start(bf16[8,24,768]{2,1,0:T(8,128)(2,1)} %bitcast.82), channel_id=1, source_target_pairs={{0,0},{1,16},{2,2},{3,18},{4,4},{5,20},{6,6},{7,22},{8,1},{9,17},{... | collective-permute-start | bytes 884744 | tf_op jit(solution)/shard_map/ppermute | solution.py:689
  213.3 5.0 %collective-permute-start.27 = (bf16[8,24,768]{2,1,0:T(8,128)(2,1)}, bf16[8,24,768]{2,1,0:T(8,128)(2,1)}, u32[]{:S(2)}, u32[]{:S(2)}) collective-permute-start(bf16[8,24,768]{2,1,0:T(8,128)(2,1)} %bitcast.81), channel_id=1, source_target_pairs={{0,1},{1,17},{2,3},{3,19},{4,5},{5,21},{6,7},{7,23},{8,0},{9,16},{... | collective-permute-start | bytes 884744 | tf_op jit(solution)/shard_map/ppermute | solution.py:689
  220.5 11.2 %shard_map.240 = (bf16[1024,768]{1,0:T(8,128)(2,1)}, f32[2,8,768]{2,1,0:T(8,128)}) custom-call(bf16[1024,768]{1,0:T(8,128)(2,1)} %bitcast.60, f32[1024,768]{1,0:T(8,128)} %get-tuple-element.101.refs_13_.refs_1_, bf16[4,1024,768]{2,1,0:T(8,128)(2,1)} %bitcast.56, bf16[4,1024,768]{2,1,0:T(8,128)(2,1)} %bitcast.50, ...), custom_call_target="tpu_custom_call" | custom-call | flops 4831838208 | bytes 17301504 | tf_op jit(solution)/shard_map/pallas_call | solution.py:75
  239.7 5.0 %collective-permute-start.35 = (bf16[4,24,768]{2,1,0:T(8,128)(2,1)}, bf16[4,24,768]{2,1,0:T(8,128)(2,1)}, u32[]{:S(2)}, u32[]{:S(2)}) collective-permute-start(bf16[4,24,768]{2,1,0:T(8,128)(2,1)} %bitcast.83), channel_id=1, source_target_pairs={{0,9},{1,25},{2,11},{3,27},{4,13},{5,29},{6,15},{7,31},{8,8},{9,24... | collective-permute-start | bytes 442376 | tf_op jit(solution)/shard_map/ppermute | solution.py:689
  246.0 7.9 %collective-permute-done.34.refs_7_ = bf16[4,24,768]{2,1,0:T(8,128)(2,1)} collective-permute-done((bf16[4,24,768]{2,1,0:T(8,128)(2,1)}, bf16[4,24,768]{2,1,0:T(8,128)(2,1)}, u32[]{:S(2)}, u32[]{:S(2)}) %collective-permute-start.34) | collective-permute-done | bytes 147488 | tf_op jit(solution)/shard_map/ppermute | solution.py:689
  253.9 3.7 %shard_map.242 = (f32[12,24,768]{2,1,0:T(8,128)}, bf16[32,24,768]{2,1,0:T(8,128)(2,1)}, f32[24,768]{1,0:T(8,128)}) custom-call(s32[32]{0:T(128)} %broadcast_add_fusion.refs_0_, bf16[8,24,768]{2,1,0:T(8,128)(2,1)} %collective-permute-done.26.refs_1_, bf16[8,24,768]{2,1,0:T(8,128)(2,1)} %collective-permute-done.27.refs_2_, ...), custom_call_target="tpu_custom_call" | custom-call | bytes 3538944 | tf_op jit(solution)/shard_map/pallas_call | solution.py:75
  257.7 5.9 %all-to-all-start.1 = ((bf16[32,24,768]{2,1,0:T(8,128)(2,1)}), bf16[32,24,768]{2,1,0:T(8,128)(2,1)}, u32[]{:S(2)}, u32[]{:S(2)}) async-start(bf16[32,24,768]{2,1,0:T(8,128)(2,1)} %get-tuple-element.122), calls=%async_computation.1 | async-start | bytes 2359296 | tf_op jit(solution)/shard_map/all_to_all | solution.py:886
  268.8 6.7 %collective-permute-done.37 = f32[16,768]{1,0:T(8,128)S(1)} collective-permute-done((f32[16,768]{1,0:T(8,128)S(1)}, f32[16,768]{1,0:T(8,128)S(1)}, u32[]{:S(2)}, u32[]{:S(2)}) %collective-permute-start.37) | collective-permute-done | bytes 49184 | tf_op jit(solution)/shard_map/ppermute | solution.py:584
  278.0 5.7 %collective-permute-start.41 = (f32[16,768]{1,0:T(8,128)}, f32[16,768]{1,0:T(8,128)}, u32[]{:S(2)}, u32[]{:S(2)}) collective-permute-start(f32[16,768]{1,0:T(8,128)} %add_add_fusion.1.refs_0_), channel_id=1, source_target_pairs={{0,16},{1,17},{2,18},{3,19},{4,20},{5,21},{6,22},{7,23},{8,24},{9,... | collective-permute-start | bytes 147464 | tf_op jit(solution)/shard_map/ppermute | solution.py:698
  283.7 3.5 %shard_map.243 = (bf16[768,768]{1,0:T(8,128)(2,1)}, bf16[768,768]{1,0:T(8,128)(2,1)}) custom-call(f32[768,768]{1,0:T(8,128)} %bitcast.63, f32[768,768]{1,0:T(8,128)} %bitcast.64, f32[24,768]{1,0:T(8,128)} %get-tuple-element.115.refs_2_), custom_call_target="tpu_custom_call" | custom-call | bytes 7077888 | tf_op jit(solution)/shard_map/pallas_call | solution.py:75
  287.2 9.1 %collective-permute-done.41.refs_2_ = f32[16,768]{1,0:T(8,128)} collective-permute-done((f32[16,768]{1,0:T(8,128)}, f32[16,768]{1,0:T(8,128)}, u32[]{:S(2)}, u32[]{:S(2)}) %collective-permute-start.41) | collective-permute-done | bytes 49184 | tf_op jit(solution)/shard_map/ppermute | solution.py:698
  296.3 5.7 %shard_map.245 = bf16[768,768]{1,0:T(8,128)(2,1)} custom-call(bf16[768,768]{1,0:T(8,128)(2,1)} %bitcast.29.s_ref, bf16[768,768]{1,0:T(8,128)(2,1)} %get-tuple-element.116.refs_7_.l_ref, bf16[768,768]{1,0:T(8,128)(2,1)} %get-tuple-element.123.r_ref, f32[16,768]{1,0:T(8,128)} %add_add_fusion.1.refs_0_, f32[16,768]{1,0:T(8,128)} %collective-permute-done.40.refs_1_, ...), custom_call_target="tpu_custom_call" | custom-call | flops 1811939328 | bytes 4718592 | tf_op jit(solution)/shard_map/pallas_call | solution.py:75
  302.0 3.5 %all-to-all-start.2 = ((bf16[32,24,768]{2,1,0:T(8,128)(2,1)}), bf16[32,24,768]{2,1,0:T(8,128)(2,1)}, u32[]{:S(2)}, u32[]{:S(2)}) async-start(bf16[32,24,768]{2,1,0:T(8,128)(2,1)} %bitcast.68), calls=%async_computation.2 | async-start | bytes 2359296 | tf_op jit(solution)/shard_map/all_to_all | solution.py:886
  311.7 11.0 %shard_map.244 = bf16[1024,768]{1,0:T(8,128)(2,1)} custom-call(bf16[1024,768]{1,0:T(8,128)(2,1)} %bitcast.61, bf16[4,1024,768]{2,1,0:T(8,128)(2,1)} %get-tuple-element.76.refs_3_.refs_5_.refs_2_.refs_1_, bf16[4,1024,768]{2,1,0:T(8,128)(2,1)} %bitcast.57, bf16[4,1024,768]{2,1,0:T(8,128)(2,1)} %bitcast.51, ...), custom_call_target="tpu_custom_call" | custom-call | flops 6039797760 | bytes 16908288 | tf_op jit(solution)/shard_map/pallas_call | solution.py:75
  322.8 7.2 %shard_map.247 = (f32[768,768]{1,0:T(8,128)}, f32[768,768]{1,0:T(8,128)}) custom-call(s32[1]{0:T(128)} %bitcast.31.has_ref, f32[2]{0:T(128)} %pad_maximum_fusion.1.refs_8_.scale_ref, bf16[768,768]{1,0:T(8,128)(2,1)} %bitcast.29.s_ref, f32[768,768]{1,0:T(8,128)} %bitcast.77, f32[768,768]{1,0:T(8,128)} %bitcast.78), custom_call_target="tpu_custom_call" | custom-call | flops 1811939328 | bytes 10616832 | tf_op jit(solution)/shard_map/pallas_call | solution.py:75
  329.9 4.6 %all-to-all-done.2.p_ref = bf16[32,24,768]{2,1,0:T(8,128)(2,1)} async-done(((bf16[32,24,768]{2,1,0:T(8,128)(2,1)}), bf16[32,24,768]{2,1,0:T(8,128)(2,1)}, u32[]{:S(2)}, u32[]{:S(2)}) %all-to-all-start.2) | async-done | bytes 1179680 | tf_op jit(solution)/shard_map/all_to_all | solution.py:886
  334.5 3.3 shard_map.246
  (168 shorter events, 73.9 us)
Async XLA Ops:
  7.2 96.1 %all-gather.2.cloned.1.call-start = ((), (), s32[]{:S(2)}) async-start(), calls=%async_computation.3 | async-start | bytes 9732096 | tf_op jit(solution)/shard_map/all_gather | solution.py:917
  24.9 15.3 %collective-permute-start.3 = (bf16[4,4,24,768]{3,2,1,0:T(8,128)(2,1)S(1)}, bf16[4,4,24,768]{3,2,1,0:T(8,128)(2,1)S(1)}, u32[]{:S(2)}, u32[]{:S(2)}) collective-permute-start(bf16[4,4,24,768]{3,2,1,0:T(8,128)(2,1)S(1)} %pad_maximum_fusion.refs_0_), channel_id=1, source_target_pairs={{0,2},{1,3},{2,0},{3,1},{4,6},{5,7},{6,4},{7,5},{8,10},{9,11},{10,... | collective-permute-start | bytes 1769480 | tf_op jit(solution)/shard_map/ppermute | solution.py:584
  26.4 15.6 %collective-permute-start.4 = (bf16[4,4,24,768]{3,2,1,0:T(8,128)(2,1)S(1)}, bf16[4,4,24,768]{3,2,1,0:T(8,128)(2,1)S(1)}, u32[]{:S(2)}, u32[]{:S(2)}) collective-permute-start(bf16[4,4,24,768]{3,2,1,0:T(8,128)(2,1)S(1)} %pad_maximum_fusion.refs_0_), channel_id=1, source_target_pairs={{0,4},{1,5},{2,6},{3,7},{4,0},{5,1},{6,2},{7,3},{8,12},{9,13},{10,... | collective-permute-start | bytes 1769480 | tf_op jit(solution)/shard_map/ppermute | solution.py:588
  30.1 30.2 %all-to-all-start = ((bf16[32,2,156]{2,1,0:T(2,128)(2,1)}), bf16[32,2,156]{2,1,0:T(2,128)(2,1)S(1)}, u32[]{:S(2)}, u32[]{:S(2)}) async-start(bf16[32,2,156]{2,1,0:T(2,128)(2,1)} %reshape.151), calls=%async_computation | async-start | bytes 65536 | tf_op jit(solution)/shard_map/all_to_all | solution.py:886
  40.2 13.8 %collective-permute-start.5 = (bf16[2,4,24,768]{3,2,1,0:T(8,128)(2,1)S(1)}, bf16[2,4,24,768]{3,2,1,0:T(8,128)(2,1)S(1)}, u32[]{:S(2)}, u32[]{:S(2)}) collective-permute-start(bf16[2,4,24,768]{3,2,1,0:T(8,128)(2,1)S(1)} %slice.33), channel_id=1, source_target_pairs={{0,4},{1,5},{2,6},{3,7},{4,0},{5,1},{6,2},{7,3},{8,12},{9,13},{10,... | collective-permute-start | bytes 884744 | tf_op jit(solution)/shard_map/ppermute | solution.py:588
  42.0 16.0 %collective-permute-start.6 = (bf16[2,4,24,768]{3,2,1,0:T(8,128)(2,1)S(1)}, bf16[2,4,24,768]{3,2,1,0:T(8,128)(2,1)}, u32[]{:S(2)}, u32[]{:S(2)}) collective-permute-start(bf16[2,4,24,768]{3,2,1,0:T(8,128)(2,1)S(1)} %slice.34), channel_id=1, source_target_pairs={{0,2},{1,3},{2,0},{3,1},{4,6},{5,7},{6,4},{7,5},{8,10},{9,11},{10,... | collective-permute-start | bytes 884744 | tf_op jit(solution)/shard_map/ppermute | solution.py:584
  43.6 17.9 %collective-permute-start.7 = (bf16[4,4,24,768]{3,2,1,0:T(8,128)(2,1)S(1)}, bf16[4,4,24,768]{3,2,1,0:T(8,128)(2,1)S(1)}, u32[]{:S(2)}, u32[]{:S(2)}) collective-permute-start(bf16[4,4,24,768]{3,2,1,0:T(8,128)(2,1)S(1)} %pad_maximum_fusion.refs_0_), channel_id=1, source_target_pairs={{0,1},{1,0},{2,3},{3,2},{4,5},{5,4},{6,7},{7,6},{8,9},{9,8},{10,11... | collective-permute-start | bytes 1769480 | tf_op jit(solution)/shard_map/ppermute | solution.py:580
  43.6 17.9 %collective-permute-start.8 = (bf16[4,4,24,768]{3,2,1,0:T(8,128)(2,1)S(1)}, bf16[4,4,24,768]{3,2,1,0:T(8,128)(2,1)}, u32[]{:S(2)}, u32[]{:S(2)}) collective-permute-start(bf16[4,4,24,768]{3,2,1,0:T(8,128)(2,1)S(1)} %collective-permute-done.3.refs_1_), channel_id=1, source_target_pairs={{0,1},{1,0},{2,3},{3,2},{4,5},{5,4},{6,7},{7,6},{8,9},{9,8},{10,11... | collective-permute-start | bytes 1769480 | tf_op jit(solution)/shard_map/ppermute | solution.py:580
  44.1 17.4 %collective-permute-start.9 = (bf16[4,4,24,768]{3,2,1,0:T(8,128)(2,1)S(1)}, bf16[4,4,24,768]{3,2,1,0:T(8,128)(2,1)}, u32[]{:S(2)}, u32[]{:S(2)}) collective-permute-start(bf16[4,4,24,768]{3,2,1,0:T(8,128)(2,1)S(1)} %collective-permute-done.4.refs_2_), channel_id=1, source_target_pairs={{0,1},{1,0},{2,3},{3,2},{4,5},{5,4},{6,7},{7,6},{8,9},{9,8},{10,11... | collective-permute-start | bytes 1769480 | tf_op jit(solution)/shard_map/ppermute | solution.py:580
  102.7 14.0 %collective-permute-start.12 = (bf16[3,1024,768]{2,1,0:T(8,128)(2,1)}, bf16[3,1024,768]{2,1,0:T(8,128)(2,1)}, u32[]{:S(2)}, u32[]{:S(2)}) collective-permute-start(bf16[3,1024,768]{2,1,0:T(8,128)(2,1)} %get-tuple-element.77.a2_ref.dy_ref.refs_0_.refs_1_.refs_7_), channel_id=1, source_target_pairs={{0,1},{1,0},{2,3},{3,2},{4,5},{5,4},{6,7},{7,6},{8,9},{9,8},{10,11... | collective-permute-start | bytes 14155784 | tf_op jit(solution)/shard_map/ppermute | solution.py:580
  103.3 26.6 %collective-permute-start.14 = (bf16[4,1024,768]{2,1,0:T(8,128)(2,1)}, bf16[4,1024,768]{2,1,0:T(8,128)(2,1)}, u32[]{:S(2)}, u32[]{:S(2)}) collective-permute-start(bf16[4,1024,768]{2,1,0:T(8,128)(2,1)} %get-tuple-element.76.refs_3_.refs_5_.refs_2_.refs_1_), channel_id=1, source_target_pairs={{0,1},{1,0},{2,3},{3,2},{4,5},{5,4},{6,7},{7,6},{8,9},{9,8},{10,11... | collective-permute-start | bytes 18874376 | tf_op jit(solution)/shard_map/ppermute | solution.py:580
  116.3 27.1 %collective-permute-start.17 = (bf16[4,1024,768]{2,1,0:T(8,128)(2,1)}, bf16[4,1024,768]{2,1,0:T(8,128)(2,1)}, u32[]{:S(2)}, u32[]{:S(2)}) collective-permute-start(bf16[4,1024,768]{2,1,0:T(8,128)(2,1)} %bitcast.52), channel_id=1, source_target_pairs={{0,1},{1,0},{2,3},{3,2},{4,5},{5,4},{6,7},{7,6},{8,9},{9,8},{10,11... | collective-permute-start | bytes 18874376 | tf_op jit(solution)/shard_map/ppermute | solution.py:580
  129.8 35.1 %collective-permute-start.13 = (bf16[4,1024,768]{2,1,0:T(8,128)(2,1)}, bf16[4,1024,768]{2,1,0:T(8,128)(2,1)}, u32[]{:S(2)}, u32[]{:S(2)}) collective-permute-start(bf16[4,1024,768]{2,1,0:T(8,128)(2,1)} %bitcast.46), channel_id=1, source_target_pairs={{0,1},{1,0},{2,3},{3,2},{4,5},{5,4},{6,7},{7,6},{8,9},{9,8},{10,11... | collective-permute-start | bytes 18874376 | tf_op jit(solution)/shard_map/ppermute | solution.py:580
  141.3 16.0 %collective-permute-start.15 = (bf16[4,2,2,2,24,384]{5,4,3,2,1,0:T(8,128)(2,1)}, bf16[4,2,2,2,24,384]{5,4,3,2,1,0:T(8,128)(2,1)}, u32[]{:S(2)}, u32[]{:S(2)}) collective-permute-start(bf16[4,2,2,2,24,384]{5,4,3,2,1,0:T(8,128)(2,1)} %get-tuple-element.82), channel_id=1, source_target_pairs={{0,2},{1,3},{2,0},{3,1},{4,6},{5,7},{6,4},{7,5},{8,10},{9,11},{10,... | collective-permute-start | bytes 1769480 | tf_op jit(solution)/shard_map/ppermute | solution.py:584
  142.2 15.5 %collective-permute-start.16 = (bf16[4,2,2,2,24,384]{5,4,3,2,1,0:T(8,128)(2,1)}, bf16[4,2,2,2,24,384]{5,4,3,2,1,0:T(8,128)(2,1)}, u32[]{:S(2)}, u32[]{:S(2)}) collective-permute-start(bf16[4,2,2,2,24,384]{5,4,3,2,1,0:T(8,128)(2,1)} %get-tuple-element.84), channel_id=1, source_target_pairs={{0,4},{1,5},{2,6},{3,7},{4,0},{5,1},{6,2},{7,3},{8,12},{9,13},{10,... | collective-permute-start | bytes 1769480 | tf_op jit(solution)/shard_map/ppermute | solution.py:588
  160.8 16.6 %collective-permute-start.20 = (bf16[4,2,2,24,384]{4,3,2,1,0:T(8,128)(2,1)}, bf16[4,2,2,24,384]{4,3,2,1,0:T(8,128)(2,1)}, u32[]{:S(2)}, u32[]{:S(2)}) collective-permute-start(bf16[4,2,2,24,384]{4,3,2,1,0:T(8,128)(2,1)} %get-tuple-element.91), channel_id=1, source_target_pairs={{0,4},{1,5},{2,6},{3,7},{4,0},{5,1},{6,2},{7,3},{8,12},{9,13},{10,... | collective-permute-start | bytes 884744 | tf_op jit(solution)/shard_map/ppermute | solution.py:588
  162.3 15.9 %collective-permute-start.21 = (bf16[4,2,2,24,384]{4,3,2,1,0:T(8,128)(2,1)}, bf16[4,2,2,24,384]{4,3,2,1,0:T(8,128)(2,1)}, u32[]{:S(2)}, u32[]{:S(2)}) collective-permute-start(bf16[4,2,2,24,384]{4,3,2,1,0:T(8,128)(2,1)} %get-tuple-element.93), channel_id=1, source_target_pairs={{0,2},{1,3},{2,0},{3,1},{4,6},{5,7},{6,4},{7,5},{8,10},{9,11},{10,... | collective-permute-start | bytes 884744 | tf_op jit(solution)/shard_map/ppermute | solution.py:584
  162.9 22.3 %collective-permute-start.22 = (bf16[4,2,2,2,24,384]{5,4,3,2,1,0:T(8,128)(2,1)}, bf16[4,2,2,2,24,384]{5,4,3,2,1,0:T(8,128)(2,1)}, u32[]{:S(2)}, u32[]{:S(2)}) collective-permute-start(bf16[4,2,2,2,24,384]{5,4,3,2,1,0:T(8,128)(2,1)} %get-tuple-element.94), channel_id=1, source_target_pairs={{0,2},{1,3},{2,0},{3,1},{4,6},{5,7},{6,4},{7,5},{8,10},{9,11},{10,... | collective-permute-start | bytes 1769480 | tf_op jit(solution)/shard_map/ppermute | solution.py:584
  164.3 20.9 %collective-permute-start.23 = (bf16[4,2,2,2,24,384]{5,4,3,2,1,0:T(8,128)(2,1)}, bf16[4,2,2,2,24,384]{5,4,3,2,1,0:T(8,128)(2,1)}, u32[]{:S(2)}, u32[]{:S(2)}) collective-permute-start(bf16[4,2,2,2,24,384]{5,4,3,2,1,0:T(8,128)(2,1)} %get-tuple-element.96), channel_id=1, source_target_pairs={{0,4},{1,5},{2,6},{3,7},{4,0},{5,1},{6,2},{7,3},{8,12},{9,13},{10,... | collective-permute-start | bytes 1769480 | tf_op jit(solution)/shard_map/ppermute | solution.py:588
  176.1 24.0 %collective-permute-start.18 = (bf16[4,2,2,2,24,384]{5,4,3,2,1,0:T(8,128)(2,1)}, bf16[4,2,2,2,24,384]{5,4,3,2,1,0:T(8,128)(2,1)}, u32[]{:S(2)}, u32[]{:S(2)}) collective-permute-start(bf16[4,2,2,2,24,384]{5,4,3,2,1,0:T(8,128)(2,1)} %get-tuple-element.88), channel_id=1, source_target_pairs={{0,2},{1,3},{2,0},{3,1},{4,6},{5,7},{6,4},{7,5},{8,10},{9,11},{10,... | collective-permute-start | bytes 1769480 | tf_op jit(solution)/shard_map/ppermute | solution.py:584
  177.5 22.6 %collective-permute-start.19 = (bf16[4,2,2,2,24,384]{5,4,3,2,1,0:T(8,128)(2,1)}, bf16[4,2,2,2,24,384]{5,4,3,2,1,0:T(8,128)(2,1)}, u32[]{:S(2)}, u32[]{:S(2)}) collective-permute-start(bf16[4,2,2,2,24,384]{5,4,3,2,1,0:T(8,128)(2,1)} %get-tuple-element.90), channel_id=1, source_target_pairs={{0,4},{1,5},{2,6},{3,7},{4,0},{5,1},{6,2},{7,3},{8,12},{9,13},{10,... | collective-permute-start | bytes 1769480 | tf_op jit(solution)/shard_map/ppermute | solution.py:588
  188.9 13.2 %collective-permute-start.25 = (bf16[4,2,2,24,384]{4,3,2,1,0:T(8,128)(2,1)}, bf16[4,2,2,24,384]{4,3,2,1,0:T(8,128)(2,1)}, u32[]{:S(2)}, u32[]{:S(2)}) collective-permute-start(bf16[4,2,2,24,384]{4,3,2,1,0:T(8,128)(2,1)} %get-tuple-element.100), channel_id=1, source_target_pairs={{0,2},{1,3},{2,0},{3,1},{4,6},{5,7},{6,4},{7,5},{8,10},{9,11},{10,... | collective-permute-start | bytes 884744 | tf_op jit(solution)/shard_map/ppermute | solution.py:584
  208.2 23.5 %collective-permute-start.31 = (bf16[4,2,2,24,384]{4,3,2,1,0:T(8,128)(2,1)}, bf16[4,2,2,24,384]{4,3,2,1,0:T(8,128)(2,1)}, u32[]{:S(2)}, u32[]{:S(2)}) collective-permute-start(bf16[4,2,2,24,384]{4,3,2,1,0:T(8,128)(2,1)} %get-tuple-element.109), channel_id=1, source_target_pairs={{0,2},{1,3},{2,0},{3,1},{4,6},{5,7},{6,4},{7,5},{8,10},{9,11},{10,... | collective-permute-start | bytes 884744 | tf_op jit(solution)/shard_map/ppermute | solution.py:584
  209.6 27.7 %collective-permute-start.26 = (bf16[8,24,768]{2,1,0:T(8,128)(2,1)}, bf16[8,24,768]{2,1,0:T(8,128)(2,1)}, u32[]{:S(2)}, u32[]{:S(2)}) collective-permute-start(bf16[8,24,768]{2,1,0:T(8,128)(2,1)} %bitcast.82), channel_id=1, source_target_pairs={{0,0},{1,16},{2,2},{3,18},{4,4},{5,20},{6,6},{7,22},{8,1},{9,17},{... | collective-permute-start | bytes 884744 | tf_op jit(solution)/shard_map/ppermute | solution.py:689
  213.3 26.0 %collective-permute-start.27 = (bf16[8,24,768]{2,1,0:T(8,128)(2,1)}, bf16[8,24,768]{2,1,0:T(8,128)(2,1)}, u32[]{:S(2)}, u32[]{:S(2)}) collective-permute-start(bf16[8,24,768]{2,1,0:T(8,128)(2,1)} %bitcast.81), channel_id=1, source_target_pairs={{0,1},{1,17},{2,3},{3,19},{4,5},{5,21},{6,7},{7,23},{8,0},{9,16},{... | collective-permute-start | bytes 884744 | tf_op jit(solution)/shard_map/ppermute | solution.py:689
  218.4 21.3 %collective-permute-start.28 = (bf16[8,24,768]{2,1,0:T(8,128)(2,1)}, bf16[8,24,768]{2,1,0:T(8,128)(2,1)}, u32[]{:S(2)}, u32[]{:S(2)}) collective-permute-start(bf16[8,24,768]{2,1,0:T(8,128)(2,1)} %bitcast.80), channel_id=1, source_target_pairs={{0,8},{1,24},{2,10},{3,26},{4,12},{5,28},{6,14},{7,30},{8,9},{9,25... | collective-permute-start | bytes 884744 | tf_op jit(solution)/shard_map/ppermute | solution.py:689
  218.4 27.5 %collective-permute-start.29 = (bf16[8,24,768]{2,1,0:T(8,128)(2,1)}, bf16[8,24,768]{2,1,0:T(8,128)(2,1)}, u32[]{:S(2)}, u32[]{:S(2)}) collective-permute-start(bf16[8,24,768]{2,1,0:T(8,128)(2,1)} %bitcast.79), channel_id=1, source_target_pairs={{0,9},{1,25},{2,11},{3,27},{4,13},{5,29},{6,15},{7,31},{8,8},{9,24... | collective-permute-start | bytes 884744 | tf_op jit(solution)/shard_map/ppermute | solution.py:689
  239.4 14.6 %collective-permute-start.34 = (bf16[4,24,768]{2,1,0:T(8,128)(2,1)}, bf16[4,24,768]{2,1,0:T(8,128)(2,1)}, u32[]{:S(2)}, u32[]{:S(2)}) collective-permute-start(bf16[4,24,768]{2,1,0:T(8,128)(2,1)} %bitcast.84), channel_id=1, source_target_pairs={{0,8},{1,24},{2,10},{3,26},{4,12},{5,28},{6,14},{7,30},{8,9},{9,25... | collective-permute-start | bytes 442376 | tf_op jit(solution)/shard_map/ppermute | solution.py:689
  239.7 14.3 %collective-permute-start.35 = (bf16[4,24,768]{2,1,0:T(8,128)(2,1)}, bf16[4,24,768]{2,1,0:T(8,128)(2,1)}, u32[]{:S(2)}, u32[]{:S(2)}) collective-permute-start(bf16[4,24,768]{2,1,0:T(8,128)(2,1)} %bitcast.83), channel_id=1, source_target_pairs={{0,9},{1,25},{2,11},{3,27},{4,13},{5,29},{6,15},{7,31},{8,8},{9,24... | collective-permute-start | bytes 442376 | tf_op jit(solution)/shard_map/ppermute | solution.py:689
  257.7 38.6 %all-to-all-start.1 = ((bf16[32,24,768]{2,1,0:T(8,128)(2,1)}), bf16[32,24,768]{2,1,0:T(8,128)(2,1)}, u32[]{:S(2)}, u32[]{:S(2)}) async-start(bf16[32,24,768]{2,1,0:T(8,128)(2,1)} %get-tuple-element.122), calls=%async_computation.1 | async-start | bytes 2359296 | tf_op jit(solution)/shard_map/all_to_all | solution.py:886
  278.0 18.2 %collective-permute-start.41 = (f32[16,768]{1,0:T(8,128)}, f32[16,768]{1,0:T(8,128)}, u32[]{:S(2)}, u32[]{:S(2)}) collective-permute-start(f32[16,768]{1,0:T(8,128)} %add_add_fusion.1.refs_0_), channel_id=1, source_target_pairs={{0,16},{1,17},{2,18},{3,19},{4,20},{5,21},{6,22},{7,23},{8,24},{9,... | collective-permute-start | bytes 147464 | tf_op jit(solution)/shard_map/ppermute | solution.py:698
  302.0 32.6 %all-to-all-start.2 = ((bf16[32,24,768]{2,1,0:T(8,128)(2,1)}), bf16[32,24,768]{2,1,0:T(8,128)(2,1)}, u32[]{:S(2)}, u32[]{:S(2)}) async-start(bf16[32,24,768]{2,1,0:T(8,128)(2,1)} %bitcast.68), calls=%async_computation.2 | async-start | bytes 2359296 | tf_op jit(solution)/shard_map/all_to_all | solution.py:886
  (35 other events, 445.5 us)
Sparse Core Ops, SparseCore 0:
  11.0 91.7 all-gather.1

commit v11 on v10

--- a/solution.py
+++ b/solution.py
@@ -949,8 +949,8 @@
         part, one_sums = grad_one(flat_tokens, dy, (og, 0, 3), attn_weights, vecs, after=(low.made,))
         terms = [advance(place, [high], [attn, low], after=(part,))]
         es, dus = [(v, 0, half) for v in (ed0, ed1)], [(v, half, half) for v in (ed0, ed1)]
+        terms.append(advance(place, [], [high]))
         grad_in, two_sums = grad_two(flat_tokens, part, dus, mlp_weights, vecs, after=(high.made,))
-        terms.append(advance(place, [], [high], after=(grad_in,)))
         orders = [orders[0] + orders[1], orders[2]]
     else:
         ed0, up_sum0 = hidden(0, acts, mlp_weights, vecs)

time: 347 us -> 350 us (level)
  waiting for transfers between devices: 63.6 us -> 69.5 us
    ppermute x8, waiting for transfers between devices: 8.38 us -> 14.8 us  [advance(): lax.ppermute(v, AXES, to_place(lambda z, y, x, c, m=m: (2 * c + ((z ^ m)...]
  transfers between devices with their start and end apart: 47 -> 47, of which waited for: 17 -> 15; matrix products, arithmetic and copies ran while one was open for 5% -> 5% of each run, Pallas kernels for 44% -> 43%
where the time goes in v11:
time: 350 us; the launch traced here: 348 us
  Pallas kernels  168 us (48%)
  starting transfers between devices  73.5 us (21%)
  waiting for transfers between devices  69.5 us (20%)
  between operations  17.8 us (5%)
  other arithmetic  12.9 us (4%)
  local copies, waits for them, and re-layouts  6.62 us (2%)
    pallas_call x19, Pallas kernels, call(): return lambda *operands: made(*operands, *after)  168 us
    ppermute x9, waiting for transfers between devices, over_x(): lax.ppermute(value, AXES, to_place(lambda z, y, x, c: (z, y, 1 - x, c)))  21 us
    all_to_all x3, starting transfers between devices, to_all(): return lax.all_to_all(value, AXES, split_axis=0, concat_axis=0, tiled=True)  19.1 us
    ppermute x8, starting transfers between devices, advance(): lax.ppermute(v, AXES, to_place(lambda z, y, x, c, m=m: (2 * c + ((z ^ m)...  17.9 us
    ppermute x8, waiting for transfers between devices, advance(): lax.ppermute(v, AXES, to_place(lambda z, y, x, c, m=m: (2 * c + ((z ^ m)...  14.8 us
    ppermute x9, starting transfers between devices, over_x(): lax.ppermute(value, AXES, to_place(lambda z, y, x, c: (z, y, 1 - x, c)))  11.9 us
    ppermute x4, waiting for transfers between devices, get(): return lax.ppermute(value, AXES, to_place(move))  10.7 us
    ppermute x9, starting transfers between devices, over_y(): lax.ppermute(value, AXES, to_place(lambda z, y, x, c: (z, 1 - y, x, c)))  9.98 us
  transfers between devices with their start and end apart: 47, of which 15 were waited for; matrix products, arithmetic and copies ran while one was open for 5% of the time, Pallas kernels for 43%

profile of v11, /device:TPU:0, one launch (start us, length us, event | category | flops | bytes accessed | tf_op | source)
XLA Modules:
  0.0 348.0 jit_solution(5598006757705563656)
XLA Ops:
  9.3 4.1 %collective-permute-start.1 = (bf16[4,24,768]{2,1,0:T(8,128)(2,1)S(1)}, bf16[4,24,768]{2,1,0:T(8,128)(2,1)S(1)}, u32[]{:S(2)}, u32[]{:S(2)}) collective-permute-start(bf16[4,24,768]{2,1,0:T(8,128)(2,1)S(1)} %get-tuple-element.135), channel_id=1, source_target_pairs={{0,16},{1,17},{2,18},{3,19},{4,20},{5,21},{6,22},{7,23},{8,24},{9,... | collective-permute-start | bytes 442376 | tf_op jit(solution)/shard_map/ppermute | solution.py:592
  15.4 6.6 %collective-permute-done.1 = bf16[4,24,768]{2,1,0:T(8,128)(2,1)S(1)} collective-permute-done((bf16[4,24,768]{2,1,0:T(8,128)(2,1)S(1)}, bf16[4,24,768]{2,1,0:T(8,128)(2,1)S(1)}, u32[]{:S(2)}, u32[]{:S(2)}) %collective-permute-start.1) | collective-permute-done | bytes 147488 | tf_op jit(solution)/shard_map/ppermute | solution.py:592
  30.1 9.6 %all-to-all-start = ((bf16[32,2,156]{2,1,0:T(2,128)(2,1)}), bf16[32,2,156]{2,1,0:T(2,128)(2,1)S(1)}, u32[]{:S(2)}, u32[]{:S(2)}) async-start(bf16[32,2,156]{2,1,0:T(2,128)(2,1)} %reshape.151), calls=%async_computation | async-start | bytes 65536 | tf_op jit(solution)/shard_map/all_to_all | solution.py:886
  44.2 3.2 fusion
  47.4 6.6 %collective-permute-done.5.refs_3_ = bf16[2,4,24,768]{3,2,1,0:T(8,128)(2,1)S(1)} collective-permute-done((bf16[2,4,24,768]{3,2,1,0:T(8,128)(2,1)S(1)}, bf16[2,4,24,768]{3,2,1,0:T(8,128)(2,1)S(1)}, u32[]{:S(2)}, u32[]{:S(2)}) %collective-permute-start.5) | collective-permute-done | bytes 294944 | tf_op jit(solution)/shard_map/ppermute | solution.py:588
  54.1 3.9 %collective-permute-done.6.refs_4_ = bf16[2,4,24,768]{3,2,1,0:T(8,128)(2,1)} collective-permute-done((bf16[2,4,24,768]{3,2,1,0:T(8,128)(2,1)S(1)}, bf16[2,4,24,768]{3,2,1,0:T(8,128)(2,1)}, u32[]{:S(2)}, u32[]{:S(2)}) %collective-permute-start.6) | collective-permute-done | bytes 294944 | tf_op jit(solution)/shard_map/ppermute | solution.py:584
  63.1 14.2 %shard_map.229 = (bf16[1024,768]{1,0:T(8,128)(2,1)}, bf16[1024,768]{1,0:T(8,128)(2,1)}, bf16[1024,768]{1,0:T(8,128)(2,1)}, bf16[1024,768]{1,0:T(8,128)(2,1)}, bf...) custom-call(s32[4]{0:T(128)} %pad_add_fusion.place_ref.refs_0_, bf16[1024,768]{1,0:T(8,128)(2,1)} %bitcast.58, ...), custom_call_target="tpu_custom_call" | custom-call | flops 4831838208 | bytes 25165824 | tf_op jit(solution)/shard_map/pallas_call | solution.py:75
  77.3 25.5 %shard_map.230 = (bf16[4,1024,768]{2,1,0:T(8,128)(2,1)}, f32[3,16,768]{2,1,0:T(8,128)}, bf16[3,1024,768]{2,1,0:T(8,128)(2,1)}) custom-call(bf16[3,1024,768]{2,1,0:T(8,128)(2,1)} %get-tuple-element.71.acts_ref, s32[1024,1]{1,0:T(8,128)} %bitcast.69, s32[2,1,512]{2,1,0:T(1,128)} %broadcast_in_dim.44.row_ref, ...), custom_call_target="tpu_custom_call", output_to_operand_aliasing={{2}: (0, {})} | custom-call | flops 9663676416 | bytes 18874368 | tf_op jit(solution)/shard_map/pallas_call | solution.py:75
  103.3 13.0 %shard_map.231 = (bf16[2,2,1024,768]{3,2,1,0:T(8,128)(2,1)}, f32[2,8,768]{2,1,0:T(8,128)}) custom-call(bf16[3,1024,768]{2,1,0:T(8,128)(2,1)} %get-tuple-element.77.a2_ref.dy_ref.refs_0_.refs_1_.refs_7_, bf16[3,1024,768]{2,1,0:T(8,128)(2,1)} %get-tuple-element.77.a2_ref.dy_ref.refs_0_.refs_1_.refs_7_, ...), custom_call_target="tpu_custom_call" | custom-call | flops 4831838208 | bytes 17301504 | tf_op jit(solution)/shard_map/pallas_call | solution.py:75
  116.7 13.1 %shard_map.232 = (bf16[2,2,1024,768]{3,2,1,0:T(8,128)(2,1)}, f32[2,8,768]{2,1,0:T(8,128)}) custom-call(bf16[3,1024,768]{2,1,0:T(8,128)(2,1)} %get-tuple-element.77.a2_ref.dy_ref.refs_0_.refs_1_.refs_7_, bf16[3,1024,768]{2,1,0:T(8,128)(2,1)} %get-tuple-element.77.a2_ref.dy_ref.refs_0_.refs_1_.refs_7_, ...), custom_call_target="tpu_custom_call" | custom-call | flops 4831838208 | bytes 17301504 | tf_op jit(solution)/shard_map/pallas_call | solution.py:75
  129.9 11.4 %shard_map.233 = (bf16[4,2,2,2,24,384]{5,4,3,2,1,0:T(8,128)(2,1)}, bf16[4,2,2,2,24,384]{5,4,3,2,1,0:T(8,128)(2,1)}, bf16[4,2,2,2,24,384]{5,4,3,2,1,0:T(8,128)(2,1)}, bf16[4,2,2,2,24,384]{5,4,3,2,1,0:T(8,128)(2,1)}) custom-call(s32[4]{0:T(128)} %pad_add_fusion.place_ref.refs_0_, bf16[3,1024,768]{2,1,0:T(8,128)(2,1)} %get-tuple-element.77.a2_ref.dy_ref.refs_0_.refs_1_.refs_7_, ...), custom_call_target="tpu_custom_call" | custom-call | flops 4831838208 | bytes 12582912 | tf_op jit(solution)/shard_map/pallas_call | solution.py:75
  143.4 11.2 %shard_map.234 = (bf16[4,2,2,2,24,384]{5,4,3,2,1,0:T(8,128)(2,1)}, bf16[4,2,2,2,24,384]{5,4,3,2,1,0:T(8,128)(2,1)}, bf16[4,2,2,2,24,384]{5,4,3,2,1,0:T(8,128)(2,1)}, bf16[4,2,2,2,24,384]{5,4,3,2,1,0:T(8,128)(2,1)}) custom-call(s32[4]{0:T(128)} %pad_add_fusion.place_ref.refs_0_, bf16[3,1024,768]{2,1,0:T(8,128)(2,1)} %get-tuple-element.77.a2_ref.dy_ref.refs_0_.refs_1_.refs_7_, ...), custom_call_target="tpu_custom_call" | custom-call | flops 4831838208 | bytes 12582912 | tf_op jit(solution)/shard_map/pallas_call | solution.py:75
  164.9 11.2 %shard_map.236 = (bf16[4,2,2,2,24,384]{5,4,3,2,1,0:T(8,128)(2,1)}, bf16[4,2,2,2,24,384]{5,4,3,2,1,0:T(8,128)(2,1)}, bf16[4,2,2,2,24,384]{5,4,3,2,1,0:T(8,128)(2,1)}, bf16[4,2,2,2,24,384]{5,4,3,2,1,0:T(8,128)(2,1)}) custom-call(s32[4]{0:T(128)} %pad_add_fusion.place_ref.refs_0_, bf16[3,1024,768]{2,1,0:T(8,128)(2,1)} %get-tuple-element.77.a2_ref.dy_ref.refs_0_.refs_1_.refs_7_, ...), custom_call_target="tpu_custom_call" | custom-call | flops 4831838208 | bytes 12582912 | tf_op jit(solution)/shard_map/pallas_call | solution.py:75
  178.7 6.5 %collective-permute-done.22.refs_2_ = bf16[4,2,2,2,24,384]{5,4,3,2,1,0:T(8,128)(2,1)} collective-permute-done((bf16[4,2,2,2,24,384]{5,4,3,2,1,0:T(8,128)(2,1)}, bf16[4,2,2,2,24,384]{5,4,3,2,1,0:T(8,128)(2,1)}, u32[]{:S(2)}, u32[]{:S(2)}) %collective-permute-start.22) | collective-permute-done | bytes 589856 | tf_op jit(solution)/shard_map/ppermute | solution.py:584
  190.3 9.8 %shard_map.238 = (f32[1024,768]{1,0:T(8,128)}, f32[3,8,768]{2,1,0:T(8,128)}) custom-call(bf16[1024,768]{1,0:T(8,128)(2,1)} %bitcast.59, bf16[1024,768]{1,0:T(8,128)(2,1)} %bitcast.67, bf16[4,1024,768]{2,1,0:T(8,128)(2,1)} %get-tuple-element.76.refs_3_.refs_5_.refs_2_.refs_1_, bf16[4,768,768]{2,1,0:T(8,128)(2,1)} %get-tuple-element.80.refs_3_.refs_4_, ...), custom_call_target="tpu_custom_call" | custom-call | flops 3623878656 | bytes 14548992 | tf_op jit(solution)/shard_map/pallas_call | solution.py:75
  202.1 4.1 %shard_map.239 = (bf16[4,2,2,24,384]{4,3,2,1,0:T(8,128)(2,1)}, bf16[4,2,2,24,384]{4,3,2,1,0:T(8,128)(2,1)}, bf16[4,2,2,24,384]{4,3,2,1,0:T(8,128)(2,1)}, bf16[4,...) custom-call(s32[4]{0:T(128)} %pad_add_fusion.place_ref.refs_0_, ...), custom_call_target="tpu_custom_call" | custom-call | bytes 9437184 | tf_op jit(solution)/shard_map/pallas_call | solution.py:75
  208.3 3.8 %collective-permute-start.26 = (bf16[8,24,768]{2,1,0:T(8,128)(2,1)}, bf16[8,24,768]{2,1,0:T(8,128)(2,1)}, u32[]{:S(2)}, u32[]{:S(2)}) collective-permute-start(bf16[8,24,768]{2,1,0:T(8,128)(2,1)} %bitcast.83), channel_id=1, source_target_pairs={{0,0},{1,16},{2,2},{3,18},{4,4},{5,20},{6,6},{7,22},{8,1},{9,17},{... | collective-permute-start | bytes 884744 | tf_op jit(solution)/shard_map/ppermute | solution.py:689
  212.1 5.0 %collective-permute-start.27 = (bf16[8,24,768]{2,1,0:T(8,128)(2,1)}, bf16[8,24,768]{2,1,0:T(8,128)(2,1)}, u32[]{:S(2)}, u32[]{:S(2)}) collective-permute-start(bf16[8,24,768]{2,1,0:T(8,128)(2,1)} %bitcast.82), channel_id=1, source_target_pairs={{0,1},{1,17},{2,3},{3,19},{4,5},{5,21},{6,7},{7,23},{8,0},{9,16},{... | collective-permute-start | bytes 884744 | tf_op jit(solution)/shard_map/ppermute | solution.py:689
  228.4 14.8 %collective-permute-done.28.refs_3_ = bf16[8,24,768]{2,1,0:T(8,128)(2,1)} collective-permute-done((bf16[8,24,768]{2,1,0:T(8,128)(2,1)}, bf16[8,24,768]{2,1,0:T(8,128)(2,1)}, u32[]{:S(2)}, u32[]{:S(2)}) %collective-permute-start.28) | collective-permute-done | bytes 294944 | tf_op jit(solution)/shard_map/ppermute | solution.py:689
  245.1 11.0 %shard_map.241 = (bf16[1024,768]{1,0:T(8,128)(2,1)}, f32[2,8,768]{2,1,0:T(8,128)}) custom-call(bf16[1024,768]{1,0:T(8,128)(2,1)} %bitcast.60, f32[1024,768]{1,0:T(8,128)} %get-tuple-element.101.refs_13_.refs_1_, bf16[4,1024,768]{2,1,0:T(8,128)(2,1)} %bitcast.56, bf16[4,1024,768]{2,1,0:T(8,128)(2,1)} %bitcast.50, ...), custom_call_target="tpu_custom_call" | custom-call | flops 4831838208 | bytes 17301504 | tf_op jit(solution)/shard_map/pallas_call | solution.py:75
  256.1 3.7 %shard_map.242 = (f32[12,24,768]{2,1,0:T(8,128)}, bf16[32,24,768]{2,1,0:T(8,128)(2,1)}, f32[24,768]{1,0:T(8,128)}) custom-call(s32[32]{0:T(128)} %broadcast_add_fusion.refs_0_, bf16[8,24,768]{2,1,0:T(8,128)(2,1)} %collective-permute-done.26.refs_1_, bf16[8,24,768]{2,1,0:T(8,128)(2,1)} %collective-permute-done.27.refs_2_, ...), custom_call_target="tpu_custom_call" | custom-call | bytes 3538944 | tf_op jit(solution)/shard_map/pallas_call | solution.py:75
  259.9 6.0 %all-to-all-start.1 = ((bf16[32,24,768]{2,1,0:T(8,128)(2,1)}), bf16[32,24,768]{2,1,0:T(8,128)(2,1)}, u32[]{:S(2)}, u32[]{:S(2)}) async-start(bf16[32,24,768]{2,1,0:T(8,128)(2,1)} %get-tuple-element.122), calls=%async_computation.1 | async-start | bytes 2359296 | tf_op jit(solution)/shard_map/all_to_all | solution.py:886
  271.0 6.7 %collective-permute-done.37 = f32[16,768]{1,0:T(8,128)S(1)} collective-permute-done((f32[16,768]{1,0:T(8,128)S(1)}, f32[16,768]{1,0:T(8,128)S(1)}, u32[]{:S(2)}, u32[]{:S(2)}) %collective-permute-start.37) | collective-permute-done | bytes 49184 | tf_op jit(solution)/shard_map/ppermute | solution.py:584
  280.3 5.7 %collective-permute-start.41 = (f32[16,768]{1,0:T(8,128)}, f32[16,768]{1,0:T(8,128)}, u32[]{:S(2)}, u32[]{:S(2)}) collective-permute-start(f32[16,768]{1,0:T(8,128)} %add_add_fusion.1.refs_0_), channel_id=1, source_target_pairs={{0,16},{1,17},{2,18},{3,19},{4,20},{5,21},{6,22},{7,23},{8,24},{9,... | collective-permute-start | bytes 147464 | tf_op jit(solution)/shard_map/ppermute | solution.py:698
  285.9 3.5 shard_map.243
  289.4 9.1 %collective-permute-done.41.refs_2_ = f32[16,768]{1,0:T(8,128)} collective-permute-done((f32[16,768]{1,0:T(8,128)}, f32[16,768]{1,0:T(8,128)}, u32[]{:S(2)}, u32[]{:S(2)}) %collective-permute-start.41) | collective-permute-done | bytes 49184 | tf_op jit(solution)/shard_map/ppermute | solution.py:698
  298.5 5.7 %shard_map.245 = bf16[768,768]{1,0:T(8,128)(2,1)} custom-call(bf16[768,768]{1,0:T(8,128)(2,1)} %bitcast.29.s_ref, bf16[768,768]{1,0:T(8,128)(2,1)} %get-tuple-element.116.refs_7_.l_ref, bf16[768,768]{1,0:T(8,128)(2,1)} %get-tuple-element.123.r_ref, f32[16,768]{1,0:T(8,128)} %add_add_fusion.1.refs_0_, f32[16,768]{1,0:T(8,128)} %collective-permute-done.40.refs_1_, ...), custom_call_target="tpu_custom_call" | custom-call | flops 1811939328 | bytes 4718592 | tf_op jit(solution)/shard_map/pallas_call | solution.py:75
  304.2 3.5 %all-to-all-start.2 = ((bf16[32,24,768]{2,1,0:T(8,128)(2,1)}), bf16[32,24,768]{2,1,0:T(8,128)(2,1)}, u32[]{:S(2)}, u32[]{:S(2)}) async-start(bf16[32,24,768]{2,1,0:T(8,128)(2,1)} %bitcast.68), calls=%async_computation.2 | async-start | bytes 2359296 | tf_op jit(solution)/shard_map/all_to_all | solution.py:886
  313.9 11.0 %shard_map.244 = bf16[1024,768]{1,0:T(8,128)(2,1)} custom-call(bf16[1024,768]{1,0:T(8,128)(2,1)} %bitcast.61, bf16[4,1024,768]{2,1,0:T(8,128)(2,1)} %get-tuple-element.76.refs_3_.refs_5_.refs_2_.refs_1_, bf16[4,1024,768]{2,1,0:T(8,128)(2,1)} %bitcast.57, bf16[4,1024,768]{2,1,0:T(8,128)(2,1)} %bitcast.51, ...), custom_call_target="tpu_custom_call" | custom-call | flops 6039797760 | bytes 16908288 | tf_op jit(solution)/shard_map/pallas_call | solution.py:75
  325.0 7.2 %shard_map.247 = (f32[768,768]{1,0:T(8,128)}, f32[768,768]{1,0:T(8,128)}) custom-call(s32[1]{0:T(128)} %bitcast.31.has_ref, f32[2]{0:T(128)} %pad_maximum_fusion.1.refs_8_.scale_ref, bf16[768,768]{1,0:T(8,128)(2,1)} %bitcast.29.s_ref, f32[768,768]{1,0:T(8,128)} %bitcast.78, f32[768,768]{1,0:T(8,128)} %bitcast.79), custom_call_target="tpu_custom_call" | custom-call | flops 1811939328 | bytes 10616832 | tf_op jit(solution)/shard_map/pallas_call | solution.py:75
  332.1 4.7 %all-to-all-done.2.p_ref = bf16[32,24,768]{2,1,0:T(8,128)(2,1)} async-done(((bf16[32,24,768]{2,1,0:T(8,128)(2,1)}), bf16[32,24,768]{2,1,0:T(8,128)(2,1)}, u32[]{:S(2)}, u32[]{:S(2)}) %all-to-all-start.2) | async-done | bytes 1179680 | tf_op jit(solution)/shard_map/all_to_all | solution.py:886
  336.8 3.3 shard_map.246
  (168 shorter events, 71.8 us)
Async XLA Ops:
  7.2 96.1 %all-gather.2.cloned.1.call-start = ((), (), s32[]{:S(2)}) async-start(), calls=%async_computation.3 | async-start | bytes 9732096 | tf_op jit(solution)/shard_map/all_gather | solution.py:917
  24.9 15.3 %collective-permute-start.3 = (bf16[4,4,24,768]{3,2,1,0:T(8,128)(2,1)S(1)}, bf16[4,4,24,768]{3,2,1,0:T(8,128)(2,1)S(1)}, u32[]{:S(2)}, u32[]{:S(2)}) collective-permute-start(bf16[4,4,24,768]{3,2,1,0:T(8,128)(2,1)S(1)} %pad_maximum_fusion.refs_0_), channel_id=1, source_target_pairs={{0,2},{1,3},{2,0},{3,1},{4,6},{5,7},{6,4},{7,5},{8,10},{9,11},{10,... | collective-permute-start | bytes 1769480 | tf_op jit(solution)/shard_map/ppermute | solution.py:584
  26.4 15.6 %collective-permute-start.4 = (bf16[4,4,24,768]{3,2,1,0:T(8,128)(2,1)S(1)}, bf16[4,4,24,768]{3,2,1,0:T(8,128)(2,1)S(1)}, u32[]{:S(2)}, u32[]{:S(2)}) collective-permute-start(bf16[4,4,24,768]{3,2,1,0:T(8,128)(2,1)S(1)} %pad_maximum_fusion.refs_0_), channel_id=1, source_target_pairs={{0,4},{1,5},{2,6},{3,7},{4,0},{5,1},{6,2},{7,3},{8,12},{9,13},{10,... | collective-permute-start | bytes 1769480 | tf_op jit(solution)/shard_map/ppermute | solution.py:588
  30.1 30.2 %all-to-all-start = ((bf16[32,2,156]{2,1,0:T(2,128)(2,1)}), bf16[32,2,156]{2,1,0:T(2,128)(2,1)S(1)}, u32[]{:S(2)}, u32[]{:S(2)}) async-start(bf16[32,2,156]{2,1,0:T(2,128)(2,1)} %reshape.151), calls=%async_computation | async-start | bytes 65536 | tf_op jit(solution)/shard_map/all_to_all | solution.py:886
  40.2 13.8 %collective-permute-start.5 = (bf16[2,4,24,768]{3,2,1,0:T(8,128)(2,1)S(1)}, bf16[2,4,24,768]{3,2,1,0:T(8,128)(2,1)S(1)}, u32[]{:S(2)}, u32[]{:S(2)}) collective-permute-start(bf16[2,4,24,768]{3,2,1,0:T(8,128)(2,1)S(1)} %slice.33), channel_id=1, source_target_pairs={{0,4},{1,5},{2,6},{3,7},{4,0},{5,1},{6,2},{7,3},{8,12},{9,13},{10,... | collective-permute-start | bytes 884744 | tf_op jit(solution)/shard_map/ppermute | solution.py:588
  42.0 16.0 %collective-permute-start.6 = (bf16[2,4,24,768]{3,2,1,0:T(8,128)(2,1)S(1)}, bf16[2,4,24,768]{3,2,1,0:T(8,128)(2,1)}, u32[]{:S(2)}, u32[]{:S(2)}) collective-permute-start(bf16[2,4,24,768]{3,2,1,0:T(8,128)(2,1)S(1)} %slice.34), channel_id=1, source_target_pairs={{0,2},{1,3},{2,0},{3,1},{4,6},{5,7},{6,4},{7,5},{8,10},{9,11},{10,... | collective-permute-start | bytes 884744 | tf_op jit(solution)/shard_map/ppermute | solution.py:584
  43.6 17.9 %collective-permute-start.7 = (bf16[4,4,24,768]{3,2,1,0:T(8,128)(2,1)S(1)}, bf16[4,4,24,768]{3,2,1,0:T(8,128)(2,1)S(1)}, u32[]{:S(2)}, u32[]{:S(2)}) collective-permute-start(bf16[4,4,24,768]{3,2,1,0:T(8,128)(2,1)S(1)} %pad_maximum_fusion.refs_0_), channel_id=1, source_target_pairs={{0,1},{1,0},{2,3},{3,2},{4,5},{5,4},{6,7},{7,6},{8,9},{9,8},{10,11... | collective-permute-start | bytes 1769480 | tf_op jit(solution)/shard_map/ppermute | solution.py:580
  43.6 17.9 %collective-permute-start.8 = (bf16[4,4,24,768]{3,2,1,0:T(8,128)(2,1)S(1)}, bf16[4,4,24,768]{3,2,1,0:T(8,128)(2,1)}, u32[]{:S(2)}, u32[]{:S(2)}) collective-permute-start(bf16[4,4,24,768]{3,2,1,0:T(8,128)(2,1)S(1)} %collective-permute-done.3.refs_1_), channel_id=1, source_target_pairs={{0,1},{1,0},{2,3},{3,2},{4,5},{5,4},{6,7},{7,6},{8,9},{9,8},{10,11... | collective-permute-start | bytes 1769480 | tf_op jit(solution)/shard_map/ppermute | solution.py:580
  44.1 17.4 %collective-permute-start.9 = (bf16[4,4,24,768]{3,2,1,0:T(8,128)(2,1)S(1)}, bf16[4,4,24,768]{3,2,1,0:T(8,128)(2,1)}, u32[]{:S(2)}, u32[]{:S(2)}) collective-permute-start(bf16[4,4,24,768]{3,2,1,0:T(8,128)(2,1)S(1)} %collective-permute-done.4.refs_2_), channel_id=1, source_target_pairs={{0,1},{1,0},{2,3},{3,2},{4,5},{5,4},{6,7},{7,6},{8,9},{9,8},{10,11... | collective-permute-start | bytes 1769480 | tf_op jit(solution)/shard_map/ppermute | solution.py:580
  102.7 14.0 %collective-permute-start.12 = (bf16[3,1024,768]{2,1,0:T(8,128)(2,1)}, bf16[3,1024,768]{2,1,0:T(8,128)(2,1)}, u32[]{:S(2)}, u32[]{:S(2)}) collective-permute-start(bf16[3,1024,768]{2,1,0:T(8,128)(2,1)} %get-tuple-element.77.a2_ref.dy_ref.refs_0_.refs_1_.refs_7_), channel_id=1, source_target_pairs={{0,1},{1,0},{2,3},{3,2},{4,5},{5,4},{6,7},{7,6},{8,9},{9,8},{10,11... | collective-permute-start | bytes 14155784 | tf_op jit(solution)/shard_map/ppermute | solution.py:580
  103.3 26.6 %collective-permute-start.14 = (bf16[4,1024,768]{2,1,0:T(8,128)(2,1)}, bf16[4,1024,768]{2,1,0:T(8,128)(2,1)}, u32[]{:S(2)}, u32[]{:S(2)}) collective-permute-start(bf16[4,1024,768]{2,1,0:T(8,128)(2,1)} %get-tuple-element.76.refs_3_.refs_5_.refs_2_.refs_1_), channel_id=1, source_target_pairs={{0,1},{1,0},{2,3},{3,2},{4,5},{5,4},{6,7},{7,6},{8,9},{9,8},{10,11... | collective-permute-start | bytes 18874376 | tf_op jit(solution)/shard_map/ppermute | solution.py:580
  116.3 27.1 %collective-permute-start.17 = (bf16[4,1024,768]{2,1,0:T(8,128)(2,1)}, bf16[4,1024,768]{2,1,0:T(8,128)(2,1)}, u32[]{:S(2)}, u32[]{:S(2)}) collective-permute-start(bf16[4,1024,768]{2,1,0:T(8,128)(2,1)} %bitcast.52), channel_id=1, source_target_pairs={{0,1},{1,0},{2,3},{3,2},{4,5},{5,4},{6,7},{7,6},{8,9},{9,8},{10,11... | collective-permute-start | bytes 18874376 | tf_op jit(solution)/shard_map/ppermute | solution.py:580
  129.8 35.1 %collective-permute-start.13 = (bf16[4,1024,768]{2,1,0:T(8,128)(2,1)}, bf16[4,1024,768]{2,1,0:T(8,128)(2,1)}, u32[]{:S(2)}, u32[]{:S(2)}) collective-permute-start(bf16[4,1024,768]{2,1,0:T(8,128)(2,1)} %bitcast.46), channel_id=1, source_target_pairs={{0,1},{1,0},{2,3},{3,2},{4,5},{5,4},{6,7},{7,6},{8,9},{9,8},{10,11... | collective-permute-start | bytes 18874376 | tf_op jit(solution)/shard_map/ppermute | solution.py:580
  141.3 16.0 %collective-permute-start.15 = (bf16[4,2,2,2,24,384]{5,4,3,2,1,0:T(8,128)(2,1)}, bf16[4,2,2,2,24,384]{5,4,3,2,1,0:T(8,128)(2,1)}, u32[]{:S(2)}, u32[]{:S(2)}) collective-permute-start(bf16[4,2,2,2,24,384]{5,4,3,2,1,0:T(8,128)(2,1)} %get-tuple-element.82), channel_id=1, source_target_pairs={{0,2},{1,3},{2,0},{3,1},{4,6},{5,7},{6,4},{7,5},{8,10},{9,11},{10,... | collective-permute-start | bytes 1769480 | tf_op jit(solution)/shard_map/ppermute | solution.py:584
  142.2 15.5 %collective-permute-start.16 = (bf16[4,2,2,2,24,384]{5,4,3,2,1,0:T(8,128)(2,1)}, bf16[4,2,2,2,24,384]{5,4,3,2,1,0:T(8,128)(2,1)}, u32[]{:S(2)}, u32[]{:S(2)}) collective-permute-start(bf16[4,2,2,2,24,384]{5,4,3,2,1,0:T(8,128)(2,1)} %get-tuple-element.84), channel_id=1, source_target_pairs={{0,4},{1,5},{2,6},{3,7},{4,0},{5,1},{6,2},{7,3},{8,12},{9,13},{10,... | collective-permute-start | bytes 1769480 | tf_op jit(solution)/shard_map/ppermute | solution.py:588
  160.8 16.6 %collective-permute-start.20 = (bf16[4,2,2,24,384]{4,3,2,1,0:T(8,128)(2,1)}, bf16[4,2,2,24,384]{4,3,2,1,0:T(8,128)(2,1)}, u32[]{:S(2)}, u32[]{:S(2)}) collective-permute-start(bf16[4,2,2,24,384]{4,3,2,1,0:T(8,128)(2,1)} %get-tuple-element.91), channel_id=1, source_target_pairs={{0,4},{1,5},{2,6},{3,7},{4,0},{5,1},{6,2},{7,3},{8,12},{9,13},{10,... | collective-permute-start | bytes 884744 | tf_op jit(solution)/shard_map/ppermute | solution.py:588
  162.3 16.4 %collective-permute-start.21 = (bf16[4,2,2,24,384]{4,3,2,1,0:T(8,128)(2,1)}, bf16[4,2,2,24,384]{4,3,2,1,0:T(8,128)(2,1)}, u32[]{:S(2)}, u32[]{:S(2)}) collective-permute-start(bf16[4,2,2,24,384]{4,3,2,1,0:T(8,128)(2,1)} %get-tuple-element.93), channel_id=1, source_target_pairs={{0,2},{1,3},{2,0},{3,1},{4,6},{5,7},{6,4},{7,5},{8,10},{9,11},{10,... | collective-permute-start | bytes 884744 | tf_op jit(solution)/shard_map/ppermute | solution.py:584
  162.9 22.3 %collective-permute-start.22 = (bf16[4,2,2,2,24,384]{5,4,3,2,1,0:T(8,128)(2,1)}, bf16[4,2,2,2,24,384]{5,4,3,2,1,0:T(8,128)(2,1)}, u32[]{:S(2)}, u32[]{:S(2)}) collective-permute-start(bf16[4,2,2,2,24,384]{5,4,3,2,1,0:T(8,128)(2,1)} %get-tuple-element.94), channel_id=1, source_target_pairs={{0,2},{1,3},{2,0},{3,1},{4,6},{5,7},{6,4},{7,5},{8,10},{9,11},{10,... | collective-permute-start | bytes 1769480 | tf_op jit(solution)/shard_map/ppermute | solution.py:584
  164.3 20.9 %collective-permute-start.23 = (bf16[4,2,2,2,24,384]{5,4,3,2,1,0:T(8,128)(2,1)}, bf16[4,2,2,2,24,384]{5,4,3,2,1,0:T(8,128)(2,1)}, u32[]{:S(2)}, u32[]{:S(2)}) collective-permute-start(bf16[4,2,2,2,24,384]{5,4,3,2,1,0:T(8,128)(2,1)} %get-tuple-element.96), channel_id=1, source_target_pairs={{0,4},{1,5},{2,6},{3,7},{4,0},{5,1},{6,2},{7,3},{8,12},{9,13},{10,... | collective-permute-start | bytes 1769480 | tf_op jit(solution)/shard_map/ppermute | solution.py:588
  176.1 24.0 %collective-permute-start.18 = (bf16[4,2,2,2,24,384]{5,4,3,2,1,0:T(8,128)(2,1)}, bf16[4,2,2,2,24,384]{5,4,3,2,1,0:T(8,128)(2,1)}, u32[]{:S(2)}, u32[]{:S(2)}) collective-permute-start(bf16[4,2,2,2,24,384]{5,4,3,2,1,0:T(8,128)(2,1)} %get-tuple-element.88), channel_id=1, source_target_pairs={{0,2},{1,3},{2,0},{3,1},{4,6},{5,7},{6,4},{7,5},{8,10},{9,11},{10,... | collective-permute-start | bytes 1769480 | tf_op jit(solution)/shard_map/ppermute | solution.py:584
  177.5 22.6 %collective-permute-start.19 = (bf16[4,2,2,2,24,384]{5,4,3,2,1,0:T(8,128)(2,1)}, bf16[4,2,2,2,24,384]{5,4,3,2,1,0:T(8,128)(2,1)}, u32[]{:S(2)}, u32[]{:S(2)}) collective-permute-start(bf16[4,2,2,2,24,384]{5,4,3,2,1,0:T(8,128)(2,1)} %get-tuple-element.90), channel_id=1, source_target_pairs={{0,4},{1,5},{2,6},{3,7},{4,0},{5,1},{6,2},{7,3},{8,12},{9,13},{10,... | collective-permute-start | bytes 1769480 | tf_op jit(solution)/shard_map/ppermute | solution.py:588
  206.9 13.6 %collective-permute-start.31 = (bf16[4,2,2,24,384]{4,3,2,1,0:T(8,128)(2,1)}, bf16[4,2,2,24,384]{4,3,2,1,0:T(8,128)(2,1)}, u32[]{:S(2)}, u32[]{:S(2)}) collective-permute-start(bf16[4,2,2,24,384]{4,3,2,1,0:T(8,128)(2,1)} %get-tuple-element.109), channel_id=1, source_target_pairs={{0,2},{1,3},{2,0},{3,1},{4,6},{5,7},{6,4},{7,5},{8,10},{9,11},{10,... | collective-permute-start | bytes 884744 | tf_op jit(solution)/shard_map/ppermute | solution.py:584
  208.3 17.7 %collective-permute-start.26 = (bf16[8,24,768]{2,1,0:T(8,128)(2,1)}, bf16[8,24,768]{2,1,0:T(8,128)(2,1)}, u32[]{:S(2)}, u32[]{:S(2)}) collective-permute-start(bf16[8,24,768]{2,1,0:T(8,128)(2,1)} %bitcast.83), channel_id=1, source_target_pairs={{0,0},{1,16},{2,2},{3,18},{4,4},{5,20},{6,6},{7,22},{8,1},{9,17},{... | collective-permute-start | bytes 884744 | tf_op jit(solution)/shard_map/ppermute | solution.py:689
  212.1 16.3 %collective-permute-start.27 = (bf16[8,24,768]{2,1,0:T(8,128)(2,1)}, bf16[8,24,768]{2,1,0:T(8,128)(2,1)}, u32[]{:S(2)}, u32[]{:S(2)}) collective-permute-start(bf16[8,24,768]{2,1,0:T(8,128)(2,1)} %bitcast.82), channel_id=1, source_target_pairs={{0,1},{1,17},{2,3},{3,19},{4,5},{5,21},{6,7},{7,23},{8,0},{9,16},{... | collective-permute-start | bytes 884744 | tf_op jit(solution)/shard_map/ppermute | solution.py:689
  217.1 26.0 %collective-permute-start.28 = (bf16[8,24,768]{2,1,0:T(8,128)(2,1)}, bf16[8,24,768]{2,1,0:T(8,128)(2,1)}, u32[]{:S(2)}, u32[]{:S(2)}) collective-permute-start(bf16[8,24,768]{2,1,0:T(8,128)(2,1)} %bitcast.81), channel_id=1, source_target_pairs={{0,8},{1,24},{2,10},{3,26},{4,12},{5,28},{6,14},{7,30},{8,9},{9,25... | collective-permute-start | bytes 884744 | tf_op jit(solution)/shard_map/ppermute | solution.py:689
  218.4 37.7 %collective-permute-start.29 = (bf16[8,24,768]{2,1,0:T(8,128)(2,1)}, bf16[8,24,768]{2,1,0:T(8,128)(2,1)}, u32[]{:S(2)}, u32[]{:S(2)}) collective-permute-start(bf16[8,24,768]{2,1,0:T(8,128)(2,1)} %bitcast.80), channel_id=1, source_target_pairs={{0,9},{1,25},{2,11},{3,27},{4,13},{5,29},{6,15},{7,31},{8,8},{9,24... | collective-permute-start | bytes 884744 | tf_op jit(solution)/shard_map/ppermute | solution.py:689
  223.3 32.8 %collective-permute-start.32 = (bf16[4,24,768]{2,1,0:T(8,128)(2,1)}, bf16[4,24,768]{2,1,0:T(8,128)(2,1)}, u32[]{:S(2)}, u32[]{:S(2)}) collective-permute-start(bf16[4,24,768]{2,1,0:T(8,128)(2,1)} %bitcast.86), channel_id=1, source_target_pairs={{0,0},{1,16},{2,2},{3,18},{4,4},{5,20},{6,6},{7,22},{8,1},{9,17},{... | collective-permute-start | bytes 442376 | tf_op jit(solution)/shard_map/ppermute | solution.py:689
  226.1 30.0 %collective-permute-start.33 = (bf16[4,24,768]{2,1,0:T(8,128)(2,1)}, bf16[4,24,768]{2,1,0:T(8,128)(2,1)}, u32[]{:S(2)}, u32[]{:S(2)}) collective-permute-start(bf16[4,24,768]{2,1,0:T(8,128)(2,1)} %bitcast.85), channel_id=1, source_target_pairs={{0,1},{1,17},{2,3},{3,19},{4,5},{5,21},{6,7},{7,23},{8,0},{9,16},{... | collective-permute-start | bytes 442376 | tf_op jit(solution)/shard_map/ppermute | solution.py:689
  228.4 27.7 %collective-permute-start.34 = (bf16[4,24,768]{2,1,0:T(8,128)(2,1)}, bf16[4,24,768]{2,1,0:T(8,128)(2,1)}, u32[]{:S(2)}, u32[]{:S(2)}) collective-permute-start(bf16[4,24,768]{2,1,0:T(8,128)(2,1)} %bitcast.84), channel_id=1, source_target_pairs={{0,8},{1,24},{2,10},{3,26},{4,12},{5,28},{6,14},{7,30},{8,9},{9,25... | collective-permute-start | bytes 442376 | tf_op jit(solution)/shard_map/ppermute | solution.py:689
  259.9 38.7 %all-to-all-start.1 = ((bf16[32,24,768]{2,1,0:T(8,128)(2,1)}), bf16[32,24,768]{2,1,0:T(8,128)(2,1)}, u32[]{:S(2)}, u32[]{:S(2)}) async-start(bf16[32,24,768]{2,1,0:T(8,128)(2,1)} %get-tuple-element.122), calls=%async_computation.1 | async-start | bytes 2359296 | tf_op jit(solution)/shard_map/all_to_all | solution.py:886
  280.3 18.2 %collective-permute-start.41 = (f32[16,768]{1,0:T(8,128)}, f32[16,768]{1,0:T(8,128)}, u32[]{:S(2)}, u32[]{:S(2)}) collective-permute-start(f32[16,768]{1,0:T(8,128)} %add_add_fusion.1.refs_0_), channel_id=1, source_target_pairs={{0,16},{1,17},{2,18},{3,19},{4,20},{5,21},{6,22},{7,23},{8,24},{9,... | collective-permute-start | bytes 147464 | tf_op jit(solution)/shard_map/ppermute | solution.py:698
  304.2 32.6 %all-to-all-start.2 = ((bf16[32,24,768]{2,1,0:T(8,128)(2,1)}), bf16[32,24,768]{2,1,0:T(8,128)(2,1)}, u32[]{:S(2)}, u32[]{:S(2)}) async-start(bf16[32,24,768]{2,1,0:T(8,128)(2,1)} %bitcast.68), calls=%async_computation.2 | async-start | bytes 2359296 | tf_op jit(solution)/shard_map/all_to_all | solution.py:886
  (35 other events, 451.8 us)
Sparse Core Ops, SparseCore 0:
  11.0 91.7 all-gather.1
